TPU v7x, 512 devices: a whole 4x4x16 slice. The times are simulated.
512 devices in a mesh: dp: 4 (over y), expert: 8 (over x, core), ctx: 16 (over z).
Axes of the slice: x: 4, y: 4, z: 16, core: 2. Of those that a mesh axis runs over, the one named last changes fastest.
Arguments:
- mamba_in: bfloat16 [4, 4096, 4096], P('dp', 'ctx', 'expert'), may hold values from -6 to 6
- shared_in: bfloat16 [4, 4096, 256], P('dp', 'ctx'), may hold values from -6 to 6
- dt_raw: float32 [4, 64, 4096], P('dp', 'expert', 'ctx'), may hold values from -3 to 3
- dt_bias: float32 [64], P('expert'), may hold values from -1 to 0.5
- a_log: float32 [64], P('expert'), as said below
- d_skip: float32 [64], P('expert'), may hold values from 0.5 to 1.5
- conv_x: float32 [4, 4096], P(None, 'expert'), may hold values from -3 to 3
- conv_bc: float32 [4, 256], replicated, may hold values from -1.5 to 1.5
- mamba_cot: bfloat16 [4, 4096, 4096], P('dp', 'ctx', 'expert'), may hold values from -6 to 6
- moe_in: bfloat16 [4, 4096, 4096], P('dp', 'expert', 'ctx'), may hold values from -6 to 6
- moe_cot: bfloat16 [4, 4096, 4096], P('dp', 'expert', 'ctx'), may hold values from -6 to 6
- slot_tok: int32 [4, 8, 8, 128], P('dp', 'expert'), may hold values from 0 to 511, as said below
- slot_count: int32 [4, 8, 8], P('dp', 'expert'), may hold values from 32 to 128, as said below
- route_w: bfloat16 [4, 8, 8, 128], P('dp', 'expert'), may hold values from 0.049804688 to 0.5
- w_gate: bfloat16 [8, 4096, 768], P('expert', 'ctx'), may hold values from -0.09375 to 0.09375
- w_up: bfloat16 [8, 4096, 768], P('expert', 'ctx'), may hold values from -0.09375 to 0.09375
- w_down: bfloat16 [8, 768, 4096], P('expert', None, 'ctx'), may hold values from -0.21875 to 0.21875
- gate_act: bfloat16 [4, 8, 1024, 768], P('dp', 'expert', 'ctx'), may hold values from -6 to 6
- up_act: bfloat16 [4, 8, 1024, 768], P('dp', 'expert', 'ctx'), may hold values from -6 to 6
Outputs:
- d_mamba_in: bfloat16 [4, 4096, 4096], P('dp', 'ctx', 'expert')
- d_shared_in: bfloat16 [4, 4096, 256], P('dp', 'ctx')
- d_dt_raw: float32 [4, 64, 4096], P('dp', 'expert', 'ctx')
- d_conv_x: float32 [4, 4096], P('dp', 'expert')
- d_conv_bc: float32 [4, 256], P('dp')
- d_a_log: float32 [64], P('expert')
- d_moe_in: bfloat16 [4, 4096, 4096], P('dp', 'expert', 'ctx')
- d_route: float32 [4, 8, 8, 128], P('dp', 'expert')
- d_w_gate: bfloat16 [8, 4096, 768], P('expert', 'ctx', 'dp')
- d_w_up: bfloat16 [8, 4096, 768], P('expert', 'ctx', 'dp')
- d_w_down: bfloat16 [8, 768, 4096], P('expert', 'dp', 'ctx')
Inputs may be any that keep to these rules, and one draw needn't show every extreme that they name: slot_tok[r, s, e, k] is a token of source s's 512 tokens; the live slots of one group name distinct tokens; slots at k >= slot_count[r, s, e] are padding and are ignored; a token may be live in the groups of several experts. `slot_count`: in every replica one expert receives a full group of 128 live slots from every source. exp(a_log) lies between 0.2 / 4096 and 0.1.
All inputs are finite; a program needn't handle non-finite values.
Results may differ from a plain program's by a relative error of at most 0.02.
Values may be sent and summed in bfloat16 or wider, within the bound.
No kernel may reach another device: no remote copies, remote signals or barrier semaphores. Data moves between devices by JAX's collectives and lax.ppermute only.
A program may use at most 128 MiB of HBM per device.

v0:
```python
import jax
import jax.numpy as jnp
from jax import lax
from jax.sharding import PartitionSpec as P

PRECISE = lax.Precision.HIGHEST


def passed_along(value, axis, steps):
    count = lax.axis_size(axis)
    first, last = (max(0, -steps), min(count, count - steps))
    return lax.ppermute(value, axis, [(source, source + steps) for source in range(first, last)])


def prefix(shard, axis, join, neutral):
    place = lax.axis_index(axis)
    gathered = jax.tree.map(
        lambda a, kind: lax.all_gather(a.astype(kind), axis), shard, (jnp.bfloat16, jnp.bfloat16)
    )
    state = jax.tree.map(lambda a, e: jnp.zeros_like(a) + jnp.asarray(e, a.dtype), shard, neutral)

    def one(step, state):
        return join(
            state,
            jax.tree.map(
                lambda a, own: lax.dynamic_index_in_dim(a, step, 0, False).astype(own.dtype),
                gathered,
                shard,
            ),
        )

    return lax.fori_loop(0, place, one, state)


def carried_in(value, axis, join, neutral):
    count, mine = (lax.axis_size(axis), lax.axis_index(axis))
    pieces = jax.tree.map(lambda part: lax.all_gather(part, axis), value)
    pieces = jax.tree.map(lambda part: part[::-1], pieces)
    mine = count - 1 - mine
    so_far = jax.tree.map(
        lambda part, zero: jnp.full_like(part, 0) + jnp.asarray(zero, part.dtype), value, neutral
    )

    def step(position, so_far):
        longer = join(so_far, jax.tree.map(lambda part: part[position], pieces))
        return jax.tree.map(lambda new, old: jnp.where(position < mine, new, old), longer, so_far)

    return lax.fori_loop(0, count - 1, step, so_far)


def causal_taps(padded_values, kernel):
    taps_count = kernel.shape[0]
    length = padded_values.shape[0] - taps_count + 1
    summed = kernel[0][None, :] * padded_values[0:length]
    for offset in range(1, taps_count):
        summed = summed + kernel[offset][None, :] * padded_values[offset : offset + length]
    return summed


def conv_front(padded_values, kernel):
    return jax.nn.silu(causal_taps(padded_values, kernel))


def state_block(heads_in, b_rows, c_rows, step_size, log_decay, skip_gain, state_in):
    length = heads_in.shape[0]
    cumulative = jnp.cumsum(log_decay, axis=1)
    lower_mask = jnp.tril(jnp.ones((length, length), dtype=bool))
    spacing = jnp.where(lower_mask[None], cumulative[:, :, None] - cumulative[:, None, :], 0.0)
    decays = jnp.where(lower_mask[None], jnp.exp(spacing), 0.0)
    scores = jnp.dot(c_rows, b_rows.T, precision=PRECISE)
    mixing = decays * scores[None] * step_size[:, None, :]
    output = jnp.einsum("hts,shp->thp", mixing, heads_in, precision=PRECISE)
    carried = jnp.einsum("tn,hpn->thp", c_rows, state_in, precision=PRECISE)
    output = (
        output + jnp.exp(cumulative).T[:, :, None] * carried + skip_gain[None, :, None] * heads_in
    )
    ending = cumulative[:, -1]
    tail_weight = jnp.exp(ending[:, None] - cumulative) * step_size
    fresh_state = jnp.einsum("ht,thp,tn->hpn", tail_weight, heads_in, b_rows, precision=PRECISE)
    return (output, jnp.exp(ending)[:, None, None] * state_in + fresh_state)


def affine_join(earlier, later):
    return (earlier[0] * later[0], later[0][:, None, None] * earlier[1] + later[1])


def hidden_from(gate_vals, up_vals):
    return (jax.nn.silu(gate_vals) * up_vals).astype(jnp.bfloat16)


def hidden_grads(grad_hidden, gate_vals, up_vals):
    sigmoid_vals = jax.nn.sigmoid(gate_vals)
    activated = gate_vals * sigmoid_vals
    slope = sigmoid_vals * (1.0 + gate_vals * (1.0 - sigmoid_vals))
    return (
        (grad_hidden * up_vals * slope).astype(jnp.bfloat16),
        (grad_hidden * activated).astype(jnp.bfloat16),
    )


def body(
    mamba_in,
    shared_in,
    dt_raw,
    dt_bias,
    a_log,
    d_skip,
    conv_x,
    conv_bc,
    mamba_cot,
    moe_in,
    moe_cot,
    slot_tok,
    slot_count,
    route_w,
    w_gate,
    w_up,
    w_down,
    gate_act,
    up_act,
):
    rim_rows = conv_x.shape[0] - 1
    head_rows = mamba_in[0]
    shared_rows = shared_in[0]
    length = head_rows.shape[0]
    heads_here = dt_bias.shape[0]
    head_width = head_rows.shape[1] // heads_here
    state_width = shared_rows.shape[1] // 2
    before_heads, before_shared = passed_along(
        (head_rows[length - rim_rows :], shared_rows[length - rim_rows :]), "ctx", 1
    )
    padded_heads = jnp.concatenate([before_heads, head_rows], axis=0).astype(jnp.float32)
    padded_shared = jnp.concatenate([before_shared, shared_rows], axis=0).astype(jnp.float32)
    conv_heads, pull_heads = jax.vjp(conv_front, padded_heads, conv_x)
    conv_shared, pull_shared = jax.vjp(conv_front, padded_shared, conv_bc)
    b_rows = conv_shared[:, :state_width]
    c_rows = conv_shared[:, state_width:]
    heads_in = conv_heads.reshape(length, heads_here, head_width)
    raw_step = dt_raw[0]
    step_size = jax.nn.softplus(raw_step + dt_bias[:, None])
    log_decay = -jnp.exp(a_log)[:, None] * step_size
    cumulative = jnp.cumsum(log_decay, axis=1)
    block_decay = jnp.exp(cumulative[:, -1])
    tail_weight = jnp.exp(cumulative[:, -1:] - cumulative) * step_size
    local_state = jnp.einsum("ht,thp,tn->hpn", tail_weight, heads_in, b_rows, precision=PRECISE)
    cotangent = mamba_cot[0].astype(jnp.float32).reshape(length, heads_here, head_width)
    local_pull = jnp.einsum(
        "ht,thp,tn->hpn", jnp.exp(cumulative), cotangent, c_rows, precision=PRECISE
    )
    neutral = (jnp.ones_like(block_decay), jnp.zeros_like(local_state))
    entering = prefix((block_decay, local_state), "ctx", affine_join, neutral)[1]
    leaving_grad = carried_in((block_decay, local_pull), "ctx", affine_join, neutral)[1]

    def core(heads_arg, b_arg, c_arg, step_arg, rate_arg, state_arg):
        sizes_now = jax.nn.softplus(step_arg + dt_bias[:, None])
        decay_now = -jnp.exp(rate_arg)[:, None] * sizes_now
        return state_block(heads_arg, b_arg, c_arg, sizes_now, decay_now, d_skip, state_arg)

    _, pull_core = jax.vjp(core, heads_in, b_rows, c_rows, raw_step, a_log, entering)
    grad_heads, grad_b, grad_c, grad_step, grad_rate, _ = pull_core((cotangent, leaving_grad))
    total_b, total_c = (
        lax.psum(grad_b.astype(jnp.bfloat16), "expert").astype(jnp.float32),
        lax.psum(grad_c.astype(jnp.bfloat16), "expert").astype(jnp.float32),
    )
    grad_padded_heads, grad_kernel_heads = pull_heads(
        grad_heads.reshape(length, heads_here * head_width)
    )
    grad_padded_shared, grad_kernel_shared = pull_shared(
        jnp.concatenate([total_b, total_c], axis=1)
    )
    after_heads, after_shared = passed_along(
        (grad_padded_heads[:rim_rows], grad_padded_shared[:rim_rows]), "ctx", -1
    )
    edge_pad = ((length - rim_rows, 0), (0, 0))
    grad_mamba_in = (grad_padded_heads[rim_rows:] + jnp.pad(after_heads, edge_pad)).astype(
        jnp.bfloat16
    )[None]
    grad_shared_in = (grad_padded_shared[rim_rows:] + jnp.pad(after_shared, edge_pad)).astype(
        jnp.bfloat16
    )[None]
    col_width = moe_in.shape[2]
    token_count = moe_in.shape[1]
    expert_count = slot_tok.shape[2]
    slot_width = slot_tok.shape[3]
    slot_ids = slot_tok[0, 0]
    live_slots = jnp.arange(slot_width, dtype=jnp.int32)[None, :] < slot_count[0, 0][:, None]
    flat_ids = slot_ids.reshape(-1)
    flat_live = live_slots.reshape(-1)
    zero_half = jnp.zeros((), jnp.bfloat16)
    send_in = jnp.where(
        flat_live[:, None], jnp.take(moe_in[0], flat_ids, axis=0), zero_half
    ).reshape(expert_count, slot_width, col_width)
    send_cot = jnp.where(
        flat_live[:, None], jnp.take(moe_cot[0], flat_ids, axis=0), zero_half
    ).reshape(expert_count, slot_width, col_width)
    send_weight = jnp.where(live_slots, route_w[0, 0], zero_half)
    rows_in, rows_cot, rows_weight = (
        lax.all_to_all(send_in, "expert", split_axis=0, concat_axis=0, tiled=True),
        lax.all_to_all(send_cot, "expert", split_axis=0, concat_axis=0, tiled=True),
        lax.all_to_all(send_weight, "expert", split_axis=0, concat_axis=0, tiled=True),
    )
    row_total = rows_in.shape[0] * slot_width
    rows_in = rows_in.reshape(row_total, col_width)
    rows_cot = rows_cot.reshape(row_total, col_width)
    scaled_cot = (
        rows_weight.reshape(row_total).astype(jnp.float32)[:, None] * rows_cot.astype(jnp.float32)
    ).astype(jnp.bfloat16)
    gate_share = gate_act[0, 0]
    up_share = up_act[0, 0]
    weight_down = w_down[0]
    gate_rows, up_rows = (
        lax.all_gather(gate_share, "ctx", axis=0, tiled=True),
        lax.all_gather(up_share, "ctx", axis=0, tiled=True),
    )
    gate_vals = gate_rows.astype(jnp.float32)
    up_vals = up_rows.astype(jnp.float32)
    hidden = hidden_from(gate_vals, up_vals)
    partial_grad = jnp.dot(scaled_cot, weight_down.T, preferred_element_type=jnp.float32)
    grad_hidden = lax.psum(partial_grad.astype(jnp.bfloat16), "ctx").astype(jnp.float32)
    grad_gate_rows, grad_up_rows = hidden_grads(grad_hidden, gate_vals, up_vals)
    expert_out = jnp.dot(hidden, weight_down, preferred_element_type=jnp.float32)
    route_part = jnp.sum(rows_cot.astype(jnp.float32) * expert_out, axis=1)
    grad_down = jnp.einsum("rf,rd->fd", hidden, scaled_cot, preferred_element_type=jnp.float32)
    grad_gate = jnp.einsum("rd,rf->df", rows_in, grad_gate_rows, preferred_element_type=jnp.float32)
    grad_up = jnp.einsum("rd,rf->df", rows_in, grad_up_rows, preferred_element_type=jnp.float32)
    rows_grad = jnp.dot(grad_gate_rows, w_gate[0].T, preferred_element_type=jnp.float32)
    rows_grad = rows_grad + jnp.dot(grad_up_rows, w_up[0].T, preferred_element_type=jnp.float32)
    route_part = lax.psum(route_part, "ctx")
    back_rows, back_route = (
        lax.all_to_all(
            rows_grad.reshape(expert_count, slot_width, col_width).astype(jnp.bfloat16),
            "expert",
            split_axis=0,
            concat_axis=0,
            tiled=True,
        ).astype(jnp.float32),
        lax.all_to_all(
            route_part.reshape(expert_count, slot_width).astype(jnp.bfloat16),
            "expert",
            split_axis=0,
            concat_axis=0,
            tiled=True,
        ).astype(jnp.float32),
    )
    token_index = jnp.arange(token_count, dtype=jnp.int32)
    scatter_table = jnp.where(
        (flat_ids[None, :] == token_index[:, None]) & flat_live[None, :], 1.0, 0.0
    ).astype(jnp.float32)
    grad_tokens = jnp.dot(scatter_table, back_rows.reshape(-1, col_width), precision=PRECISE)
    kernel_heads_sum, kernel_shared_sum, rate_sum = lax.psum(
        (grad_kernel_heads, grad_kernel_shared, grad_rate), "ctx"
    )
    route_total = back_route
    route_total = jnp.where(live_slots, route_total, 0.0)
    gate_parts, up_parts = (
        lax.all_to_all(
            grad_gate[None].astype(jnp.bfloat16), "dp", split_axis=2, concat_axis=0, tiled=True
        ).astype(jnp.float32),
        lax.all_to_all(
            grad_up[None].astype(jnp.bfloat16), "dp", split_axis=2, concat_axis=0, tiled=True
        ).astype(jnp.float32),
    )
    down_parts, heads_parts, shared_parts = (
        lax.all_to_all(
            grad_down[None].astype(jnp.bfloat16), "dp", split_axis=1, concat_axis=0, tiled=True
        ).astype(jnp.float32),
        lax.all_to_all(
            kernel_heads_sum[None].astype(jnp.bfloat16),
            "dp",
            split_axis=1,
            concat_axis=0,
            tiled=True,
        ).astype(jnp.float32),
        lax.all_to_all(
            kernel_shared_sum[None].astype(jnp.bfloat16),
            "dp",
            split_axis=1,
            concat_axis=0,
            tiled=True,
        ).astype(jnp.float32),
    )
    rate_parts = lax.all_gather(rate_sum[None], "dp", axis=0, tiled=True)
    gate_total = jnp.sum(gate_parts, axis=0)
    up_total = jnp.sum(up_parts, axis=0)
    down_total = jnp.sum(down_parts, axis=0)
    taps_heads = jnp.sum(heads_parts, axis=0)
    taps_shared = jnp.sum(shared_parts, axis=0)
    rate_total = jnp.sum(rate_parts, axis=0)
    return (
        grad_mamba_in,
        grad_shared_in,
        grad_step[None],
        taps_heads,
        taps_shared,
        rate_total,
        grad_tokens.astype(jnp.bfloat16)[None],
        route_total[None, None],
        gate_total.astype(jnp.bfloat16)[None],
        up_total.astype(jnp.bfloat16)[None],
        down_total.astype(jnp.bfloat16)[None],
    )


def solution(mesh):
    placed = (
        P("dp", "ctx", "expert"),
        P("dp", "ctx", None),
        P("dp", "expert", "ctx"),
        P("expert"),
        P("expert"),
        P("expert"),
        P(None, "expert"),
        P(),
        P("dp", "ctx", "expert"),
        P("dp", "expert", "ctx"),
        P("dp", "expert", "ctx"),
        P("dp", "expert", None, None),
        P("dp", "expert", None),
        P("dp", "expert", None, None),
        P("expert", "ctx", None),
        P("expert", "ctx", None),
        P("expert", None, "ctx"),
        P("dp", "expert", "ctx", None),
        P("dp", "expert", "ctx", None),
    )
    return jax.shard_map(
        body,
        mesh=mesh,
        in_specs=placed,
        out_specs=(
            P("dp", "ctx", "expert"),
            P("dp", "ctx", None),
            P("dp", "expert", "ctx"),
            P("dp", "expert"),
            P("dp", None),
            P("expert"),
            P("dp", "expert", "ctx"),
            P("dp", "expert", None, None),
            P("expert", "ctx", "dp"),
            P("expert", "ctx", "dp"),
            P("expert", "dp", "ctx"),
        ),
        check_vma=False,
    )
```

profile of v0, /device:TPU:1, one launch (start us, length us, event | category | flops | bytes accessed | tf_op | source)
XLA Modules:
  0.0 700.2 jit_solution(2382496062535985719)
XLA Ops:
  8.1 4.4 collective-permute-start
  21.2 7.0 %all-to-all-start.2 = ((bf16[8,1,128]{2,1,0:T(2,128)(2,1)}), bf16[8,1,128]{2,1,0:T(2,128)(2,1)S(1)}, u32[]{:S(2)}, u32[]{:S(2)}) async-start(bf16[8,1,128]{2,1,0:T(2,128)(2,1)} %copy.80), calls=%async_computation.2 | async-start | bytes 8192 | tf_op jit(solution)/shard_map/all_to_all | solution.py:200
  28.3 3.9 gather_fusion
  32.3 3.9 gather_fusion.1
  38.8 4.8 all-to-all-start.3
  43.7 9.5 %all-to-all-done.3 = bf16[8,128,256]{1,2,0:T(8,128)(2,1)S(1)} async-done(((bf16[8,128,256]{1,2,0:T(8,128)(2,1)}), bf16[8,128,256]{1,2,0:T(8,128)(2,1)S(1)}, u32[]{:S(2)}, u32[]{:S(2)}) %all-to-all-start.3) | async-done | bytes 524320 | tf_op jit(solution)/shard_map/all_to_all | solution.py:199
  57.9 5.2 all-to-all-start.6
  66.2 29.2 %all-reduce.19 = f32[128]{0:T(128)S(1)} all-reduce(f32[128]{0:T(128)S(1)} %dynamic-update-slice), channel_id=2, replica_groups=mesh['dp'=4,'expert'=8,'ctx'=16] {'ctx'}, use_global_device_ids=true, to_apply=%add.19 | all-reduce | flops 128 | bytes 1024
  97.1 4.7 rev.7
  101.9 16.4 %while.27 = (s32[]{:T(128)}, f32[8,64,128]{2,1,0:T(8,128)S(1)}, s32[]{:T(128)}, f32[16,8]{1,0:T(8,128)S(1)}, f32[16,8,64,128]{3,2,1,0:T(8,128)}, /*index=5*/s32[]{:T(128)}, s32[]{:T(128)}) while((s32[]{:T(128)}, f32[8,64,128]{2,1,0:T(8,128)S(1)}, s32[]{:T(128)}, f32[16,8]{1,0:T(8,128)S(1)}, f32[16,8,64,128]{3,2,1,0:T(8,128)}, ...), condition=%wide.region_3.4_spmd.clone, body=%wide.region_2.3_spmd.clone.sunk | while | flops 262148 | bytes 786633 | solution.py:48
  126.3 108.6 %all-reduce.26.cloned.1.call-done = bf16[1024,768]{1,0:T(8,128)(2,1)} async-done(((bf16[1024,768]{1,0:T(8,128)(2,1)}), bf16[1024,768]{1,0:T(8,128)(2,1)}) %all-reduce.26.cloned.1.call-update) | async-done | bytes 1572880 | tf_op jit(solution)/shard_map/psum | solution.py:219
  234.8 70.3 %all-gather.16.cloned.1.call-done = bf16[1,1,1024,768]{3,2,1,0:T(8,128)(2,1)} async-done(((bf16[1,1,64,768]{3,2,1,0:T(8,128)(2,1)}), bf16[1,1,1024,768]{3,2,1,0:T(8,128)(2,1)}) %all-gather.16.cloned.1.call-update) | async-done | bytes 1572880 | tf_op jit(solution)/shard_map/all_gather | solution.py:213
  305.1 71.4 %all-gather.18.cloned.1.call-done = bf16[1,1,1024,768]{3,2,1,0:T(8,128)(2,1)} async-done(((bf16[1,1,64,768]{3,2,1,0:T(8,128)(2,1)}), bf16[1,1,1024,768]{3,2,1,0:T(8,128)(2,1)}) %all-gather.18.cloned.1.call-update) | async-done | bytes 1572880 | tf_op jit(solution)/shard_map/all_gather | solution.py:212
  376.6 4.5 fusion.1
  384.4 4.7 reduce.34
  391.0 4.3 all-to-all-start.9
  401.2 4.7 reduce.32
  413.2 4.7 reduce.33
  419.8 4.1 all-to-all-start.7
  427.0 3.2 all-to-all-done.7
  430.2 4.1 all-to-all-start.8
  437.1 4.9 all-to-all-done.8
  442.0 17.3 %all-to-all-start.4 = ((bf16[8,128,256]{2,1,0:T(8,128)(2,1)}), bf16[8,128,256]{2,1,0:T(8,128)(2,1)S(1)}, u32[]{:S(2)}, u32[]{:S(2)}) async-start(bf16[8,128,256]{2,1,0:T(8,128)(2,1)} %bitcast.269), calls=%async_computation.4 | async-start | bytes 1048576 | tf_op jit(solution)/shard_map/all_to_all | solution.py:230
  459.7 22.1 %all-reduce.20 = bf16[128]{0:T(256)(128)(2,1)S(1)} all-reduce(bf16[128]{0:T(256)(128)(2,1)S(1)} %dynamic-update-slice.1), channel_id=7, replica_groups=mesh['dp'=4,'expert'=8,'ctx'=16] {'ctx'}, use_global_device_ids=true, to_apply=%add.20 | all-reduce | flops 128 | bytes 512
  510.1 87.1 %all-reduce.28.cloned.1.call-done = (bf16[256,128]{1,0:T(8,128)(2,1)}, bf16[256,128]{1,0:T(8,128)(2,1)}) async-done(((bf16[256,128]{1,0:T(8,128)(2,1)}, bf16[256,128]{1,0:T(8,128)(2,1)}), (bf16[256,128]{1,0:T(8,128)(2,1)}, bf16[256,128]{1,0:T(8,128)(2,1)})) %all-reduce.28.cloned.1.call-update) | async-done | bytes 131088 | tf_op jit(solution)/shard_map/psum | solution.py:163
  598.4 42.5 %all-reduce.21 = (bf16[4,512]{1,0:T(4,128)(2,1)S(1)}, bf16[4,256]{1,0:T(4,128)(2,1)S(1)}, f32[1,8]{1,0:T(1,128)S(1)}, bf16[1024]{0:T(1024)(128)(2,1)S(1)}) all-reduce(f32[4,512]{1,0:T(4,128)S(1)} %pad_add_fusion.3, f32[4,256]{1,0:T(4,128)S(1)} %pad_add_fusion.5, ...), channel_id=1, replica_groups=mesh['dp'=4,'expert'=8,'ctx'=16] {'ctx'}, use_global_device_ids=true, to_apply=%region_21.22 | all-reduce | flops 4104 | bytes 24640 | tf_op jit(solution)/shard_map/psum | solution.py:250
  642.2 4.0 all-to-all-start.1
  646.4 7.8 %all-gather.6 = f32[4,1,8]{2,1,0:T(1,128)S(1)} all-gather(f32[1,1,8]{2,1,0:T(1,128)S(1)} %bitcast.323), channel_id=1, replica_groups=mesh['dp'=4,'expert'=8,'ctx'=16] {'dp'}, dimensions={0}, use_global_device_ids=true | all-gather | bytes 160 | tf_op jit(solution)/shard_map/all_gather | solution.py:282
  658.0 22.2 %all-to-all-start.5 = ((bf16[8,1,128]{2,1,0:T(2,128)(2,1)}), bf16[8,1,128]{2,1,0:T(2,128)(2,1)S(1)}, u32[]{:S(2)}, u32[]{:S(2)}) async-start(bf16[8,1,128]{2,1,0:T(2,128)(2,1)} %copy.84), calls=%async_computation.5 | async-start | bytes 8192 | tf_op jit(solution)/shard_map/all_to_all | solution.py:237
  680.7 3.9 all-to-all-done.5
  684.6 3.2 all-to-all-start
  688.6 3.4 all-to-all-done
  (305 shorter events, 107.8 us)
Async XLA Ops:
  7.2 46.4 %copy-start = (bf16[1,768,256]{2,1,0:T(8,128)(2,1)S(1)}, bf16[1,768,256]{2,1,0:T(8,128)(2,1)}, u32[]{:S(2)}) copy-start(bf16[1,768,256]{2,1,0:T(8,128)(2,1)} %param.41) | copy-start | bytes 1179652
  7.2 89.9 %all-gather.12.cloned.1.call-start = ((), (), s32[]{:S(2)}) async-start(), calls=%async_computation.11 | async-start | bytes 4456448 | tf_op jit(solution)/shard_map/all_gather | solution.py:37
  8.1 9.3 %collective-permute-start = (bf16[3,256]{1,0:T(4,128)(2,1)S(1)}, bf16[3,256]{1,0:T(4,128)(2,1)S(1)}, u32[]{:S(2)}, u32[]{:S(2)}) collective-permute-start(bf16[3,256]{1,0:T(4,128)(2,1)S(1)} %slice_bitcast_fusion.1), channel_id=1, source_target_pairs={{0,1},{1,2},{2,3},{3,4},{4,5},{5,6},{6,7},{7,8},{8,9},{9,10},{10,1... | collective-permute-start | bytes 4616 | tf_op jit(solution)/shard_map/ppermute | solution.py:12
  19.2 105.7 %copy-start.6 = (f32[256,256]{1,0:T(8,128)}, f32[256,256]{1,0:T(8,128)S(1)}, u32[]{:S(2)}) copy-start(f32[256,256]{1,0:T(8,128)S(1)} %get-tuple-element.226) | copy-start | bytes 786436
  21.2 17.6 %all-to-all-start.2 = ((bf16[8,1,128]{2,1,0:T(2,128)(2,1)}), bf16[8,1,128]{2,1,0:T(2,128)(2,1)S(1)}, u32[]{:S(2)}, u32[]{:S(2)}) async-start(bf16[8,1,128]{2,1,0:T(2,128)(2,1)} %copy.80), calls=%async_computation.2 | async-start | bytes 8192 | tf_op jit(solution)/shard_map/all_to_all | solution.py:200
  38.8 14.3 %all-to-all-start.3 = ((bf16[8,128,256]{1,2,0:T(8,128)(2,1)}), bf16[8,128,256]{1,2,0:T(8,128)(2,1)S(1)}, u32[]{:S(2)}, u32[]{:S(2)}) async-start(bf16[8,128,256]{1,2,0:T(8,128)(2,1)} %copy.81), calls=%async_computation.3 | async-start | bytes 1048576 | tf_op jit(solution)/shard_map/all_to_all | solution.py:199
  43.6 191.2 %all-reduce.26.cloned.1.call-start = ((), (), s32[]{:S(2)}) async-start(), calls=%async_computation.10 | async-start | bytes 3145728 | tf_op jit(solution)/shard_map/psum | solution.py:219
  55.4 40.1 %copy-start.35 = (f32[8]{0:T(128)S(1)}, f32[8]{0:T(128)}, u32[]{:S(2)}) copy-start(f32[8]{0:T(128)} %param.28) | copy-start | bytes 100
  55.4 40.2 %copy-start.53 = (f32[4,512]{1,0:T(4,128)S(1)}, f32[4,512]{1,0:T(4,128)}, u32[]{:S(2)}) copy-start(f32[4,512]{1,0:T(4,128)} %param.31) | copy-start | bytes 24580
  55.4 249.7 %all-gather.16.cloned.1.call-start = ((), (), s32[]{:S(2)}) async-start(), calls=%async_computation.13 | async-start | bytes 1671168 | tf_op jit(solution)/shard_map/all_gather | solution.py:213
  56.2 40.6 %collective-permute-start.1 = (bf16[3,512]{1,0:T(4,128)(2,1)S(1)}, bf16[3,512]{1,0:T(4,128)(2,1)S(1)}, u32[]{:S(2)}, u32[]{:S(2)}) collective-permute-start(bf16[3,512]{1,0:T(4,128)(2,1)S(1)} %slice_bitcast_fusion), channel_id=1, source_target_pairs={{0,1},{1,2},{2,3},{3,4},{4,5},{5,6},{6,7},{7,8},{8,9},{9,10},{10,1... | collective-permute-start | bytes 9224 | tf_op jit(solution)/shard_map/ppermute | solution.py:12
  57.9 333.0 %all-to-all-start.6 = ((bf16[8,128,256]{2,1,0:T(8,128)(2,1)}), bf16[8,128,256]{2,1,0:T(8,128)(2,1)}, u32[]{:S(2)}, u32[]{:S(2)}) async-start(bf16[8,128,256]{2,1,0:T(8,128)(2,1)} %bitcast.83), calls=%async_computation.6 | async-start | bytes 1048576 | tf_op jit(solution)/shard_map/all_to_all | solution.py:198
  63.1 313.4 %all-gather.18.cloned.1.call-start = ((), (), s32[]{:S(2)}) async-start(), calls=%async_computation.14 | async-start | bytes 1671168 | tf_op jit(solution)/shard_map/all_gather | solution.py:212
  63.7 439.7 %all-gather.14.cloned.1.call-start = ((), (), s32[]{:S(2)}) async-start(), calls=%async_computation.12 | async-start | bytes 2228224 | tf_op jit(solution)/shard_map/all_gather | solution.py:18
  63.8 55.1 %copy-start.24 = (pred[256,256]{1,0:T(8,128)(4,1)}, pred[256,256]{1,0:T(8,128)(4,1)S(1)}, u32[]{:S(2)}) copy-start(pred[256,256]{1,0:T(8,128)(4,1)S(1)} %iota_compare_fusion.1) | copy-start | bytes 196612
  125.0 180.2 %copy-start.4 = (f32[256,512]{0,1:T(8,128)}, f32[256,512]{0,1:T(8,128)S(1)}, u32[]{:S(2)}) copy-start(f32[256,512]{0,1:T(8,128)S(1)} %copy.75) | copy-start | bytes 1572868
  391.0 28.8 %all-to-all-start.9 = ((bf16[4,2,24576]{2,1,0:T(2,128)(2,1)}), bf16[4,2,24576]{2,1,0:T(2,128)(2,1)}, u32[]{:S(2)}, u32[]{:S(2)}) async-start(bf16[4,2,24576]{2,1,0:T(2,128)(2,1)} %reshape.555), calls=%async_computation.9 | async-start | bytes 786432 | tf_op jit(solution)/shard_map/all_to_all | solution.py:264
  419.8 10.4 %all-to-all-start.7 = ((bf16[4,2,24576]{2,1,0:T(2,128)(2,1)}), bf16[4,2,24576]{2,1,0:T(2,128)(2,1)}, u32[]{:S(2)}, u32[]{:S(2)}) async-start(bf16[4,2,24576]{2,1,0:T(2,128)(2,1)} %reshape.551), calls=%async_computation.7 | async-start | bytes 786432 | tf_op jit(solution)/shard_map/all_to_all | solution.py:256
  430.2 11.8 %all-to-all-start.8 = ((bf16[4,2,24576]{2,1,0:T(2,128)(2,1)}), bf16[4,2,24576]{2,1,0:T(2,128)(2,1)}, u32[]{:S(2)}, u32[]{:S(2)}) async-start(bf16[4,2,24576]{2,1,0:T(2,128)(2,1)} %reshape.553), calls=%async_computation.8 | async-start | bytes 786432 | tf_op jit(solution)/shard_map/all_to_all | solution.py:259
  442.0 50.7 %all-to-all-start.4 = ((bf16[8,128,256]{2,1,0:T(8,128)(2,1)}), bf16[8,128,256]{2,1,0:T(8,128)(2,1)S(1)}, u32[]{:S(2)}, u32[]{:S(2)}) async-start(bf16[8,128,256]{2,1,0:T(8,128)(2,1)} %bitcast.269), calls=%async_computation.4 | async-start | bytes 1048576 | tf_op jit(solution)/shard_map/all_to_all | solution.py:230
  459.3 138.0 %all-reduce.28.cloned.1.call-start = ((), (), s32[]{:S(2)}) async-start(), calls=%async_computation.15 | async-start | bytes 262144 | tf_op jit(solution)/shard_map/psum | solution.py:163
  495.3 7.3 %collective-permute-start.2 = (f32[3,512]{1,0:T(4,128)S(1)}, f32[3,512]{1,0:T(4,128)S(1)}, u32[]{:S(2)}, u32[]{:S(2)}) collective-permute-start(f32[3,512]{1,0:T(4,128)S(1)} %pad_add_fusion.2), channel_id=1, source_target_pairs={{1,0},{2,1},{3,2},{4,3},{5,4},{6,5},{7,6},{8,7},{9,8},{10,9},{11,1... | collective-permute-start | bytes 18440 | tf_op jit(solution)/shard_map/ppermute | solution.py:12
  503.5 93.8 %copy-start.14 = (f32[256,256]{1,0:T(8,128)S(1)}, f32[256,256]{1,0:T(8,128)}, u32[]{:S(2)}) copy-start(f32[256,256]{1,0:T(8,128)} %get-tuple-element.227) | copy-start | bytes 786436
  503.6 142.6 %copy-start.42 = (f32[1,256]{1,0:T(1,128)S(1)}, f32[1,256]{1,0:T(1,128)}, u32[]{:S(2)}) copy-start(f32[1,256]{1,0:T(1,128)} %copy-done.41) | copy-start | bytes 3076
  503.6 142.6 %copy-start.44 = (f32[1,256]{1,0:T(1,128)S(1)}, f32[1,256]{1,0:T(1,128)}, u32[]{:S(2)}) copy-start(f32[1,256]{1,0:T(1,128)} %copy-done.43) | copy-start | bytes 3076
  503.6 142.6 %copy-start.46 = (f32[1,256]{1,0:T(1,128)S(1)}, f32[1,256]{1,0:T(1,128)}, u32[]{:S(2)}) copy-start(f32[1,256]{1,0:T(1,128)} %copy-done.45) | copy-start | bytes 3076
  503.6 142.6 %copy-start.48 = (f32[1,256]{1,0:T(1,128)S(1)}, f32[1,256]{1,0:T(1,128)}, u32[]{:S(2)}) copy-start(f32[1,256]{1,0:T(1,128)} %copy-done.47) | copy-start | bytes 3076
  598.4 89.5 %copy-start.59 = (s32[1,1,8]{2,1,0:T(1,128)S(1)}, s32[1,1,8]{2,1,0:T(1,128)}, u32[]{:S(2)}) copy-start(s32[1,1,8]{2,1,0:T(1,128)} %param.37) | copy-start | bytes 100
  642.2 15.8 %all-to-all-start.1 = ((bf16[4,2,128]{2,1,0:T(2,128)(2,1)}), bf16[4,2,128]{2,1,0:T(2,128)(2,1)S(1)}, u32[]{:S(2)}, u32[]{:S(2)}) async-start(bf16[4,2,128]{2,1,0:T(2,128)(2,1)} %reshape.549), calls=%async_computation.1 | async-start | bytes 4096 | tf_op jit(solution)/shard_map/all_to_all | solution.py:274
  656.7 36.0 %collective-permute-start.3 = (f32[3,256]{1,0:T(4,128)S(1)}, f32[3,256]{1,0:T(4,128)S(1)}, u32[]{:S(2)}, u32[]{:S(2)}) collective-permute-start(f32[3,256]{1,0:T(4,128)S(1)} %pad_add_fusion.4), channel_id=1, source_target_pairs={{1,0},{2,1},{3,2},{4,3},{5,4},{6,5},{7,6},{8,7},{9,8},{10,9},{11,1... | collective-permute-start | bytes 9224 | tf_op jit(solution)/shard_map/ppermute | solution.py:12
  658.0 26.7 %all-to-all-start.5 = ((bf16[8,1,128]{2,1,0:T(2,128)(2,1)}), bf16[8,1,128]{2,1,0:T(2,128)(2,1)S(1)}, u32[]{:S(2)}, u32[]{:S(2)}) async-start(bf16[8,1,128]{2,1,0:T(2,128)(2,1)} %copy.84), calls=%async_computation.5 | async-start | bytes 8192 | tf_op jit(solution)/shard_map/all_to_all | solution.py:237
  684.6 7.4 %all-to-all-start = ((bf16[4,2,256]{2,1,0:T(2,128)(2,1)}), bf16[4,2,256]{2,1,0:T(2,128)(2,1)S(1)}, u32[]{:S(2)}, u32[]{:S(2)}) async-start(bf16[4,2,256]{2,1,0:T(2,128)(2,1)} %reshape.547), calls=%async_computation | async-start | bytes 8192 | tf_op jit(solution)/shard_map/all_to_all | solution.py:267
  (53 other events, 548.6 us)
Sparse Core Ops, SparseCore 0:
  20.7 74.4 all-gather.11
  97.5 137.3 all-reduce.25
  237.1 67.9 all-gather.15
  307.3 69.2 all-gather.17
  379.3 71.4 all-gather.13
  510.2 87.0 all-reduce.27
where the time goes:
time: 704 us; the launch traced here: 700 us
  waiting for transfers between devices  364 us (52%)
  blocking collectives  102 us (14%)
  starting transfers between devices  85.5 us (12%)
  other arithmetic  56 us (8%)
  local copies, waits for them, and re-layouts  44.3 us (6%)
  matrix products  32.6 us (5%)
  between operations  16 us (2%)
    psum x1, waiting for transfers between devices, body(): lax.psum(partial_grad.astype(jnp.bfloat16), 'ctx').astype(jnp.float32)  109 us
    psum x1, waiting for transfers between devices, body(): lax.psum(grad_c.astype(jnp.bfloat16), 'expert').astype(jnp.float32)  87.1 us
    all_gather x1, waiting for transfers between devices, body(): lax.all_gather(gate_share, 'ctx', axis=0, tiled=True)  71.4 us
    all_gather x1, waiting for transfers between devices, body(): lax.all_gather(up_share, 'ctx', axis=0, tiled=True)  70.3 us
    unnamed x2, blocking collectives  51.3 us
    psum x1, blocking collectives, body(): lax.psum((grad_kernel_heads, grad_kernel_shared, grad_rate), 'ctx')  42.5 us
    all_to_all x1, starting transfers between devices, body(): lax.all_to_all(route_part.reshape(expert_count, slot_width).astype(jnp.bf...  22.2 us
    unnamed x150, local copies, waits for them, and re-layouts  17.6 us
  transfers between devices with their start and end apart: 20, of which 9 were waited for; matrix products, arithmetic and copies ran while one was open for 17% of the time, Pallas kernels for 0%

commit v1 on v0

v1 whole, which is shorter than its diff:
```python
import jax
import jax.numpy as jnp
from jax import lax
from jax.experimental import pallas as pl
from jax.experimental.pallas import tpu as pltpu
from jax.sharding import PartitionSpec as P

PRECISE = lax.Precision.HIGHEST
F32 = jnp.float32
BF16 = jnp.bfloat16


def passed_along(value, axis, steps):
    count = lax.axis_size(axis)
    first, last = (max(0, -steps), min(count, count - steps))
    return lax.ppermute(value, axis, [(source, source + steps) for source in range(first, last)])


def exchange(value, axis):
    return lax.all_to_all(value, axis, split_axis=0, concat_axis=0, tiled=True)


def copies(value, count):
    return jnp.broadcast_to(value[None], (count,) + value.shape)


def causal_taps(padded_values, kernel):
    taps_count = kernel.shape[0]
    length = padded_values.shape[0] - taps_count + 1
    summed = kernel[0][None, :] * padded_values[0:length]
    for offset in range(1, taps_count):
        summed = summed + kernel[offset][None, :] * padded_values[offset : offset + length]
    return summed


def conv_front(padded_values, kernel):
    return jax.nn.silu(causal_taps(padded_values, kernel))


def state_block(heads_in, b_rows, c_rows, step_size, log_decay, skip_gain, state_in):
    length = heads_in.shape[0]
    cumulative = jnp.cumsum(log_decay, axis=1)
    lower_mask = jnp.tril(jnp.ones((length, length), dtype=bool))
    spacing = jnp.where(lower_mask[None], cumulative[:, :, None] - cumulative[:, None, :], 0.0)
    decays = jnp.where(lower_mask[None], jnp.exp(spacing), 0.0)
    scores = jnp.dot(c_rows, b_rows.T, precision=PRECISE)
    mixing = decays * scores[None] * step_size[:, None, :]
    output = jnp.einsum("hts,shp->thp", mixing, heads_in, precision=PRECISE)
    carried = jnp.einsum("tn,hpn->thp", c_rows, state_in, precision=PRECISE)
    output = (
        output + jnp.exp(cumulative).T[:, :, None] * carried + skip_gain[None, :, None] * heads_in
    )
    ending = cumulative[:, -1]
    tail_weight = jnp.exp(ending[:, None] - cumulative) * step_size
    fresh_state = jnp.einsum("ht,thp,tn->hpn", tail_weight, heads_in, b_rows, precision=PRECISE)
    return (output, jnp.exp(ending)[:, None, None] * state_in + fresh_state)


def scan_kernel(got_ref, out_ref):
    places, half = got_ref.shape[0], out_ref.shape[1] // 2
    width = got_ref.shape[2]
    decay = [
        jnp.exp(
            got_ref[j, 2 * half : 2 * half + 1, :].astype(F32)
            + got_ref[j, 2 * half + 1 : 2 * half + 2, :].astype(F32)
        )
        for j in range(places)
    ]
    state = jnp.zeros((half, width), F32)
    for j in range(places):
        out_ref[j, :half, :] = state.astype(BF16)
        state = decay[j] * state + got_ref[j, :half, :].astype(F32)
    state = jnp.zeros((half, width), F32)
    for j in reversed(range(places)):
        out_ref[j, half:, :] = state.astype(BF16)
        state = decay[j] * state + got_ref[j, half : 2 * half, :].astype(F32)


def states_across(local_state, local_pull, ending):
    heads, width, state_width = local_state.shape
    count = lax.axis_size("ctx")
    rows = heads * width // count
    fresh = local_state.astype(BF16).reshape(count, rows, state_width)
    pulls = local_pull.astype(BF16).reshape(count, rows, state_width)
    coarse = ending.astype(BF16)
    fine = (ending - coarse.astype(F32)).astype(BF16)
    per_head = count // heads
    marks = jnp.stack([jnp.repeat(coarse, per_head), jnp.repeat(fine, per_head)], axis=1)
    marks = jnp.broadcast_to(marks[:, :, None], (count, 2, state_width))
    marks = jnp.pad(marks, ((0, 0), (0, 14), (0, 0)))
    got = exchange(jnp.concatenate([fresh, pulls, marks], axis=1), "ctx")
    entered = pl.pallas_call(
        scan_kernel,
        out_shape=jax.ShapeDtypeStruct((count, 2 * rows, state_width), BF16),
    )(got)
    back = exchange(entered, "ctx").astype(F32)
    shape = (heads, width, state_width)
    return back[:, :rows].reshape(shape), back[:, rows:].reshape(shape)


def body(
    mamba_in,
    shared_in,
    dt_raw,
    dt_bias,
    a_log,
    d_skip,
    conv_x,
    conv_bc,
    mamba_cot,
    moe_in,
    moe_cot,
    slot_tok,
    slot_count,
    route_w,
    w_gate,
    w_up,
    w_down,
    gate_act,
    up_act,
):
    col_width = moe_in.shape[2]
    token_count = moe_in.shape[1]
    expert_count = slot_tok.shape[2]
    slot_width = slot_tok.shape[3]
    hidden_width = w_gate.shape[2]
    slot_ids = slot_tok[0, 0]
    live_slots = jnp.arange(slot_width, dtype=jnp.int32)[None, :] < slot_count[0, 0][:, None]
    chosen = jnp.where(live_slots, slot_ids, -1).reshape(-1)
    token_index = jnp.arange(token_count, dtype=jnp.int32)
    table = jnp.where(chosen[:, None] == token_index[None, :], 1.0, 0.0).astype(BF16)
    send_cot = jnp.dot(table, moe_cot[0], preferred_element_type=F32).astype(BF16)
    send_weight = jnp.where(live_slots, route_w[0, 0], jnp.zeros((), BF16))
    send_weight = jnp.pad(send_weight[:, None, :], ((0, 0), (0, 15), (0, col_width - slot_width)))
    send_cot = send_cot.reshape(expert_count, slot_width, col_width)
    got_cot = exchange(jnp.concatenate([send_cot, send_weight], axis=1), "expert")
    rows_cot = got_cot[:, :slot_width].reshape(-1, col_width)
    rows_weight = got_cot[:, slot_width, :slot_width].reshape(-1).astype(F32)
    unscaled = jnp.dot(rows_cot, w_down[0].T, preferred_element_type=F32)
    mine = lax.psum_scatter(unscaled.astype(BF16), "ctx", scatter_dimension=0, tiled=True)
    send_in = jnp.dot(table, moe_in[0], preferred_element_type=F32).astype(BF16)
    rows_in = exchange(send_in.reshape(expert_count, slot_width, col_width), "expert")
    rows_in = rows_in.reshape(-1, col_width)
    scaled_cot = (rows_weight[:, None] * rows_cot.astype(F32)).astype(BF16)

    rim_rows = conv_x.shape[0] - 1
    head_rows = mamba_in[0]
    shared_rows = shared_in[0]
    length = head_rows.shape[0]
    heads_here = dt_bias.shape[0]
    head_width = head_rows.shape[1] // heads_here
    state_width = shared_rows.shape[1] // 2
    both_rows = jnp.concatenate([head_rows, shared_rows], axis=1)
    before = passed_along(both_rows[length - rim_rows :], "ctx", 1)
    split_at = head_rows.shape[1]
    padded_heads = jnp.concatenate([before[:, :split_at], head_rows], axis=0).astype(F32)
    padded_shared = jnp.concatenate([before[:, split_at:], shared_rows], axis=0).astype(F32)
    conv_heads, pull_heads = jax.vjp(conv_front, padded_heads, conv_x)
    conv_shared, pull_shared = jax.vjp(conv_front, padded_shared, conv_bc)
    b_rows = conv_shared[:, :state_width]
    c_rows = conv_shared[:, state_width:]
    heads_in = conv_heads.reshape(length, heads_here, head_width)
    raw_step = dt_raw[0]
    step_size = jax.nn.softplus(raw_step + dt_bias[:, None])
    log_decay = -jnp.exp(a_log)[:, None] * step_size
    cumulative = jnp.cumsum(log_decay, axis=1)
    tail_weight = jnp.exp(cumulative[:, -1:] - cumulative) * step_size
    local_state = jnp.einsum("ht,thp,tn->hpn", tail_weight, heads_in, b_rows)
    cotangent = mamba_cot[0].astype(F32).reshape(length, heads_here, head_width)
    local_pull = jnp.einsum("ht,thp,tn->hpn", jnp.exp(cumulative), cotangent, c_rows)
    entering, leaving_grad = states_across(local_state, local_pull, cumulative[:, -1])

    def core(heads_arg, b_arg, c_arg, step_arg, rate_arg, state_arg):
        sizes_now = jax.nn.softplus(step_arg + dt_bias[:, None])
        decay_now = -jnp.exp(rate_arg)[:, None] * sizes_now
        return state_block(heads_arg, b_arg, c_arg, sizes_now, decay_now, d_skip, state_arg)

    _, pull_core = jax.vjp(core, heads_in, b_rows, c_rows, raw_step, a_log, entering)
    grad_heads, grad_b, grad_c, grad_step, grad_rate, _ = pull_core((cotangent, leaving_grad))
    grad_bc = jnp.concatenate([grad_b, grad_c], axis=1).astype(BF16)
    total_bc = jnp.sum(
        exchange(copies(grad_bc, lax.axis_size("expert")), "expert").astype(F32), axis=0
    )
    grad_padded_heads, grad_kernel_heads = pull_heads(
        grad_heads.reshape(length, heads_here * head_width)
    )
    grad_padded_shared, grad_kernel_shared = pull_shared(total_bc)
    after = passed_along(
        jnp.concatenate([grad_padded_heads[:rim_rows], grad_padded_shared[:rim_rows]], axis=1),
        "ctx",
        -1,
    )
    edge_pad = ((length - rim_rows, 0), (0, 0))
    grad_mamba_in = (
        grad_padded_heads[rim_rows:] + jnp.pad(after[:, :split_at], edge_pad)
    ).astype(BF16)[None]
    grad_shared_in = (
        grad_padded_shared[rim_rows:] + jnp.pad(after[:, split_at:], edge_pad)
    ).astype(BF16)[None]
    taps = jnp.concatenate([grad_kernel_heads, grad_kernel_shared], axis=1)
    dp_count = lax.axis_size("dp")
    rates = jnp.broadcast_to(jnp.pad(grad_rate, (0, 128 - heads_here))[None], (dp_count, 128))
    small = jnp.concatenate([taps, rates, jnp.zeros((dp_count, 128), F32)], axis=1)
    small = jnp.sum(exchange(small.reshape(dp_count, 8, 128), "dp"), axis=0)
    small = jnp.sum(exchange(copies(small, lax.axis_size("ctx")), "ctx"), axis=0).reshape(1, -1)
    taps_heads = small[:, :split_at]
    taps_shared = small[:, split_at : split_at + 2 * state_width]
    rate_total = small[0, split_at + 2 * state_width :][:heads_here]

    gate_vals = gate_act[0, 0].astype(F32)
    up_vals = up_act[0, 0].astype(F32)
    own = gate_vals.shape[0]
    unscaled_own = mine.astype(F32)
    weight_own = lax.dynamic_slice_in_dim(rows_weight, lax.axis_index("ctx") * own, own, 0)
    grad_hidden = weight_own[:, None] * unscaled_own
    sigmoid_vals = jax.nn.sigmoid(gate_vals)
    activated = gate_vals * sigmoid_vals
    hidden_own = (activated * up_vals).astype(BF16)
    slope = sigmoid_vals * (1.0 + gate_vals * (1.0 - sigmoid_vals))
    gate_own = (grad_hidden * up_vals * slope).astype(BF16)
    up_own = (grad_hidden * activated).astype(BF16)
    route_own = jnp.sum(hidden_own.astype(F32) * unscaled_own, axis=1)
    route_coarse = route_own.astype(BF16)
    route_fine = (route_own - route_coarse.astype(F32)).astype(BF16)
    route_cols = jnp.pad(jnp.stack([route_coarse, route_fine], axis=1), ((0, 0), (0, 126)))
    everything = lax.all_gather(
        jnp.concatenate([gate_own, up_own, hidden_own, route_cols], axis=1),
        "ctx",
        axis=0,
        tiled=True,
    )
    gate_rows = everything[:, :hidden_width]
    up_rows = everything[:, hidden_width : 2 * hidden_width]
    hidden = everything[:, 2 * hidden_width : 3 * hidden_width]
    route_pair = everything[:, 3 * hidden_width : 3 * hidden_width + 2]
    rows_grad = jnp.dot(gate_rows, w_gate[0].T, preferred_element_type=F32)
    rows_grad = rows_grad + jnp.dot(up_rows, w_up[0].T, preferred_element_type=F32)
    route_back = route_pair.reshape(expert_count, slot_width, 2).transpose(0, 2, 1)
    route_back = jnp.pad(
        route_back.reshape(expert_count, 1, 2 * slot_width), ((0, 0), (0, 15), (0, 0))
    )
    back = exchange(
        jnp.concatenate(
            [rows_grad.astype(BF16).reshape(expert_count, slot_width, col_width), route_back],
            axis=1,
        ),
        "expert",
    )
    grad_tokens = lax.dot_general(
        table,
        back[:, :slot_width].reshape(-1, col_width),
        (((0,), (0,)), ((), ())),
        preferred_element_type=F32,
    )
    route_got = back[:, slot_width].astype(F32)
    route_total = jnp.where(
        live_slots, route_got[:, :slot_width] + route_got[:, slot_width:], 0.0
    )
    share = hidden_width // dp_count

    def weight_grad(left, right):
        full = lax.dot_general(
            left, right, (((0,), (0,)), ((), ())), preferred_element_type=F32
        )
        return full.astype(BF16).reshape(dp_count, share, col_width)

    parts = exchange(
        jnp.concatenate(
            [
                weight_grad(gate_rows, rows_in),
                weight_grad(up_rows, rows_in),
                weight_grad(hidden, scaled_cot),
            ],
            axis=1,
        ),
        "dp",
    )
    totals = jnp.sum(parts.astype(F32), axis=0).astype(BF16)
    return (
        grad_mamba_in,
        grad_shared_in,
        grad_step[None],
        taps_heads,
        taps_shared,
        rate_total,
        grad_tokens.astype(BF16)[None],
        route_total[None, None],
        totals[:share].T[None],
        totals[share : 2 * share].T[None],
        totals[2 * share :][None],
    )


def solution(mesh):
    placed = (
        P("dp", "ctx", "expert"),
        P("dp", "ctx", None),
        P("dp", "expert", "ctx"),
        P("expert"),
        P("expert"),
        P("expert"),
        P(None, "expert"),
        P(),
        P("dp", "ctx", "expert"),
        P("dp", "expert", "ctx"),
        P("dp", "expert", "ctx"),
        P("dp", "expert", None, None),
        P("dp", "expert", None),
        P("dp", "expert", None, None),
        P("expert", "ctx", None),
        P("expert", "ctx", None),
        P("expert", None, "ctx"),
        P("dp", "expert", "ctx", None),
        P("dp", "expert", "ctx", None),
    )
    return jax.shard_map(
        body,
        mesh=mesh,
        in_specs=placed,
        out_specs=(
            P("dp", "ctx", "expert"),
            P("dp", "ctx", None),
            P("dp", "expert", "ctx"),
            P("dp", "expert"),
            P("dp", None),
            P("expert"),
            P("dp", "expert", "ctx"),
            P("dp", "expert", None, None),
            P("expert", "ctx", "dp"),
            P("expert", "ctx", "dp"),
            P("expert", "dp", "ctx"),
        ),
        check_vma=False,
    )
```

time: 704 us -> 286 us (0.41)
  waiting for transfers between devices: 364 us -> 112 us
  blocking collectives: 102 us -> 41.6 us
  other arithmetic: 56 us -> 16.7 us
  local copies, waits for them, and re-layouts: 44.3 us -> 8.71 us
  starting transfers between devices: 85.5 us -> 56.6 us
    psum x2 -> x0, waiting for transfers between devices: 196 us -> none  [the longest x1 109 us: body(): lax.psum(partial_grad.astype(jnp.bfloat16), 'ctx').astype(jnp.float32)]
    all_gather x4 -> x1, waiting for transfers between devices: 142 us -> 0.02 us  [body(): lax.all_gather(jnp.concatenate([gate_own, up_own, hidden_own, route_cols]...]
    reduce_scatter x0 -> x1, waiting for transfers between devices: none -> 55.9 us  [body(): lax.psum_scatter(unscaled.astype(BF16), 'ctx', scatter_dimension=0, tiled...]
    unnamed x2 -> x0, blocking collectives: 51.3 us -> none
    psum x1 -> x0, blocking collectives: 42.5 us -> none  [body(): lax.psum((grad_kernel_heads, grad_kernel_shared, grad_rate), 'ctx')]
    all_to_all x0 -> x2, blocking collectives: none -> 41.6 us  [exchange(): return lax.all_to_all(value, axis, split_axis=0, concat_axis=0, tiled=True)]
    all_to_all x10 -> x7, waiting for transfers between devices: 24.9 us -> 56.4 us  [exchange(): return lax.all_to_all(value, axis, split_axis=0, concat_axis=0, tiled=True)]
    all_to_all x10 -> x7, starting transfers between devices: 76.3 us -> 54 us  [exchange(): return lax.all_to_all(value, axis, split_axis=0, concat_axis=0, tiled=True)]
  transfers between devices with their start and end apart: 20 -> 11, of which waited for: 9 -> 8; matrix products, arithmetic and copies ran while one was open for 17% -> 17% of each run, Pallas kernels for 0% -> 1%
where the time goes in v1:
time: 286 us; the launch traced here: 285 us
  waiting for transfers between devices  112 us (39%)
  starting transfers between devices  56.6 us (20%)
  blocking collectives  41.6 us (15%)
  matrix products  31.9 us (11%)
  other arithmetic  16.7 us (6%)
  between operations  15.1 us (5%)
  local copies, waits for them, and re-layouts  8.71 us (3%)
    all_to_all x7, waiting for transfers between devices, exchange(): return lax.all_to_all(value, axis, split_axis=0, concat_axis=0, tiled=True)  56.4 us
    reduce_scatter x1, waiting for transfers between devices, body(): lax.psum_scatter(unscaled.astype(BF16), 'ctx', scatter_dimension=0, tiled...  55.9 us
    all_to_all x7, starting transfers between devices, exchange(): return lax.all_to_all(value, axis, split_axis=0, concat_axis=0, tiled=True)  54 us
    all_to_all x2, blocking collectives, exchange(): return lax.all_to_all(value, axis, split_axis=0, concat_axis=0, tiled=True)  41.6 us
    dot_general x2, matrix products, state_block(): output = jnp.einsum('hts,shp->thp', mixing, heads_in, precision=PRECISE)  7.59 us
    dot_general x3, matrix products, weight_grad(): lax.dot_general(left, right, (((0,), (0,)), ((), ())), preferred_element_...  6.45 us
  transfers between devices with their start and end apart: 11, of which 8 were waited for; matrix products, arithmetic and copies ran while one was open for 17% of the time, Pallas kernels for 1%

profile of v1, /device:TPU:1, one launch (start us, length us, event | category | flops | bytes accessed | tf_op | source)
XLA Modules:
  0.0 284.8 jit_solution(6740009995402670378)
XLA Ops:
  8.8 1.4 fusion.25
  10.3 19.6 %all_to_all.45 = bf16[8,144,256]{2,1,0:T(8,128)(2,1)S(1)} all-to-all(bf16[8,144,256]{2,1,0:T(8,128)(2,1)S(1)} %fusion.68), channel_id=1, replica_groups=mesh['dp'=4,'expert'=8,'ctx'=16] {'expert'}, dimensions={0} | all-to-all | bytes 1179648 | tf_op jit(solution)/shard_map/all_to_all | solution.py:20
  30.1 1.8 convolution_convert_fusion
  31.9 1.3 collective-permute-start
  36.8 55.9 %reduce-scatter.2.cloned.1.call-done = bf16[64,768]{1,0:T(8,128)(2,1)} async-done(((bf16[1024,768]{1,0:T(8,128)(2,1)}), bf16[64,768]{1,0:T(8,128)(2,1)}) %reduce-scatter.2.cloned.1.call-update) | async-done | bytes 98320 | tf_op jit(solution)/shard_map/reduce_scatter | solution.py:140
  96.4 22.0 %all_to_all.46.got_ref = bf16[16,80,128]{2,1,0:T(8,128)(2,1)} all-to-all(bf16[16,80,128]{2,1,0:T(8,128)(2,1)S(1)} %fusion.81), channel_id=1, replica_groups=mesh['dp'=4,'expert'=8,'ctx'=16] {'ctx'}, dimensions={0} | all-to-all | bytes 655360 | tf_op jit(solution)/shard_map/all_to_all | solution.py:20
  118.3 1.8 shard_map.266
  120.1 6.8 %all-to-all-start.1 = ((bf16[16,64,128]{2,1,0:T(8,128)(2,1)}), bf16[16,64,128]{2,1,0:T(8,128)(2,1)S(1)}, u32[]{:S(2)}, u32[]{:S(2)}) async-start(bf16[16,64,128]{2,1,0:T(8,128)(2,1)} %shard_map.266), calls=%async_computation.1 | async-start | bytes 524288 | tf_op jit(solution)/shard_map/all_to_all | solution.py:20
  127.0 2.2 fusion.26
  130.4 12.1 %all-to-all-done.1 = bf16[16,64,128]{2,1,0:T(8,128)(2,1)S(1)} async-done(((bf16[16,64,128]{2,1,0:T(8,128)(2,1)}), bf16[16,64,128]{2,1,0:T(8,128)(2,1)S(1)}, u32[]{:S(2)}, u32[]{:S(2)}) %all-to-all-start.1) | async-done | bytes 262176 | tf_op jit(solution)/shard_map/all_to_all | solution.py:20
  145.0 4.2 %fusion.50 = (f32[8,256]{1,0:T(8,128)S(1)}, f32[8,256]{1,0:T(8,128)S(1)}, f32[8,256]{1,0:T(8,128)}, f32[256,256]{1,0:T(8,128)}) fusion(f32[8,256]{1,0:T(8,128)S(1)} %get-tuple-element.60, f32[256,256]{1,0:T(8,128)} %fusion.114, f32[8,256]{1,0:T(8,128)S(1)} %get-tuple-element.43, pred[256,256]{1,0:T(8,128)(4,1)S(1)} %iota_compare_fusion.4, ...), kind=kOutput, calls=%fused_computation.53 | convolution fusion | flops 410445824 | bytes 1417216 | tf_op jit(solution)/shard_map/transpose(jvp(hts,shp->thp))/dot_general | solution.py:48
  149.3 2.5 reduce-window.16
  151.9 3.4 %fusion.39 = f32[256,8,64]{0,2,1:T(8,128)} fusion(bf16[8,64,256]{2,1,0:T(8,128)(2,1)S(1)} %bitcast.228, f32[8,256]{1,0:T(8,128)S(1)} %get-tuple-element.60, f32[256,256]{1,0:T(8,128)S(1)} %copy-done.12, f32[8,256]{1,0:T(8,128)S(1)} %get-tuple-element.43, pred[256,256]{1,0:T(8,128)(4,1)S(1)} %iota_compare_fusion.4, bf16[256,8,64]{0,2,1:T(8,128)(2,1)S(1)} %bitcast.227, ...), kind=kOutput, calls=%fused_computation.36 | convolution fusion | flops 405929984 | bytes 1925152 | tf_op jit(solution)/shard_map/transpose(jvp(hts,shp->thp))/dot_general | solution.py:48
  160.3 19.7 %all-to-all-start.2 = ((bf16[8,256,256]{2,1,0:T(8,128)(2,1)}), bf16[8,256,256]{2,1,0:T(8,128)(2,1)S(1)}, u32[]{:S(2)}, u32[]{:S(2)}) async-start(bf16[8,256,256]{2,1,0:T(8,128)(2,1)} %broadcast_in_dim.136), calls=%async_computation.2 | async-start | bytes 2097152 | tf_op jit(solution)/shard_map/all_to_all | solution.py:20
  182.5 12.6 %all-to-all-done.2 = bf16[8,256,256]{2,1,0:T(8,128)(2,1)S(1)} async-done(((bf16[8,256,256]{2,1,0:T(8,128)(2,1)}), bf16[8,256,256]{2,1,0:T(8,128)(2,1)S(1)}, u32[]{:S(2)}, u32[]{:S(2)}) %all-to-all-start.2) | async-done | bytes 1048608 | tf_op jit(solution)/shard_map/all_to_all | solution.py:20
  195.7 1.3 collective-permute-start.1
  197.6 3.8 %all-to-all-start.3 = ((f32[4,8,128]{2,1,0:T(8,128)}), f32[4,8,128]{2,1,0:T(8,128)S(1)}, u32[]{:S(2)}, u32[]{:S(2)}) async-start(f32[4,8,128]{2,1,0:T(8,128)} %bitcast.219), calls=%async_computation.3 | async-start | bytes 32768 | tf_op jit(solution)/shard_map/all_to_all | solution.py:20
  202.1 3.4 %all-to-all-done.3 = f32[4,8,128]{2,1,0:T(8,128)S(1)} async-done(((f32[4,8,128]{2,1,0:T(8,128)}), f32[4,8,128]{2,1,0:T(8,128)S(1)}, u32[]{:S(2)}, u32[]{:S(2)}) %all-to-all-start.3) | async-done | bytes 16416 | tf_op jit(solution)/shard_map/all_to_all | solution.py:20
  205.6 5.7 %all-to-all-start.7 = ((bf16[8,128,256]{2,1,0:T(8,128)(2,1)}), bf16[8,128,256]{2,1,0:T(8,128)(2,1)S(1)}, u32[]{:S(2)}, u32[]{:S(2)}) async-start(bf16[8,128,256]{2,1,0:T(8,128)(2,1)} %bitcast.80), calls=%async_computation.8 | async-start | bytes 1048576 | tf_op jit(solution)/shard_map/all_to_all | solution.py:20
  211.3 3.1 %fusion.13 = f32[1024,256]{1,0:T(8,128)} fusion(bf16[1024,2432]{1,0:T(8,128)(2,1)} %all-gather.2.cloned.1.call-done, bf16[1,256,768]{2,1,0:T(8,128)(2,1)} %param.34), kind=kOutput, calls=%fused_computation.21 | convolution fusion | flops 402653184 | bytes 3014656 | tf_op jit(solution)/shard_map/dot_general | solution.py:237
  214.6 2.3 fusion.22
  217.8 3.0 %all-to-all-done.7 = bf16[8,128,256]{2,1,0:T(8,128)(2,1)S(1)} async-done(((bf16[8,128,256]{2,1,0:T(8,128)(2,1)}), bf16[8,128,256]{2,1,0:T(8,128)(2,1)S(1)}, u32[]{:S(2)}, u32[]{:S(2)}) %all-to-all-start.7) | async-done | bytes 524320 | tf_op jit(solution)/shard_map/all_to_all | solution.py:20
  221.4 8.8 %all-to-all-start.4 = ((f32[16,8,128]{2,1,0:T(8,128)}), f32[16,8,128]{2,1,0:T(8,128)S(1)}, u32[]{:S(2)}, u32[]{:S(2)}) async-start(f32[16,8,128]{2,1,0:T(8,128)} %broadcast_in_dim.142), calls=%async_computation.4 | async-start | bytes 131072 | tf_op jit(solution)/shard_map/all_to_all | solution.py:20
  230.2 2.0 fusion.27
  232.3 9.5 %all-to-all-done.4 = f32[16,8,128]{2,1,0:T(8,128)S(1)} async-done(((f32[16,8,128]{2,1,0:T(8,128)}), f32[16,8,128]{2,1,0:T(8,128)S(1)}, u32[]{:S(2)}, u32[]{:S(2)}) %all-to-all-start.4) | async-done | bytes 65568 | tf_op jit(solution)/shard_map/all_to_all | solution.py:20
  241.8 5.7 %all-to-all-start.6 = ((bf16[8,144,256]{2,1,0:T(8,128)(2,1)}), bf16[8,144,256]{2,1,0:T(8,128)(2,1)S(1)}, u32[]{:S(2)}, u32[]{:S(2)}) async-start(bf16[8,144,256]{2,1,0:T(8,128)(2,1)} %fusion.69), calls=%async_computation.7 | async-start | bytes 1179648 | tf_op jit(solution)/shard_map/all_to_all | solution.py:20
  247.5 2.2 fusion.30
  249.8 2.2 fusion.33
  253.1 4.6 %all-to-all-done.6 = bf16[8,144,256]{2,1,0:T(8,128)(2,1)S(1)} async-done(((bf16[8,144,256]{2,1,0:T(8,128)(2,1)}), bf16[8,144,256]{2,1,0:T(8,128)(2,1)S(1)}, u32[]{:S(2)}, u32[]{:S(2)}) %all-to-all-start.6) | async-done | bytes 589856 | tf_op jit(solution)/shard_map/all_to_all | solution.py:20
  257.7 3.5 %all-to-all-start.8 = ((bf16[4,576,256]{2,1,0:T(8,128)(2,1)}), bf16[4,576,256]{2,1,0:T(8,128)(2,1)S(1)}, u32[]{:S(2)}, u32[]{:S(2)}) async-start(bf16[4,576,256]{2,1,0:T(8,128)(2,1)} %pad_maximum_fusion), calls=%async_computation.9 | async-start | bytes 2359296 | tf_op jit(solution)/shard_map/all_to_all | solution.py:20
  263.8 1.4 fusion.46
  265.8 11.1 %all-to-all-done.8 = bf16[4,576,256]{2,1,0:T(8,128)(2,1)S(1)} async-done(((bf16[4,576,256]{2,1,0:T(8,128)(2,1)}), bf16[4,576,256]{2,1,0:T(8,128)(2,1)S(1)}, u32[]{:S(2)}, u32[]{:S(2)}) %all-to-all-start.8) | async-done | bytes 1179680 | tf_op jit(solution)/shard_map/all_to_all | solution.py:20
  (219 shorter events, 28.7 us)
Async XLA Ops:
  7.2 22.8 %copy-start = (bf16[1,768,256]{2,1,0:T(8,128)(2,1)S(1)}, bf16[1,768,256]{2,1,0:T(8,128)(2,1)}, u32[]{:S(2)}) copy-start(bf16[1,768,256]{2,1,0:T(8,128)(2,1)} %param.35) | copy-start | bytes 1179652
  7.2 85.5 %reduce-scatter.2.cloned.1.call-start = ((), (), s32[]{:S(2)}) async-start(), calls=%async_computation.10 | async-start | bytes 1671168 | tf_op jit(solution)/shard_map/reduce_scatter | solution.py:140
  8.0 119.0 %copy-start.40 = (s32[1024]{0:T(1024)}, s32[1024]{0:T(1024)S(1)}, u32[]{:S(2)}) copy-start(s32[1024]{0:T(1024)S(1)} %bitcast_select_fusion) | copy-start | bytes 12292
  31.9 179.4 %all-gather.2.cloned.1.call-start = ((), (), s32[]{:S(2)}) async-start(), calls=%async_computation.11 | async-start | bytes 5292032 | tf_op jit(solution)/shard_map/all_gather | solution.py:226
  31.9 3.3 %collective-permute-start = (bf16[3,768]{1,0:T(4,128)(2,1)S(1)}, bf16[3,768]{1,0:T(4,128)(2,1)S(1)}, u32[]{:S(2)}, u32[]{:S(2)}) collective-permute-start(bf16[3,768]{1,0:T(4,128)(2,1)S(1)} %pad_maximum_fusion.3), channel_id=1, source_target_pairs={{0,1},{1,2},{2,3},{3,4},{4,5},{5,6},{6,7},{7,8},{8,9},{9,10},{10,1... | collective-permute-start | bytes 13832 | tf_op jit(solution)/shard_map/ppermute | solution.py:16
  34.8 60.1 %copy-start.28 = (f32[1,256]{1,0:T(1,128)}, f32[1,256]{1,0:T(1,128)S(1)}, u32[]{:S(2)}) copy-start(f32[1,256]{1,0:T(1,128)S(1)} %get-tuple-element.65) | copy-start | bytes 3076
  34.8 60.1 %copy-start.30 = (f32[1,256]{1,0:T(1,128)}, f32[1,256]{1,0:T(1,128)S(1)}, u32[]{:S(2)}) copy-start(f32[1,256]{1,0:T(1,128)S(1)} %get-tuple-element.66) | copy-start | bytes 3076
  34.8 60.1 %copy-start.32 = (f32[1,256]{1,0:T(1,128)}, f32[1,256]{1,0:T(1,128)S(1)}, u32[]{:S(2)}) copy-start(f32[1,256]{1,0:T(1,128)S(1)} %get-tuple-element.67) | copy-start | bytes 3076
  34.8 60.1 %copy-start.34 = (f32[1,256]{1,0:T(1,128)}, f32[1,256]{1,0:T(1,128)S(1)}, u32[]{:S(2)}) copy-start(f32[1,256]{1,0:T(1,128)S(1)} %get-tuple-element.68) | copy-start | bytes 3076
  35.4 57.3 %copy-start.13 = (bf16[1,1,64,768]{3,2,1,0:T(8,128)(2,1)S(1)}, bf16[1,1,64,768]{3,2,1,0:T(8,128)(2,1)}, u32[]{:S(2)}) copy-start(bf16[1,1,64,768]{3,2,1,0:T(8,128)(2,1)} %param.37) | copy-start | bytes 294916
  36.7 59.5 %copy-start.42 = (f32[8,1,128]{2,1,0:T(1,128)}, f32[8,1,128]{2,1,0:T(1,128)S(1)}, u32[]{:S(2)}) copy-start(f32[8,1,128]{2,1,0:T(1,128)S(1)} %slice_convert_fusion.1) | copy-start | bytes 12292
  120.1 22.4 %all-to-all-start.1 = ((bf16[16,64,128]{2,1,0:T(8,128)(2,1)}), bf16[16,64,128]{2,1,0:T(8,128)(2,1)S(1)}, u32[]{:S(2)}, u32[]{:S(2)}) async-start(bf16[16,64,128]{2,1,0:T(8,128)(2,1)} %shard_map.266), calls=%async_computation.1 | async-start | bytes 524288 | tf_op jit(solution)/shard_map/all_to_all | solution.py:20
  127.0 16.7 %copy-start.23 = (f32[8]{0:T(128)S(1)}, f32[8]{0:T(128)}, u32[]{:S(2)}) copy-start(f32[8]{0:T(128)} %param.22) | copy-start | bytes 100
  127.0 16.7 %copy-start.26 = (f32[8]{0:T(128)S(1)}, f32[8]{0:T(128)}, u32[]{:S(2)}) copy-start(f32[8]{0:T(128)} %copy-done.25) | copy-start | bytes 100
  158.7 21.5 %copy-start.49 = (f32[8]{0:T(128)S(1)}, f32[8]{0:T(128)}, u32[]{:S(2)}) copy-start(f32[8]{0:T(128)} %param.23) | copy-start | bytes 100
  158.7 21.6 %copy-start.3 = (f32[256,512]{1,0:T(8,128)S(1)}, f32[256,512]{1,0:T(8,128)}, u32[]{:S(2)}) copy-start(f32[256,512]{1,0:T(8,128)} %get-tuple-element.39) | copy-start | bytes 1572868
  160.3 34.8 %all-to-all-start.2 = ((bf16[8,256,256]{2,1,0:T(8,128)(2,1)}), bf16[8,256,256]{2,1,0:T(8,128)(2,1)S(1)}, u32[]{:S(2)}, u32[]{:S(2)}) async-start(bf16[8,256,256]{2,1,0:T(8,128)(2,1)} %broadcast_in_dim.136), calls=%async_computation.2 | async-start | bytes 2097152 | tf_op jit(solution)/shard_map/all_to_all | solution.py:20
  181.1 14.2 %copy-start.6 = (f32[256,256]{1,0:T(8,128)S(1)}, f32[256,256]{1,0:T(8,128)}, u32[]{:S(2)}) copy-start(f32[256,256]{1,0:T(8,128)} %get-tuple-element.41) | copy-start | bytes 786436
  181.4 14.1 %copy-start.29 = (f32[1,256]{1,0:T(1,128)S(1)}, f32[1,256]{1,0:T(1,128)}, u32[]{:S(2)}) copy-start(f32[1,256]{1,0:T(1,128)} %copy-done.28) | copy-start | bytes 3076
  181.4 14.1 %copy-start.31 = (f32[1,256]{1,0:T(1,128)S(1)}, f32[1,256]{1,0:T(1,128)}, u32[]{:S(2)}) copy-start(f32[1,256]{1,0:T(1,128)} %copy-done.30) | copy-start | bytes 3076
  181.4 14.1 %copy-start.33 = (f32[1,256]{1,0:T(1,128)S(1)}, f32[1,256]{1,0:T(1,128)}, u32[]{:S(2)}) copy-start(f32[1,256]{1,0:T(1,128)} %copy-done.32) | copy-start | bytes 3076
  181.4 14.1 %copy-start.35 = (f32[1,256]{1,0:T(1,128)S(1)}, f32[1,256]{1,0:T(1,128)}, u32[]{:S(2)}) copy-start(f32[1,256]{1,0:T(1,128)} %copy-done.34) | copy-start | bytes 3076
  195.7 5.7 %collective-permute-start.1 = (f32[3,768]{1,0:T(4,128)S(1)}, f32[3,768]{1,0:T(4,128)S(1)}, u32[]{:S(2)}, u32[]{:S(2)}) collective-permute-start(f32[3,768]{1,0:T(4,128)S(1)} %pad_maximum_fusion.2), channel_id=1, source_target_pairs={{1,0},{2,1},{3,2},{4,3},{5,4},{6,5},{7,6},{8,7},{9,8},{10,9},{11,1... | collective-permute-start | bytes 27656 | tf_op jit(solution)/shard_map/ppermute | solution.py:16
  197.6 8.0 %all-to-all-start.3 = ((f32[4,8,128]{2,1,0:T(8,128)}), f32[4,8,128]{2,1,0:T(8,128)S(1)}, u32[]{:S(2)}, u32[]{:S(2)}) async-start(f32[4,8,128]{2,1,0:T(8,128)} %bitcast.219), calls=%async_computation.3 | async-start | bytes 32768 | tf_op jit(solution)/shard_map/all_to_all | solution.py:20
  201.4 13.1 %copy-start.24 = (f32[3,768]{1,0:T(4,128)}, f32[3,768]{1,0:T(4,128)S(1)}, u32[]{:S(2)}) copy-start(f32[3,768]{1,0:T(4,128)S(1)} %collective-permute-done.1) | copy-start | bytes 27652
  205.6 15.2 %all-to-all-start.7 = ((bf16[8,128,256]{2,1,0:T(8,128)(2,1)}), bf16[8,128,256]{2,1,0:T(8,128)(2,1)S(1)}, u32[]{:S(2)}, u32[]{:S(2)}) async-start(bf16[8,128,256]{2,1,0:T(8,128)(2,1)} %bitcast.80), calls=%async_computation.8 | async-start | bytes 1048576 | tf_op jit(solution)/shard_map/all_to_all | solution.py:20
  220.8 11.5 %copy-start.9 = (bf16[8,128,256]{2,1,0:T(8,128)(2,1)}, bf16[8,128,256]{2,1,0:T(8,128)(2,1)S(1)}, u32[]{:S(2)}) copy-start(bf16[8,128,256]{2,1,0:T(8,128)(2,1)S(1)} %all-to-all-done.7) | copy-start | bytes 1572868
  221.4 20.4 %all-to-all-start.4 = ((f32[16,8,128]{2,1,0:T(8,128)}), f32[16,8,128]{2,1,0:T(8,128)S(1)}, u32[]{:S(2)}, u32[]{:S(2)}) async-start(f32[16,8,128]{2,1,0:T(8,128)} %broadcast_in_dim.142), calls=%async_computation.4 | async-start | bytes 131072 | tf_op jit(solution)/shard_map/all_to_all | solution.py:20
  241.8 15.9 %all-to-all-start.6 = ((bf16[8,144,256]{2,1,0:T(8,128)(2,1)}), bf16[8,144,256]{2,1,0:T(8,128)(2,1)S(1)}, u32[]{:S(2)}, u32[]{:S(2)}) async-start(bf16[8,144,256]{2,1,0:T(8,128)(2,1)} %fusion.69), calls=%async_computation.7 | async-start | bytes 1179648 | tf_op jit(solution)/shard_map/all_to_all | solution.py:20
  252.0 9.3 %slice-start.1 = ((f32[3,768]{1,0:T(4,128)}), f32[3,256]{1,0:T(4,128)S(1)}, s32[]{:S(2)}) async-start(f32[3,768]{1,0:T(4,128)} %copy-done.24), calls=%async_computation.13 | async-start | bytes 8192 | tf_op jit(solution)/shard_map/slice | solution.py:198
  253.1 10.7 %copy-start.41 = (s32[1024]{0:T(1024)S(1)}, s32[1024]{0:T(1024)}, u32[]{:S(2)}) copy-start(s32[1024]{0:T(1024)} %copy-done.40) | copy-start | bytes 12292
  257.7 19.2 %all-to-all-start.8 = ((bf16[4,576,256]{2,1,0:T(8,128)(2,1)}), bf16[4,576,256]{2,1,0:T(8,128)(2,1)S(1)}, u32[]{:S(2)}, u32[]{:S(2)}) async-start(bf16[4,576,256]{2,1,0:T(8,128)(2,1)} %pad_maximum_fusion), calls=%async_computation.9 | async-start | bytes 2359296 | tf_op jit(solution)/shard_map/all_to_all | solution.py:20
  (31 other events, 79.3 us)
Sparse Core Ops, SparseCore 0:
  32.0 60.6 reduce-scatter.1
  95.0 96.1 all-gather.1

commit v2 on v1

v2 whole, which is shorter than its diff:
```python
import jax
import jax.numpy as jnp
from jax import lax
from jax.experimental import pallas as pl
from jax.experimental.pallas import tpu as pltpu
from jax.sharding import PartitionSpec as P

PRECISE = lax.Precision.HIGHEST
F32 = jnp.float32
BF16 = jnp.bfloat16


def passed_along(value, axis, steps):
    count = lax.axis_size(axis)
    first, last = (max(0, -steps), min(count, count - steps))
    return lax.ppermute(value, axis, [(source, source + steps) for source in range(first, last)])


def exchange(value, axis):
    return lax.all_to_all(value, axis, split_axis=0, concat_axis=0, tiled=True)


def copies(value, count):
    return jnp.broadcast_to(value[None], (count,) + value.shape)


def dot(a, b, ca, cb, precise=False):
    return lax.dot_general(
        a,
        b,
        (((ca,), (cb,)), ((), ())),
        precision=PRECISE if precise else None,
        preferred_element_type=F32,
    )


def iota(shape, axis):
    return lax.broadcasted_iota(jnp.int32, shape, axis)


def conv_pre(rows_ref, before_ref, taps_ref, pad_ref):
    length, width = rows_ref.shape
    taps = taps_ref.shape[0]
    pad_ref[0:8, :] = jnp.zeros((8, width), F32)
    pad_ref[8 - (taps - 1) : 8, :] = before_ref[...].astype(F32)
    pad_ref[8:, :] = rows_ref[...].astype(F32)
    pre = None
    for k in range(taps):
        start = 8 - (taps - 1) + k
        term = taps_ref[k : k + 1, :] * pad_ref[start : start + length, :]
        pre = term if pre is None else pre + term
    sig = jax.nn.sigmoid(pre)
    return pre, sig


def conv_pull(grad_pre, taps_ref, pad_ref, dv_ref):
    length, width = grad_pre.shape
    taps = taps_ref.shape[0]
    dv_ref[0:8, :] = jnp.zeros((8, width), F32)
    dv_ref[8 : 8 + length, :] = grad_pre
    dv_ref[8 + length :, :] = jnp.zeros((8, width), F32)
    rows = None
    rim = None
    sums = []
    for k in range(taps):
        weight = taps_ref[k : k + 1, :]
        start = 8 + (taps - 1) - k
        term = weight * dv_ref[start : start + length, :]
        rows = term if rows is None else rows + term
        edge = weight * dv_ref[8 - k : 16 - k, :]
        rim = edge if rim is None else rim + edge
        start = 8 - (taps - 1) + k
        sums.append(jnp.sum(grad_pre * pad_ref[start : start + length, :], axis=0, keepdims=True))
    rim = jnp.where(iota(rim.shape, 0) < taps - 1, rim, 0.0)
    return rows, rim, sums


def steps_of(raw_ref, bias_ref, rate_ref):
    shifted = raw_ref[...] + bias_ref[...]
    step = jnp.maximum(shifted, 0.0) + jnp.log1p(jnp.exp(-jnp.abs(shifted)))
    rate = jnp.exp(rate_ref[...])
    log_decay = -rate * step
    length = shifted.shape[1]
    square = (length, length)
    upto = jnp.where(iota(square, 0) <= iota(square, 1), 1.0, 0.0)
    cumulative = dot(log_decay, upto, 1, 0, True)
    return shifted, step, rate, log_decay, upto, cumulative


def head_spread(heads, width):
    spread = (heads, heads * width)
    return jnp.where(iota(spread, 1) // width == iota(spread, 0), 1.0, 0.0)


def front_kernel(
    rows_ref, shared_ref, beforeh_ref, befores_ref, raw_ref, bias_ref, rate_ref, tapsx_ref,
    tapsbc_ref, cot_ref, out_ref, padh_ref, pads_ref,
):
    heads = raw_ref.shape[0]
    width = rows_ref.shape[1] // heads
    states = shared_ref.shape[1] // 2
    places = out_ref.shape[0]
    part = heads * width // places
    pre, sig = conv_pre(rows_ref, beforeh_ref, tapsx_ref, padh_ref)
    x = pre * sig
    pre_s, sig_s = conv_pre(shared_ref, befores_ref, tapsbc_ref, pads_ref)
    bc = (pre_s * sig_s).astype(BF16)
    _, step, _, _, _, cumulative = steps_of(raw_ref, bias_ref, rate_ref)
    length = step.shape[1]
    ending = cumulative[:, length - 1 :]
    spread = head_spread(heads, width)
    weight = dot(jnp.exp(ending - cumulative) * step, spread, 0, 0, True)
    grown = dot(jnp.exp(cumulative), spread, 0, 0, True)
    fresh = dot((x * weight).astype(BF16), bc[:, :states], 0, 0)
    pulls = dot((cot_ref[...].astype(F32) * grown).astype(BF16), bc[:, states:], 0, 0)
    out_ref[:, :part, :] = fresh.astype(BF16).reshape(places, part, states)
    out_ref[:, part : 2 * part, :] = pulls.astype(BF16).reshape(places, part, states)
    coarse = ending.astype(BF16).astype(F32)
    fine = ending - coarse
    per_head = places // heads
    mark = (16, states)
    for place in range(places):
        head = place // per_head
        marks = jnp.where(
            iota(mark, 0) == 0,
            jnp.broadcast_to(coarse[head : head + 1], mark),
            jnp.broadcast_to(fine[head : head + 1], mark),
        )
        out_ref[place, 2 * part :, :] = marks.astype(BF16)


def back_kernel(
    rows_ref, shared_ref, beforeh_ref, befores_ref, raw_ref, bias_ref, rate_ref, skip_ref,
    tapsx_ref, tapsbc_ref, cot_ref, got_ref,
    main_ref, tail_ref, rim_ref, bc_ref, raw_out_ref, taps_out_ref, rate_out_ref,
    padh_ref, pads_ref, dv_ref, sums_ref,
):
    heads, length = raw_ref.shape
    width = rows_ref.shape[1] // heads
    states = shared_ref.shape[1] // 2
    part = got_ref.shape[1] // 2
    pre, sig = conv_pre(rows_ref, beforeh_ref, tapsx_ref, padh_ref)
    x = pre * sig
    pre_s, sig_s = conv_pre(shared_ref, befores_ref, tapsbc_ref, pads_ref)
    bc = (pre_s * sig_s).astype(BF16)
    b_rows, c_rows = bc[:, :states], bc[:, states:]
    shifted, step, rate, log_decay, upto, cumulative = steps_of(raw_ref, bias_ref, rate_ref)
    ending = cumulative[:, length - 1 :]
    spread = head_spread(heads, width)
    weight = dot(jnp.exp(ending - cumulative) * step, spread, 0, 0, True)
    grown = dot(jnp.exp(cumulative), spread, 0, 0, True)
    step_cols = dot(step, spread, 0, 0, True)
    skip_cols = jnp.sum(skip_ref[...] * spread, axis=0, keepdims=True)
    state_in = got_ref[:, :part, :].reshape(heads * width, states)
    pull_out = got_ref[:, part:, :].reshape(heads * width, states)
    cot = cot_ref[...]
    cot_wide = cot.astype(F32)
    b_pull = dot(b_rows, pull_out, 1, 1)
    c_state = dot(c_rows, state_in, 1, 1)
    cot_grown = cot_wide * grown
    x_weight = x * weight
    grad_c = dot(cot_grown.astype(BF16), state_in, 1, 0)
    grad_b = dot(x_weight.astype(BF16), pull_out, 1, 0)
    lane = (heads * width, 128)
    lane_of, head_of = iota(lane, 1), iota(lane, 0) // width
    pick = jnp.where((lane_of == head_of) | (lane_of == 2 * heads + head_of), 1.0, 0.0)
    pick_next = jnp.where(lane_of == heads + head_of, 1.0, 0.0)
    columns = dot(x_weight * b_pull, pick, 1, 0, True)
    columns = columns + dot(cot_grown * c_state, pick_next, 1, 0, True)
    scores = dot(b_rows, c_rows, 1, 1)
    square = (length, length)
    earlier = iota(square, 0) <= iota(square, 1)
    cumulative_cols = dot(upto, log_decay, 0, 1, True)
    x_step = (x * step_cols).astype(BF16)
    pair = max(1, 128 // width)
    block = pair * width
    lane_head = iota((length, block), 1) // width
    column_lane = iota((length, 128), 1)
    grad_scores = jnp.zeros(square, F32)
    inner = []
    for base in range(0, heads, pair):
        at = base * width
        x_pair = x_step[:, at : at + block]
        cot_pair = cot[:, at : at + block]
        sum_pair = None
        for i in range(pair):
            head = base + i
            cot_one = jnp.where(lane_head == i, cot_pair, jnp.zeros((), BF16))
            grad_mix = dot(x_pair, cot_one, 1, 1)
            gap = cumulative[head : head + 1, :] - cumulative_cols[:, head : head + 1]
            decay = jnp.exp(jnp.where(earlier, gap, -1e30))
            mix = decay * scores
            grad_scores = grad_scores + decay * grad_mix
            moved = mix * grad_mix
            sums_ref[head : head + 1, :] = jnp.sum(moved, axis=0, keepdims=True)
            columns = columns + jnp.where(
                column_lane == head, jnp.sum(moved, axis=1, keepdims=True), 0.0
            )
            term = dot(mix.astype(BF16), cot_one, 1, 0)
            sum_pair = term if sum_pair is None else sum_pair + term
        inner.append(sum_pair)
    inner = jnp.concatenate(inner, axis=1)
    grad_scores = grad_scores.astype(BF16)
    grad_b = grad_b + dot(grad_scores, c_rows, 1, 0)
    grad_c = grad_c + dot(grad_scores, b_rows, 0, 0)
    grad_bc = jnp.concatenate([grad_b, grad_c], axis=1).astype(BF16)
    for copy in range(bc_ref.shape[0]):
        bc_ref[copy] = grad_bc
    turned = columns.T
    left = turned[:heads]
    came = sums_ref[...] + turned[heads : 2 * heads]
    state_pull = state_in.astype(F32) * pull_out.astype(F32)
    state_pull = jnp.sum(state_pull.reshape(heads, width, states), axis=1)
    state_pull = jnp.exp(ending) * jnp.sum(state_pull, axis=1, keepdims=True)
    to_last = jnp.sum(turned[2 * heads : 3 * heads], axis=1, keepdims=True)
    grad_decay = dot(came - left, upto, 1, 1, True) + to_last + state_pull
    grad_step = left / step - rate * grad_decay
    raw_out_ref[...] = grad_step * jax.nn.sigmoid(shifted)
    grad_rate = jnp.sum(grad_decay * log_decay, axis=1, keepdims=True)
    eye = jnp.where(iota((heads, 128), 0) == iota((heads, 128), 1), 1.0, 0.0)
    rate_out_ref[...] = jnp.sum(grad_rate * eye, axis=0, keepdims=True)
    grad_x = inner * step_cols + skip_cols * cot_wide + weight * b_pull
    grad_pre = grad_x * (sig * (1.0 + pre * (1.0 - sig)))
    rows, rim, sums = conv_pull(grad_pre, tapsx_ref, padh_ref, dv_ref)
    main_ref[...] = rows.astype(BF16)
    tail_ref[...] = rows[length - 16 :]
    rim_ref[...] = rim
    for k, total in enumerate(sums):
        taps_out_ref[k : k + 1, :] = total


def shared_kernel(
    shared_ref, befores_ref, tapsbc_ref, got_ref,
    main_ref, tail_ref, rim_ref, taps_out_ref, pads_ref, dv_ref,
):
    length = shared_ref.shape[0]
    pre, sig = conv_pre(shared_ref, befores_ref, tapsbc_ref, pads_ref)
    total = got_ref[0].astype(F32)
    for source in range(1, got_ref.shape[0]):
        total = total + got_ref[source].astype(F32)
    grad_pre = total * (sig * (1.0 + pre * (1.0 - sig)))
    rows, rim, sums = conv_pull(grad_pre, tapsbc_ref, pads_ref, dv_ref)
    main_ref[...] = rows.astype(BF16)
    tail_ref[...] = rows[length - 16 :]
    rim_ref[...] = rim
    for k, value in enumerate(sums):
        taps_out_ref[k : k + 1, :] = value


def own_rows_kernel(mine_ref, weight_ref, gate_ref, up_ref, after_ref, out_ref):
    del after_ref
    width = mine_ref.shape[1]
    unscaled = mine_ref[...].astype(F32)
    gate = gate_ref[...].astype(F32)
    up = up_ref[...].astype(F32)
    grad_hidden = weight_ref[...] * unscaled
    sig = jax.nn.sigmoid(gate)
    activated = gate * sig
    hidden = (activated * up).astype(BF16)
    slope = sig * (1.0 + gate * (1.0 - sig))
    out_ref[:, :width] = (grad_hidden * up * slope).astype(BF16)
    out_ref[:, width : 2 * width] = (grad_hidden * activated).astype(BF16)
    out_ref[:, 2 * width : 3 * width] = hidden
    route = jnp.sum(hidden.astype(F32) * unscaled, axis=1, keepdims=True)
    coarse = route.astype(BF16).astype(F32)
    lanes = (mine_ref.shape[0], 128)
    out_ref[:, 3 * width :] = jnp.where(
        iota(lanes, 1) == 0, coarse, jnp.where(iota(lanes, 1) == 1, route - coarse, 0.0)
    ).astype(BF16)


def rows_kernel(all_ref, in_ref, cot_ref, gatew_ref, upw_ref, after_ref, back_ref, parts_ref):
    del after_ref
    groups, slots, cols = in_ref.shape
    width = gatew_ref.shape[1]
    owners, share3 = parts_ref.shape[0], parts_ref.shape[1]
    share = share3 // 3
    rows_grad = dot(all_ref[:, :width], gatew_ref[...], 1, 1)
    rows_grad = rows_grad + dot(all_ref[:, width : 2 * width], upw_ref[...], 1, 1)
    back_ref[:, :slots, :] = rows_grad.astype(BF16).reshape(groups, slots, cols)
    route = all_ref[:, 3 * width :].astype(F32)
    scaled = []
    for group in range(groups):
        turned = route[group * slots : (group + 1) * slots].T
        line = jnp.concatenate([turned[0:1], turned[1:2]], axis=1)
        back_ref[group, slots:, :] = jnp.broadcast_to(line, (16, cols)).astype(BF16)
        weight = cot_ref[group, slots:, :slots].astype(F32).T[:, 0:1]
        scaled.append((cot_ref[group, :slots, :].astype(F32) * weight).astype(BF16))
    scaled = jnp.concatenate(scaled, axis=0)
    rows_in = in_ref[...].reshape(groups * slots, cols)
    grads = [
        dot(all_ref[:, :width], rows_in, 0, 0).astype(BF16),
        dot(all_ref[:, width : 2 * width], rows_in, 0, 0).astype(BF16),
        dot(all_ref[:, 2 * width : 3 * width], scaled, 0, 0).astype(BF16),
    ]
    for owner in range(owners):
        for kind in range(3):
            parts_ref[owner, kind * share : (kind + 1) * share, :] = grads[kind][
                owner * share : (owner + 1) * share
            ]


def scan_kernel(got_ref, out_ref):
    places, half = got_ref.shape[0], out_ref.shape[1] // 2
    width = got_ref.shape[2]
    decay = [
        jnp.exp(
            got_ref[j, 2 * half : 2 * half + 1, :].astype(F32)
            + got_ref[j, 2 * half + 1 : 2 * half + 2, :].astype(F32)
        )
        for j in range(places)
    ]
    state = jnp.zeros((half, width), F32)
    for j in range(places):
        out_ref[j, :half, :] = state.astype(BF16)
        state = decay[j] * state + got_ref[j, :half, :].astype(F32)
    state = jnp.zeros((half, width), F32)
    for j in reversed(range(places)):
        out_ref[j, half:, :] = state.astype(BF16)
        state = decay[j] * state + got_ref[j, half : 2 * half, :].astype(F32)


def whole(kernel, outs, scratch=(), late=0, inputs=0, limit=None):
    specs = [pl.BlockSpec(memory_space=pltpu.VMEM)] * inputs
    specs += [pl.BlockSpec(memory_space=pl.ANY)] * late
    return pl.pallas_call(
        kernel,
        out_shape=[jax.ShapeDtypeStruct(shape, kind) for shape, kind in outs],
        in_specs=specs,
        out_specs=[pl.BlockSpec(memory_space=pltpu.VMEM)] * len(outs),
        scratch_shapes=[pltpu.VMEM(shape, kind) for shape, kind in scratch],
        compiler_params=pltpu.CompilerParams(vmem_limit_bytes=limit),
    )


def with_last_rows(main, tail, after):
    rows = tail.shape[0]
    given = jnp.pad(after, ((rows - after.shape[0], 0), (0, 0)))
    return lax.dynamic_update_slice(
        main, (tail + given).astype(BF16), (main.shape[0] - rows, 0)
    )


def body(
    mamba_in,
    shared_in,
    dt_raw,
    dt_bias,
    a_log,
    d_skip,
    conv_x,
    conv_bc,
    mamba_cot,
    moe_in,
    moe_cot,
    slot_tok,
    slot_count,
    route_w,
    w_gate,
    w_up,
    w_down,
    gate_act,
    up_act,
):
    dp_count, expert_places, ctx_places = (
        lax.axis_size("dp"),
        lax.axis_size("expert"),
        lax.axis_size("ctx"),
    )
    col_width = moe_in.shape[2]
    token_count = moe_in.shape[1]
    expert_count = slot_tok.shape[2]
    slot_width = slot_tok.shape[3]
    hidden_width = w_gate.shape[2]
    slot_ids = slot_tok[0, 0]
    live_slots = jnp.arange(slot_width, dtype=jnp.int32)[None, :] < slot_count[0, 0][:, None]
    chosen = jnp.where(live_slots, slot_ids, -1).reshape(-1)
    token_index = jnp.arange(token_count, dtype=jnp.int32)
    table = jnp.where(chosen[:, None] == token_index[None, :], 1.0, 0.0).astype(BF16)
    send_cot = jnp.dot(table, moe_cot[0], preferred_element_type=F32).astype(BF16)
    send_weight = jnp.where(live_slots, route_w[0, 0], jnp.zeros((), BF16))
    send_weight = jnp.pad(send_weight[:, None, :], ((0, 0), (0, 15), (0, col_width - slot_width)))
    send_cot = send_cot.reshape(expert_count, slot_width, col_width)
    got_cot = exchange(jnp.concatenate([send_cot, send_weight], axis=1), "expert")
    rows_cot = got_cot[:, :slot_width].reshape(-1, col_width)
    rows_weight = got_cot[:, slot_width, :slot_width].reshape(-1).astype(F32)
    unscaled = jnp.dot(rows_cot, w_down[0].T, preferred_element_type=F32)
    mine = lax.psum_scatter(unscaled.astype(BF16), "ctx", scatter_dimension=0, tiled=True)
    send_in = jnp.dot(table, moe_in[0], preferred_element_type=F32).astype(BF16)
    rows_in = exchange(send_in.reshape(expert_count, slot_width, col_width), "expert")

    rim_rows = conv_x.shape[0] - 1
    head_rows = mamba_in[0]
    shared_rows = shared_in[0]
    cot_rows = mamba_cot[0]
    raw_step = dt_raw[0]
    length, split_at = head_rows.shape
    shared_width = shared_rows.shape[1]
    state_width = shared_width // 2
    heads_here = dt_bias.shape[0]
    part = split_at // ctx_places
    bias, rate, skip = dt_bias[:, None], a_log[:, None], d_skip[:, None]
    before = passed_along(
        jnp.concatenate([head_rows[length - rim_rows :], shared_rows[length - rim_rows :]], axis=1),
        "ctx",
        1,
    )
    before_heads, before_shared = before[:, :split_at], before[:, split_at:]
    pad_heads = ((8 + length, split_at), F32)
    pad_shared = ((8 + length, shared_width), F32)
    (states,) = whole(
        front_kernel,
        [((ctx_places, 2 * part + 16, state_width), BF16)],
        [pad_heads, pad_shared],
        inputs=10,
    )(
        head_rows, shared_rows, before_heads, before_shared, raw_step, bias, rate, conv_x,
        conv_bc, cot_rows,
    )
    (entered,) = whole(
        scan_kernel, [((ctx_places, 2 * part, state_width), BF16)], inputs=1
    )(exchange(states, "ctx"))
    main_heads, tail_heads, rim_heads, grad_bc, grad_step, taps_heads, grad_rate = whole(
        back_kernel,
        [
            ((length, split_at), BF16),
            ((16, split_at), F32),
            ((8, split_at), F32),
            ((expert_places, length, shared_width), BF16),
            ((heads_here, length), F32),
            ((rim_rows + 1, split_at), F32),
            ((1, 128), F32),
        ],
        [pad_heads, pad_shared, ((16 + length, split_at), F32), ((heads_here, length), F32)],
        inputs=12,
        limit=48 * 2**20,
    )(
        head_rows, shared_rows, before_heads, before_shared, raw_step, bias, rate, skip, conv_x,
        conv_bc, cot_rows, exchange(entered, "ctx"),
    )
    after_heads = passed_along(rim_heads[:rim_rows], "ctx", -1)
    grad_mamba_in = with_last_rows(main_heads, tail_heads, after_heads)
    main_shared, tail_shared, rim_shared, taps_shared = whole(
        shared_kernel,
        [
            ((length, shared_width), BF16),
            ((16, shared_width), F32),
            ((8, shared_width), F32),
            ((rim_rows + 1, shared_width), F32),
        ],
        [pad_shared, ((16 + length, shared_width), F32)],
        inputs=4,
    )(shared_rows, before_shared, conv_bc, exchange(grad_bc, "expert"))
    after_shared = passed_along(rim_shared[:rim_rows], "ctx", -1)
    grad_shared_in = with_last_rows(main_shared, tail_shared, after_shared)
    small = jnp.concatenate(
        [
            taps_heads,
            taps_shared,
            jnp.broadcast_to(grad_rate, (dp_count, 128)),
            jnp.zeros((dp_count, 128), F32),
        ],
        axis=1,
    )
    small = jnp.sum(exchange(small.reshape(dp_count, 8, 128), "dp"), axis=0)
    small = jnp.sum(exchange(copies(small, ctx_places), "ctx"), axis=0).reshape(1, -1)
    taps_heads = small[:, :split_at]
    taps_shared = small[:, split_at : split_at + shared_width]
    rate_total = small[0, split_at + shared_width :][:heads_here]

    own = gate_act.shape[2]
    weight_own = lax.dynamic_slice_in_dim(rows_weight, lax.axis_index("ctx") * own, own, 0)
    (own_rows,) = whole(
        own_rows_kernel,
        [((own, 3 * hidden_width + 128), BF16)],
        inputs=4,
        late=1,
    )(mine, weight_own[:, None], gate_act[0, 0], up_act[0, 0], grad_step)
    everything = lax.all_gather(own_rows, "ctx", axis=0, tiled=True)
    share = hidden_width // dp_count
    back, parts = whole(
        rows_kernel,
        [
            ((expert_count, slot_width + 16, col_width), BF16),
            ((dp_count, 3 * share, col_width), BF16),
        ],
        inputs=5,
        late=1,
        limit=56 * 2**20,
    )(everything, rows_in, got_cot, w_gate[0], w_up[0], small)
    back = exchange(back, "expert")
    parts = exchange(parts, "dp")
    grad_tokens = lax.dot_general(
        table,
        back[:, :slot_width].reshape(-1, col_width),
        (((0,), (0,)), ((), ())),
        preferred_element_type=F32,
    )
    route_got = back[:, slot_width].astype(F32)
    route_total = jnp.where(
        live_slots, route_got[:, :slot_width] + route_got[:, slot_width:], 0.0
    )
    totals = jnp.sum(parts.astype(F32), axis=0).astype(BF16)
    return (
        grad_mamba_in[None],
        grad_shared_in[None],
        grad_step[None],
        taps_heads,
        taps_shared,
        rate_total,
        grad_tokens.astype(BF16)[None],
        route_total[None, None],
        totals[:share].T[None],
        totals[share : 2 * share].T[None],
        totals[2 * share :][None],
    )


def solution(mesh):
    placed = (
        P("dp", "ctx", "expert"),
        P("dp", "ctx", None),
        P("dp", "expert", "ctx"),
        P("expert"),
        P("expert"),
        P("expert"),
        P(None, "expert"),
        P(),
        P("dp", "ctx", "expert"),
        P("dp", "expert", "ctx"),
        P("dp", "expert", "ctx"),
        P("dp", "expert", None, None),
        P("dp", "expert", None),
        P("dp", "expert", None, None),
        P("expert", "ctx", None),
        P("expert", "ctx", None),
        P("expert", None, "ctx"),
        P("dp", "expert", "ctx", None),
        P("dp", "expert", "ctx", None),
    )
    return jax.shard_map(
        body,
        mesh=mesh,
        in_specs=placed,
        out_specs=(
            P("dp", "ctx", "expert"),
            P("dp", "ctx", None),
            P("dp", "expert", "ctx"),
            P("dp", "expert"),
            P("dp", None),
            P("expert"),
            P("dp", "expert", "ctx"),
            P("dp", "expert", None, None),
            P("expert", "ctx", "dp"),
            P("expert", "ctx", "dp"),
            P("expert", "dp", "ctx"),
        ),
        check_vma=False,
    )
```

time: 286 us -> 249 us (0.87)
  waiting for transfers between devices: 112 us -> 72 us
  matrix products: 31.9 us -> 5.95 us
  Pallas kernels: 1.76 us -> 24.1 us
  blocking collectives: 41.6 us -> 60.2 us
  other arithmetic: 16.7 us -> 5.12 us
    reduce_scatter x1, waiting for transfers between devices: 55.9 us -> 0.01 us  [body(): lax.psum_scatter(unscaled.astype(BF16), 'ctx', scatter_dimension=0, tiled...]
    dot_general x16 -> x0, matrix products: 25.1 us -> none  [the longest x2 7.59 us: state_block(): output = jnp.einsum('hts,shp->thp', mixing, heads_in, precision=PRECISE)]
    pallas_call x1 -> x6, Pallas kernels: 1.76 us -> 24.1 us  [the longest x1 7.37 us: body(): whole(back_kernel, [((length, split_at), BF16), ((16, split_at), F32), ((...]
    all_to_all x2 -> x3, blocking collectives: 41.6 us -> 60.2 us  [exchange(): return lax.all_to_all(value, axis, split_axis=0, concat_axis=0, tiled=True)]
    all_to_all x7 -> x6, waiting for transfers between devices: 56.4 us -> 65.7 us  [exchange(): return lax.all_to_all(value, axis, split_axis=0, concat_axis=0, tiled=True)]
    all_gather x1, waiting for transfers between devices: 0.02 us -> 4.2 us  [body(): everything = lax.all_gather(own_rows, 'ctx', axis=0, tiled=True)]
    another operation x7 -> x0, other arithmetic: 3.27 us -> none
    all_to_all x7 -> x6, starting transfers between devices: 54 us -> 53.3 us  [exchange(): return lax.all_to_all(value, axis, split_axis=0, concat_axis=0, tiled=True)]
  transfers between devices with their start and end apart: 11 -> 11, of which waited for: 8 -> 8; matrix products, arithmetic and copies ran while one was open for 17% -> 5% of each run, Pallas kernels for 1% -> 6%
where the time goes in v2:
time: 249 us; the launch traced here: 248 us
  waiting for transfers between devices  72 us (29%)
  blocking collectives  60.2 us (24%)
  starting transfers between devices  57.2 us (23%)
  Pallas kernels  24.1 us (10%)
  between operations  14.3 us (6%)
  local copies, waits for them, and re-layouts  9.07 us (4%)
  matrix products  5.95 us (2%)
  other arithmetic  5.12 us (2%)
    all_to_all x6, waiting for transfers between devices, exchange(): return lax.all_to_all(value, axis, split_axis=0, concat_axis=0, tiled=True)  65.7 us
    all_to_all x3, blocking collectives, exchange(): return lax.all_to_all(value, axis, split_axis=0, concat_axis=0, tiled=True)  60.2 us
    all_to_all x6, starting transfers between devices, exchange(): return lax.all_to_all(value, axis, split_axis=0, concat_axis=0, tiled=True)  53.3 us
    pallas_call x1, Pallas kernels, body(): whole(back_kernel, [((length, split_at), BF16), ((16, split_at), F32), ((...  7.37 us
    pallas_call x1, Pallas kernels, body(): whole(rows_kernel, [((expert_count, slot_width + 16, col_width), BF16), (...  6.31 us
  transfers between devices with their start and end apart: 11, of which 8 were waited for; matrix products, arithmetic and copies ran while one was open for 5% of the time, Pallas kernels for 6%

profile of v2, /device:TPU:1, one launch (start us, length us, event | category | flops | bytes accessed | tf_op | source)
XLA Modules:
  0.0 248.0 jit_solution(4927436560518388593)
XLA Ops:
  7.2 0.8 bitcast_select_fusion
  8.8 1.4 fusion.3
  10.3 19.6 %all_to_all.45.cot_ref = bf16[8,144,256]{2,1,0:T(8,128)(2,1)S(1)} all-to-all(bf16[8,144,256]{2,1,0:T(8,128)(2,1)S(1)} %fusion.17), channel_id=1, replica_groups=mesh['dp'=4,'expert'=8,'ctx'=16] {'expert'}, dimensions={0} | all-to-all | bytes 1179648 | tf_op jit(solution)/shard_map/all_to_all | solution.py:20
  30.0 1.8 convolution_convert_fusion
  33.3 1.3 collective-permute-start
  37.2 3.9 %shard_map.266 = bf16[16,80,128]{2,1,0:T(8,128)(2,1)} custom-call(bf16[256,512]{1,0:T(8,128)(2,1)} %bitcast.81, bf16[256,256]{1,0:T(8,128)(2,1)} %bitcast.78, bf16[3,512]{1,0:T(4,128)(2,1)} %slice.86.beforeh_ref, bf16[3,256]{1,0:T(4,128)(2,1)} %slice.87.befores_ref, f32[8,256]{1,0:T(8,128)} %bitcast.85, f32[8,1]{1,0:T(8,128)} %copy.45.bias_ref, ...), custom_call_target="tpu_custom_call" | custom-call | tf_op jit(solution)/shard_map/pallas_call | solution.py:411
  41.0 31.6 %all_to_all.46.got_ref = bf16[16,80,128]{2,1,0:T(8,128)(2,1)} all-to-all(bf16[16,80,128]{2,1,0:T(8,128)(2,1)} %shard_map.266), channel_id=1, replica_groups=mesh['dp'=4,'expert'=8,'ctx'=16] {'ctx'}, dimensions={0} | all-to-all | bytes 655360 | tf_op jit(solution)/shard_map/all_to_all | solution.py:20
  72.6 1.8 shard_map.267
  74.4 12.3 %all-to-all-start.1 = ((bf16[16,64,128]{2,1,0:T(8,128)(2,1)}), bf16[16,64,128]{2,1,0:T(8,128)(2,1)S(1)}, u32[]{:S(2)}, u32[]{:S(2)}) async-start(bf16[16,64,128]{2,1,0:T(8,128)(2,1)} %shard_map.267), calls=%async_computation.1 | async-start | bytes 524288 | tf_op jit(solution)/shard_map/all_to_all | solution.py:20
  87.6 15.3 %all-to-all-done.1.got_ref = bf16[16,64,128]{2,1,0:T(8,128)(2,1)S(1)} async-done(((bf16[16,64,128]{2,1,0:T(8,128)(2,1)}), bf16[16,64,128]{2,1,0:T(8,128)(2,1)S(1)}, u32[]{:S(2)}, u32[]{:S(2)}) %all-to-all-start.1) | async-done | bytes 262176 | tf_op jit(solution)/shard_map/all_to_all | solution.py:20
  103.0 7.4 %shard_map.268 = (bf16[256,512]{1,0:T(8,128)(2,1)}, f32[16,512]{1,0:T(8,128)S(1)}, f32[8,512]{1,0:T(8,128)S(1)}, bf16[8,256,256]{2,1,0:T(8,128)(2,1)}, f32[8,256...) custom-call(bf16[256,512]{1,0:T(8,128)(2,1)S(1)} %bitcast.82, bf16[256,256]{1,0:T(8,128)(2,1)S(1)} %bitcast.80, ...), custom_call_target="tpu_custom_call" | custom-call | tf_op jit(solution)/shard_map/pallas_call | solution.py:423
  110.4 1.9 shard_map.270
  112.3 9.7 %all-to-all-start.2 = ((bf16[8,256,256]{2,1,0:T(8,128)(2,1)}), bf16[8,256,256]{2,1,0:T(8,128)(2,1)S(1)}, u32[]{:S(2)}, u32[]{:S(2)}) async-start(bf16[8,256,256]{2,1,0:T(8,128)(2,1)} %get-tuple-element.27), calls=%async_computation.2 | async-start | bytes 2097152 | tf_op jit(solution)/shard_map/all_to_all | solution.py:20
  122.1 15.1 %all-to-all-done.2.got_ref = bf16[8,256,256]{2,1,0:T(8,128)(2,1)S(1)} async-done(((bf16[8,256,256]{2,1,0:T(8,128)(2,1)}), bf16[8,256,256]{2,1,0:T(8,128)(2,1)S(1)}, u32[]{:S(2)}, u32[]{:S(2)}) %all-to-all-start.2) | async-done | bytes 1048608 | tf_op jit(solution)/shard_map/all_to_all | solution.py:20
  137.2 1.0 copy-done.12
  138.2 2.9 %shard_map.269 = (bf16[256,256]{1,0:T(8,128)(2,1)}, f32[16,256]{1,0:T(8,128)}, f32[8,256]{1,0:T(8,128)}, f32[4,256]{1,0:T(4,128)}) custom-call(bf16[256,256]{1,0:T(8,128)(2,1)} %bitcast.79, bf16[3,256]{1,0:T(4,128)(2,1)} %slice.87.befores_ref, f32[4,256]{1,0:T(4,128)} %tapsbc_ref.5, bf16[8,256,256]{2,1,0:T(8,128)(2,1)} %copy-done.12), custom_call_target="tpu_custom_call" | custom-call | tf_op jit(solution)/shard_map/pallas_call | solution.py:443
  141.7 9.0 %all_to_all.47 = f32[4,8,128]{2,1,0:T(8,128)S(1)} all-to-all(f32[4,8,128]{2,1,0:T(8,128)S(1)} %bitcast.95), channel_id=1, replica_groups=mesh['dp'=4,'expert'=8,'ctx'=16] {'dp'}, dimensions={0} | all-to-all | bytes 32768 | tf_op jit(solution)/shard_map/all_to_all | solution.py:20
  151.4 8.8 %all-to-all-start.4 = ((f32[16,8,128]{2,1,0:T(8,128)}), f32[16,8,128]{2,1,0:T(8,128)S(1)}, u32[]{:S(2)}, u32[]{:S(2)}) async-start(f32[16,8,128]{2,1,0:T(8,128)} %broadcast_in_dim.90), calls=%async_computation.4 | async-start | bytes 131072 | tf_op jit(solution)/shard_map/all_to_all | solution.py:20
  160.2 1.3 fusion.4
  161.5 10.6 %all-to-all-done.4 = f32[16,8,128]{2,1,0:T(8,128)S(1)} async-done(((f32[16,8,128]{2,1,0:T(8,128)}), f32[16,8,128]{2,1,0:T(8,128)S(1)}, u32[]{:S(2)}, u32[]{:S(2)}) %all-to-all-start.4) | async-done | bytes 65568 | tf_op jit(solution)/shard_map/all_to_all | solution.py:20
  172.1 7.2 %all-to-all-start.6 = ((bf16[8,128,256]{2,1,0:T(8,128)(2,1)}), bf16[8,128,256]{2,1,0:T(8,128)(2,1)S(1)}, u32[]{:S(2)}, u32[]{:S(2)}) async-start(bf16[8,128,256]{2,1,0:T(8,128)(2,1)} %bitcast.30), calls=%async_computation.7 | async-start | bytes 1048576 | tf_op jit(solution)/shard_map/all_to_all | solution.py:20
  179.9 8.9 %all-to-all-done.6.in_ref = bf16[8,128,256]{2,1,0:T(8,128)(2,1)S(1)} async-done(((bf16[8,128,256]{2,1,0:T(8,128)(2,1)}), bf16[8,128,256]{2,1,0:T(8,128)(2,1)S(1)}, u32[]{:S(2)}, u32[]{:S(2)}) %all-to-all-start.6) | async-done | bytes 524320 | tf_op jit(solution)/shard_map/all_to_all | solution.py:20
  188.8 4.2 %all-gather.2.cloned.1.call-done.all_ref = bf16[1024,2432]{1,0:T(8,128)(2,1)} async-done(((bf16[64,2432]{1,0:T(8,128)(2,1)}), bf16[1024,2432]{1,0:T(8,128)(2,1)}) %all-gather.2.cloned.1.call-update) | async-done | bytes 4980752 | tf_op jit(solution)/shard_map/all_gather | solution.py:479
  193.0 6.3 %shard_map.271 = (bf16[8,144,256]{2,1,0:T(8,128)(2,1)}, bf16[4,576,256]{2,1,0:T(8,128)(2,1)}) custom-call(bf16[1024,2432]{1,0:T(8,128)(2,1)} %all-gather.2.cloned.1.call-done.all_ref, bf16[8,128,256]{2,1,0:T(8,128)(2,1)} %copy-done.13, bf16[8,144,256]{2,1,0:T(8,128)(2,1)} %copy-done.11, bf16[256,768]{1,0:T(8,128)(2,1)} %bitcast.91, ...), custom_call_target="tpu_custom_call" | custom-call | tf_op jit(solution)/shard_map/pallas_call | solution.py:481
  199.3 11.2 %all-to-all-start.7 = ((bf16[8,144,256]{2,1,0:T(8,128)(2,1)}), bf16[8,144,256]{2,1,0:T(8,128)(2,1)S(1)}, u32[]{:S(2)}, u32[]{:S(2)}) async-start(bf16[8,144,256]{2,1,0:T(8,128)(2,1)} %get-tuple-element.35), calls=%async_computation.8 | async-start | bytes 1179648 | tf_op jit(solution)/shard_map/all_to_all | solution.py:20
  210.5 1.3 collective-permute-start.1
  211.9 1.3 collective-permute-start.2
  213.2 2.1 collective-permute-done.1
  215.8 4.9 %all-to-all-done.7 = bf16[8,144,256]{2,1,0:T(8,128)(2,1)S(1)} async-done(((bf16[8,144,256]{2,1,0:T(8,128)(2,1)}), bf16[8,144,256]{2,1,0:T(8,128)(2,1)S(1)}, u32[]{:S(2)}, u32[]{:S(2)}) %all-to-all-start.7) | async-done | bytes 589856 | tf_op jit(solution)/shard_map/all_to_all | solution.py:20
  220.7 4.0 %all-to-all-start.8 = ((bf16[4,576,256]{2,1,0:T(8,128)(2,1)}), bf16[4,576,256]{2,1,0:T(8,128)(2,1)S(1)}, u32[]{:S(2)}, u32[]{:S(2)}) async-start(bf16[4,576,256]{2,1,0:T(8,128)(2,1)} %get-tuple-element.36), calls=%async_computation.9 | async-start | bytes 2359296 | tf_op jit(solution)/shard_map/all_to_all | solution.py:20
  227.1 1.4 fusion.7
  229.1 11.0 %all-to-all-done.8 = bf16[4,576,256]{2,1,0:T(8,128)(2,1)S(1)} async-done(((bf16[4,576,256]{2,1,0:T(8,128)(2,1)}), bf16[4,576,256]{2,1,0:T(8,128)(2,1)S(1)}, u32[]{:S(2)}, u32[]{:S(2)}) %all-to-all-start.8) | async-done | bytes 1179680 | tf_op jit(solution)/shard_map/all_to_all | solution.py:20
  (85 shorter events, 12.5 us)
Async XLA Ops:
  7.2 22.8 %copy-start = (bf16[1,768,256]{2,1,0:T(8,128)(2,1)S(1)}, bf16[1,768,256]{2,1,0:T(8,128)(2,1)}, u32[]{:S(2)}) copy-start(bf16[1,768,256]{2,1,0:T(8,128)(2,1)} %param.35) | copy-start | bytes 1179652
  7.2 103.2 %reduce-scatter.2.cloned.1.call-start = ((), (), s32[]{:S(2)}) async-start(), calls=%async_computation.10 | async-start | bytes 1671168 | tf_op jit(solution)/shard_map/reduce_scatter | solution.py:388
  29.9 56.9 %copy-start.11 = (bf16[8,144,256]{2,1,0:T(8,128)(2,1)}, bf16[8,144,256]{2,1,0:T(8,128)(2,1)S(1)}, u32[]{:S(2)}) copy-start(bf16[8,144,256]{2,1,0:T(8,128)(2,1)S(1)} %all_to_all.45.cot_ref) | copy-start | bytes 1769476
  29.9 4.7 %copy-start.18 = (f32[8]{0:T(128)S(1)}, f32[8]{0:T(128)}, u32[]{:S(2)}) copy-start(f32[8]{0:T(128)} %param.22) | copy-start | bytes 100
  30.0 5.4 %copy-start.19 = (f32[8]{0:T(128)S(1)}, f32[8]{0:T(128)}, u32[]{:S(2)}) copy-start(f32[8]{0:T(128)} %param.23) | copy-start | bytes 100
  31.8 55.0 %copy-start.20 = (f32[8]{0:T(128)S(1)}, f32[8]{0:T(128)}, u32[]{:S(2)}) copy-start(f32[8]{0:T(128)} %param.24) | copy-start | bytes 100
  31.8 71.2 %copy-start.1 = (bf16[1,256,256]{2,1,0:T(8,128)(2,1)S(1)}, bf16[1,256,256]{2,1,0:T(8,128)(2,1)}, u32[]{:S(2)}) copy-start(bf16[1,256,256]{2,1,0:T(8,128)(2,1)} %param.20) | copy-start | bytes 393220
  31.8 71.2 %copy-start.2 = (bf16[1,256,512]{2,1,0:T(8,128)(2,1)S(1)}, bf16[1,256,512]{2,1,0:T(8,128)(2,1)}, u32[]{:S(2)}) copy-start(bf16[1,256,512]{2,1,0:T(8,128)(2,1)} %param.19) | copy-start | bytes 786436
  31.8 71.2 %copy-start.3 = (bf16[1,256,512]{2,1,0:T(8,128)(2,1)S(1)}, bf16[1,256,512]{2,1,0:T(8,128)(2,1)}, u32[]{:S(2)}) copy-start(bf16[1,256,512]{2,1,0:T(8,128)(2,1)} %param.27) | copy-start | bytes 786436
  31.8 71.2 %copy-start.4 = (f32[4,256]{1,0:T(4,128)S(1)}, f32[4,256]{1,0:T(4,128)}, u32[]{:S(2)}) copy-start(f32[4,256]{1,0:T(4,128)} %tapsbc_ref.5) | copy-start | bytes 12292
  31.8 71.2 %copy-start.8 = (f32[1,8,256]{2,1,0:T(8,128)S(1)}, f32[1,8,256]{2,1,0:T(8,128)}, u32[]{:S(2)}) copy-start(f32[1,8,256]{2,1,0:T(8,128)} %param.21) | copy-start | bytes 24580
  31.8 71.2 %copy-start.9 = (f32[4,512]{1,0:T(4,128)S(1)}, f32[4,512]{1,0:T(4,128)}, u32[]{:S(2)}) copy-start(f32[4,512]{1,0:T(4,128)} %tapsx_ref.3) | copy-start | bytes 24580
  33.3 2.7 %collective-permute-start = (bf16[3,768]{1,0:T(4,128)(2,1)S(1)}, bf16[3,768]{1,0:T(4,128)(2,1)S(1)}, u32[]{:S(2)}, u32[]{:S(2)}) collective-permute-start(bf16[3,768]{1,0:T(4,128)(2,1)S(1)} %pad_maximum_fusion), channel_id=1, source_target_pairs={{0,1},{1,2},{2,3},{3,4},{4,5},{5,6},{6,7},{7,8},{8,9},{9,10},{10,1... | collective-permute-start | bytes 13832 | tf_op jit(solution)/shard_map/ppermute | solution.py:16
  35.3 67.7 %copy-start.5 = (f32[8,1]{1,0:T(8,128)S(1)}, f32[8,1]{1,0:T(8,128)}, u32[]{:S(2)}) copy-start(f32[8,1]{1,0:T(8,128)} %copy.45.bias_ref) | copy-start | bytes 100
  36.0 67.0 %copy-start.6 = (f32[8,1]{1,0:T(8,128)S(1)}, f32[8,1]{1,0:T(8,128)}, u32[]{:S(2)}) copy-start(f32[8,1]{1,0:T(8,128)} %copy.46.rate_ref) | copy-start | bytes 100
  36.6 66.4 %copy-start.10 = (bf16[3,256]{1,0:T(4,128)(2,1)S(1)}, bf16[3,256]{1,0:T(4,128)(2,1)}, u32[]{:S(2)}) copy-start(bf16[3,256]{1,0:T(4,128)(2,1)} %slice.87.befores_ref) | copy-start | bytes 4612
  37.2 65.8 %copy-start.7 = (bf16[3,512]{1,0:T(4,128)(2,1)S(1)}, bf16[3,512]{1,0:T(4,128)(2,1)}, u32[]{:S(2)}) copy-start(bf16[3,512]{1,0:T(4,128)(2,1)} %slice.86.beforeh_ref) | copy-start | bytes 9220
  74.4 28.5 %all-to-all-start.1 = ((bf16[16,64,128]{2,1,0:T(8,128)(2,1)}), bf16[16,64,128]{2,1,0:T(8,128)(2,1)S(1)}, u32[]{:S(2)}, u32[]{:S(2)}) async-start(bf16[16,64,128]{2,1,0:T(8,128)(2,1)} %shard_map.267), calls=%async_computation.1 | async-start | bytes 524288 | tf_op jit(solution)/shard_map/all_to_all | solution.py:20
  86.7 106.3 %all-gather.2.cloned.1.call-start = ((), (), s32[]{:S(2)}) async-start(), calls=%async_computation.11 | async-start | bytes 5292032 | tf_op jit(solution)/shard_map/all_gather | solution.py:479
  112.3 47.9 %copy-start.21 = (bf16[1,512,256]{2,1,0:T(8,128)(2,1)S(1)}, bf16[1,512,256]{2,1,0:T(8,128)(2,1)}, u32[]{:S(2)}) copy-start(bf16[1,512,256]{2,1,0:T(8,128)(2,1)} %param.28) | copy-start | bytes 786436
  112.3 24.8 %all-to-all-start.2 = ((bf16[8,256,256]{2,1,0:T(8,128)(2,1)}), bf16[8,256,256]{2,1,0:T(8,128)(2,1)S(1)}, u32[]{:S(2)}, u32[]{:S(2)}) async-start(bf16[8,256,256]{2,1,0:T(8,128)(2,1)} %get-tuple-element.27), calls=%async_computation.2 | async-start | bytes 2097152 | tf_op jit(solution)/shard_map/all_to_all | solution.py:20
  151.4 20.7 %all-to-all-start.4 = ((f32[16,8,128]{2,1,0:T(8,128)}), f32[16,8,128]{2,1,0:T(8,128)S(1)}, u32[]{:S(2)}, u32[]{:S(2)}) async-start(f32[16,8,128]{2,1,0:T(8,128)} %broadcast_in_dim.90), calls=%async_computation.4 | async-start | bytes 131072 | tf_op jit(solution)/shard_map/all_to_all | solution.py:20
  172.1 16.7 %all-to-all-start.6 = ((bf16[8,128,256]{2,1,0:T(8,128)(2,1)}), bf16[8,128,256]{2,1,0:T(8,128)(2,1)S(1)}, u32[]{:S(2)}, u32[]{:S(2)}) async-start(bf16[8,128,256]{2,1,0:T(8,128)(2,1)} %bitcast.30), calls=%async_computation.7 | async-start | bytes 1048576 | tf_op jit(solution)/shard_map/all_to_all | solution.py:20
  188.8 4.2 %copy-start.13 = (bf16[8,128,256]{2,1,0:T(8,128)(2,1)}, bf16[8,128,256]{2,1,0:T(8,128)(2,1)S(1)}, u32[]{:S(2)}) copy-start(bf16[8,128,256]{2,1,0:T(8,128)(2,1)S(1)} %all-to-all-done.6.in_ref) | copy-start | bytes 1572868
  193.0 18.8 %copy-start.17 = (f32[8,256]{1,0:T(8,128)S(1)}, f32[8,256]{1,0:T(8,128)}, u32[]{:S(2)}) copy-start(f32[8,256]{1,0:T(8,128)} %get-tuple-element.30) | copy-start | bytes 24580
  199.3 25.4 %copy-start.15 = (f32[16,256]{1,0:T(8,128)S(1)}, f32[16,256]{1,0:T(8,128)}, u32[]{:S(2)}) copy-start(f32[16,256]{1,0:T(8,128)} %get-tuple-element.29) | copy-start | bytes 49156
  199.3 26.0 %copy-start.14 = (f32[8,128]{1,0:T(8,128)S(1)}, f32[8,128]{1,0:T(8,128)}, u32[]{:S(2)}) copy-start(f32[8,128]{1,0:T(8,128)} %reduce_sum.31) | copy-start | bytes 12292
  199.3 21.4 %all-to-all-start.7 = ((bf16[8,144,256]{2,1,0:T(8,128)(2,1)}), bf16[8,144,256]{2,1,0:T(8,128)(2,1)S(1)}, u32[]{:S(2)}, u32[]{:S(2)}) async-start(bf16[8,144,256]{2,1,0:T(8,128)(2,1)} %get-tuple-element.35), calls=%async_computation.8 | async-start | bytes 1179648 | tf_op jit(solution)/shard_map/all_to_all | solution.py:20
  210.5 4.7 %collective-permute-start.1 = (f32[3,512]{1,0:T(4,128)S(1)}, f32[3,512]{1,0:T(4,128)S(1)}, u32[]{:S(2)}, u32[]{:S(2)}) collective-permute-start(f32[3,512]{1,0:T(4,128)S(1)} %slice.71), channel_id=1, source_target_pairs={{1,0},{2,1},{3,2},{4,3},{5,4},{6,5},{7,6},{8,7},{9,8},{10,9},{11,1... | collective-permute-start | bytes 18440 | tf_op jit(solution)/shard_map/ppermute | solution.py:16
  211.9 12.9 %collective-permute-start.2 = (f32[3,256]{1,0:T(4,128)S(1)}, f32[3,256]{1,0:T(4,128)S(1)}, u32[]{:S(2)}, u32[]{:S(2)}) collective-permute-start(f32[3,256]{1,0:T(4,128)S(1)} %slice.72), channel_id=1, source_target_pairs={{1,0},{2,1},{3,2},{4,3},{5,4},{6,5},{7,6},{8,7},{9,8},{10,9},{11,1... | collective-permute-start | bytes 9224 | tf_op jit(solution)/shard_map/ppermute | solution.py:16
  220.7 19.4 %all-to-all-start.8 = ((bf16[4,576,256]{2,1,0:T(8,128)(2,1)}), bf16[4,576,256]{2,1,0:T(8,128)(2,1)S(1)}, u32[]{:S(2)}, u32[]{:S(2)}) async-start(bf16[4,576,256]{2,1,0:T(8,128)(2,1)} %get-tuple-element.36), calls=%async_computation.9 | async-start | bytes 2359296 | tf_op jit(solution)/shard_map/all_to_all | solution.py:20
  227.0 1.5 copy-start.16
  (1 other events, 1.0 us)
Sparse Core Ops, SparseCore 0:
  32.0 74.9 reduce-scatter.1
  112.5 80.5 all-gather.1

commit v3 on v2

--- a/solution.py
+++ b/solution.py
@@ -18,6 +18,11 @@
 
 def exchange(value, axis):
     return lax.all_to_all(value, axis, split_axis=0, concat_axis=0, tiled=True)
+
+
+def shift(value, distance):
+    count = lax.axis_size("ctx")
+    return lax.ppermute(value, "ctx", [(i, (i + distance) % count) for i in range(count)])
 
 
 def copies(value, count):
@@ -38,11 +43,11 @@
     return lax.broadcasted_iota(jnp.int32, shape, axis)
 
 
-def conv_pre(rows_ref, before_ref, taps_ref, pad_ref):
+def conv_pre(rows_ref, before, taps_ref, pad_ref):
     length, width = rows_ref.shape
     taps = taps_ref.shape[0]
     pad_ref[0:8, :] = jnp.zeros((8, width), F32)
-    pad_ref[8 - (taps - 1) : 8, :] = before_ref[...].astype(F32)
+    pad_ref[8 - (taps - 1) : 8, :] = before.astype(F32)
     pad_ref[8:, :] = rows_ref[...].astype(F32)
     pre = None
     for k in range(taps):
@@ -75,10 +80,16 @@
     return rows, rim, sums
 
 
-def steps_of(raw_ref, bias_ref, rate_ref):
-    shifted = raw_ref[...] + bias_ref[...]
+def gain_column(gains_ref, which):
+    heads = gains_ref.shape[1]
+    eye = iota((heads, heads), 0) == iota((heads, heads), 1)
+    return jnp.sum(jnp.where(eye, gains_ref[which : which + 1, :], 0.0), axis=1, keepdims=True)
+
+
+def steps_of(raw_ref, gains_ref):
+    shifted = raw_ref[...] + gain_column(gains_ref, 0)
     step = jnp.maximum(shifted, 0.0) + jnp.log1p(jnp.exp(-jnp.abs(shifted)))
-    rate = jnp.exp(rate_ref[...])
+    rate = jnp.exp(gain_column(gains_ref, 1))
     log_decay = -rate * step
     length = shifted.shape[1]
     square = (length, length)
@@ -93,7 +104,7 @@
 
 
 def front_kernel(
-    rows_ref, shared_ref, beforeh_ref, befores_ref, raw_ref, bias_ref, rate_ref, tapsx_ref,
+    rows_ref, shared_ref, before_ref, raw_ref, gains_ref, tapsx_ref,
     tapsbc_ref, cot_ref, out_ref, padh_ref, pads_ref,
 ):
     heads = raw_ref.shape[0]
@@ -101,11 +112,12 @@
     states = shared_ref.shape[1] // 2
     places = out_ref.shape[0]
     part = heads * width // places
-    pre, sig = conv_pre(rows_ref, beforeh_ref, tapsx_ref, padh_ref)
+    pre, sig = conv_pre(rows_ref, before_ref[:, : rows_ref.shape[1]], tapsx_ref, padh_ref)
     x = pre * sig
-    pre_s, sig_s = conv_pre(shared_ref, befores_ref, tapsbc_ref, pads_ref)
+    before_s = before_ref[:, rows_ref.shape[1] :]
+    pre_s, sig_s = conv_pre(shared_ref, before_s, tapsbc_ref, pads_ref)
     bc = (pre_s * sig_s).astype(BF16)
-    _, step, _, _, _, cumulative = steps_of(raw_ref, bias_ref, rate_ref)
+    _, step, _, _, _, cumulative = steps_of(raw_ref, gains_ref)
     length = step.shape[1]
     ending = cumulative[:, length - 1 :]
     spread = head_spread(heads, width)
@@ -130,7 +142,7 @@
 
 
 def back_kernel(
-    rows_ref, shared_ref, beforeh_ref, befores_ref, raw_ref, bias_ref, rate_ref, skip_ref,
+    rows_ref, shared_ref, before_ref, raw_ref, gains_ref,
     tapsx_ref, tapsbc_ref, cot_ref, got_ref,
     main_ref, tail_ref, rim_ref, bc_ref, raw_out_ref, taps_out_ref, rate_out_ref,
     padh_ref, pads_ref, dv_ref, sums_ref,
@@ -139,18 +151,19 @@
     width = rows_ref.shape[1] // heads
     states = shared_ref.shape[1] // 2
     part = got_ref.shape[1] // 2
-    pre, sig = conv_pre(rows_ref, beforeh_ref, tapsx_ref, padh_ref)
+    pre, sig = conv_pre(rows_ref, before_ref[:, : rows_ref.shape[1]], tapsx_ref, padh_ref)
     x = pre * sig
-    pre_s, sig_s = conv_pre(shared_ref, befores_ref, tapsbc_ref, pads_ref)
+    before_s = before_ref[:, rows_ref.shape[1] :]
+    pre_s, sig_s = conv_pre(shared_ref, before_s, tapsbc_ref, pads_ref)
     bc = (pre_s * sig_s).astype(BF16)
     b_rows, c_rows = bc[:, :states], bc[:, states:]
-    shifted, step, rate, log_decay, upto, cumulative = steps_of(raw_ref, bias_ref, rate_ref)
+    shifted, step, rate, log_decay, upto, cumulative = steps_of(raw_ref, gains_ref)
     ending = cumulative[:, length - 1 :]
     spread = head_spread(heads, width)
     weight = dot(jnp.exp(ending - cumulative) * step, spread, 0, 0, True)
     grown = dot(jnp.exp(cumulative), spread, 0, 0, True)
     step_cols = dot(step, spread, 0, 0, True)
-    skip_cols = jnp.sum(skip_ref[...] * spread, axis=0, keepdims=True)
+    skip_cols = jnp.sum(gain_column(gains_ref, 2) * spread, axis=0, keepdims=True)
     state_in = got_ref[:, :part, :].reshape(heads * width, states)
     pull_out = got_ref[:, part:, :].reshape(heads * width, states)
     cot = cot_ref[...]
@@ -230,11 +243,12 @@
 
 
 def shared_kernel(
-    shared_ref, befores_ref, tapsbc_ref, got_ref,
+    shared_ref, before_ref, tapsbc_ref, got_ref,
     main_ref, tail_ref, rim_ref, taps_out_ref, pads_ref, dv_ref,
 ):
     length = shared_ref.shape[0]
-    pre, sig = conv_pre(shared_ref, befores_ref, tapsbc_ref, pads_ref)
+    before = before_ref[:, before_ref.shape[1] - shared_ref.shape[1] :]
+    pre, sig = conv_pre(shared_ref, before, tapsbc_ref, pads_ref)
     total = got_ref[0].astype(F32)
     for source in range(1, got_ref.shape[0]):
         total = total + got_ref[source].astype(F32)
@@ -247,57 +261,104 @@
         taps_out_ref[k : k + 1, :] = value
 
 
-def own_rows_kernel(mine_ref, weight_ref, gate_ref, up_ref, after_ref, out_ref):
-    del after_ref
-    width = mine_ref.shape[1]
-    unscaled = mine_ref[...].astype(F32)
-    gate = gate_ref[...].astype(F32)
-    up = up_ref[...].astype(F32)
-    grad_hidden = weight_ref[...] * unscaled
-    sig = jax.nn.sigmoid(gate)
-    activated = gate * sig
-    hidden = (activated * up).astype(BF16)
-    slope = sig * (1.0 + gate * (1.0 - sig))
-    out_ref[:, :width] = (grad_hidden * up * slope).astype(BF16)
-    out_ref[:, width : 2 * width] = (grad_hidden * activated).astype(BF16)
-    out_ref[:, 2 * width : 3 * width] = hidden
-    route = jnp.sum(hidden.astype(F32) * unscaled, axis=1, keepdims=True)
-    coarse = route.astype(BF16).astype(F32)
-    lanes = (mine_ref.shape[0], 128)
-    out_ref[:, 3 * width :] = jnp.where(
-        iota(lanes, 1) == 0, coarse, jnp.where(iota(lanes, 1) == 1, route - coarse, 0.0)
-    ).astype(BF16)
-
-
-def rows_kernel(all_ref, in_ref, cot_ref, gatew_ref, upw_ref, after_ref, back_ref, parts_ref):
-    del after_ref
+FAR = 5
+CENTRE = (-FAR, 0, FAR)
+OPPOSITE = 8
+
+
+def shifted_by(distance):
+    return tuple(distance + step for step in CENTRE)
+
+
+def rows_of(cot_ref, block, rows):
+    per_group = (cot_ref.shape[1] - 16) // rows
+    start = pl.multiple_of((block % per_group) * rows, rows)
+    return cot_ref[block // per_group, pl.ds(start, rows), :]
+
+
+def unscaled_kernel(place_ref, cot_ref, down_ref, *refs):
+    out_refs, rows_ref = refs[:-1], refs[-1]
+    places = rows_ref.shape[0] // out_refs[-1].shape[0]
+    rows = out_refs[-1].shape[0]
+    place = place_ref[0]
+    at = 0
+    for distances in (shifted_by(-2), shifted_by(2), shifted_by(-1), shifted_by(1), CENTRE, (OPPOSITE,)):
+        for distance in distances:
+            block = lax.rem(place + distance + places, places)
+            rows_ref[at : at + rows, :] = rows_of(cot_ref, block, rows)
+            at += rows
+    product = dot(rows_ref[...], down_ref[...], 1, 1).astype(BF16)
+    at = 0
+    for out_ref in out_refs:
+        out_ref[...] = product[at : at + out_ref.shape[0]]
+        at += out_ref.shape[0]
+
+
+def scaled_rows(cot_ref, group):
+    slots = cot_ref.shape[1] - 16
+    weight = cot_ref[group, slots:, :slots].astype(F32).T[:, 0:1]
+    return weight, (cot_ref[group, :slots, :].astype(F32) * weight).astype(BF16)
+
+
+def down_kernel(acts_ref, cot_ref, parts_ref):
+    width = acts_ref.shape[1] // 2
+    gate = acts_ref[:, :width].astype(F32)
+    up = acts_ref[:, width:].astype(F32)
+    hidden = (gate * jax.nn.sigmoid(gate) * up).astype(BF16)
+    groups = cot_ref.shape[0]
+    scaled = jnp.concatenate([scaled_rows(cot_ref, group)[1] for group in range(groups)], axis=0)
+    parts_ref[...] = dot(hidden, scaled, 0, 0).astype(BF16).reshape(parts_ref.shape)
+
+
+def rows_kernel(
+    place_ref, centre_ref, left1_ref, right1_ref, left2_ref, right2_ref, opposite_ref,
+    acts_ref, in_ref, cot_ref, gatew_ref, upw_ref, *refs,
+):
+    back_ref, parts_ref, all_ref, gate_ref, up_ref = refs[-5:]
     groups, slots, cols = in_ref.shape
-    width = gatew_ref.shape[1]
-    owners, share3 = parts_ref.shape[0], parts_ref.shape[1]
-    share = share3 // 3
-    rows_grad = dot(all_ref[:, :width], gatew_ref[...], 1, 1)
-    rows_grad = rows_grad + dot(all_ref[:, width : 2 * width], upw_ref[...], 1, 1)
+    total, width = all_ref.shape
+    owners = parts_ref.shape[0]
+    share = parts_ref.shape[1] // 2
+    rows = opposite_ref.shape[0]
+    places = total // rows
+    place = place_ref[0]
+    pieces = (
+        (centre_ref, 0), (left1_ref, -1), (right1_ref, 1), (left2_ref, -2), (right2_ref, 2)
+    )
+    for piece_ref, distance in pieces:
+        for i, step in enumerate(shifted_by(distance)):
+            block = lax.rem(place + step + places, places)
+            start = pl.multiple_of(block * rows, rows)
+            all_ref[pl.ds(start, rows), :] = piece_ref[i * rows : (i + 1) * rows, :]
+    block = lax.rem(place + OPPOSITE, places)
+    all_ref[pl.ds(pl.multiple_of(block * rows, rows), rows), :] = opposite_ref[...]
+    for group in range(groups):
+        span = slice(group * slots, (group + 1) * slots)
+        unscaled = all_ref[span, :].astype(F32)
+        gate = acts_ref[span, :width].astype(F32)
+        up = acts_ref[span, width:].astype(F32)
+        weight = cot_ref[group, slots:, :slots].astype(F32).T[:, 0:1]
+        sig = jax.nn.sigmoid(gate)
+        activated = gate * sig
+        hidden = (activated * up).astype(BF16).astype(F32)
+        grad_hidden = weight * unscaled
+        slope = sig * (1.0 + gate * (1.0 - sig))
+        gate_ref[span, :] = (grad_hidden * up * slope).astype(BF16)
+        up_ref[span, :] = (grad_hidden * activated).astype(BF16)
+        route = jnp.sum(hidden * unscaled, axis=1, keepdims=True)
+        line = jnp.broadcast_to(route, (slots, 128)).T[0:1]
+        coarse = line.astype(BF16).astype(F32)
+        line = jnp.concatenate([coarse, line - coarse], axis=1)
+        back_ref[group, slots:, :] = jnp.broadcast_to(line, (16, cols)).astype(BF16)
+    rows_grad = dot(gate_ref[...], gatew_ref[...], 1, 1) + dot(up_ref[...], upw_ref[...], 1, 1)
     back_ref[:, :slots, :] = rows_grad.astype(BF16).reshape(groups, slots, cols)
-    route = all_ref[:, 3 * width :].astype(F32)
-    scaled = []
-    for group in range(groups):
-        turned = route[group * slots : (group + 1) * slots].T
-        line = jnp.concatenate([turned[0:1], turned[1:2]], axis=1)
-        back_ref[group, slots:, :] = jnp.broadcast_to(line, (16, cols)).astype(BF16)
-        weight = cot_ref[group, slots:, :slots].astype(F32).T[:, 0:1]
-        scaled.append((cot_ref[group, :slots, :].astype(F32) * weight).astype(BF16))
-    scaled = jnp.concatenate(scaled, axis=0)
-    rows_in = in_ref[...].reshape(groups * slots, cols)
-    grads = [
-        dot(all_ref[:, :width], rows_in, 0, 0).astype(BF16),
-        dot(all_ref[:, width : 2 * width], rows_in, 0, 0).astype(BF16),
-        dot(all_ref[:, 2 * width : 3 * width], scaled, 0, 0).astype(BF16),
-    ]
-    for owner in range(owners):
-        for kind in range(3):
-            parts_ref[owner, kind * share : (kind + 1) * share, :] = grads[kind][
-                owner * share : (owner + 1) * share
-            ]
+    rows_in = in_ref[...].reshape(total, cols)
+    parts_ref[:, :share, :] = (
+        dot(gate_ref[...], rows_in, 0, 0).astype(BF16).reshape(owners, share, cols)
+    )
+    parts_ref[:, share:, :] = (
+        dot(up_ref[...], rows_in, 0, 0).astype(BF16).reshape(owners, share, cols)
+    )
 
 
 def scan_kernel(got_ref, out_ref):
@@ -320,8 +381,9 @@
         state = decay[j] * state + got_ref[j, half : 2 * half, :].astype(F32)
 
 
-def whole(kernel, outs, scratch=(), late=0, inputs=0, limit=None):
-    specs = [pl.BlockSpec(memory_space=pltpu.VMEM)] * inputs
+def whole(kernel, outs, scratch=(), inputs=0, scalars=0, late=0, limit=None):
+    specs = [pl.BlockSpec(memory_space=pltpu.SMEM)] * scalars
+    specs += [pl.BlockSpec(memory_space=pltpu.VMEM)] * inputs
     specs += [pl.BlockSpec(memory_space=pl.ANY)] * late
     return pl.pallas_call(
         kernel,
@@ -367,11 +429,32 @@
         lax.axis_size("expert"),
         lax.axis_size("ctx"),
     )
+    place = lax.axis_index("ctx").astype(jnp.int32).reshape(1)
+    rim_rows = conv_x.shape[0] - 1
+    head_rows = mamba_in[0]
+    shared_rows = shared_in[0]
+    cot_rows = mamba_cot[0]
+    raw_step = dt_raw[0]
+    length, split_at = head_rows.shape
+    shared_width = shared_rows.shape[1]
+    state_width = shared_width // 2
+    heads_here = dt_bias.shape[0]
+    part = split_at // ctx_places
+    before = passed_along(
+        jnp.concatenate([head_rows[length - rim_rows :], shared_rows[length - rim_rows :]], axis=1),
+        "ctx",
+        1,
+    )
+    acts = lax.all_gather(
+        jnp.concatenate([gate_act[0, 0], up_act[0, 0]], axis=1), "ctx", axis=0, tiled=True
+    )
+
     col_width = moe_in.shape[2]
     token_count = moe_in.shape[1]
     expert_count = slot_tok.shape[2]
     slot_width = slot_tok.shape[3]
     hidden_width = w_gate.shape[2]
+    own = gate_act.shape[2]
     slot_ids = slot_tok[0, 0]
     live_slots = jnp.arange(slot_width, dtype=jnp.int32)[None, :] < slot_count[0, 0][:, None]
     chosen = jnp.where(live_slots, slot_ids, -1).reshape(-1)
@@ -382,44 +465,45 @@
     send_weight = jnp.pad(send_weight[:, None, :], ((0, 0), (0, 15), (0, col_width - slot_width)))
     send_cot = send_cot.reshape(expert_count, slot_width, col_width)
     got_cot = exchange(jnp.concatenate([send_cot, send_weight], axis=1), "expert")
-    rows_cot = got_cot[:, :slot_width].reshape(-1, col_width)
-    rows_weight = got_cot[:, slot_width, :slot_width].reshape(-1).astype(F32)
-    unscaled = jnp.dot(rows_cot, w_down[0].T, preferred_element_type=F32)
-    mine = lax.psum_scatter(unscaled.astype(BF16), "ctx", scatter_dimension=0, tiled=True)
     send_in = jnp.dot(table, moe_in[0], preferred_element_type=F32).astype(BF16)
     rows_in = exchange(send_in.reshape(expert_count, slot_width, col_width), "expert")
 
-    rim_rows = conv_x.shape[0] - 1
-    head_rows = mamba_in[0]
-    shared_rows = shared_in[0]
-    cot_rows = mamba_cot[0]
-    raw_step = dt_raw[0]
-    length, split_at = head_rows.shape
-    shared_width = shared_rows.shape[1]
-    state_width = shared_width // 2
-    heads_here = dt_bias.shape[0]
-    part = split_at // ctx_places
-    bias, rate, skip = dt_bias[:, None], a_log[:, None], d_skip[:, None]
-    before = passed_along(
-        jnp.concatenate([head_rows[length - rim_rows :], shared_rows[length - rim_rows :]], axis=1),
-        "ctx",
-        1,
-    )
-    before_heads, before_shared = before[:, :split_at], before[:, split_at:]
+    gains = jnp.stack([dt_bias, a_log, d_skip])
     pad_heads = ((8 + length, split_at), F32)
     pad_shared = ((8 + length, shared_width), F32)
     (states,) = whole(
         front_kernel,
         [((ctx_places, 2 * part + 16, state_width), BF16)],
         [pad_heads, pad_shared],
-        inputs=10,
-    )(
-        head_rows, shared_rows, before_heads, before_shared, raw_step, bias, rate, conv_x,
-        conv_bc, cot_rows,
-    )
+        inputs=8,
+    )(head_rows, shared_rows, before, raw_step, gains, conv_x, conv_bc, cot_rows)
     (entered,) = whole(
         scan_kernel, [((ctx_places, 2 * part, state_width), BF16)], inputs=1
     )(exchange(states, "ctx"))
+
+    three, one = (3 * own, hidden_width), (own, hidden_width)
+    left2, right2, left1, right1, centre, opposite = whole(
+        unscaled_kernel,
+        [(three, BF16)] * 5 + [(one, BF16)],
+        [((ctx_places * own, col_width), BF16)],
+        inputs=2,
+        scalars=1,
+    )(place, got_cot, w_down[0])
+    opposite = shift(opposite, 3)
+    left1 = (left1.astype(F32) + shift(left2, -1).astype(F32)).astype(BF16)
+    right1 = (right1.astype(F32) + shift(right2, 1).astype(F32)).astype(BF16)
+    centre = centre.astype(F32) + shift(left1, -1).astype(F32) + shift(right1, 1).astype(F32)
+    far_left = shift(centre[:own].astype(BF16), -FAR)
+    far_right = shift((centre[2 * own :] + opposite.astype(F32)).astype(BF16), FAR)
+    mine = centre[own : 2 * own] + far_left.astype(F32) + far_right.astype(F32)
+    mine = mine.astype(BF16)
+
+    from_left, from_right = shift(mine, FAR), shift(mine, -FAR)
+    opposite = shift(from_right, -3)
+    centre = jnp.concatenate([from_left, mine, from_right], axis=0)
+    left1, right1 = shift(centre, 1), shift(centre, -1)
+    left2, right2 = shift(left1, 1), shift(right1, -1)
+
     main_heads, tail_heads, rim_heads, grad_bc, grad_step, taps_heads, grad_rate = whole(
         back_kernel,
         [
@@ -432,11 +516,11 @@
             ((1, 128), F32),
         ],
         [pad_heads, pad_shared, ((16 + length, split_at), F32), ((heads_here, length), F32)],
-        inputs=12,
+        inputs=9,
         limit=48 * 2**20,
     )(
-        head_rows, shared_rows, before_heads, before_shared, raw_step, bias, rate, skip, conv_x,
-        conv_bc, cot_rows, exchange(entered, "ctx"),
+        head_rows, shared_rows, before, raw_step, gains, conv_x, conv_bc, cot_rows,
+        exchange(entered, "ctx"),
     )
     after_heads = passed_along(rim_heads[:rim_rows], "ctx", -1)
     grad_mamba_in = with_last_rows(main_heads, tail_heads, after_heads)
@@ -450,7 +534,7 @@
         ],
         [pad_shared, ((16 + length, shared_width), F32)],
         inputs=4,
-    )(shared_rows, before_shared, conv_bc, exchange(grad_bc, "expert"))
+    )(shared_rows, before, conv_bc, exchange(grad_bc, "expert"))
     after_shared = passed_along(rim_shared[:rim_rows], "ctx", -1)
     grad_shared_in = with_last_rows(main_shared, tail_shared, after_shared)
     small = jnp.concatenate(
@@ -468,26 +552,26 @@
     taps_shared = small[:, split_at : split_at + shared_width]
     rate_total = small[0, split_at + shared_width :][:heads_here]
 
-    own = gate_act.shape[2]
-    weight_own = lax.dynamic_slice_in_dim(rows_weight, lax.axis_index("ctx") * own, own, 0)
-    (own_rows,) = whole(
-        own_rows_kernel,
-        [((own, 3 * hidden_width + 128), BF16)],
-        inputs=4,
-        late=1,
-    )(mine, weight_own[:, None], gate_act[0, 0], up_act[0, 0], grad_step)
-    everything = lax.all_gather(own_rows, "ctx", axis=0, tiled=True)
     share = hidden_width // dp_count
+    (down_parts,) = whole(
+        down_kernel, [((dp_count, share, col_width), BF16)], inputs=2, limit=48 * 2**20
+    )(acts, got_cot)
+    down_total = jnp.sum(exchange(down_parts, "dp").astype(F32), axis=0).astype(BF16)
+    all_rows = ((ctx_places * own, hidden_width), BF16)
     back, parts = whole(
         rows_kernel,
         [
             ((expert_count, slot_width + 16, col_width), BF16),
-            ((dp_count, 3 * share, col_width), BF16),
+            ((dp_count, 2 * share, col_width), BF16),
         ],
-        inputs=5,
-        late=1,
+        [all_rows] * 3,
+        inputs=11,
+        scalars=1,
         limit=56 * 2**20,
-    )(everything, rows_in, got_cot, w_gate[0], w_up[0], small)
+    )(
+        place, centre, left1, right1, left2, right2, opposite, acts, rows_in, got_cot,
+        w_gate[0], w_up[0],
+    )
     back = exchange(back, "expert")
     parts = exchange(parts, "dp")
     grad_tokens = lax.dot_general(
@@ -511,8 +595,8 @@
         grad_tokens.astype(BF16)[None],
         route_total[None, None],
         totals[:share].T[None],
-        totals[share : 2 * share].T[None],
-        totals[2 * share :][None],
+        totals[share:].T[None],
+        down_total[None],
     )
 
 

time: 249 us -> 291 us (1.17)
  starting transfers between devices: 57.2 us -> 142 us
  blocking collectives: 60.2 us -> 0 us
  waiting for transfers between devices: 72 us -> 81.1 us
  other arithmetic: 5.12 us -> 9.78 us
  Pallas kernels: 24.1 us -> 27.6 us
    ppermute x0 -> x14, starting transfers between devices: none -> 60.7 us  [shift(): lax.ppermute(value, 'ctx', [(i, (i + distance) % count) for i in range(co...]
    all_to_all x3 -> x0, blocking collectives: 60.2 us -> none  [exchange(): return lax.all_to_all(value, axis, split_axis=0, concat_axis=0, tiled=True)]
    ppermute x0 -> x14, waiting for transfers between devices: none -> 33.6 us  [shift(): lax.ppermute(value, 'ctx', [(i, (i + distance) % count) for i in range(co...]
    all_to_all x6 -> x10, starting transfers between devices: 53.3 us -> 74.2 us  [exchange(): return lax.all_to_all(value, axis, split_axis=0, concat_axis=0, tiled=True)]
    all_to_all x6 -> x10, waiting for transfers between devices: 65.7 us -> 47.4 us  [exchange(): return lax.all_to_all(value, axis, split_axis=0, concat_axis=0, tiled=True)]
    all_gather x1, waiting for transfers between devices: 4.2 us -> 0.02 us  [body(): lax.all_gather(jnp.concatenate([gate_act[0, 0], up_act[0, 0]], axis=1), '...]
    unnamed x46 -> x62, local copies, waits for them, and re-layouts: 1.12 us -> 5.04 us
    ppermute x3, starting transfers between devices: 3.86 us -> 6.95 us  [passed_along(): lax.ppermute(value, axis, [(source, source + steps) for source in range(f...]
  transfers between devices with their start and end apart: 11 -> 28, of which waited for: 8 -> 12; matrix products, arithmetic and copies ran while one was open for 5% -> 5% of each run, Pallas kernels for 6% -> 10%
where the time goes in v3:
time: 291 us; the launch traced here: 288 us
  starting transfers between devices  142 us (49%)
  waiting for transfers between devices  81.1 us (28%)
  Pallas kernels  27.6 us (9%)
  between operations  14.7 us (5%)
  other arithmetic  9.78 us (3%)
  local copies, waits for them, and re-layouts  9.52 us (3%)
  matrix products  3.16 us (1%)
    all_to_all x10, starting transfers between devices, exchange(): return lax.all_to_all(value, axis, split_axis=0, concat_axis=0, tiled=True)  74.2 us
    ppermute x14, starting transfers between devices, shift(): lax.ppermute(value, 'ctx', [(i, (i + distance) % count) for i in range(co...  60.7 us
    all_to_all x10, waiting for transfers between devices, exchange(): return lax.all_to_all(value, axis, split_axis=0, concat_axis=0, tiled=True)  47.4 us
    ppermute x14, waiting for transfers between devices, shift(): lax.ppermute(value, 'ctx', [(i, (i + distance) % count) for i in range(co...  33.6 us
    pallas_call x1, Pallas kernels, body(): whole(rows_kernel, [((expert_count, slot_width + 16, col_width), BF16), (...  7.29 us
    ppermute x3, starting transfers between devices, passed_along(): lax.ppermute(value, axis, [(source, source + steps) for source in range(f...  6.95 us
    pallas_call x1, Pallas kernels, body(): whole(back_kernel, [((length, split_at), BF16), ((16, split_at), F32), ((...  6.94 us
  transfers between devices with their start and end apart: 28, of which 12 were waited for; matrix products, arithmetic and copies ran while one was open for 5% of the time, Pallas kernels for 10%

profile of v3, /device:TPU:1, one launch (start us, length us, event | category | flops | bytes accessed | tf_op | source)
XLA Modules:
  0.0 287.7 jit_solution(13865228234320510149)
XLA Ops:
  10.4 4.4 %collective-permute-start = (bf16[3,768]{1,0:T(4,128)(2,1)S(1)}, bf16[3,768]{1,0:T(4,128)(2,1)S(1)}, u32[]{:S(2)}, u32[]{:S(2)}) collective-permute-start(bf16[3,768]{1,0:T(4,128)(2,1)S(1)} %pad_maximum_fusion.2), channel_id=1, source_target_pairs={{0,1},{1,2},{2,3},{3,4},{4,5},{5,6},{6,7},{7,8},{8,9},{9,10},{10,1... | collective-permute-start | bytes 13832 | tf_op jit(solution)/shard_map/ppermute | solution.py:16
  16.6 3.9 %shard_map.266 = bf16[16,80,128]{2,1,0:T(8,128)(2,1)} custom-call(bf16[256,512]{1,0:T(8,128)(2,1)} %bitcast.74, bf16[256,256]{1,0:T(8,128)(2,1)} %bitcast.71, bf16[3,768]{1,0:T(4,128)(2,1)} %copy-done.7, f32[8,256]{1,0:T(8,128)} %bitcast.78, f32[3,8]{1,0:T(4,128)} %pad_maximum_fusion.3.gains_ref, f32[4,512]{1,0:T(4,128)} %tapsx_ref.3, f32[4,256]{1,0:T(4,128)} %tapsbc_ref.5, ...), custom_call_target="tpu_custom_call" | custom-call | tf_op jit(solution)/shard_map/pallas_call | solution.py:474
  20.5 15.7 %all-to-all-start = ((bf16[16,80,128]{2,1,0:T(8,128)(2,1)}), bf16[16,80,128]{2,1,0:T(8,128)(2,1)S(1)}, u32[]{:S(2)}, u32[]{:S(2)}) async-start(bf16[16,80,128]{2,1,0:T(8,128)(2,1)} %shard_map.266), calls=%async_computation | async-start | bytes 655360 | tf_op jit(solution)/shard_map/all_to_all | solution.py:20
  37.8 19.2 %all-to-all-done.got_ref = bf16[16,80,128]{2,1,0:T(8,128)(2,1)S(1)} async-done(((bf16[16,80,128]{2,1,0:T(8,128)(2,1)}), bf16[16,80,128]{2,1,0:T(8,128)(2,1)S(1)}, u32[]{:S(2)}, u32[]{:S(2)}) %all-to-all-start) | async-done | bytes 327712 | tf_op jit(solution)/shard_map/all_to_all | solution.py:20
  56.9 10.4 %all-to-all-start.5 = ((bf16[8,144,256]{2,1,0:T(8,128)(2,1)}), bf16[8,144,256]{2,1,0:T(8,128)(2,1)S(1)}, u32[]{:S(2)}, u32[]{:S(2)}) async-start(bf16[8,144,256]{2,1,0:T(8,128)(2,1)} %fusion.17), calls=%async_computation.5 | async-start | bytes 1179648 | tf_op jit(solution)/shard_map/all_to_all | solution.py:20
  69.1 8.4 %all-to-all-done.5.cot_ref = bf16[8,144,256]{2,1,0:T(8,128)(2,1)S(1)} async-done(((bf16[8,144,256]{2,1,0:T(8,128)(2,1)}), bf16[8,144,256]{2,1,0:T(8,128)(2,1)S(1)}, u32[]{:S(2)}, u32[]{:S(2)}) %all-to-all-start.5) | async-done | bytes 589856 | tf_op jit(solution)/shard_map/all_to_all | solution.py:20
  77.5 4.7 %all-to-all-start.1 = ((bf16[16,64,128]{2,1,0:T(8,128)(2,1)}), bf16[16,64,128]{2,1,0:T(8,128)(2,1)S(1)}, u32[]{:S(2)}, u32[]{:S(2)}) async-start(bf16[16,64,128]{2,1,0:T(8,128)(2,1)} %shard_map.267), calls=%async_computation.1 | async-start | bytes 524288 | tf_op jit(solution)/shard_map/all_to_all | solution.py:20
  85.1 4.6 %collective-permute-start.3 = (bf16[192,768]{1,0:T(8,128)(2,1)}, bf16[192,768]{1,0:T(8,128)(2,1)S(1)}, u32[]{:S(2)}, u32[]{:S(2)}) collective-permute-start(bf16[192,768]{1,0:T(8,128)(2,1)} %get-tuple-element.43), channel_id=1, source_target_pairs={{0,15},{1,0},{2,1},{3,2},{4,3},{5,4},{6,5},{7,6},{8,7},{9,8},{10,9... | collective-permute-start | bytes 884744 | tf_op jit(solution)/shard_map/ppermute | solution.py:25
  91.6 17.8 %collective-permute-done.3 = bf16[192,768]{1,0:T(8,128)(2,1)S(1)} collective-permute-done((bf16[192,768]{1,0:T(8,128)(2,1)}, bf16[192,768]{1,0:T(8,128)(2,1)S(1)}, u32[]{:S(2)}, u32[]{:S(2)}) %collective-permute-start.3) | collective-permute-done | bytes 294944 | tf_op jit(solution)/shard_map/ppermute | solution.py:25
  110.5 3.0 %collective-permute-start.4 = (bf16[192,768]{1,0:T(8,128)(2,1)S(1)}, bf16[192,768]{1,0:T(8,128)(2,1)}, u32[]{:S(2)}, u32[]{:S(2)}) collective-permute-start(bf16[192,768]{1,0:T(8,128)(2,1)S(1)} %add_convert_fusion.1), channel_id=1, source_target_pairs={{0,15},{1,0},{2,1},{3,2},{4,3},{5,4},{6,5},{7,6},{8,7},{9,8},{10,9... | collective-permute-start | bytes 884744 | tf_op jit(solution)/shard_map/ppermute | solution.py:25
  113.6 6.9 %shard_map.268 = (bf16[256,512]{1,0:T(8,128)(2,1)}, f32[16,512]{1,0:T(8,128)S(1)}, f32[8,512]{1,0:T(8,128)S(1)}, bf16[8,256,256]{2,1,0:T(8,128)(2,1)}, f32[8,256...) custom-call(bf16[256,512]{1,0:T(8,128)(2,1)S(1)} %bitcast.75, bf16[256,256]{1,0:T(8,128)(2,1)S(1)} %bitcast.73, ...), custom_call_target="tpu_custom_call" | custom-call | tf_op jit(solution)/shard_map/pallas_call | solution.py:507
  120.5 5.0 %all-to-all-start.2 = ((bf16[8,256,256]{2,1,0:T(8,128)(2,1)}), bf16[8,256,256]{2,1,0:T(8,128)(2,1)S(1)}, u32[]{:S(2)}, u32[]{:S(2)}) async-start(bf16[8,256,256]{2,1,0:T(8,128)(2,1)} %get-tuple-element.33), calls=%async_computation.2 | async-start | bytes 2097152 | tf_op jit(solution)/shard_map/all_to_all | solution.py:20
  127.8 6.7 %collective-permute-start.8 = (bf16[64,768]{1,0:T(8,128)(2,1)S(1)}, bf16[64,768]{1,0:T(8,128)(2,1)S(1)}, u32[]{:S(2)}, u32[]{:S(2)}) collective-permute-start(bf16[64,768]{1,0:T(8,128)(2,1)S(1)} %copy-done.29), channel_id=1, source_target_pairs={{0,3},{1,4},{2,5},{3,6},{4,7},{5,8},{6,9},{7,10},{8,11},{9,12},{10... | collective-permute-start | bytes 294920 | tf_op jit(solution)/shard_map/ppermute | solution.py:25
  134.6 3.1 %collective-permute-done.6 = bf16[192,768]{1,0:T(8,128)(2,1)S(1)} collective-permute-done((bf16[192,768]{1,0:T(8,128)(2,1)S(1)}, bf16[192,768]{1,0:T(8,128)(2,1)S(1)}, u32[]{:S(2)}, u32[]{:S(2)}) %collective-permute-start.6) | collective-permute-done | bytes 294944 | tf_op jit(solution)/shard_map/ppermute | solution.py:25
  139.8 9.6 %collective-permute-start.9 = (bf16[64,768]{1,0:T(8,128)(2,1)S(1)}, bf16[64,768]{1,0:T(8,128)(2,1)S(1)}, u32[]{:S(2)}, u32[]{:S(2)}) collective-permute-start(bf16[64,768]{1,0:T(8,128)(2,1)S(1)} %fusion.20), channel_id=1, source_target_pairs={{0,5},{1,6},{2,7},{3,8},{4,9},{5,10},{6,11},{7,12},{8,13},{9,14},{... | collective-permute-start | bytes 294920 | tf_op jit(solution)/shard_map/ppermute | solution.py:25
  156.5 5.9 %all-to-all-start.3 = ((f32[4,8,128]{2,1,0:T(8,128)}), f32[4,8,128]{2,1,0:T(8,128)S(1)}, u32[]{:S(2)}, u32[]{:S(2)}) async-start(f32[4,8,128]{2,1,0:T(8,128)} %bitcast.69), calls=%async_computation.3 | async-start | bytes 32768 | tf_op jit(solution)/shard_map/all_to_all | solution.py:20
  163.7 3.2 %all-to-all-done.3 = f32[4,8,128]{2,1,0:T(8,128)S(1)} async-done(((f32[4,8,128]{2,1,0:T(8,128)}), f32[4,8,128]{2,1,0:T(8,128)S(1)}, u32[]{:S(2)}, u32[]{:S(2)}) %all-to-all-start.3) | async-done | bytes 16416 | tf_op jit(solution)/shard_map/all_to_all | solution.py:20
  166.9 8.3 %all-to-all-start.6 = ((bf16[8,128,256]{2,1,0:T(8,128)(2,1)}), bf16[8,128,256]{2,1,0:T(8,128)(2,1)S(1)}, u32[]{:S(2)}, u32[]{:S(2)}) async-start(bf16[8,128,256]{2,1,0:T(8,128)(2,1)} %bitcast.28), calls=%async_computation.6 | async-start | bytes 1048576 | tf_op jit(solution)/shard_map/all_to_all | solution.py:20
  175.3 5.5 %collective-permute-start.10 = (bf16[64,768]{1,0:T(8,128)(2,1)S(1)}, bf16[64,768]{1,0:T(8,128)(2,1)S(1)}, u32[]{:S(2)}, u32[]{:S(2)}) collective-permute-start(bf16[64,768]{1,0:T(8,128)(2,1)S(1)} %fusion.22), channel_id=1, source_target_pairs={{0,5},{1,6},{2,7},{3,8},{4,9},{5,10},{6,11},{7,12},{8,13},{9,14},{... | collective-permute-start | bytes 294920 | tf_op jit(solution)/shard_map/ppermute | solution.py:25
  180.8 5.8 %collective-permute-start.11 = (bf16[64,768]{1,0:T(8,128)(2,1)S(1)}, bf16[64,768]{1,0:T(8,128)(2,1)S(1)}, u32[]{:S(2)}, u32[]{:S(2)}) collective-permute-start(bf16[64,768]{1,0:T(8,128)(2,1)S(1)} %fusion.22), channel_id=1, source_target_pairs={{0,11},{1,12},{2,13},{3,14},{4,15},{5,0},{6,1},{7,2},{8,3},{9,4},{... | collective-permute-start | bytes 294920 | tf_op jit(solution)/shard_map/ppermute | solution.py:25
  189.1 8.6 %collective-permute-done.11 = bf16[64,768]{1,0:T(8,128)(2,1)S(1)} collective-permute-done((bf16[64,768]{1,0:T(8,128)(2,1)S(1)}, bf16[64,768]{1,0:T(8,128)(2,1)S(1)}, u32[]{:S(2)}, u32[]{:S(2)}) %collective-permute-start.11) | collective-permute-done | bytes 98336 | tf_op jit(solution)/shard_map/ppermute | solution.py:25
  199.7 7.0 %collective-permute-start.13 = (bf16[192,768]{1,0:T(8,128)(2,1)S(1)}, bf16[192,768]{1,0:T(8,128)(2,1)S(1)}, u32[]{:S(2)}, u32[]{:S(2)}) collective-permute-start(bf16[192,768]{1,0:T(8,128)(2,1)S(1)} %pad_maximum_fusion.centre_ref), channel_id=1, source_target_pairs={{0,15},{1,0},{2,1},{3,2},{4,3},{5,4},{6,5},{7,6},{8,7},{9,8},{10,9... | collective-permute-start | bytes 884744 | tf_op jit(solution)/shard_map/ppermute | solution.py:25
  207.4 6.3 %all-to-all-start.4 = ((f32[16,8,128]{2,1,0:T(8,128)}), f32[16,8,128]{2,1,0:T(8,128)S(1)}, u32[]{:S(2)}, u32[]{:S(2)}) async-start(f32[16,8,128]{2,1,0:T(8,128)} %broadcast_in_dim.75), calls=%async_computation.4 | async-start | bytes 131072 | tf_op jit(solution)/shard_map/all_to_all | solution.py:20
  213.7 3.3 %collective-permute-start.14 = (bf16[192,768]{1,0:T(8,128)(2,1)S(1)}, bf16[192,768]{1,0:T(8,128)(2,1)S(1)}, u32[]{:S(2)}, u32[]{:S(2)}) collective-permute-start(bf16[192,768]{1,0:T(8,128)(2,1)S(1)} %collective-permute-done.12.left1_ref), channel_id=1, source_target_pairs={{0,1},{1,2},{2,3},{3,4},{4,5},{5,6},{6,7},{7,8},{8,9},{9,10},{10,1... | collective-permute-start | bytes 884744 | tf_op jit(solution)/shard_map/ppermute | solution.py:25
  217.0 3.2 %collective-permute-start.15 = (bf16[192,768]{1,0:T(8,128)(2,1)S(1)}, bf16[192,768]{1,0:T(8,128)(2,1)S(1)}, u32[]{:S(2)}, u32[]{:S(2)}) collective-permute-start(bf16[192,768]{1,0:T(8,128)(2,1)S(1)} %collective-permute-done.13.right1_ref), channel_id=1, source_target_pairs={{0,15},{1,0},{2,1},{3,2},{4,3},{5,4},{6,5},{7,6},{8,7},{9,8},{10,9... | collective-permute-start | bytes 884744 | tf_op jit(solution)/shard_map/ppermute | solution.py:25
  225.3 3.5 %all-to-all-start.9 = ((bf16[4,192,256]{2,1,0:T(8,128)(2,1)}), bf16[4,192,256]{2,1,0:T(8,128)(2,1)S(1)}, u32[]{:S(2)}, u32[]{:S(2)}) async-start(bf16[4,192,256]{2,1,0:T(8,128)(2,1)} %shard_map.272), calls=%async_computation.9 | async-start | bytes 786432 | tf_op jit(solution)/shard_map/all_to_all | solution.py:20
  228.8 4.1 %collective-permute-start.16 = (bf16[64,768]{1,0:T(8,128)(2,1)S(1)}, bf16[64,768]{1,0:T(8,128)(2,1)S(1)}, u32[]{:S(2)}, u32[]{:S(2)}) collective-permute-start(bf16[64,768]{1,0:T(8,128)(2,1)S(1)} %collective-permute-done.11), channel_id=1, source_target_pairs={{0,13},{1,14},{2,15},{3,0},{4,1},{5,2},{6,3},{7,4},{8,5},{9,6},{10... | collective-permute-start | bytes 294920 | tf_op jit(solution)/shard_map/ppermute | solution.py:25
  237.0 7.3 %shard_map.271 = (bf16[8,144,256]{2,1,0:T(8,128)(2,1)}, bf16[4,384,256]{2,1,0:T(8,128)(2,1)}) custom-call(s32[1]{0:T(128)} %bitcast.20.place_ref, bf16[192,768]{1,0:T(8,128)(2,1)} %copy-done.16, bf16[192,768]{1,0:T(8,128)(2,1)} %copy-done.18, bf16[192,768]{1,0:T(8,128)(2,1)} %copy-done.19, bf16[192,768]{1,0:T(8,128)(2,1)} %copy-done.20, ...), custom_call_target="tpu_custom_call" | custom-call | tf_op jit(solution)/shard_map/pallas_call | solution.py:561
  244.3 9.6 %all-to-all-start.7 = ((bf16[8,144,256]{2,1,0:T(8,128)(2,1)}), bf16[8,144,256]{2,1,0:T(8,128)(2,1)S(1)}, u32[]{:S(2)}, u32[]{:S(2)}) async-start(bf16[8,144,256]{2,1,0:T(8,128)(2,1)} %get-tuple-element.47), calls=%async_computation.7 | async-start | bytes 1179648 | tf_op jit(solution)/shard_map/all_to_all | solution.py:20
  257.5 6.6 %all-to-all-done.7 = bf16[8,144,256]{2,1,0:T(8,128)(2,1)S(1)} async-done(((bf16[8,144,256]{2,1,0:T(8,128)(2,1)}), bf16[8,144,256]{2,1,0:T(8,128)(2,1)S(1)}, u32[]{:S(2)}, u32[]{:S(2)}) %all-to-all-start.7) | async-done | bytes 589856 | tf_op jit(solution)/shard_map/all_to_all | solution.py:20
  264.1 4.7 %all-to-all-start.8 = ((bf16[4,384,256]{2,1,0:T(8,128)(2,1)}), bf16[4,384,256]{2,1,0:T(8,128)(2,1)S(1)}, u32[]{:S(2)}, u32[]{:S(2)}) async-start(bf16[4,384,256]{2,1,0:T(8,128)(2,1)} %get-tuple-element.48), calls=%async_computation.8 | async-start | bytes 1572864 | tf_op jit(solution)/shard_map/all_to_all | solution.py:20
  270.9 9.0 %all-to-all-done.8 = bf16[4,384,256]{2,1,0:T(8,128)(2,1)S(1)} async-done(((bf16[4,384,256]{2,1,0:T(8,128)(2,1)}), bf16[4,384,256]{2,1,0:T(8,128)(2,1)S(1)}, u32[]{:S(2)}, u32[]{:S(2)}) %all-to-all-start.8) | async-done | bytes 786464 | tf_op jit(solution)/shard_map/all_to_all | solution.py:20
  (132 shorter events, 47.6 us)
Async XLA Ops:
  7.2 213.0 %all-gather.2.cloned.1.call-start = ((), (), s32[]{:S(2)}) async-start(), calls=%async_computation.10 | async-start | bytes 3342336 | tf_op jit(solution)/shard_map/all_gather | solution.py:448
  10.4 5.7 %collective-permute-start = (bf16[3,768]{1,0:T(4,128)(2,1)S(1)}, bf16[3,768]{1,0:T(4,128)(2,1)S(1)}, u32[]{:S(2)}, u32[]{:S(2)}) collective-permute-start(bf16[3,768]{1,0:T(4,128)(2,1)S(1)} %pad_maximum_fusion.2), channel_id=1, source_target_pairs={{0,1},{1,2},{2,3},{3,4},{4,5},{5,6},{6,7},{7,8},{8,9},{9,10},{10,1... | collective-permute-start | bytes 13832 | tf_op jit(solution)/shard_map/ppermute | solution.py:16
  20.5 36.4 %all-to-all-start = ((bf16[16,80,128]{2,1,0:T(8,128)(2,1)}), bf16[16,80,128]{2,1,0:T(8,128)(2,1)S(1)}, u32[]{:S(2)}, u32[]{:S(2)}) async-start(bf16[16,80,128]{2,1,0:T(8,128)(2,1)} %shard_map.266), calls=%async_computation | async-start | bytes 655360 | tf_op jit(solution)/shard_map/all_to_all | solution.py:20
  37.7 75.8 %copy-start.8 = (bf16[3,768]{1,0:T(4,128)(2,1)S(1)}, bf16[3,768]{1,0:T(4,128)(2,1)}, u32[]{:S(2)}) copy-start(bf16[3,768]{1,0:T(4,128)(2,1)} %copy-done.7) | copy-start | bytes 13828
  37.7 75.8 %copy-start.9 = (f32[4,256]{1,0:T(4,128)S(1)}, f32[4,256]{1,0:T(4,128)}, u32[]{:S(2)}) copy-start(f32[4,256]{1,0:T(4,128)} %tapsbc_ref.5) | copy-start | bytes 12292
  37.7 75.8 %copy-start.10 = (f32[1,8,256]{2,1,0:T(8,128)S(1)}, f32[1,8,256]{2,1,0:T(8,128)}, u32[]{:S(2)}) copy-start(f32[1,8,256]{2,1,0:T(8,128)} %param.21) | copy-start | bytes 24580
  37.7 75.8 %copy-start.11 = (f32[4,512]{1,0:T(4,128)S(1)}, f32[4,512]{1,0:T(4,128)}, u32[]{:S(2)}) copy-start(f32[4,512]{1,0:T(4,128)} %tapsx_ref.3) | copy-start | bytes 24580
  56.9 20.6 %all-to-all-start.5 = ((bf16[8,144,256]{2,1,0:T(8,128)(2,1)}), bf16[8,144,256]{2,1,0:T(8,128)(2,1)S(1)}, u32[]{:S(2)}, u32[]{:S(2)}) async-start(bf16[8,144,256]{2,1,0:T(8,128)(2,1)} %fusion.17), calls=%async_computation.5 | async-start | bytes 1179648 | tf_op jit(solution)/shard_map/all_to_all | solution.py:20
  77.5 35.9 %all-to-all-start.1 = ((bf16[16,64,128]{2,1,0:T(8,128)(2,1)}), bf16[16,64,128]{2,1,0:T(8,128)(2,1)S(1)}, u32[]{:S(2)}, u32[]{:S(2)}) async-start(bf16[16,64,128]{2,1,0:T(8,128)(2,1)} %shard_map.267), calls=%async_computation.1 | async-start | bytes 524288 | tf_op jit(solution)/shard_map/all_to_all | solution.py:20
  85.1 24.4 %collective-permute-start.3 = (bf16[192,768]{1,0:T(8,128)(2,1)}, bf16[192,768]{1,0:T(8,128)(2,1)S(1)}, u32[]{:S(2)}, u32[]{:S(2)}) collective-permute-start(bf16[192,768]{1,0:T(8,128)(2,1)} %get-tuple-element.43), channel_id=1, source_target_pairs={{0,15},{1,0},{2,1},{3,2},{4,3},{5,4},{6,5},{7,6},{8,7},{9,8},{10,9... | collective-permute-start | bytes 884744 | tf_op jit(solution)/shard_map/ppermute | solution.py:25
  89.7 35.8 %collective-permute-start.5 = (bf16[192,768]{1,0:T(8,128)(2,1)}, bf16[192,768]{1,0:T(8,128)(2,1)S(1)}, u32[]{:S(2)}, u32[]{:S(2)}) collective-permute-start(bf16[192,768]{1,0:T(8,128)(2,1)} %get-tuple-element.45), channel_id=1, source_target_pairs={{0,1},{1,2},{2,3},{3,4},{4,5},{5,6},{6,7},{7,8},{8,9},{9,10},{10,1... | collective-permute-start | bytes 884744 | tf_op jit(solution)/shard_map/ppermute | solution.py:25
  110.5 24.1 %collective-permute-start.4 = (bf16[192,768]{1,0:T(8,128)(2,1)S(1)}, bf16[192,768]{1,0:T(8,128)(2,1)}, u32[]{:S(2)}, u32[]{:S(2)}) collective-permute-start(bf16[192,768]{1,0:T(8,128)(2,1)S(1)} %add_convert_fusion.1), channel_id=1, source_target_pairs={{0,15},{1,0},{2,1},{3,2},{4,3},{5,4},{6,5},{7,6},{8,7},{9,8},{10,9... | collective-permute-start | bytes 884744 | tf_op jit(solution)/shard_map/ppermute | solution.py:25
  120.5 30.8 %all-to-all-start.2 = ((bf16[8,256,256]{2,1,0:T(8,128)(2,1)}), bf16[8,256,256]{2,1,0:T(8,128)(2,1)S(1)}, u32[]{:S(2)}, u32[]{:S(2)}) async-start(bf16[8,256,256]{2,1,0:T(8,128)(2,1)} %get-tuple-element.33), calls=%async_computation.2 | async-start | bytes 2097152 | tf_op jit(solution)/shard_map/all_to_all | solution.py:20
  125.6 12.1 %collective-permute-start.6 = (bf16[192,768]{1,0:T(8,128)(2,1)S(1)}, bf16[192,768]{1,0:T(8,128)(2,1)S(1)}, u32[]{:S(2)}, u32[]{:S(2)}) collective-permute-start(bf16[192,768]{1,0:T(8,128)(2,1)S(1)} %add_convert_fusion), channel_id=1, source_target_pairs={{0,1},{1,2},{2,3},{3,4},{4,5},{5,6},{6,7},{7,8},{8,9},{9,10},{10,1... | collective-permute-start | bytes 884744 | tf_op jit(solution)/shard_map/ppermute | solution.py:25
  127.8 12.0 %collective-permute-start.8 = (bf16[64,768]{1,0:T(8,128)(2,1)S(1)}, bf16[64,768]{1,0:T(8,128)(2,1)S(1)}, u32[]{:S(2)}, u32[]{:S(2)}) collective-permute-start(bf16[64,768]{1,0:T(8,128)(2,1)S(1)} %copy-done.29), channel_id=1, source_target_pairs={{0,3},{1,4},{2,5},{3,6},{4,7},{5,8},{6,9},{7,10},{8,11},{9,12},{10... | collective-permute-start | bytes 294920 | tf_op jit(solution)/shard_map/ppermute | solution.py:25
  139.8 35.4 %collective-permute-start.9 = (bf16[64,768]{1,0:T(8,128)(2,1)S(1)}, bf16[64,768]{1,0:T(8,128)(2,1)S(1)}, u32[]{:S(2)}, u32[]{:S(2)}) collective-permute-start(bf16[64,768]{1,0:T(8,128)(2,1)S(1)} %fusion.20), channel_id=1, source_target_pairs={{0,5},{1,6},{2,7},{3,8},{4,9},{5,10},{6,11},{7,12},{8,13},{9,14},{... | collective-permute-start | bytes 294920 | tf_op jit(solution)/shard_map/ppermute | solution.py:25
  149.4 25.9 %collective-permute-start.7 = (bf16[64,768]{1,0:T(8,128)(2,1)S(1)}, bf16[64,768]{1,0:T(8,128)(2,1)S(1)}, u32[]{:S(2)}, u32[]{:S(2)}) collective-permute-start(bf16[64,768]{1,0:T(8,128)(2,1)S(1)} %slice.112), channel_id=1, source_target_pairs={{0,11},{1,12},{2,13},{3,14},{4,15},{5,0},{6,1},{7,2},{8,3},{9,4},{... | collective-permute-start | bytes 294920 | tf_op jit(solution)/shard_map/ppermute | solution.py:25
  156.5 10.5 %all-to-all-start.3 = ((f32[4,8,128]{2,1,0:T(8,128)}), f32[4,8,128]{2,1,0:T(8,128)S(1)}, u32[]{:S(2)}, u32[]{:S(2)}) async-start(f32[4,8,128]{2,1,0:T(8,128)} %bitcast.69), calls=%async_computation.3 | async-start | bytes 32768 | tf_op jit(solution)/shard_map/all_to_all | solution.py:20
  166.9 39.7 %all-to-all-start.6 = ((bf16[8,128,256]{2,1,0:T(8,128)(2,1)}), bf16[8,128,256]{2,1,0:T(8,128)(2,1)S(1)}, u32[]{:S(2)}, u32[]{:S(2)}) async-start(bf16[8,128,256]{2,1,0:T(8,128)(2,1)} %bitcast.28), calls=%async_computation.6 | async-start | bytes 1048576 | tf_op jit(solution)/shard_map/all_to_all | solution.py:20
  175.3 13.8 %collective-permute-start.10 = (bf16[64,768]{1,0:T(8,128)(2,1)S(1)}, bf16[64,768]{1,0:T(8,128)(2,1)S(1)}, u32[]{:S(2)}, u32[]{:S(2)}) collective-permute-start(bf16[64,768]{1,0:T(8,128)(2,1)S(1)} %fusion.22), channel_id=1, source_target_pairs={{0,5},{1,6},{2,7},{3,8},{4,9},{5,10},{6,11},{7,12},{8,13},{9,14},{... | collective-permute-start | bytes 294920 | tf_op jit(solution)/shard_map/ppermute | solution.py:25
  180.8 16.9 %collective-permute-start.11 = (bf16[64,768]{1,0:T(8,128)(2,1)S(1)}, bf16[64,768]{1,0:T(8,128)(2,1)S(1)}, u32[]{:S(2)}, u32[]{:S(2)}) collective-permute-start(bf16[64,768]{1,0:T(8,128)(2,1)S(1)} %fusion.22), channel_id=1, source_target_pairs={{0,11},{1,12},{2,13},{3,14},{4,15},{5,0},{6,1},{7,2},{8,3},{9,4},{... | collective-permute-start | bytes 294920 | tf_op jit(solution)/shard_map/ppermute | solution.py:25
  197.7 15.9 %collective-permute-start.12 = (bf16[192,768]{1,0:T(8,128)(2,1)S(1)}, bf16[192,768]{1,0:T(8,128)(2,1)S(1)}, u32[]{:S(2)}, u32[]{:S(2)}) collective-permute-start(bf16[192,768]{1,0:T(8,128)(2,1)S(1)} %pad_maximum_fusion.centre_ref), channel_id=1, source_target_pairs={{0,1},{1,2},{2,3},{3,4},{4,5},{5,6},{6,7},{7,8},{8,9},{9,10},{10,1... | collective-permute-start | bytes 884744 | tf_op jit(solution)/shard_map/ppermute | solution.py:25
  199.7 17.3 %collective-permute-start.13 = (bf16[192,768]{1,0:T(8,128)(2,1)S(1)}, bf16[192,768]{1,0:T(8,128)(2,1)S(1)}, u32[]{:S(2)}, u32[]{:S(2)}) collective-permute-start(bf16[192,768]{1,0:T(8,128)(2,1)S(1)} %pad_maximum_fusion.centre_ref), channel_id=1, source_target_pairs={{0,15},{1,0},{2,1},{3,2},{4,3},{5,4},{6,5},{7,6},{8,7},{9,8},{10,9... | collective-permute-start | bytes 884744 | tf_op jit(solution)/shard_map/ppermute | solution.py:25
  207.4 17.9 %all-to-all-start.4 = ((f32[16,8,128]{2,1,0:T(8,128)}), f32[16,8,128]{2,1,0:T(8,128)S(1)}, u32[]{:S(2)}, u32[]{:S(2)}) async-start(f32[16,8,128]{2,1,0:T(8,128)} %broadcast_in_dim.75), calls=%async_computation.4 | async-start | bytes 131072 | tf_op jit(solution)/shard_map/all_to_all | solution.py:20
  213.7 22.4 %collective-permute-start.14 = (bf16[192,768]{1,0:T(8,128)(2,1)S(1)}, bf16[192,768]{1,0:T(8,128)(2,1)S(1)}, u32[]{:S(2)}, u32[]{:S(2)}) collective-permute-start(bf16[192,768]{1,0:T(8,128)(2,1)S(1)} %collective-permute-done.12.left1_ref), channel_id=1, source_target_pairs={{0,1},{1,2},{2,3},{3,4},{4,5},{5,6},{6,7},{7,8},{8,9},{9,10},{10,1... | collective-permute-start | bytes 884744 | tf_op jit(solution)/shard_map/ppermute | solution.py:25
  217.0 19.1 %collective-permute-start.15 = (bf16[192,768]{1,0:T(8,128)(2,1)S(1)}, bf16[192,768]{1,0:T(8,128)(2,1)S(1)}, u32[]{:S(2)}, u32[]{:S(2)}) collective-permute-start(bf16[192,768]{1,0:T(8,128)(2,1)S(1)} %collective-permute-done.13.right1_ref), channel_id=1, source_target_pairs={{0,15},{1,0},{2,1},{3,2},{4,3},{5,4},{6,5},{7,6},{8,7},{9,8},{10,9... | collective-permute-start | bytes 884744 | tf_op jit(solution)/shard_map/ppermute | solution.py:25
  225.3 19.0 %all-to-all-start.9 = ((bf16[4,192,256]{2,1,0:T(8,128)(2,1)}), bf16[4,192,256]{2,1,0:T(8,128)(2,1)S(1)}, u32[]{:S(2)}, u32[]{:S(2)}) async-start(bf16[4,192,256]{2,1,0:T(8,128)(2,1)} %shard_map.272), calls=%async_computation.9 | async-start | bytes 786432 | tf_op jit(solution)/shard_map/all_to_all | solution.py:20
  228.8 7.3 %collective-permute-start.16 = (bf16[64,768]{1,0:T(8,128)(2,1)S(1)}, bf16[64,768]{1,0:T(8,128)(2,1)S(1)}, u32[]{:S(2)}, u32[]{:S(2)}) collective-permute-start(bf16[64,768]{1,0:T(8,128)(2,1)S(1)} %collective-permute-done.11), channel_id=1, source_target_pairs={{0,13},{1,14},{2,15},{3,0},{4,1},{5,2},{6,3},{7,4},{8,5},{9,6},{10... | collective-permute-start | bytes 294920 | tf_op jit(solution)/shard_map/ppermute | solution.py:25
  232.9 21.0 %collective-permute-start.1 = (f32[3,512]{1,0:T(4,128)S(1)}, f32[3,512]{1,0:T(4,128)S(1)}, u32[]{:S(2)}, u32[]{:S(2)}) collective-permute-start(f32[3,512]{1,0:T(4,128)S(1)} %slice.64), channel_id=1, source_target_pairs={{1,0},{2,1},{3,2},{4,3},{5,4},{6,5},{7,6},{8,7},{9,8},{10,9},{11,1... | collective-permute-start | bytes 18440 | tf_op jit(solution)/shard_map/ppermute | solution.py:16
  234.2 20.3 %collective-permute-start.2 = (f32[3,256]{1,0:T(4,128)S(1)}, f32[3,256]{1,0:T(4,128)S(1)}, u32[]{:S(2)}, u32[]{:S(2)}) collective-permute-start(f32[3,256]{1,0:T(4,128)S(1)} %slice.65), channel_id=1, source_target_pairs={{1,0},{2,1},{3,2},{4,3},{5,4},{6,5},{7,6},{8,7},{9,8},{10,9},{11,1... | collective-permute-start | bytes 9224 | tf_op jit(solution)/shard_map/ppermute | solution.py:16
  244.3 19.8 %all-to-all-start.7 = ((bf16[8,144,256]{2,1,0:T(8,128)(2,1)}), bf16[8,144,256]{2,1,0:T(8,128)(2,1)S(1)}, u32[]{:S(2)}, u32[]{:S(2)}) async-start(bf16[8,144,256]{2,1,0:T(8,128)(2,1)} %get-tuple-element.47), calls=%async_computation.7 | async-start | bytes 1179648 | tf_op jit(solution)/shard_map/all_to_all | solution.py:20
  264.1 15.9 %all-to-all-start.8 = ((bf16[4,384,256]{2,1,0:T(8,128)(2,1)}), bf16[4,384,256]{2,1,0:T(8,128)(2,1)S(1)}, u32[]{:S(2)}, u32[]{:S(2)}) async-start(bf16[4,384,256]{2,1,0:T(8,128)(2,1)} %get-tuple-element.48), calls=%async_computation.8 | async-start | bytes 1572864 | tf_op jit(solution)/shard_map/all_to_all | solution.py:20
  (26 other events, 701.3 us)
Sparse Core Ops, SparseCore 0:
  10.1 97.3 all-gather.1

commit v4 on v3

--- a/solution.py
+++ b/solution.py
@@ -23,6 +23,10 @@
 def shift(value, distance):
     count = lax.axis_size("ctx")
     return lax.ppermute(value, "ctx", [(i, (i + distance) % count) for i in range(count)])
+
+
+def after(value, *earlier):
+    return lax.optimization_barrier((value,) + earlier)[0]
 
 
 def copies(value, count):
@@ -276,7 +280,8 @@
     return cot_ref[block // per_group, pl.ds(start, rows), :]
 
 
-def unscaled_kernel(place_ref, cot_ref, down_ref, *refs):
+def unscaled_kernel(place_ref, cot_ref, down_ref, earlier_ref, *refs):
+    del earlier_ref
     out_refs, rows_ref = refs[:-1], refs[-1]
     places = rows_ref.shape[0] // out_refs[-1].shape[0]
     rows = out_refs[-1].shape[0]
@@ -297,68 +302,88 @@
 def scaled_rows(cot_ref, group):
     slots = cot_ref.shape[1] - 16
     weight = cot_ref[group, slots:, :slots].astype(F32).T[:, 0:1]
-    return weight, (cot_ref[group, :slots, :].astype(F32) * weight).astype(BF16)
-
-
-def down_kernel(acts_ref, cot_ref, parts_ref):
-    width = acts_ref.shape[1] // 2
-    gate = acts_ref[:, :width].astype(F32)
-    up = acts_ref[:, width:].astype(F32)
-    hidden = (gate * jax.nn.sigmoid(gate) * up).astype(BF16)
-    groups = cot_ref.shape[0]
-    scaled = jnp.concatenate([scaled_rows(cot_ref, group)[1] for group in range(groups)], axis=0)
-    parts_ref[...] = dot(hidden, scaled, 0, 0).astype(BF16).reshape(parts_ref.shape)
-
-
-def rows_kernel(
-    place_ref, centre_ref, left1_ref, right1_ref, left2_ref, right2_ref, opposite_ref,
-    acts_ref, in_ref, cot_ref, gatew_ref, upw_ref, *refs,
-):
-    back_ref, parts_ref, all_ref, gate_ref, up_ref = refs[-5:]
+    return (cot_ref[group, :slots, :].astype(F32) * weight).astype(BF16)
+
+
+def own_rows_kernel(mine_ref, weight_ref, gate_ref, up_ref, earlier_ref, out_ref):
+    del earlier_ref
+    width = mine_ref.shape[1]
+    unscaled = mine_ref[...].astype(F32)
+    gate = gate_ref[...].astype(F32)
+    up = up_ref[...].astype(F32)
+    grad_hidden = weight_ref[...] * unscaled
+    sig = jax.nn.sigmoid(gate)
+    activated = gate * sig
+    hidden = (activated * up).astype(BF16)
+    slope = sig * (1.0 + gate * (1.0 - sig))
+    out_ref[:, :width] = (grad_hidden * up * slope).astype(BF16)
+    out_ref[:, width : 2 * width] = (grad_hidden * activated).astype(BF16)
+    out_ref[:, 2 * width : 3 * width] = hidden
+    route = jnp.sum(hidden.astype(F32) * unscaled, axis=1, keepdims=True)
+    coarse = route.astype(BF16).astype(F32)
+    lanes = (mine_ref.shape[0], 128)
+    out_ref[:, 3 * width :] = jnp.where(
+        iota(lanes, 1) == 0, coarse, jnp.where(iota(lanes, 1) == 1, route - coarse, 0.0)
+    ).astype(BF16)
+
+
+def weights_kernel(place_ref, all_ref, in_ref, cot_ref, small_ref, *refs):
+    out_refs, grads_ref = refs[:-1], refs[-1]
     groups, slots, cols = in_ref.shape
-    total, width = all_ref.shape
-    owners = parts_ref.shape[0]
-    share = parts_ref.shape[1] // 2
-    rows = opposite_ref.shape[0]
-    places = total // rows
-    place = place_ref[0]
-    pieces = (
-        (centre_ref, 0), (left1_ref, -1), (right1_ref, 1), (left2_ref, -2), (right2_ref, 2)
-    )
-    for piece_ref, distance in pieces:
-        for i, step in enumerate(shifted_by(distance)):
-            block = lax.rem(place + step + places, places)
-            start = pl.multiple_of(block * rows, rows)
-            all_ref[pl.ds(start, rows), :] = piece_ref[i * rows : (i + 1) * rows, :]
-    block = lax.rem(place + OPPOSITE, places)
-    all_ref[pl.ds(pl.multiple_of(block * rows, rows), rows), :] = opposite_ref[...]
+    width = grads_ref.shape[1]
+    owners = len(out_refs)
+    share = width // owners
+    rows_in = in_ref[...].reshape(groups * slots, cols)
+    scaled = jnp.concatenate([scaled_rows(cot_ref, group) for group in range(groups)], axis=0)
+    grads_ref[0] = dot(all_ref[:, :width], rows_in, 0, 0).astype(BF16)
+    grads_ref[1] = dot(all_ref[:, width : 2 * width], rows_in, 0, 0).astype(BF16)
+    grads_ref[2] = dot(all_ref[:, 2 * width : 3 * width], scaled, 0, 0).astype(BF16)
+    for ahead in range(owners):
+        owner = lax.rem(place_ref[0] + ahead, owners)
+        start = pl.multiple_of(owner * share, 64)
+        for kind in range(3):
+            out_refs[ahead][kind * share : (kind + 1) * share, :] = grads_ref[
+                kind, pl.ds(start, share), :
+            ]
+        line = small_ref[pl.ds(owner, 1), :]
+        coarse = line.astype(BF16).astype(F32)
+        fine = line - coarse
+        lines = [
+            value[:, i * cols : (i + 1) * cols] for value in (coarse, fine) for i in range(4)
+        ]
+        lines.append(jnp.zeros((8, cols), F32))
+        out_refs[ahead][3 * share :, :] = jnp.concatenate(lines, axis=0).astype(BF16)
+
+
+def rows_kernel(all_ref, gatew_ref, upw_ref, back_ref):
+    width = gatew_ref.shape[1]
+    groups, slots, cols = back_ref.shape
+    slots = slots - 16
+    rows_grad = dot(all_ref[:, :width], gatew_ref[...], 1, 1)
+    rows_grad = rows_grad + dot(all_ref[:, width : 2 * width], upw_ref[...], 1, 1)
+    back_ref[:, :slots, :] = rows_grad.astype(BF16).reshape(groups, slots, cols)
+    route = all_ref[:, 3 * width :].astype(F32)
     for group in range(groups):
-        span = slice(group * slots, (group + 1) * slots)
-        unscaled = all_ref[span, :].astype(F32)
-        gate = acts_ref[span, :width].astype(F32)
-        up = acts_ref[span, width:].astype(F32)
-        weight = cot_ref[group, slots:, :slots].astype(F32).T[:, 0:1]
-        sig = jax.nn.sigmoid(gate)
-        activated = gate * sig
-        hidden = (activated * up).astype(BF16).astype(F32)
-        grad_hidden = weight * unscaled
-        slope = sig * (1.0 + gate * (1.0 - sig))
-        gate_ref[span, :] = (grad_hidden * up * slope).astype(BF16)
-        up_ref[span, :] = (grad_hidden * activated).astype(BF16)
-        route = jnp.sum(hidden * unscaled, axis=1, keepdims=True)
-        line = jnp.broadcast_to(route, (slots, 128)).T[0:1]
-        coarse = line.astype(BF16).astype(F32)
-        line = jnp.concatenate([coarse, line - coarse], axis=1)
+        turned = route[group * slots : (group + 1) * slots].T
+        line = jnp.concatenate([turned[0:1], turned[1:2]], axis=1)
         back_ref[group, slots:, :] = jnp.broadcast_to(line, (16, cols)).astype(BF16)
-    rows_grad = dot(gate_ref[...], gatew_ref[...], 1, 1) + dot(up_ref[...], upw_ref[...], 1, 1)
-    back_ref[:, :slots, :] = rows_grad.astype(BF16).reshape(groups, slots, cols)
-    rows_in = in_ref[...].reshape(total, cols)
-    parts_ref[:, :share, :] = (
-        dot(gate_ref[...], rows_in, 0, 0).astype(BF16).reshape(owners, share, cols)
-    )
-    parts_ref[:, share:, :] = (
-        dot(up_ref[...], rows_in, 0, 0).astype(BF16).reshape(owners, share, cols)
-    )
+
+
+def totals_kernel(*refs):
+    part_refs, (gate_ref, up_ref, down_ref, small_ref) = refs[:-4], refs[-4:]
+    share = down_ref.shape[0]
+
+    def total(first, last):
+        value = part_refs[0][first:last, :].astype(F32)
+        for part_ref in part_refs[1:]:
+            value = value + part_ref[first:last, :].astype(F32)
+        return value
+
+    gate_ref[...] = total(0, share).T.astype(BF16)
+    up_ref[...] = total(share, 2 * share).T.astype(BF16)
+    down_ref[...] = total(2 * share, 3 * share).astype(BF16)
+    small = total(3 * share, 3 * share + 16)
+    small_ref[...] = small[:4] + small[4:8]
 
 
 def scan_kernel(got_ref, out_ref):
@@ -445,10 +470,6 @@
         "ctx",
         1,
     )
-    acts = lax.all_gather(
-        jnp.concatenate([gate_act[0, 0], up_act[0, 0]], axis=1), "ctx", axis=0, tiled=True
-    )
-
     col_width = moe_in.shape[2]
     token_count = moe_in.shape[1]
     expert_count = slot_tok.shape[2]
@@ -479,7 +500,7 @@
     )(head_rows, shared_rows, before, raw_step, gains, conv_x, conv_bc, cot_rows)
     (entered,) = whole(
         scan_kernel, [((ctx_places, 2 * part, state_width), BF16)], inputs=1
-    )(exchange(states, "ctx"))
+    )(exchange(after(states, got_cot), "ctx"))
 
     three, one = (3 * own, hidden_width), (own, hidden_width)
     left2, right2, left1, right1, centre, opposite = whole(
@@ -488,7 +509,8 @@
         [((ctx_places * own, col_width), BF16)],
         inputs=2,
         scalars=1,
-    )(place, got_cot, w_down[0])
+        late=1,
+    )(place, got_cot, w_down[0], states)
     opposite = shift(opposite, 3)
     left1 = (left1.astype(F32) + shift(left2, -1).astype(F32)).astype(BF16)
     right1 = (right1.astype(F32) + shift(right2, 1).astype(F32)).astype(BF16)
@@ -496,13 +518,12 @@
     far_left = shift(centre[:own].astype(BF16), -FAR)
     far_right = shift((centre[2 * own :] + opposite.astype(F32)).astype(BF16), FAR)
     mine = centre[own : 2 * own] + far_left.astype(F32) + far_right.astype(F32)
-    mine = mine.astype(BF16)
-
-    from_left, from_right = shift(mine, FAR), shift(mine, -FAR)
-    opposite = shift(from_right, -3)
-    centre = jnp.concatenate([from_left, mine, from_right], axis=0)
-    left1, right1 = shift(centre, 1), shift(centre, -1)
-    left2, right2 = shift(left1, 1), shift(right1, -1)
+    rows_weight = got_cot[:, slot_width, :slot_width].reshape(-1).astype(F32)
+    weight_own = lax.dynamic_slice_in_dim(rows_weight, place[0] * own, own, 0)
+    (own_rows,) = whole(
+        own_rows_kernel, [((own, 3 * hidden_width + 128), BF16)], inputs=4, late=1
+    )(mine, weight_own[:, None], gate_act[0, 0], up_act[0, 0], entered)
+    everything = lax.all_gather(own_rows, "ctx", axis=0, tiled=True)
 
     main_heads, tail_heads, rim_heads, grad_bc, grad_step, taps_heads, grad_rate = whole(
         back_kernel,
@@ -546,34 +567,45 @@
         ],
         axis=1,
     )
-    small = jnp.sum(exchange(small.reshape(dp_count, 8, 128), "dp"), axis=0)
-    small = jnp.sum(exchange(copies(small, ctx_places), "ctx"), axis=0).reshape(1, -1)
+    small = small.reshape(dp_count * 8, 128)
+    small = jnp.sum(exchange(copies(small, ctx_places), "ctx"), axis=0).reshape(dp_count, -1)
+
+    share = hidden_width // dp_count
+    block = ((3 * share + 16, col_width), BF16)
+    owner = lax.axis_index("dp").astype(jnp.int32).reshape(1)
+    parts = whole(
+        weights_kernel,
+        [block] * dp_count,
+        [((3, hidden_width, col_width), BF16)],
+        inputs=4,
+        scalars=1,
+        limit=56 * 2**20,
+    )(owner, everything, rows_in, got_cot, small)
+    parts = [parts[0]] + [
+        lax.ppermute(parts[k], "dp", [(i, (i + k) % dp_count) for i in range(dp_count)])
+        for k in range(1, dp_count)
+    ]
+    (back,) = whole(
+        rows_kernel,
+        [((expert_count, slot_width + 16, col_width), BF16)],
+        inputs=3,
+        limit=48 * 2**20,
+    )(everything, w_gate[0], w_up[0])
+    back = exchange(back, "expert")
+    gate_total, up_total, down_total, small = whole(
+        totals_kernel,
+        [
+            ((col_width, share), BF16),
+            ((col_width, share), BF16),
+            ((share, col_width), BF16),
+            ((4, col_width), F32),
+        ],
+        inputs=dp_count,
+    )(*parts)
+    small = small.reshape(1, -1)
     taps_heads = small[:, :split_at]
     taps_shared = small[:, split_at : split_at + shared_width]
     rate_total = small[0, split_at + shared_width :][:heads_here]
-
-    share = hidden_width // dp_count
-    (down_parts,) = whole(
-        down_kernel, [((dp_count, share, col_width), BF16)], inputs=2, limit=48 * 2**20
-    )(acts, got_cot)
-    down_total = jnp.sum(exchange(down_parts, "dp").astype(F32), axis=0).astype(BF16)
-    all_rows = ((ctx_places * own, hidden_width), BF16)
-    back, parts = whole(
-        rows_kernel,
-        [
-            ((expert_count, slot_width + 16, col_width), BF16),
-            ((dp_count, 2 * share, col_width), BF16),
-        ],
-        [all_rows] * 3,
-        inputs=11,
-        scalars=1,
-        limit=56 * 2**20,
-    )(
-        place, centre, left1, right1, left2, right2, opposite, acts, rows_in, got_cot,
-        w_gate[0], w_up[0],
-    )
-    back = exchange(back, "expert")
-    parts = exchange(parts, "dp")
     grad_tokens = lax.dot_general(
         table,
         back[:, :slot_width].reshape(-1, col_width),
@@ -584,7 +616,6 @@
     route_total = jnp.where(
         live_slots, route_got[:, :slot_width] + route_got[:, slot_width:], 0.0
     )
-    totals = jnp.sum(parts.astype(F32), axis=0).astype(BF16)
     return (
         grad_mamba_in[None],
         grad_shared_in[None],
@@ -594,8 +625,8 @@
         rate_total,
         grad_tokens.astype(BF16)[None],
         route_total[None, None],
-        totals[:share].T[None],
-        totals[share:].T[None],
+        gate_total[None],
+        up_total[None],
         down_total[None],
     )
 

time: 291 us -> 259 us (0.89)
  starting transfers between devices: 142 us -> 95.2 us
  blocking collectives: 0 us -> 23.2 us
  waiting for transfers between devices: 81.1 us -> 66.6 us
  Pallas kernels: 27.6 us -> 32 us
  local copies, waits for them, and re-layouts: 9.52 us -> 13.2 us
    ppermute x14 -> x7, starting transfers between devices: 60.7 us -> 32.7 us  [shift(): lax.ppermute(value, 'ctx', [(i, (i + distance) % count) for i in range(co...]
    all_to_all x10 -> x6, starting transfers between devices: 74.2 us -> 48.5 us  [exchange(): return lax.all_to_all(value, axis, split_axis=0, concat_axis=0, tiled=True)]
    all_to_all x0 -> x1, blocking collectives: none -> 23.2 us  [exchange(): return lax.all_to_all(value, axis, split_axis=0, concat_axis=0, tiled=True)]
    ppermute x14 -> x7, waiting for transfers between devices: 33.6 us -> 20.4 us  [shift(): lax.ppermute(value, 'ctx', [(i, (i + distance) % count) for i in range(co...]
    all_to_all x10 -> x6, waiting for transfers between devices: 47.4 us -> 36.8 us  [exchange(): return lax.all_to_all(value, axis, split_axis=0, concat_axis=0, tiled=True)]
    ppermute x0 -> x3, starting transfers between devices: none -> 10.1 us  [body(): lax.ppermute(parts[k], 'dp', [(i, (i + k) % dp_count) for i in range(dp_c...]
    ppermute x0 -> x3, waiting for transfers between devices: none -> 9.25 us  [body(): lax.ppermute(parts[k], 'dp', [(i, (i + k) % dp_count) for i in range(dp_c...]
    pallas_call x2 -> x4, Pallas kernels: 9.41 us -> 13.9 us  [the longest x1 5.64 us: body(): whole(weights_kernel, [block] * dp_count, [((3, hidden_width, col_width),...]
  transfers between devices with their start and end apart: 28 -> 20, of which waited for: 12 -> 11; matrix products, arithmetic and copies ran while one was open for 5% -> 6% of each run, Pallas kernels for 10% -> 10%
where the time goes in v4:
time: 259 us; the launch traced here: 257 us
  starting transfers between devices  95.2 us (37%)
  waiting for transfers between devices  66.6 us (26%)
  Pallas kernels  32 us (12%)
  blocking collectives  23.2 us (9%)
  between operations  14.5 us (6%)
  local copies, waits for them, and re-layouts  13.2 us (5%)
  other arithmetic  9.26 us (4%)
  matrix products  3.16 us (1%)
    all_to_all x6, starting transfers between devices, exchange(): return lax.all_to_all(value, axis, split_axis=0, concat_axis=0, tiled=True)  48.5 us
    all_to_all x6, waiting for transfers between devices, exchange(): return lax.all_to_all(value, axis, split_axis=0, concat_axis=0, tiled=True)  36.8 us
    ppermute x7, starting transfers between devices, shift(): lax.ppermute(value, 'ctx', [(i, (i + distance) % count) for i in range(co...  32.7 us
    all_to_all x1, blocking collectives, exchange(): return lax.all_to_all(value, axis, split_axis=0, concat_axis=0, tiled=True)  23.2 us
    ppermute x7, waiting for transfers between devices, shift(): lax.ppermute(value, 'ctx', [(i, (i + distance) % count) for i in range(co...  20.4 us
    ppermute x3, starting transfers between devices, body(): lax.ppermute(parts[k], 'dp', [(i, (i + k) % dp_count) for i in range(dp_c...  10.1 us
    ppermute x3, waiting for transfers between devices, body(): lax.ppermute(parts[k], 'dp', [(i, (i + k) % dp_count) for i in range(dp_c...  9.25 us
    unnamed x60, local copies, waits for them, and re-layouts  7.95 us
  transfers between devices with their start and end apart: 20, of which 11 were waited for; matrix products, arithmetic and copies ran while one was open for 6% of the time, Pallas kernels for 10%

profile of v4, /device:TPU:1, one launch (start us, length us, event | category | flops | bytes accessed | tf_op | source)
XLA Modules:
  0.0 257.3 jit_solution(9016871983172732587)
XLA Ops:
  10.2 10.3 %all-to-all-start = ((bf16[8,144,256]{2,1,0:T(8,128)(2,1)}), bf16[8,144,256]{2,1,0:T(8,128)(2,1)S(1)}, u32[]{:S(2)}, u32[]{:S(2)}) async-start(bf16[8,144,256]{2,1,0:T(8,128)(2,1)} %fusion.17), calls=%async_computation | async-start | bytes 1179648 | tf_op jit(solution)/shard_map/all_to_all | solution.py:20
  24.5 3.8 %shard_map.266.earlier_ref = bf16[16,80,128]{2,1,0:T(8,128)(2,1)} custom-call(bf16[256,512]{1,0:T(8,128)(2,1)} %bitcast.69, bf16[256,256]{1,0:T(8,128)(2,1)} %bitcast.66, bf16[3,768]{1,0:T(4,128)(2,1)} %copy-done.6, f32[8,256]{1,0:T(8,128)} %bitcast.75, f32[3,8]{1,0:T(4,128)} %pad_maximum_fusion.1.gains_ref, f32[4,512]{1,0:T(4,128)} %tapsx_ref.3, ...), custom_call_target="tpu_custom_call" | custom-call | tf_op jit(solution)/shard_map/pallas_call | solution.py:495
  28.4 2.3 all-to-all-done.cot_ref
  31.5 2.7 %shard_map.270 = (bf16[192,768]{1,0:T(8,128)(2,1)}, bf16[192,768]{1,0:T(8,128)(2,1)}, bf16[192,768]{1,0:T(8,128)(2,1)}, bf16[192,768]{1,0:T(8,128)(2,1)}, bf16[1...) custom-call(s32[1]{0:T(128)} %bitcast.21.place_ref, bf16[8,144,256]{2,1,0:T(8,128)(2,1)} %copy-done.12, ...), custom_call_target="tpu_custom_call" | custom-call | tf_op jit(solution)/shard_map/pallas_call | solution.py:506
  34.3 7.0 %collective-permute-start.3 = (bf16[192,768]{1,0:T(8,128)(2,1)}, bf16[192,768]{1,0:T(8,128)(2,1)S(1)}, u32[]{:S(2)}, u32[]{:S(2)}) collective-permute-start(bf16[192,768]{1,0:T(8,128)(2,1)} %get-tuple-element.48), channel_id=1, source_target_pairs={{0,15},{1,0},{2,1},{3,2},{4,3},{5,4},{6,5},{7,6},{8,7},{9,8},{10,9... | collective-permute-start | bytes 884744 | tf_op jit(solution)/shard_map/ppermute | solution.py:25
  41.3 1.9 collective-permute-start.5
  43.3 8.4 %all-to-all-start.1 = ((bf16[16,80,128]{2,1,0:T(8,128)(2,1)}), bf16[16,80,128]{2,1,0:T(8,128)(2,1)S(1)}, u32[]{:S(2)}, u32[]{:S(2)}) async-start(bf16[16,80,128]{2,1,0:T(8,128)(2,1)} %shard_map.266.earlier_ref), calls=%async_computation.1 | async-start | bytes 655360 | tf_op jit(solution)/shard_map/all_to_all | solution.py:20
  52.7 4.5 %collective-permute-start.4 = (bf16[192,768]{1,0:T(8,128)(2,1)S(1)}, bf16[192,768]{1,0:T(8,128)(2,1)S(1)}, u32[]{:S(2)}, u32[]{:S(2)}) collective-permute-start(bf16[192,768]{1,0:T(8,128)(2,1)S(1)} %add_convert_fusion.1), channel_id=1, source_target_pairs={{0,15},{1,0},{2,1},{3,2},{4,3},{5,4},{6,5},{7,6},{8,7},{9,8},{10,9... | collective-permute-start | bytes 884744 | tf_op jit(solution)/shard_map/ppermute | solution.py:25
  58.3 1.9 collective-permute-start.6
  60.2 5.2 %collective-permute-start.8 = (bf16[64,768]{1,0:T(8,128)(2,1)S(1)}, bf16[64,768]{1,0:T(8,128)(2,1)S(1)}, u32[]{:S(2)}, u32[]{:S(2)}) collective-permute-start(bf16[64,768]{1,0:T(8,128)(2,1)S(1)} %copy-done.27), channel_id=1, source_target_pairs={{0,3},{1,4},{2,5},{3,6},{4,7},{5,8},{6,9},{7,10},{8,11},{9,12},{10... | collective-permute-start | bytes 294920 | tf_op jit(solution)/shard_map/ppermute | solution.py:25
  66.1 7.7 %collective-permute-done.4 = bf16[192,768]{1,0:T(8,128)(2,1)S(1)} collective-permute-done((bf16[192,768]{1,0:T(8,128)(2,1)S(1)}, bf16[192,768]{1,0:T(8,128)(2,1)S(1)}, u32[]{:S(2)}, u32[]{:S(2)}) %collective-permute-start.4) | collective-permute-done | bytes 294944 | tf_op jit(solution)/shard_map/ppermute | solution.py:25
  75.5 7.8 %collective-permute-start.7 = (bf16[64,768]{1,0:T(8,128)(2,1)S(1)}, bf16[64,768]{1,0:T(8,128)(2,1)S(1)}, u32[]{:S(2)}, u32[]{:S(2)}) collective-permute-start(bf16[64,768]{1,0:T(8,128)(2,1)S(1)} %slice.104), channel_id=1, source_target_pairs={{0,11},{1,12},{2,13},{3,14},{4,15},{5,0},{6,1},{7,2},{8,3},{9,4},{... | collective-permute-start | bytes 294920 | tf_op jit(solution)/shard_map/ppermute | solution.py:25
  83.3 4.3 %collective-permute-start.9 = (bf16[64,768]{1,0:T(8,128)(2,1)S(1)}, bf16[64,768]{1,0:T(8,128)(2,1)S(1)}, u32[]{:S(2)}, u32[]{:S(2)}) collective-permute-start(bf16[64,768]{1,0:T(8,128)(2,1)S(1)} %fusion.20), channel_id=1, source_target_pairs={{0,5},{1,6},{2,7},{3,8},{4,9},{5,10},{6,11},{7,12},{8,13},{9,14},{... | collective-permute-start | bytes 294920 | tf_op jit(solution)/shard_map/ppermute | solution.py:25
  88.5 11.2 %collective-permute-done.9 = bf16[64,768]{1,0:T(8,128)(2,1)S(1)} collective-permute-done((bf16[64,768]{1,0:T(8,128)(2,1)S(1)}, bf16[64,768]{1,0:T(8,128)(2,1)S(1)}, u32[]{:S(2)}, u32[]{:S(2)}) %collective-permute-start.9) | collective-permute-done | bytes 98336 | tf_op jit(solution)/shard_map/ppermute | solution.py:25
  102.8 2.0 shard_map.271
  104.8 23.2 %all_to_all.35.got_ref = bf16[16,64,128]{2,1,0:T(8,128)(2,1)S(1)} all-to-all(bf16[16,64,128]{2,1,0:T(8,128)(2,1)} %shard_map.267.earlier_ref), channel_id=1, replica_groups=mesh['dp'=4,'expert'=8,'ctx'=16] {'ctx'}, dimensions={0} | all-to-all | bytes 524288 | tf_op jit(solution)/shard_map/all_to_all | solution.py:20
  128.1 6.9 %shard_map.268 = (bf16[256,512]{1,0:T(8,128)(2,1)}, f32[16,512]{1,0:T(8,128)S(1)}, f32[8,512]{1,0:T(8,128)S(1)}, bf16[8,256,256]{2,1,0:T(8,128)(2,1)}, f32[8,256...) custom-call(bf16[256,512]{1,0:T(8,128)(2,1)S(1)} %bitcast.70, bf16[256,256]{1,0:T(8,128)(2,1)S(1)} %bitcast.68, ...), custom_call_target="tpu_custom_call" | custom-call | tf_op jit(solution)/shard_map/pallas_call | solution.py:528
  135.0 11.9 %all-to-all-start.3 = ((bf16[8,256,256]{2,1,0:T(8,128)(2,1)}), bf16[8,256,256]{2,1,0:T(8,128)(2,1)S(1)}, u32[]{:S(2)}, u32[]{:S(2)}) async-start(bf16[8,256,256]{2,1,0:T(8,128)(2,1)} %get-tuple-element.41), calls=%async_computation.3 | async-start | bytes 2097152 | tf_op jit(solution)/shard_map/all_to_all | solution.py:20
  147.0 15.1 %all-to-all-done.3.got_ref = bf16[8,256,256]{2,1,0:T(8,128)(2,1)S(1)} async-done(((bf16[8,256,256]{2,1,0:T(8,128)(2,1)}), bf16[8,256,256]{2,1,0:T(8,128)(2,1)S(1)}, u32[]{:S(2)}, u32[]{:S(2)}) %all-to-all-start.3) | async-done | bytes 1048608 | tf_op jit(solution)/shard_map/all_to_all | solution.py:20
  163.0 2.9 %shard_map.269 = (bf16[256,256]{1,0:T(8,128)(2,1)}, f32[16,256]{1,0:T(8,128)}, f32[8,256]{1,0:T(8,128)}, f32[4,256]{1,0:T(4,128)}) custom-call(bf16[256,256]{1,0:T(8,128)(2,1)} %bitcast.67, bf16[3,768]{1,0:T(4,128)(2,1)} %copy-done.6, f32[4,256]{1,0:T(4,128)} %tapsbc_ref.5, bf16[8,256,256]{2,1,0:T(8,128)(2,1)} %copy-done.13), custom_call_target="tpu_custom_call" | custom-call | tf_op jit(solution)/shard_map/pallas_call | solution.py:548
  167.3 5.9 %all-to-all-start.5 = ((f32[16,32,128]{2,1,0:T(8,128)}), f32[16,32,128]{2,1,0:T(8,128)S(1)}, u32[]{:S(2)}, u32[]{:S(2)}) async-start(f32[16,32,128]{2,1,0:T(8,128)} %broadcast_in_dim.85), calls=%async_computation.5 | async-start | bytes 524288 | tf_op jit(solution)/shard_map/all_to_all | solution.py:20
  174.5 17.5 %all-to-all-done.5 = f32[16,32,128]{2,1,0:T(8,128)S(1)} async-done(((f32[16,32,128]{2,1,0:T(8,128)}), f32[16,32,128]{2,1,0:T(8,128)S(1)}, u32[]{:S(2)}, u32[]{:S(2)}) %all-to-all-start.5) | async-done | bytes 262176 | tf_op jit(solution)/shard_map/all_to_all | solution.py:20
  192.0 7.8 %all-to-all-start.4 = ((bf16[8,128,256]{2,1,0:T(8,128)(2,1)}), bf16[8,128,256]{2,1,0:T(8,128)(2,1)S(1)}, u32[]{:S(2)}, u32[]{:S(2)}) async-start(bf16[8,128,256]{2,1,0:T(8,128)(2,1)} %bitcast.28), calls=%async_computation.4 | async-start | bytes 1048576 | tf_op jit(solution)/shard_map/all_to_all | solution.py:20
  203.0 4.2 %shard_map.274 = bf16[8,144,256]{2,1,0:T(8,128)(2,1)} custom-call(bf16[1024,2432]{1,0:T(8,128)(2,1)} %all-gather.2.cloned.1.call-done.all_ref, bf16[256,768]{1,0:T(8,128)(2,1)S(1)} %bitcast.73, bf16[256,768]{1,0:T(8,128)(2,1)S(1)} %bitcast.74), custom_call_target="tpu_custom_call" | custom-call | tf_op jit(solution)/shard_map/pallas_call | solution.py:588
  207.3 2.0 all-to-all-done.4.in_ref
  209.2 4.3 %all-to-all-start.6 = ((bf16[8,144,256]{2,1,0:T(8,128)(2,1)}), bf16[8,144,256]{2,1,0:T(8,128)(2,1)S(1)}, u32[]{:S(2)}, u32[]{:S(2)}) async-start(bf16[8,144,256]{2,1,0:T(8,128)(2,1)} %shard_map.274), calls=%async_computation.6 | async-start | bytes 1179648 | tf_op jit(solution)/shard_map/all_to_all | solution.py:20
  213.6 5.6 %shard_map.272 = (bf16[592,256]{1,0:T(8,128)(2,1)}, bf16[592,256]{1,0:T(8,128)(2,1)}, bf16[592,256]{1,0:T(8,128)(2,1)}, bf16[592,256]{1,0:T(8,128)(2,1)}) custom-call(s32[1]{0:T(128)} %bitcast.20.place_ref, bf16[1024,2432]{1,0:T(8,128)(2,1)} %all-gather.2.cloned.1.call-done.all_ref, bf16[8,128,256]{2,1,0:T(8,128)(2,1)} %copy-done.14, ...), custom_call_target="tpu_custom_call" | custom-call | tf_op jit(solution)/shard_map/pallas_call | solution.py:576
  219.2 2.9 %collective-permute-start.10 = (bf16[592,256]{1,0:T(8,128)(2,1)}, bf16[592,256]{1,0:T(8,128)(2,1)S(1)}, u32[]{:S(2)}, u32[]{:S(2)}) collective-permute-start(bf16[592,256]{1,0:T(8,128)(2,1)} %get-tuple-element.56), channel_id=1, source_target_pairs={{0,128},{128,256},{256,384},{384,0},{1,129},{129,257},{257,385},{3... | collective-permute-start | bytes 909320 | tf_op jit(solution)/shard_map/ppermute | solution.py:585
  222.1 4.3 %collective-permute-start.11 = (bf16[592,256]{1,0:T(8,128)(2,1)}, bf16[592,256]{1,0:T(8,128)(2,1)S(1)}, u32[]{:S(2)}, u32[]{:S(2)}) collective-permute-start(bf16[592,256]{1,0:T(8,128)(2,1)} %get-tuple-element.57), channel_id=1, source_target_pairs={{0,256},{128,384},{256,0},{384,128},{1,257},{129,385},{257,1},{385... | collective-permute-start | bytes 909320 | tf_op jit(solution)/shard_map/ppermute | solution.py:585
  226.4 3.0 %collective-permute-start.12 = (bf16[592,256]{1,0:T(8,128)(2,1)}, bf16[592,256]{1,0:T(8,128)(2,1)S(1)}, u32[]{:S(2)}, u32[]{:S(2)}) collective-permute-start(bf16[592,256]{1,0:T(8,128)(2,1)} %get-tuple-element.58), channel_id=1, source_target_pairs={{0,384},{128,0},{256,128},{384,256},{1,385},{129,1},{257,129},{385... | collective-permute-start | bytes 909320 | tf_op jit(solution)/shard_map/ppermute | solution.py:585
  231.2 7.2 %collective-permute-done.11.refs_2_ = bf16[592,256]{1,0:T(8,128)(2,1)S(1)} collective-permute-done((bf16[592,256]{1,0:T(8,128)(2,1)}, bf16[592,256]{1,0:T(8,128)(2,1)S(1)}, u32[]{:S(2)}, u32[]{:S(2)}) %collective-permute-start.11) | collective-permute-done | bytes 303136 | tf_op jit(solution)/shard_map/ppermute | solution.py:585
  240.6 2.1 shard_map.273
  (116 shorter events, 35.0 us)
Async XLA Ops:
  10.2 20.5 %all-to-all-start = ((bf16[8,144,256]{2,1,0:T(8,128)(2,1)}), bf16[8,144,256]{2,1,0:T(8,128)(2,1)S(1)}, u32[]{:S(2)}, u32[]{:S(2)}) async-start(bf16[8,144,256]{2,1,0:T(8,128)(2,1)} %fusion.17), calls=%async_computation | async-start | bytes 1179648 | tf_op jit(solution)/shard_map/all_to_all | solution.py:20
  21.9 2.1 collective-permute-start
  34.3 41.0 %copy-start.19 = (bf16[192,768]{1,0:T(8,128)(2,1)S(1)}, bf16[192,768]{1,0:T(8,128)(2,1)}, u32[]{:S(2)}) copy-start(bf16[192,768]{1,0:T(8,128)(2,1)} %get-tuple-element.46) | copy-start | bytes 884740
  34.3 17.4 %collective-permute-start.3 = (bf16[192,768]{1,0:T(8,128)(2,1)}, bf16[192,768]{1,0:T(8,128)(2,1)S(1)}, u32[]{:S(2)}, u32[]{:S(2)}) collective-permute-start(bf16[192,768]{1,0:T(8,128)(2,1)} %get-tuple-element.48), channel_id=1, source_target_pairs={{0,15},{1,0},{2,1},{3,2},{4,3},{5,4},{6,5},{7,6},{8,7},{9,8},{10,9... | collective-permute-start | bytes 884744 | tf_op jit(solution)/shard_map/ppermute | solution.py:25
  41.3 15.9 %collective-permute-start.5 = (bf16[192,768]{1,0:T(8,128)(2,1)}, bf16[192,768]{1,0:T(8,128)(2,1)S(1)}, u32[]{:S(2)}, u32[]{:S(2)}) collective-permute-start(bf16[192,768]{1,0:T(8,128)(2,1)} %get-tuple-element.50), channel_id=1, source_target_pairs={{0,1},{1,2},{2,3},{3,4},{4,5},{5,6},{6,7},{7,8},{8,9},{9,10},{10,1... | collective-permute-start | bytes 884744 | tf_op jit(solution)/shard_map/ppermute | solution.py:25
  43.3 57.1 %all-to-all-start.1 = ((bf16[16,80,128]{2,1,0:T(8,128)(2,1)}), bf16[16,80,128]{2,1,0:T(8,128)(2,1)S(1)}, u32[]{:S(2)}, u32[]{:S(2)}) async-start(bf16[16,80,128]{2,1,0:T(8,128)(2,1)} %shard_map.266.earlier_ref), calls=%async_computation.1 | async-start | bytes 655360 | tf_op jit(solution)/shard_map/all_to_all | solution.py:20
  51.6 151.4 %all-gather.2.cloned.1.call-start = ((), (), s32[]{:S(2)}) async-start(), calls=%async_computation.7 | async-start | bytes 5292032 | tf_op jit(solution)/shard_map/all_gather | solution.py:526
  52.7 21.1 %collective-permute-start.4 = (bf16[192,768]{1,0:T(8,128)(2,1)S(1)}, bf16[192,768]{1,0:T(8,128)(2,1)S(1)}, u32[]{:S(2)}, u32[]{:S(2)}) collective-permute-start(bf16[192,768]{1,0:T(8,128)(2,1)S(1)} %add_convert_fusion.1), channel_id=1, source_target_pairs={{0,15},{1,0},{2,1},{3,2},{4,3},{5,4},{6,5},{7,6},{8,7},{9,8},{10,9... | collective-permute-start | bytes 884744 | tf_op jit(solution)/shard_map/ppermute | solution.py:25
  58.3 17.0 %collective-permute-start.6 = (bf16[192,768]{1,0:T(8,128)(2,1)S(1)}, bf16[192,768]{1,0:T(8,128)(2,1)S(1)}, u32[]{:S(2)}, u32[]{:S(2)}) collective-permute-start(bf16[192,768]{1,0:T(8,128)(2,1)S(1)} %add_convert_fusion), channel_id=1, source_target_pairs={{0,1},{1,2},{2,3},{3,4},{4,5},{5,6},{6,7},{7,8},{8,9},{9,10},{10,1... | collective-permute-start | bytes 884744 | tf_op jit(solution)/shard_map/ppermute | solution.py:25
  60.2 23.1 %collective-permute-start.8 = (bf16[64,768]{1,0:T(8,128)(2,1)S(1)}, bf16[64,768]{1,0:T(8,128)(2,1)S(1)}, u32[]{:S(2)}, u32[]{:S(2)}) collective-permute-start(bf16[64,768]{1,0:T(8,128)(2,1)S(1)} %copy-done.27), channel_id=1, source_target_pairs={{0,3},{1,4},{2,5},{3,6},{4,7},{5,8},{6,9},{7,10},{8,11},{9,12},{10... | collective-permute-start | bytes 294920 | tf_op jit(solution)/shard_map/ppermute | solution.py:25
  75.4 52.7 %copy-start.1 = (bf16[1,256,256]{2,1,0:T(8,128)(2,1)S(1)}, bf16[1,256,256]{2,1,0:T(8,128)(2,1)}, u32[]{:S(2)}) copy-start(bf16[1,256,256]{2,1,0:T(8,128)(2,1)} %param.20) | copy-start | bytes 393220
  75.4 52.7 %copy-start.2 = (bf16[1,256,512]{2,1,0:T(8,128)(2,1)S(1)}, bf16[1,256,512]{2,1,0:T(8,128)(2,1)}, u32[]{:S(2)}) copy-start(bf16[1,256,512]{2,1,0:T(8,128)(2,1)} %param.19) | copy-start | bytes 786436
  75.4 52.7 %copy-start.3 = (bf16[1,256,512]{2,1,0:T(8,128)(2,1)S(1)}, bf16[1,256,512]{2,1,0:T(8,128)(2,1)}, u32[]{:S(2)}) copy-start(bf16[1,256,512]{2,1,0:T(8,128)(2,1)} %param.27) | copy-start | bytes 786436
  75.4 52.7 %copy-start.7 = (bf16[3,768]{1,0:T(4,128)(2,1)S(1)}, bf16[3,768]{1,0:T(4,128)(2,1)}, u32[]{:S(2)}) copy-start(bf16[3,768]{1,0:T(4,128)(2,1)} %copy-done.6) | copy-start | bytes 13828
  75.4 52.7 %copy-start.8 = (f32[4,256]{1,0:T(4,128)S(1)}, f32[4,256]{1,0:T(4,128)}, u32[]{:S(2)}) copy-start(f32[4,256]{1,0:T(4,128)} %tapsbc_ref.5) | copy-start | bytes 12292
  75.4 52.7 %copy-start.9 = (f32[1,8,256]{2,1,0:T(8,128)S(1)}, f32[1,8,256]{2,1,0:T(8,128)}, u32[]{:S(2)}) copy-start(f32[1,8,256]{2,1,0:T(8,128)} %param.21) | copy-start | bytes 24580
  75.4 52.7 %copy-start.10 = (f32[4,512]{1,0:T(4,128)S(1)}, f32[4,512]{1,0:T(4,128)}, u32[]{:S(2)}) copy-start(f32[4,512]{1,0:T(4,128)} %tapsx_ref.3) | copy-start | bytes 24580
  75.4 52.7 %copy-start.11 = (f32[3,8]{1,0:T(4,128)S(1)}, f32[3,8]{1,0:T(4,128)}, u32[]{:S(2)}) copy-start(f32[3,8]{1,0:T(4,128)} %pad_maximum_fusion.1.gains_ref) | copy-start | bytes 292
  75.5 13.0 %collective-permute-start.7 = (bf16[64,768]{1,0:T(8,128)(2,1)S(1)}, bf16[64,768]{1,0:T(8,128)(2,1)S(1)}, u32[]{:S(2)}, u32[]{:S(2)}) collective-permute-start(bf16[64,768]{1,0:T(8,128)(2,1)S(1)} %slice.104), channel_id=1, source_target_pairs={{0,11},{1,12},{2,13},{3,14},{4,15},{5,0},{6,1},{7,2},{8,3},{9,4},{... | collective-permute-start | bytes 294920 | tf_op jit(solution)/shard_map/ppermute | solution.py:25
  83.3 16.4 %collective-permute-start.9 = (bf16[64,768]{1,0:T(8,128)(2,1)S(1)}, bf16[64,768]{1,0:T(8,128)(2,1)S(1)}, u32[]{:S(2)}, u32[]{:S(2)}) collective-permute-start(bf16[64,768]{1,0:T(8,128)(2,1)S(1)} %fusion.20), channel_id=1, source_target_pairs={{0,5},{1,6},{2,7},{3,8},{4,9},{5,10},{6,11},{7,12},{8,13},{9,14},{... | collective-permute-start | bytes 294920 | tf_op jit(solution)/shard_map/ppermute | solution.py:25
  135.0 38.2 %copy-start.26 = (bf16[1,512,256]{2,1,0:T(8,128)(2,1)S(1)}, bf16[1,512,256]{2,1,0:T(8,128)(2,1)}, u32[]{:S(2)}) copy-start(bf16[1,512,256]{2,1,0:T(8,128)(2,1)} %param.28) | copy-start | bytes 786436
  135.0 27.0 %all-to-all-start.3 = ((bf16[8,256,256]{2,1,0:T(8,128)(2,1)}), bf16[8,256,256]{2,1,0:T(8,128)(2,1)S(1)}, u32[]{:S(2)}, u32[]{:S(2)}) async-start(bf16[8,256,256]{2,1,0:T(8,128)(2,1)} %get-tuple-element.41), calls=%async_computation.3 | async-start | bytes 2097152 | tf_op jit(solution)/shard_map/all_to_all | solution.py:20
  167.3 33.7 %copy-start.22 = (f32[8,256]{1,0:T(8,128)S(1)}, f32[8,256]{1,0:T(8,128)}, u32[]{:S(2)}) copy-start(f32[8,256]{1,0:T(8,128)} %get-tuple-element.44) | copy-start | bytes 24580
  167.3 24.6 %all-to-all-start.5 = ((f32[16,32,128]{2,1,0:T(8,128)}), f32[16,32,128]{2,1,0:T(8,128)S(1)}, u32[]{:S(2)}, u32[]{:S(2)}) async-start(f32[16,32,128]{2,1,0:T(8,128)} %broadcast_in_dim.85), calls=%async_computation.5 | async-start | bytes 524288 | tf_op jit(solution)/shard_map/all_to_all | solution.py:20
  173.2 29.8 %copy-start.4 = (bf16[1,256,768]{2,1,0:T(8,128)(2,1)S(1)}, bf16[1,256,768]{2,1,0:T(8,128)(2,1)}, u32[]{:S(2)}) copy-start(bf16[1,256,768]{2,1,0:T(8,128)(2,1)} %param.33) | copy-start | bytes 1179652
  192.0 17.3 %all-to-all-start.4 = ((bf16[8,128,256]{2,1,0:T(8,128)(2,1)}), bf16[8,128,256]{2,1,0:T(8,128)(2,1)S(1)}, u32[]{:S(2)}, u32[]{:S(2)}) async-start(bf16[8,128,256]{2,1,0:T(8,128)(2,1)} %bitcast.28), calls=%async_computation.4 | async-start | bytes 1048576 | tf_op jit(solution)/shard_map/all_to_all | solution.py:20
  199.7 29.6 %collective-permute-start.1 = (f32[3,512]{1,0:T(4,128)S(1)}, f32[3,512]{1,0:T(4,128)S(1)}, u32[]{:S(2)}, u32[]{:S(2)}) collective-permute-start(f32[3,512]{1,0:T(4,128)S(1)} %slice.61), channel_id=1, source_target_pairs={{1,0},{2,1},{3,2},{4,3},{5,4},{6,5},{7,6},{8,7},{9,8},{10,9},{11,1... | collective-permute-start | bytes 18440 | tf_op jit(solution)/shard_map/ppermute | solution.py:16
  201.1 28.9 %collective-permute-start.2 = (f32[3,256]{1,0:T(4,128)S(1)}, f32[3,256]{1,0:T(4,128)S(1)}, u32[]{:S(2)}, u32[]{:S(2)}) collective-permute-start(f32[3,256]{1,0:T(4,128)S(1)} %slice.62), channel_id=1, source_target_pairs={{1,0},{2,1},{3,2},{4,3},{5,4},{6,5},{7,6},{8,7},{9,8},{10,9},{11,1... | collective-permute-start | bytes 9224 | tf_op jit(solution)/shard_map/ppermute | solution.py:16
  209.2 39.1 %all-to-all-start.6 = ((bf16[8,144,256]{2,1,0:T(8,128)(2,1)}), bf16[8,144,256]{2,1,0:T(8,128)(2,1)S(1)}, u32[]{:S(2)}, u32[]{:S(2)}) async-start(bf16[8,144,256]{2,1,0:T(8,128)(2,1)} %shard_map.274), calls=%async_computation.6 | async-start | bytes 1179648 | tf_op jit(solution)/shard_map/all_to_all | solution.py:20
  219.2 12.0 %collective-permute-start.10 = (bf16[592,256]{1,0:T(8,128)(2,1)}, bf16[592,256]{1,0:T(8,128)(2,1)S(1)}, u32[]{:S(2)}, u32[]{:S(2)}) collective-permute-start(bf16[592,256]{1,0:T(8,128)(2,1)} %get-tuple-element.56), channel_id=1, source_target_pairs={{0,128},{128,256},{256,384},{384,0},{1,129},{129,257},{257,385},{3... | collective-permute-start | bytes 909320 | tf_op jit(solution)/shard_map/ppermute | solution.py:585
  222.1 16.3 %collective-permute-start.11 = (bf16[592,256]{1,0:T(8,128)(2,1)}, bf16[592,256]{1,0:T(8,128)(2,1)S(1)}, u32[]{:S(2)}, u32[]{:S(2)}) collective-permute-start(bf16[592,256]{1,0:T(8,128)(2,1)} %get-tuple-element.57), channel_id=1, source_target_pairs={{0,256},{128,384},{256,0},{384,128},{1,257},{129,385},{257,1},{385... | collective-permute-start | bytes 909320 | tf_op jit(solution)/shard_map/ppermute | solution.py:585
  226.4 13.5 %collective-permute-start.12 = (bf16[592,256]{1,0:T(8,128)(2,1)}, bf16[592,256]{1,0:T(8,128)(2,1)S(1)}, u32[]{:S(2)}, u32[]{:S(2)}) collective-permute-start(bf16[592,256]{1,0:T(8,128)(2,1)} %get-tuple-element.58), channel_id=1, source_target_pairs={{0,384},{128,0},{256,128},{384,256},{1,385},{129,1},{257,129},{385... | collective-permute-start | bytes 909320 | tf_op jit(solution)/shard_map/ppermute | solution.py:585
  (16 other events, 136.8 us)
Sparse Core Ops, SparseCore 0:
  105.0 88.8 all-gather.1

commit v5 on v4

--- a/solution.py
+++ b/solution.py
@@ -327,7 +327,7 @@
     ).astype(BF16)
 
 
-def weights_kernel(place_ref, all_ref, in_ref, cot_ref, small_ref, *refs):
+def weights_kernel(place_ref, all_ref, in_ref, cot_ref, *refs):
     out_refs, grads_ref = refs[:-1], refs[-1]
     groups, slots, cols = in_ref.shape
     width = grads_ref.shape[1]
@@ -345,14 +345,6 @@
             out_refs[ahead][kind * share : (kind + 1) * share, :] = grads_ref[
                 kind, pl.ds(start, share), :
             ]
-        line = small_ref[pl.ds(owner, 1), :]
-        coarse = line.astype(BF16).astype(F32)
-        fine = line - coarse
-        lines = [
-            value[:, i * cols : (i + 1) * cols] for value in (coarse, fine) for i in range(4)
-        ]
-        lines.append(jnp.zeros((8, cols), F32))
-        out_refs[ahead][3 * share :, :] = jnp.concatenate(lines, axis=0).astype(BF16)
 
 
 def rows_kernel(all_ref, gatew_ref, upw_ref, back_ref):
@@ -370,20 +362,14 @@
 
 
 def totals_kernel(*refs):
-    part_refs, (gate_ref, up_ref, down_ref, small_ref) = refs[:-4], refs[-4:]
-    share = down_ref.shape[0]
-
-    def total(first, last):
-        value = part_refs[0][first:last, :].astype(F32)
+    part_refs, out_refs = refs[:-3], refs[-3:]
+    share = out_refs[0].shape[0]
+    for kind, out_ref in enumerate(out_refs):
+        span = slice(kind * share, (kind + 1) * share)
+        value = part_refs[0][span, :].astype(F32)
         for part_ref in part_refs[1:]:
-            value = value + part_ref[first:last, :].astype(F32)
-        return value
-
-    gate_ref[...] = total(0, share).T.astype(BF16)
-    up_ref[...] = total(share, 2 * share).T.astype(BF16)
-    down_ref[...] = total(2 * share, 3 * share).astype(BF16)
-    small = total(3 * share, 3 * share + 16)
-    small_ref[...] = small[:4] + small[4:8]
+            value = value + part_ref[span, :].astype(F32)
+        out_ref[...] = value.astype(BF16)
 
 
 def scan_kernel(got_ref, out_ref):
@@ -498,10 +484,6 @@
         [pad_heads, pad_shared],
         inputs=8,
     )(head_rows, shared_rows, before, raw_step, gains, conv_x, conv_bc, cot_rows)
-    (entered,) = whole(
-        scan_kernel, [((ctx_places, 2 * part, state_width), BF16)], inputs=1
-    )(exchange(after(states, got_cot), "ctx"))
-
     three, one = (3 * own, hidden_width), (own, hidden_width)
     left2, right2, left1, right1, centre, opposite = whole(
         unscaled_kernel,
@@ -522,8 +504,12 @@
     weight_own = lax.dynamic_slice_in_dim(rows_weight, place[0] * own, own, 0)
     (own_rows,) = whole(
         own_rows_kernel, [((own, 3 * hidden_width + 128), BF16)], inputs=4, late=1
-    )(mine, weight_own[:, None], gate_act[0, 0], up_act[0, 0], entered)
+    )(mine, weight_own[:, None], gate_act[0, 0], up_act[0, 0], rows_in)
     everything = lax.all_gather(own_rows, "ctx", axis=0, tiled=True)
+
+    (entered,) = whole(
+        scan_kernel, [((ctx_places, 2 * part, state_width), BF16)], inputs=1
+    )(exchange(after(states, own_rows), "ctx"))
 
     main_heads, tail_heads, rim_heads, grad_bc, grad_step, taps_heads, grad_rate = whole(
         back_kernel,
@@ -567,20 +553,23 @@
         ],
         axis=1,
     )
-    small = small.reshape(dp_count * 8, 128)
-    small = jnp.sum(exchange(copies(small, ctx_places), "ctx"), axis=0).reshape(dp_count, -1)
+    small = jnp.sum(exchange(small.reshape(dp_count, 8, 128), "dp"), axis=0)
+    small = jnp.sum(exchange(copies(small, ctx_places), "ctx"), axis=0).reshape(1, -1)
+    taps_heads = small[:, :split_at]
+    taps_shared = small[:, split_at : split_at + shared_width]
+    rate_total = small[0, split_at + shared_width :][:heads_here]
 
     share = hidden_width // dp_count
-    block = ((3 * share + 16, col_width), BF16)
+    block = ((3 * share, col_width), BF16)
     owner = lax.axis_index("dp").astype(jnp.int32).reshape(1)
     parts = whole(
         weights_kernel,
         [block] * dp_count,
         [((3, hidden_width, col_width), BF16)],
-        inputs=4,
+        inputs=3,
         scalars=1,
         limit=56 * 2**20,
-    )(owner, everything, rows_in, got_cot, small)
+    )(owner, everything, rows_in, got_cot)
     parts = [parts[0]] + [
         lax.ppermute(parts[k], "dp", [(i, (i + k) % dp_count) for i in range(dp_count)])
         for k in range(1, dp_count)
@@ -592,20 +581,9 @@
         limit=48 * 2**20,
     )(everything, w_gate[0], w_up[0])
     back = exchange(back, "expert")
-    gate_total, up_total, down_total, small = whole(
-        totals_kernel,
-        [
-            ((col_width, share), BF16),
-            ((col_width, share), BF16),
-            ((share, col_width), BF16),
-            ((4, col_width), F32),
-        ],
-        inputs=dp_count,
+    gate_total, up_total, down_total = whole(
+        totals_kernel, [((share, col_width), BF16)] * 3, inputs=dp_count
     )(*parts)
-    small = small.reshape(1, -1)
-    taps_heads = small[:, :split_at]
-    taps_shared = small[:, split_at : split_at + shared_width]
-    rate_total = small[0, split_at + shared_width :][:heads_here]
     grad_tokens = lax.dot_general(
         table,
         back[:, :slot_width].reshape(-1, col_width),
@@ -625,8 +603,8 @@
         rate_total,
         grad_tokens.astype(BF16)[None],
         route_total[None, None],
-        gate_total[None],
-        up_total[None],
+        gate_total.T[None],
+        up_total.T[None],
         down_total[None],
     )
 

time: 259 us -> 262 us (1.012)
  blocking collectives: 23.2 us -> 64.4 us
  waiting for transfers between devices: 66.6 us -> 45.8 us
  starting transfers between devices: 95.2 us -> 81.7 us
  local copies, waits for them, and re-layouts: 13.2 us -> 9.33 us
    all_to_all x1 -> x3, blocking collectives: 23.2 us -> 64.4 us  [exchange(): return lax.all_to_all(value, axis, split_axis=0, concat_axis=0, tiled=True)]
    all_to_all x6 -> x5, waiting for transfers between devices: 36.8 us -> 21.3 us  [exchange(): return lax.all_to_all(value, axis, split_axis=0, concat_axis=0, tiled=True)]
    all_to_all x6 -> x5, starting transfers between devices: 48.5 us -> 38.9 us  [exchange(): return lax.all_to_all(value, axis, split_axis=0, concat_axis=0, tiled=True)]
    ppermute x7, waiting for transfers between devices: 20.4 us -> 15 us  [shift(): lax.ppermute(value, 'ctx', [(i, (i + distance) % count) for i in range(co...]
    unnamed x60 -> x56, local copies, waits for them, and re-layouts: 7.95 us -> 4.04 us
  transfers between devices with their start and end apart: 20 -> 19, of which waited for: 11 -> 10; matrix products, arithmetic and copies ran while one was open for 6% -> 5% of each run, Pallas kernels for 10% -> 11%
where the time goes in v5:
time: 262 us; the launch traced here: 260 us
  starting transfers between devices  81.7 us (31%)
  blocking collectives  64.4 us (25%)
  waiting for transfers between devices  45.8 us (17%)
  Pallas kernels  32 us (12%)
  between operations  14.5 us (6%)
  local copies, waits for them, and re-layouts  9.33 us (4%)
  other arithmetic  9.26 us (4%)
  matrix products  3.16 us (1%)
    all_to_all x3, blocking collectives, exchange(): return lax.all_to_all(value, axis, split_axis=0, concat_axis=0, tiled=True)  64.4 us
    all_to_all x5, starting transfers between devices, exchange(): return lax.all_to_all(value, axis, split_axis=0, concat_axis=0, tiled=True)  38.9 us
    ppermute x7, starting transfers between devices, shift(): lax.ppermute(value, 'ctx', [(i, (i + distance) % count) for i in range(co...  30.3 us
    all_to_all x5, waiting for transfers between devices, exchange(): return lax.all_to_all(value, axis, split_axis=0, concat_axis=0, tiled=True)  21.3 us
    ppermute x7, waiting for transfers between devices, shift(): lax.ppermute(value, 'ctx', [(i, (i + distance) % count) for i in range(co...  15 us
    ppermute x3, waiting for transfers between devices, body(): lax.ppermute(parts[k], 'dp', [(i, (i + k) % dp_count) for i in range(dp_c...  9.35 us
    ppermute x3, starting transfers between devices, body(): lax.ppermute(parts[k], 'dp', [(i, (i + k) % dp_count) for i in range(dp_c...  8.63 us
    pallas_call x1, Pallas kernels, body(): whole(back_kernel, [((length, split_at), BF16), ((16, split_at), F32), ((...  6.92 us
  transfers between devices with their start and end apart: 19, of which 10 were waited for; matrix products, arithmetic and copies ran while one was open for 5% of the time, Pallas kernels for 11%

profile of v5, /device:TPU:1, one launch (start us, length us, event | category | flops | bytes accessed | tf_op | source)
XLA Modules:
  0.0 260.2 jit_solution(9822154421542552064)
XLA Ops:
  10.2 10.3 %all-to-all-start = ((bf16[8,144,256]{2,1,0:T(8,128)(2,1)}), bf16[8,144,256]{2,1,0:T(8,128)(2,1)S(1)}, u32[]{:S(2)}, u32[]{:S(2)}) async-start(bf16[8,144,256]{2,1,0:T(8,128)(2,1)} %fusion.17), calls=%async_computation | async-start | bytes 1179648 | tf_op jit(solution)/shard_map/all_to_all | solution.py:20
  24.6 3.9 %shard_map.266.earlier_ref = bf16[16,80,128]{2,1,0:T(8,128)(2,1)} custom-call(bf16[256,512]{1,0:T(8,128)(2,1)} %bitcast.76, bf16[256,256]{1,0:T(8,128)(2,1)} %bitcast.73, bf16[3,768]{1,0:T(4,128)(2,1)} %copy-done.6, f32[8,256]{1,0:T(8,128)} %bitcast.82, f32[3,8]{1,0:T(4,128)} %pad_maximum_fusion.1.gains_ref, f32[4,512]{1,0:T(4,128)} %tapsx_ref.3, ...), custom_call_target="tpu_custom_call" | custom-call | tf_op jit(solution)/shard_map/pallas_call | solution.py:481
  28.4 2.2 all-to-all-done.cot_ref
  31.5 2.7 %shard_map.267 = (bf16[192,768]{1,0:T(8,128)(2,1)}, bf16[192,768]{1,0:T(8,128)(2,1)}, bf16[192,768]{1,0:T(8,128)(2,1)}, bf16[192,768]{1,0:T(8,128)(2,1)}, bf16[1...) custom-call(s32[1]{0:T(128)} %bitcast.9.place_ref, bf16[8,144,256]{2,1,0:T(8,128)(2,1)} %copy-done.12, ...), custom_call_target="tpu_custom_call" | custom-call | tf_op jit(solution)/shard_map/pallas_call | solution.py:488
  34.2 7.0 %collective-permute-start.1 = (bf16[192,768]{1,0:T(8,128)(2,1)}, bf16[192,768]{1,0:T(8,128)(2,1)S(1)}, u32[]{:S(2)}, u32[]{:S(2)}) collective-permute-start(bf16[192,768]{1,0:T(8,128)(2,1)} %get-tuple-element.38), channel_id=1, source_target_pairs={{0,15},{1,0},{2,1},{3,2},{4,3},{5,4},{6,5},{7,6},{8,7},{9,8},{10,9... | collective-permute-start | bytes 884744 | tf_op jit(solution)/shard_map/ppermute | solution.py:25
  43.1 3.8 %collective-permute-done.1 = bf16[192,768]{1,0:T(8,128)(2,1)S(1)} collective-permute-done((bf16[192,768]{1,0:T(8,128)(2,1)}, bf16[192,768]{1,0:T(8,128)(2,1)S(1)}, u32[]{:S(2)}, u32[]{:S(2)}) %collective-permute-start.1) | collective-permute-done | bytes 294944 | tf_op jit(solution)/shard_map/ppermute | solution.py:25
  48.0 5.2 %collective-permute-start.2 = (bf16[192,768]{1,0:T(8,128)(2,1)S(1)}, bf16[192,768]{1,0:T(8,128)(2,1)S(1)}, u32[]{:S(2)}, u32[]{:S(2)}) collective-permute-start(bf16[192,768]{1,0:T(8,128)(2,1)S(1)} %add_convert_fusion.1), channel_id=1, source_target_pairs={{0,15},{1,0},{2,1},{3,2},{4,3},{5,4},{6,5},{7,6},{8,7},{9,8},{10,9... | collective-permute-start | bytes 884744 | tf_op jit(solution)/shard_map/ppermute | solution.py:25
  54.3 2.1 collective-permute-start.4
  57.7 6.5 %all-to-all-start.1 = ((bf16[8,128,256]{2,1,0:T(8,128)(2,1)}), bf16[8,128,256]{2,1,0:T(8,128)(2,1)S(1)}, u32[]{:S(2)}, u32[]{:S(2)}) async-start(bf16[8,128,256]{2,1,0:T(8,128)(2,1)} %bitcast.22), calls=%async_computation.1 | async-start | bytes 1048576 | tf_op jit(solution)/shard_map/all_to_all | solution.py:20
  67.1 8.0 %collective-permute-start.5 = (bf16[64,768]{1,0:T(8,128)(2,1)S(1)}, bf16[64,768]{1,0:T(8,128)(2,1)S(1)}, u32[]{:S(2)}, u32[]{:S(2)}) collective-permute-start(bf16[64,768]{1,0:T(8,128)(2,1)S(1)} %slice.104), channel_id=1, source_target_pairs={{0,11},{1,12},{2,13},{3,14},{4,15},{5,0},{6,1},{7,2},{8,3},{9,4},{... | collective-permute-start | bytes 294920 | tf_op jit(solution)/shard_map/ppermute | solution.py:25
  75.1 4.2 %collective-permute-start.7 = (bf16[64,768]{1,0:T(8,128)(2,1)S(1)}, bf16[64,768]{1,0:T(8,128)(2,1)S(1)}, u32[]{:S(2)}, u32[]{:S(2)}) collective-permute-start(bf16[64,768]{1,0:T(8,128)(2,1)S(1)} %fusion.20), channel_id=1, source_target_pairs={{0,5},{1,6},{2,7},{3,8},{4,9},{5,10},{6,11},{7,12},{8,13},{9,14},{... | collective-permute-start | bytes 294920 | tf_op jit(solution)/shard_map/ppermute | solution.py:25
  80.1 3.2 %collective-permute-done.5 = bf16[64,768]{1,0:T(8,128)(2,1)S(1)} collective-permute-done((bf16[64,768]{1,0:T(8,128)(2,1)S(1)}, bf16[64,768]{1,0:T(8,128)(2,1)S(1)}, u32[]{:S(2)}, u32[]{:S(2)}) %collective-permute-start.5) | collective-permute-done | bytes 98336 | tf_op jit(solution)/shard_map/ppermute | solution.py:25
  83.3 7.9 %collective-permute-done.7 = bf16[64,768]{1,0:T(8,128)(2,1)S(1)} collective-permute-done((bf16[64,768]{1,0:T(8,128)(2,1)S(1)}, bf16[64,768]{1,0:T(8,128)(2,1)S(1)}, u32[]{:S(2)}, u32[]{:S(2)}) %collective-permute-start.7) | collective-permute-done | bytes 98336 | tf_op jit(solution)/shard_map/ppermute | solution.py:25
  92.7 2.0 shard_map.268
  94.7 24.1 %all_to_all.40.got_ref = bf16[16,80,128]{2,1,0:T(8,128)(2,1)} all-to-all(bf16[16,80,128]{2,1,0:T(8,128)(2,1)S(1)} %copy-done.15), channel_id=1, replica_groups=mesh['dp'=4,'expert'=8,'ctx'=16] {'ctx'}, dimensions={0} | all-to-all | bytes 655360 | tf_op jit(solution)/shard_map/all_to_all | solution.py:20
  120.6 32.1 %all_to_all.41.got_ref = bf16[16,64,128]{2,1,0:T(8,128)(2,1)S(1)} all-to-all(bf16[16,64,128]{2,1,0:T(8,128)(2,1)} %shard_map.269), channel_id=1, replica_groups=mesh['dp'=4,'expert'=8,'ctx'=16] {'ctx'}, dimensions={0} | all-to-all | bytes 524288 | tf_op jit(solution)/shard_map/all_to_all | solution.py:20
  152.8 6.9 %shard_map.270 = (bf16[256,512]{1,0:T(8,128)(2,1)}, f32[16,512]{1,0:T(8,128)S(1)}, f32[8,512]{1,0:T(8,128)S(1)}, bf16[8,256,256]{2,1,0:T(8,128)(2,1)}, f32[8,256...) custom-call(bf16[256,512]{1,0:T(8,128)(2,1)S(1)} %bitcast.77, bf16[256,256]{1,0:T(8,128)(2,1)S(1)} %bitcast.75, ...), custom_call_target="tpu_custom_call" | custom-call | tf_op jit(solution)/shard_map/pallas_call | solution.py:514
  159.7 10.2 %all-to-all-start.4 = ((bf16[8,256,256]{2,1,0:T(8,128)(2,1)}), bf16[8,256,256]{2,1,0:T(8,128)(2,1)S(1)}, u32[]{:S(2)}, u32[]{:S(2)}) async-start(bf16[8,256,256]{2,1,0:T(8,128)(2,1)} %get-tuple-element.46), calls=%async_computation.4 | async-start | bytes 2097152 | tf_op jit(solution)/shard_map/all_to_all | solution.py:20
  170.0 15.1 %all-to-all-done.4.got_ref = bf16[8,256,256]{2,1,0:T(8,128)(2,1)S(1)} async-done(((bf16[8,256,256]{2,1,0:T(8,128)(2,1)}), bf16[8,256,256]{2,1,0:T(8,128)(2,1)S(1)}, u32[]{:S(2)}, u32[]{:S(2)}) %all-to-all-start.4) | async-done | bytes 1048608 | tf_op jit(solution)/shard_map/all_to_all | solution.py:20
  186.1 2.8 %shard_map.271 = (bf16[256,256]{1,0:T(8,128)(2,1)}, f32[16,256]{1,0:T(8,128)}, f32[8,256]{1,0:T(8,128)}, f32[4,256]{1,0:T(4,128)}) custom-call(bf16[256,256]{1,0:T(8,128)(2,1)} %bitcast.74, bf16[3,768]{1,0:T(4,128)(2,1)} %copy-done.6, f32[4,256]{1,0:T(4,128)} %tapsbc_ref.5, bf16[8,256,256]{2,1,0:T(8,128)(2,1)} %copy-done.14), custom_call_target="tpu_custom_call" | custom-call | tf_op jit(solution)/shard_map/pallas_call | solution.py:534
  189.6 8.2 %all_to_all.42 = f32[4,8,128]{2,1,0:T(8,128)S(1)} all-to-all(f32[4,8,128]{2,1,0:T(8,128)S(1)} %bitcast.90), channel_id=1, replica_groups=mesh['dp'=4,'expert'=8,'ctx'=16] {'dp'}, dimensions={0} | all-to-all | bytes 32768 | tf_op jit(solution)/shard_map/all_to_all | solution.py:20
  198.4 4.5 %all-to-all-start.6 = ((f32[16,8,128]{2,1,0:T(8,128)}), f32[16,8,128]{2,1,0:T(8,128)S(1)}, u32[]{:S(2)}, u32[]{:S(2)}) async-start(f32[16,8,128]{2,1,0:T(8,128)} %broadcast_in_dim.83), calls=%async_computation.6 | async-start | bytes 131072 | tf_op jit(solution)/shard_map/all_to_all | solution.py:20
  206.3 4.2 %shard_map.272 = bf16[8,144,256]{2,1,0:T(8,128)(2,1)} custom-call(bf16[1024,2432]{1,0:T(8,128)(2,1)} %all-gather.2.cloned.1.call-done.all_ref, bf16[256,768]{1,0:T(8,128)(2,1)S(1)} %bitcast.80, bf16[256,768]{1,0:T(8,128)(2,1)S(1)} %bitcast.81), custom_call_target="tpu_custom_call" | custom-call | tf_op jit(solution)/shard_map/pallas_call | solution.py:577
  210.5 4.0 %all-to-all-done.6 = f32[16,8,128]{2,1,0:T(8,128)S(1)} async-done(((f32[16,8,128]{2,1,0:T(8,128)}), f32[16,8,128]{2,1,0:T(8,128)S(1)}, u32[]{:S(2)}, u32[]{:S(2)}) %all-to-all-start.6) | async-done | bytes 65568 | tf_op jit(solution)/shard_map/all_to_all | solution.py:20
  214.5 7.4 %all-to-all-start.7 = ((bf16[8,144,256]{2,1,0:T(8,128)(2,1)}), bf16[8,144,256]{2,1,0:T(8,128)(2,1)S(1)}, u32[]{:S(2)}, u32[]{:S(2)}) async-start(bf16[8,144,256]{2,1,0:T(8,128)(2,1)} %shard_map.272), calls=%async_computation.7 | async-start | bytes 1179648 | tf_op jit(solution)/shard_map/all_to_all | solution.py:20
  222.5 5.7 %shard_map.273 = (bf16[576,256]{1,0:T(8,128)(2,1)}, bf16[576,256]{1,0:T(8,128)(2,1)}, bf16[576,256]{1,0:T(8,128)(2,1)}, bf16[576,256]{1,0:T(8,128)(2,1)}) custom-call(s32[1]{0:T(128)} %bitcast.36.place_ref, bf16[1024,2432]{1,0:T(8,128)(2,1)} %all-gather.2.cloned.1.call-done.all_ref, bf16[8,128,256]{2,1,0:T(8,128)(2,1)} %copy-done.13, ...), custom_call_target="tpu_custom_call" | custom-call | tf_op jit(solution)/shard_map/pallas_call | solution.py:565
  228.2 2.2 collective-permute-start.10
  230.4 3.7 %collective-permute-start.11 = (bf16[576,256]{1,0:T(8,128)(2,1)}, bf16[576,256]{1,0:T(8,128)(2,1)S(1)}, u32[]{:S(2)}, u32[]{:S(2)}) collective-permute-start(bf16[576,256]{1,0:T(8,128)(2,1)} %get-tuple-element.56), channel_id=1, source_target_pairs={{0,256},{128,384},{256,0},{384,128},{1,257},{129,385},{257,1},{385... | collective-permute-start | bytes 884744 | tf_op jit(solution)/shard_map/ppermute | solution.py:574
  234.1 2.7 %collective-permute-start.12 = (bf16[576,256]{1,0:T(8,128)(2,1)}, bf16[576,256]{1,0:T(8,128)(2,1)S(1)}, u32[]{:S(2)}, u32[]{:S(2)}) collective-permute-start(bf16[576,256]{1,0:T(8,128)(2,1)} %get-tuple-element.57), channel_id=1, source_target_pairs={{0,384},{128,0},{256,128},{384,256},{1,385},{129,1},{257,129},{385... | collective-permute-start | bytes 884744 | tf_op jit(solution)/shard_map/ppermute | solution.py:574
  240.5 5.2 %collective-permute-done.11.refs_2_ = bf16[576,256]{1,0:T(8,128)(2,1)S(1)} collective-permute-done((bf16[576,256]{1,0:T(8,128)(2,1)}, bf16[576,256]{1,0:T(8,128)(2,1)S(1)}, u32[]{:S(2)}, u32[]{:S(2)}) %collective-permute-start.11) | collective-permute-done | bytes 294944 | tf_op jit(solution)/shard_map/ppermute | solution.py:574
  245.8 2.8 %collective-permute-done.12.refs_3_ = bf16[576,256]{1,0:T(8,128)(2,1)S(1)} collective-permute-done((bf16[576,256]{1,0:T(8,128)(2,1)}, bf16[576,256]{1,0:T(8,128)(2,1)S(1)}, u32[]{:S(2)}, u32[]{:S(2)}) %collective-permute-start.12) | collective-permute-done | bytes 294944 | tf_op jit(solution)/shard_map/ppermute | solution.py:574
  249.2 2.0 shard_map.274
  (111 shorter events, 32.8 us)
Async XLA Ops:
  8.8 14.5 %copy-start.22 = (f32[8]{0:T(128)S(1)}, f32[8]{0:T(128)}, u32[]{:S(2)}) copy-start(f32[8]{0:T(128)} %param.24) | copy-start | bytes 100
  10.2 20.5 %all-to-all-start = ((bf16[8,144,256]{2,1,0:T(8,128)(2,1)}), bf16[8,144,256]{2,1,0:T(8,128)(2,1)S(1)}, u32[]{:S(2)}, u32[]{:S(2)}) async-start(bf16[8,144,256]{2,1,0:T(8,128)(2,1)} %fusion.17), calls=%async_computation | async-start | bytes 1179648 | tf_op jit(solution)/shard_map/all_to_all | solution.py:20
  20.5 35.9 %copy-start.25 = (bf16[1,512,256]{2,1,0:T(8,128)(2,1)S(1)}, bf16[1,512,256]{2,1,0:T(8,128)(2,1)}, u32[]{:S(2)}) copy-start(bf16[1,512,256]{2,1,0:T(8,128)(2,1)} %param.28) | copy-start | bytes 786436
  21.9 2.1 collective-permute-start
  34.2 12.7 %collective-permute-start.1 = (bf16[192,768]{1,0:T(8,128)(2,1)}, bf16[192,768]{1,0:T(8,128)(2,1)S(1)}, u32[]{:S(2)}, u32[]{:S(2)}) collective-permute-start(bf16[192,768]{1,0:T(8,128)(2,1)} %get-tuple-element.38), channel_id=1, source_target_pairs={{0,15},{1,0},{2,1},{3,2},{4,3},{5,4},{6,5},{7,6},{8,7},{9,8},{10,9... | collective-permute-start | bytes 884744 | tf_op jit(solution)/shard_map/ppermute | solution.py:25
  41.2 12.0 %collective-permute-start.3 = (bf16[192,768]{1,0:T(8,128)(2,1)}, bf16[192,768]{1,0:T(8,128)(2,1)S(1)}, u32[]{:S(2)}, u32[]{:S(2)}) collective-permute-start(bf16[192,768]{1,0:T(8,128)(2,1)} %get-tuple-element.40), channel_id=1, source_target_pairs={{0,1},{1,2},{2,3},{3,4},{4,5},{5,6},{6,7},{7,8},{8,9},{9,10},{10,1... | collective-permute-start | bytes 884744 | tf_op jit(solution)/shard_map/ppermute | solution.py:25
  48.0 18.8 %collective-permute-start.2 = (bf16[192,768]{1,0:T(8,128)(2,1)S(1)}, bf16[192,768]{1,0:T(8,128)(2,1)S(1)}, u32[]{:S(2)}, u32[]{:S(2)}) collective-permute-start(bf16[192,768]{1,0:T(8,128)(2,1)S(1)} %add_convert_fusion.1), channel_id=1, source_target_pairs={{0,15},{1,0},{2,1},{3,2},{4,3},{5,4},{6,5},{7,6},{8,7},{9,8},{10,9... | collective-permute-start | bytes 884744 | tf_op jit(solution)/shard_map/ppermute | solution.py:25
  54.3 12.5 %collective-permute-start.4 = (bf16[192,768]{1,0:T(8,128)(2,1)S(1)}, bf16[192,768]{1,0:T(8,128)(2,1)S(1)}, u32[]{:S(2)}, u32[]{:S(2)}) collective-permute-start(bf16[192,768]{1,0:T(8,128)(2,1)S(1)} %add_convert_fusion), channel_id=1, source_target_pairs={{0,1},{1,2},{2,3},{3,4},{4,5},{5,6},{6,7},{7,8},{8,9},{9,10},{10,1... | collective-permute-start | bytes 884744 | tf_op jit(solution)/shard_map/ppermute | solution.py:25
  57.7 34.3 %all-to-all-start.1 = ((bf16[8,128,256]{2,1,0:T(8,128)(2,1)}), bf16[8,128,256]{2,1,0:T(8,128)(2,1)S(1)}, u32[]{:S(2)}, u32[]{:S(2)}) async-start(bf16[8,128,256]{2,1,0:T(8,128)(2,1)} %bitcast.22), calls=%async_computation.1 | async-start | bytes 1048576 | tf_op jit(solution)/shard_map/all_to_all | solution.py:20
  64.1 142.1 %all-gather.2.cloned.1.call-start = ((), (), s32[]{:S(2)}) async-start(), calls=%async_computation.8 | async-start | bytes 5292032 | tf_op jit(solution)/shard_map/all_gather | solution.py:508
  64.1 10.9 %collective-permute-start.6 = (bf16[64,768]{1,0:T(8,128)(2,1)S(1)}, bf16[64,768]{1,0:T(8,128)(2,1)S(1)}, u32[]{:S(2)}, u32[]{:S(2)}) collective-permute-start(bf16[64,768]{1,0:T(8,128)(2,1)S(1)} %copy-done.26), channel_id=1, source_target_pairs={{0,3},{1,4},{2,5},{3,6},{4,7},{5,8},{6,9},{7,10},{8,11},{9,12},{10... | collective-permute-start | bytes 294920 | tf_op jit(solution)/shard_map/ppermute | solution.py:25
  66.8 27.9 %copy-start.15 = (bf16[16,80,128]{2,1,0:T(8,128)(2,1)S(1)}, bf16[16,80,128]{2,1,0:T(8,128)(2,1)}, u32[]{:S(2)}) copy-start(bf16[16,80,128]{2,1,0:T(8,128)(2,1)} %shard_map.266.earlier_ref) | copy-start | bytes 983044
  67.0 85.8 %copy-start.1 = (bf16[1,256,256]{2,1,0:T(8,128)(2,1)S(1)}, bf16[1,256,256]{2,1,0:T(8,128)(2,1)}, u32[]{:S(2)}) copy-start(bf16[1,256,256]{2,1,0:T(8,128)(2,1)} %param.20) | copy-start | bytes 393220
  67.0 85.7 %copy-start.2 = (bf16[1,256,512]{2,1,0:T(8,128)(2,1)S(1)}, bf16[1,256,512]{2,1,0:T(8,128)(2,1)}, u32[]{:S(2)}) copy-start(bf16[1,256,512]{2,1,0:T(8,128)(2,1)} %param.19) | copy-start | bytes 786436
  67.0 85.7 %copy-start.3 = (bf16[1,256,512]{2,1,0:T(8,128)(2,1)S(1)}, bf16[1,256,512]{2,1,0:T(8,128)(2,1)}, u32[]{:S(2)}) copy-start(bf16[1,256,512]{2,1,0:T(8,128)(2,1)} %param.27) | copy-start | bytes 786436
  67.0 85.7 %copy-start.7 = (bf16[3,768]{1,0:T(4,128)(2,1)S(1)}, bf16[3,768]{1,0:T(4,128)(2,1)}, u32[]{:S(2)}) copy-start(bf16[3,768]{1,0:T(4,128)(2,1)} %copy-done.6) | copy-start | bytes 13828
  67.0 85.7 %copy-start.8 = (f32[4,256]{1,0:T(4,128)S(1)}, f32[4,256]{1,0:T(4,128)}, u32[]{:S(2)}) copy-start(f32[4,256]{1,0:T(4,128)} %tapsbc_ref.5) | copy-start | bytes 12292
  67.0 85.7 %copy-start.9 = (f32[1,8,256]{2,1,0:T(8,128)S(1)}, f32[1,8,256]{2,1,0:T(8,128)}, u32[]{:S(2)}) copy-start(f32[1,8,256]{2,1,0:T(8,128)} %param.21) | copy-start | bytes 24580
  67.0 85.7 %copy-start.10 = (f32[4,512]{1,0:T(4,128)S(1)}, f32[4,512]{1,0:T(4,128)}, u32[]{:S(2)}) copy-start(f32[4,512]{1,0:T(4,128)} %tapsx_ref.3) | copy-start | bytes 24580
  67.0 85.7 %copy-start.11 = (f32[3,8]{1,0:T(4,128)S(1)}, f32[3,8]{1,0:T(4,128)}, u32[]{:S(2)}) copy-start(f32[3,8]{1,0:T(4,128)} %pad_maximum_fusion.1.gains_ref) | copy-start | bytes 292
  67.1 16.3 %collective-permute-start.5 = (bf16[64,768]{1,0:T(8,128)(2,1)S(1)}, bf16[64,768]{1,0:T(8,128)(2,1)S(1)}, u32[]{:S(2)}, u32[]{:S(2)}) collective-permute-start(bf16[64,768]{1,0:T(8,128)(2,1)S(1)} %slice.104), channel_id=1, source_target_pairs={{0,11},{1,12},{2,13},{3,14},{4,15},{5,0},{6,1},{7,2},{8,3},{9,4},{... | collective-permute-start | bytes 294920 | tf_op jit(solution)/shard_map/ppermute | solution.py:25
  75.1 16.2 %collective-permute-start.7 = (bf16[64,768]{1,0:T(8,128)(2,1)S(1)}, bf16[64,768]{1,0:T(8,128)(2,1)S(1)}, u32[]{:S(2)}, u32[]{:S(2)}) collective-permute-start(bf16[64,768]{1,0:T(8,128)(2,1)S(1)} %fusion.20), channel_id=1, source_target_pairs={{0,5},{1,6},{2,7},{3,8},{4,9},{5,10},{6,11},{7,12},{8,13},{9,14},{... | collective-permute-start | bytes 294920 | tf_op jit(solution)/shard_map/ppermute | solution.py:25
  152.8 53.5 %copy-start.4 = (bf16[1,256,768]{2,1,0:T(8,128)(2,1)S(1)}, bf16[1,256,768]{2,1,0:T(8,128)(2,1)}, u32[]{:S(2)}) copy-start(bf16[1,256,768]{2,1,0:T(8,128)(2,1)} %param.33) | copy-start | bytes 1179652
  152.8 53.5 %copy-start.5 = (bf16[1,256,768]{2,1,0:T(8,128)(2,1)S(1)}, bf16[1,256,768]{2,1,0:T(8,128)(2,1)}, u32[]{:S(2)}) copy-start(bf16[1,256,768]{2,1,0:T(8,128)(2,1)} %param.34) | copy-start | bytes 1179652
  159.7 25.3 %all-to-all-start.4 = ((bf16[8,256,256]{2,1,0:T(8,128)(2,1)}), bf16[8,256,256]{2,1,0:T(8,128)(2,1)S(1)}, u32[]{:S(2)}, u32[]{:S(2)}) async-start(bf16[8,256,256]{2,1,0:T(8,128)(2,1)} %get-tuple-element.46), calls=%async_computation.4 | async-start | bytes 2097152 | tf_op jit(solution)/shard_map/all_to_all | solution.py:20
  198.4 16.1 %all-to-all-start.6 = ((f32[16,8,128]{2,1,0:T(8,128)}), f32[16,8,128]{2,1,0:T(8,128)S(1)}, u32[]{:S(2)}, u32[]{:S(2)}) async-start(f32[16,8,128]{2,1,0:T(8,128)} %broadcast_in_dim.83), calls=%async_computation.6 | async-start | bytes 131072 | tf_op jit(solution)/shard_map/all_to_all | solution.py:20
  202.9 18.9 %collective-permute-start.8 = (f32[3,512]{1,0:T(4,128)S(1)}, f32[3,512]{1,0:T(4,128)S(1)}, u32[]{:S(2)}, u32[]{:S(2)}) collective-permute-start(f32[3,512]{1,0:T(4,128)S(1)} %slice.65), channel_id=1, source_target_pairs={{1,0},{2,1},{3,2},{4,3},{5,4},{6,5},{7,6},{8,7},{9,8},{10,9},{11,1... | collective-permute-start | bytes 18440 | tf_op jit(solution)/shard_map/ppermute | solution.py:16
  204.9 31.9 %collective-permute-start.9 = (f32[3,256]{1,0:T(4,128)S(1)}, f32[3,256]{1,0:T(4,128)S(1)}, u32[]{:S(2)}, u32[]{:S(2)}) collective-permute-start(f32[3,256]{1,0:T(4,128)S(1)} %slice.66), channel_id=1, source_target_pairs={{1,0},{2,1},{3,2},{4,3},{5,4},{6,5},{7,6},{8,7},{9,8},{10,9},{11,1... | collective-permute-start | bytes 9224 | tf_op jit(solution)/shard_map/ppermute | solution.py:16
  214.5 36.8 %all-to-all-start.7 = ((bf16[8,144,256]{2,1,0:T(8,128)(2,1)}), bf16[8,144,256]{2,1,0:T(8,128)(2,1)S(1)}, u32[]{:S(2)}, u32[]{:S(2)}) async-start(bf16[8,144,256]{2,1,0:T(8,128)(2,1)} %shard_map.272), calls=%async_computation.7 | async-start | bytes 1179648 | tf_op jit(solution)/shard_map/all_to_all | solution.py:20
  228.2 12.3 %collective-permute-start.10 = (bf16[576,256]{1,0:T(8,128)(2,1)}, bf16[576,256]{1,0:T(8,128)(2,1)S(1)}, u32[]{:S(2)}, u32[]{:S(2)}) collective-permute-start(bf16[576,256]{1,0:T(8,128)(2,1)} %get-tuple-element.55), channel_id=1, source_target_pairs={{0,128},{128,256},{256,384},{384,0},{1,129},{129,257},{257,385},{3... | collective-permute-start | bytes 884744 | tf_op jit(solution)/shard_map/ppermute | solution.py:574
  230.4 15.4 %collective-permute-start.11 = (bf16[576,256]{1,0:T(8,128)(2,1)}, bf16[576,256]{1,0:T(8,128)(2,1)S(1)}, u32[]{:S(2)}, u32[]{:S(2)}) collective-permute-start(bf16[576,256]{1,0:T(8,128)(2,1)} %get-tuple-element.56), channel_id=1, source_target_pairs={{0,256},{128,384},{256,0},{384,128},{1,257},{129,385},{257,1},{385... | collective-permute-start | bytes 884744 | tf_op jit(solution)/shard_map/ppermute | solution.py:574
  234.1 14.4 %collective-permute-start.12 = (bf16[576,256]{1,0:T(8,128)(2,1)}, bf16[576,256]{1,0:T(8,128)(2,1)S(1)}, u32[]{:S(2)}, u32[]{:S(2)}) collective-permute-start(bf16[576,256]{1,0:T(8,128)(2,1)} %get-tuple-element.57), channel_id=1, source_target_pairs={{0,384},{128,0},{256,128},{384,256},{1,385},{129,1},{257,129},{385... | collective-permute-start | bytes 884744 | tf_op jit(solution)/shard_map/ppermute | solution.py:574
  (14 other events, 83.4 us)
Sparse Core Ops, SparseCore 0:
  94.8 92.1 all-gather.1

commit v6 on v5

--- a/solution.py
+++ b/solution.py
@@ -327,12 +327,23 @@
     ).astype(BF16)
 
 
-def weights_kernel(place_ref, all_ref, in_ref, cot_ref, *refs):
+def rows_kernel(
+    place_ref, all_ref, in_ref, cot_ref, gatew_ref, upw_ref, earlier_ref, back_ref, *refs
+):
+    del earlier_ref
     out_refs, grads_ref = refs[:-1], refs[-1]
     groups, slots, cols = in_ref.shape
-    width = grads_ref.shape[1]
+    width = gatew_ref.shape[1]
     owners = len(out_refs)
     share = width // owners
+    rows_grad = dot(all_ref[:, :width], gatew_ref[...], 1, 1)
+    rows_grad = rows_grad + dot(all_ref[:, width : 2 * width], upw_ref[...], 1, 1)
+    back_ref[:, :slots, :] = rows_grad.astype(BF16).reshape(groups, slots, cols)
+    route = all_ref[:, 3 * width :].astype(F32)
+    for group in range(groups):
+        turned = route[group * slots : (group + 1) * slots].T
+        line = jnp.concatenate([turned[0:1], turned[1:2]], axis=1)
+        back_ref[group, slots:, :] = jnp.broadcast_to(line, (16, cols)).astype(BF16)
     rows_in = in_ref[...].reshape(groups * slots, cols)
     scaled = jnp.concatenate([scaled_rows(cot_ref, group) for group in range(groups)], axis=0)
     grads_ref[0] = dot(all_ref[:, :width], rows_in, 0, 0).astype(BF16)
@@ -345,20 +356,6 @@
             out_refs[ahead][kind * share : (kind + 1) * share, :] = grads_ref[
                 kind, pl.ds(start, share), :
             ]
-
-
-def rows_kernel(all_ref, gatew_ref, upw_ref, back_ref):
-    width = gatew_ref.shape[1]
-    groups, slots, cols = back_ref.shape
-    slots = slots - 16
-    rows_grad = dot(all_ref[:, :width], gatew_ref[...], 1, 1)
-    rows_grad = rows_grad + dot(all_ref[:, width : 2 * width], upw_ref[...], 1, 1)
-    back_ref[:, :slots, :] = rows_grad.astype(BF16).reshape(groups, slots, cols)
-    route = all_ref[:, 3 * width :].astype(F32)
-    for group in range(groups):
-        turned = route[group * slots : (group + 1) * slots].T
-        line = jnp.concatenate([turned[0:1], turned[1:2]], axis=1)
-        back_ref[group, slots:, :] = jnp.broadcast_to(line, (16, cols)).astype(BF16)
 
 
 def totals_kernel(*refs):
@@ -473,7 +470,6 @@
     send_cot = send_cot.reshape(expert_count, slot_width, col_width)
     got_cot = exchange(jnp.concatenate([send_cot, send_weight], axis=1), "expert")
     send_in = jnp.dot(table, moe_in[0], preferred_element_type=F32).astype(BF16)
-    rows_in = exchange(send_in.reshape(expert_count, slot_width, col_width), "expert")
 
     gains = jnp.stack([dt_bias, a_log, d_skip])
     pad_heads = ((8 + length, split_at), F32)
@@ -496,6 +492,7 @@
     opposite = shift(opposite, 3)
     left1 = (left1.astype(F32) + shift(left2, -1).astype(F32)).astype(BF16)
     right1 = (right1.astype(F32) + shift(right2, 1).astype(F32)).astype(BF16)
+    got_states = exchange(after(states, left1, right1), "ctx")
     centre = centre.astype(F32) + shift(left1, -1).astype(F32) + shift(right1, 1).astype(F32)
     far_left = shift(centre[:own].astype(BF16), -FAR)
     far_right = shift((centre[2 * own :] + opposite.astype(F32)).astype(BF16), FAR)
@@ -504,12 +501,16 @@
     weight_own = lax.dynamic_slice_in_dim(rows_weight, place[0] * own, own, 0)
     (own_rows,) = whole(
         own_rows_kernel, [((own, 3 * hidden_width + 128), BF16)], inputs=4, late=1
-    )(mine, weight_own[:, None], gate_act[0, 0], up_act[0, 0], rows_in)
+    )(mine, weight_own[:, None], gate_act[0, 0], up_act[0, 0], got_states)
     everything = lax.all_gather(own_rows, "ctx", axis=0, tiled=True)
 
     (entered,) = whole(
         scan_kernel, [((ctx_places, 2 * part, state_width), BF16)], inputs=1
-    )(exchange(after(states, own_rows), "ctx"))
+    )(got_states)
+
+    entered = exchange(entered, "ctx")
+    send_in = after(send_in.reshape(expert_count, slot_width, col_width), entered)
+    rows_in = exchange(send_in, "expert")
 
     main_heads, tail_heads, rim_heads, grad_bc, grad_step, taps_heads, grad_rate = whole(
         back_kernel,
@@ -527,8 +528,9 @@
         limit=48 * 2**20,
     )(
         head_rows, shared_rows, before, raw_step, gains, conv_x, conv_bc, cot_rows,
-        exchange(entered, "ctx"),
-    )
+        entered,
+    )
+    grad_bc = after(grad_bc, rows_in)
     after_heads = passed_along(rim_heads[:rim_rows], "ctx", -1)
     grad_mamba_in = with_last_rows(main_heads, tail_heads, after_heads)
     main_shared, tail_shared, rim_shared, taps_shared = whole(
@@ -562,25 +564,20 @@
     share = hidden_width // dp_count
     block = ((3 * share, col_width), BF16)
     owner = lax.axis_index("dp").astype(jnp.int32).reshape(1)
-    parts = whole(
-        weights_kernel,
-        [block] * dp_count,
+    back, *parts = whole(
+        rows_kernel,
+        [((expert_count, slot_width + 16, col_width), BF16)] + [block] * dp_count,
         [((3, hidden_width, col_width), BF16)],
-        inputs=3,
+        inputs=5,
         scalars=1,
+        late=1,
         limit=56 * 2**20,
-    )(owner, everything, rows_in, got_cot)
+    )(owner, everything, rows_in, got_cot, w_gate[0], w_up[0], small)
+    back = exchange(back, "expert")
     parts = [parts[0]] + [
         lax.ppermute(parts[k], "dp", [(i, (i + k) % dp_count) for i in range(dp_count)])
         for k in range(1, dp_count)
     ]
-    (back,) = whole(
-        rows_kernel,
-        [((expert_count, slot_width + 16, col_width), BF16)],
-        inputs=3,
-        limit=48 * 2**20,
-    )(everything, w_gate[0], w_up[0])
-    back = exchange(back, "expert")
     gate_total, up_total, down_total = whole(
         totals_kernel, [((share, col_width), BF16)] * 3, inputs=dp_count
     )(*parts)

time: 262 us -> 260 us (level)
  blocking collectives: 64.4 us -> 8.52 us
  waiting for transfers between devices: 45.8 us -> 82.1 us
  starting transfers between devices: 81.7 us -> 102 us
  Pallas kernels: 32 us -> 28.6 us
    all_to_all x3 -> x1, blocking collectives: 64.4 us -> 8.52 us  [exchange(): return lax.all_to_all(value, axis, split_axis=0, concat_axis=0, tiled=True)]
    all_to_all x5 -> x7, waiting for transfers between devices: 21.3 us -> 39.9 us  [exchange(): return lax.all_to_all(value, axis, split_axis=0, concat_axis=0, tiled=True)]
    all_to_all x5 -> x7, starting transfers between devices: 38.9 us -> 56.9 us  [exchange(): return lax.all_to_all(value, axis, split_axis=0, concat_axis=0, tiled=True)]
    ppermute x7, waiting for transfers between devices: 15 us -> 32.5 us  [shift(): lax.ppermute(value, 'ctx', [(i, (i + distance) % count) for i in range(co...]
    pallas_call x2 -> x1, Pallas kernels: 9.96 us -> 6.45 us  [body(): whole(rows_kernel, [((expert_count, slot_width + 16, col_width), BF16)] +...]
  transfers between devices with their start and end apart: 19 -> 21, of which waited for: 10 -> 15; matrix products, arithmetic and copies ran while one was open for 5% -> 5% of each run, Pallas kernels for 11% -> 9%
where the time goes in v6:
time: 260 us; the launch traced here: 258 us
  starting transfers between devices  102 us (39%)
  waiting for transfers between devices  82.1 us (32%)
  Pallas kernels  28.6 us (11%)
  between operations  14.5 us (6%)
  other arithmetic  9.85 us (4%)
  local copies, waits for them, and re-layouts  9.27 us (4%)
  blocking collectives  8.52 us (3%)
  matrix products  3.19 us (1%)
    all_to_all x7, starting transfers between devices, exchange(): return lax.all_to_all(value, axis, split_axis=0, concat_axis=0, tiled=True)  56.9 us
    all_to_all x7, waiting for transfers between devices, exchange(): return lax.all_to_all(value, axis, split_axis=0, concat_axis=0, tiled=True)  39.9 us
    ppermute x7, starting transfers between devices, shift(): lax.ppermute(value, 'ctx', [(i, (i + distance) % count) for i in range(co...  32.8 us
    ppermute x7, waiting for transfers between devices, shift(): lax.ppermute(value, 'ctx', [(i, (i + distance) % count) for i in range(co...  32.5 us
    ppermute x3, waiting for transfers between devices, body(): lax.ppermute(parts[k], 'dp', [(i, (i + k) % dp_count) for i in range(dp_c...  9.47 us
    ppermute x3, starting transfers between devices, body(): lax.ppermute(parts[k], 'dp', [(i, (i + k) % dp_count) for i in range(dp_c...  8.53 us
    all_to_all x1, blocking collectives, exchange(): return lax.all_to_all(value, axis, split_axis=0, concat_axis=0, tiled=True)  8.52 us
    pallas_call x1, Pallas kernels, body(): whole(back_kernel, [((length, split_at), BF16), ((16, split_at), F32), ((...  6.99 us
  transfers between devices with their start and end apart: 21, of which 15 were waited for; matrix products, arithmetic and copies ran while one was open for 5% of the time, Pallas kernels for 9%

profile of v6, /device:TPU:1, one launch (start us, length us, event | category | flops | bytes accessed | tf_op | source)
XLA Modules:
  0.0 258.2 jit_solution(16396181366627736)
XLA Ops:
  10.1 10.3 %all-to-all-start = ((bf16[8,144,256]{2,1,0:T(8,128)(2,1)}), bf16[8,144,256]{2,1,0:T(8,128)(2,1)S(1)}, u32[]{:S(2)}, u32[]{:S(2)}) async-start(bf16[8,144,256]{2,1,0:T(8,128)(2,1)} %fusion.17), calls=%async_computation | async-start | bytes 1179648 | tf_op jit(solution)/shard_map/all_to_all | solution.py:20
  24.5 3.9 %shard_map.266.earlier_ref = bf16[16,80,128]{2,1,0:T(8,128)(2,1)} custom-call(bf16[256,512]{1,0:T(8,128)(2,1)} %bitcast.76, bf16[256,256]{1,0:T(8,128)(2,1)} %bitcast.73, bf16[3,768]{1,0:T(4,128)(2,1)} %copy-done.4, f32[8,256]{1,0:T(8,128)} %bitcast.80, f32[3,8]{1,0:T(4,128)} %pad_maximum_fusion.1.gains_ref, f32[4,512]{1,0:T(4,128)} %tapsx_ref.3, ...), custom_call_target="tpu_custom_call" | custom-call | tf_op jit(solution)/shard_map/pallas_call | solution.py:477
  31.5 2.7 %shard_map.267 = (bf16[192,768]{1,0:T(8,128)(2,1)}, bf16[192,768]{1,0:T(8,128)(2,1)}, bf16[192,768]{1,0:T(8,128)(2,1)}, bf16[192,768]{1,0:T(8,128)(2,1)}, bf16[1...) custom-call(s32[1]{0:T(128)} %bitcast.9.place_ref, bf16[8,144,256]{2,1,0:T(8,128)(2,1)} %copy-done.10, ...), custom_call_target="tpu_custom_call" | custom-call | tf_op jit(solution)/shard_map/pallas_call | solution.py:484
  34.2 7.0 %collective-permute-start.1 = (bf16[192,768]{1,0:T(8,128)(2,1)}, bf16[192,768]{1,0:T(8,128)(2,1)S(1)}, u32[]{:S(2)}, u32[]{:S(2)}) collective-permute-start(bf16[192,768]{1,0:T(8,128)(2,1)} %get-tuple-element.40), channel_id=1, source_target_pairs={{0,15},{1,0},{2,1},{3,2},{4,3},{5,4},{6,5},{7,6},{8,7},{9,8},{10,9... | collective-permute-start | bytes 884744 | tf_op jit(solution)/shard_map/ppermute | solution.py:25
  43.2 3.8 %collective-permute-done.1 = bf16[192,768]{1,0:T(8,128)(2,1)S(1)} collective-permute-done((bf16[192,768]{1,0:T(8,128)(2,1)}, bf16[192,768]{1,0:T(8,128)(2,1)S(1)}, u32[]{:S(2)}, u32[]{:S(2)}) %collective-permute-start.1) | collective-permute-done | bytes 294944 | tf_op jit(solution)/shard_map/ppermute | solution.py:25
  48.1 3.9 %collective-permute-done.2 = bf16[192,768]{1,0:T(8,128)(2,1)S(1)} collective-permute-done((bf16[192,768]{1,0:T(8,128)(2,1)}, bf16[192,768]{1,0:T(8,128)(2,1)S(1)}, u32[]{:S(2)}, u32[]{:S(2)}) %collective-permute-start.2) | collective-permute-done | bytes 294944 | tf_op jit(solution)/shard_map/ppermute | solution.py:25
  53.0 7.3 %all-to-all-start.1 = ((bf16[16,80,128]{2,1,0:T(8,128)(2,1)}), bf16[16,80,128]{2,1,0:T(8,128)(2,1)S(1)}, u32[]{:S(2)}, u32[]{:S(2)}) async-start(bf16[16,80,128]{2,1,0:T(8,128)(2,1)} %shard_map.266.earlier_ref), calls=%async_computation.1 | async-start | bytes 655360 | tf_op jit(solution)/shard_map/all_to_all | solution.py:20
  60.3 3.3 %collective-permute-start.6 = (bf16[192,768]{1,0:T(8,128)(2,1)S(1)}, bf16[192,768]{1,0:T(8,128)(2,1)S(1)}, u32[]{:S(2)}, u32[]{:S(2)}) collective-permute-start(bf16[192,768]{1,0:T(8,128)(2,1)S(1)} %add_convert_fusion), channel_id=1, source_target_pairs={{0,1},{1,2},{2,3},{3,4},{4,5},{5,6},{6,7},{7,8},{8,9},{9,10},{10,1... | collective-permute-start | bytes 884744 | tf_op jit(solution)/shard_map/ppermute | solution.py:25
  63.6 3.2 %collective-permute-start.5 = (bf16[192,768]{1,0:T(8,128)(2,1)S(1)}, bf16[192,768]{1,0:T(8,128)(2,1)S(1)}, u32[]{:S(2)}, u32[]{:S(2)}) collective-permute-start(bf16[192,768]{1,0:T(8,128)(2,1)S(1)} %add_convert_fusion.1), channel_id=1, source_target_pairs={{0,15},{1,0},{2,1},{3,2},{4,3},{5,4},{6,5},{7,6},{8,7},{9,8},{10,9... | collective-permute-start | bytes 884744 | tf_op jit(solution)/shard_map/ppermute | solution.py:25
  66.8 4.8 %collective-permute-start.8 = (bf16[64,768]{1,0:T(8,128)(2,1)S(1)}, bf16[64,768]{1,0:T(8,128)(2,1)S(1)}, u32[]{:S(2)}, u32[]{:S(2)}) collective-permute-start(bf16[64,768]{1,0:T(8,128)(2,1)S(1)} %copy-done.25), channel_id=1, source_target_pairs={{0,3},{1,4},{2,5},{3,6},{4,7},{5,8},{6,9},{7,10},{8,11},{9,12},{10... | collective-permute-start | bytes 294920 | tf_op jit(solution)/shard_map/ppermute | solution.py:25
  72.4 11.0 %collective-permute-done.6 = bf16[192,768]{1,0:T(8,128)(2,1)S(1)} collective-permute-done((bf16[192,768]{1,0:T(8,128)(2,1)S(1)}, bf16[192,768]{1,0:T(8,128)(2,1)S(1)}, u32[]{:S(2)}, u32[]{:S(2)}) %collective-permute-start.6) | collective-permute-done | bytes 294944 | tf_op jit(solution)/shard_map/ppermute | solution.py:25
  83.5 4.7 %collective-permute-done.8 = bf16[64,768]{1,0:T(8,128)(2,1)S(1)} collective-permute-done((bf16[64,768]{1,0:T(8,128)(2,1)S(1)}, bf16[64,768]{1,0:T(8,128)(2,1)S(1)}, u32[]{:S(2)}, u32[]{:S(2)}) %collective-permute-start.8) | collective-permute-done | bytes 98336 | tf_op jit(solution)/shard_map/ppermute | solution.py:25
  88.3 7.5 %collective-permute-start.9 = (bf16[64,768]{1,0:T(8,128)(2,1)S(1)}, bf16[64,768]{1,0:T(8,128)(2,1)S(1)}, u32[]{:S(2)}, u32[]{:S(2)}) collective-permute-start(bf16[64,768]{1,0:T(8,128)(2,1)S(1)} %fusion.20), channel_id=1, source_target_pairs={{0,5},{1,6},{2,7},{3,8},{4,9},{5,10},{6,11},{7,12},{8,13},{9,14},{... | collective-permute-start | bytes 294920 | tf_op jit(solution)/shard_map/ppermute | solution.py:25
  95.8 5.1 %collective-permute-start.7 = (bf16[64,768]{1,0:T(8,128)(2,1)S(1)}, bf16[64,768]{1,0:T(8,128)(2,1)S(1)}, u32[]{:S(2)}, u32[]{:S(2)}) collective-permute-start(bf16[64,768]{1,0:T(8,128)(2,1)S(1)} %slice.104), channel_id=1, source_target_pairs={{0,11},{1,12},{2,13},{3,14},{4,15},{5,0},{6,1},{7,2},{8,3},{9,4},{... | collective-permute-start | bytes 294920 | tf_op jit(solution)/shard_map/ppermute | solution.py:25
  101.7 6.1 %collective-permute-done.9 = bf16[64,768]{1,0:T(8,128)(2,1)S(1)} collective-permute-done((bf16[64,768]{1,0:T(8,128)(2,1)S(1)}, bf16[64,768]{1,0:T(8,128)(2,1)S(1)}, u32[]{:S(2)}, u32[]{:S(2)}) %collective-permute-start.9) | collective-permute-done | bytes 98336 | tf_op jit(solution)/shard_map/ppermute | solution.py:25
  107.8 2.9 %collective-permute-done.7 = bf16[64,768]{1,0:T(8,128)(2,1)S(1)} collective-permute-done((bf16[64,768]{1,0:T(8,128)(2,1)S(1)}, bf16[64,768]{1,0:T(8,128)(2,1)S(1)}, u32[]{:S(2)}, u32[]{:S(2)}) %collective-permute-start.7) | collective-permute-done | bytes 98336 | tf_op jit(solution)/shard_map/ppermute | solution.py:25
  115.9 10.4 %all-to-all-start.2 = ((bf16[16,64,128]{2,1,0:T(8,128)(2,1)}), bf16[16,64,128]{2,1,0:T(8,128)(2,1)S(1)}, u32[]{:S(2)}, u32[]{:S(2)}) async-start(bf16[16,64,128]{2,1,0:T(8,128)(2,1)} %shard_map.268), calls=%async_computation.2 | async-start | bytes 524288 | tf_op jit(solution)/shard_map/all_to_all | solution.py:20
  127.7 11.7 %all-to-all-done.2.got_ref = bf16[16,64,128]{2,1,0:T(8,128)(2,1)S(1)} async-done(((bf16[16,64,128]{2,1,0:T(8,128)(2,1)}), bf16[16,64,128]{2,1,0:T(8,128)(2,1)S(1)}, u32[]{:S(2)}, u32[]{:S(2)}) %all-to-all-start.2) | async-done | bytes 262176 | tf_op jit(solution)/shard_map/all_to_all | solution.py:20
  139.5 12.2 %all-to-all-start.3 = ((bf16[8,128,256]{2,1,0:T(8,128)(2,1)}), bf16[8,128,256]{2,1,0:T(8,128)(2,1)S(1)}, u32[]{:S(2)}, u32[]{:S(2)}) async-start(bf16[8,128,256]{2,1,0:T(8,128)(2,1)} %bitcast.20), calls=%async_computation.3 | async-start | bytes 1048576 | tf_op jit(solution)/shard_map/all_to_all | solution.py:20
  151.7 7.0 %shard_map.269 = (bf16[256,512]{1,0:T(8,128)(2,1)}, f32[16,512]{1,0:T(8,128)S(1)}, f32[8,512]{1,0:T(8,128)S(1)}, bf16[8,256,256]{2,1,0:T(8,128)(2,1)}, f32[8,256...) custom-call(bf16[256,512]{1,0:T(8,128)(2,1)S(1)} %bitcast.77, bf16[256,256]{1,0:T(8,128)(2,1)S(1)} %bitcast.75, ...), custom_call_target="tpu_custom_call" | custom-call | tf_op jit(solution)/shard_map/pallas_call | solution.py:515
  161.2 4.3 %all-to-all-start.4 = ((bf16[8,256,256]{2,1,0:T(8,128)(2,1)}), bf16[8,256,256]{2,1,0:T(8,128)(2,1)S(1)}, u32[]{:S(2)}, u32[]{:S(2)}) async-start(bf16[8,256,256]{2,1,0:T(8,128)(2,1)} %get-tuple-element.49), calls=%async_computation.4 | async-start | bytes 2097152 | tf_op jit(solution)/shard_map/all_to_all | solution.py:20
  165.5 15.1 %all-to-all-done.4.got_ref = bf16[8,256,256]{2,1,0:T(8,128)(2,1)S(1)} async-done(((bf16[8,256,256]{2,1,0:T(8,128)(2,1)}), bf16[8,256,256]{2,1,0:T(8,128)(2,1)S(1)}, u32[]{:S(2)}, u32[]{:S(2)}) %all-to-all-start.4) | async-done | bytes 1048608 | tf_op jit(solution)/shard_map/all_to_all | solution.py:20
  181.7 2.9 %shard_map.270 = (bf16[256,256]{1,0:T(8,128)(2,1)}, f32[16,256]{1,0:T(8,128)}, f32[8,256]{1,0:T(8,128)}, f32[4,256]{1,0:T(4,128)}) custom-call(bf16[256,256]{1,0:T(8,128)(2,1)} %bitcast.74, bf16[3,768]{1,0:T(4,128)(2,1)} %copy-done.4, f32[4,256]{1,0:T(4,128)} %tapsbc_ref.5, bf16[8,256,256]{2,1,0:T(8,128)(2,1)} %copy-done.11), custom_call_target="tpu_custom_call" | custom-call | tf_op jit(solution)/shard_map/pallas_call | solution.py:536
  185.2 8.5 %all_to_all.40 = f32[4,8,128]{2,1,0:T(8,128)S(1)} all-to-all(f32[4,8,128]{2,1,0:T(8,128)S(1)} %bitcast.90), channel_id=1, replica_groups=mesh['dp'=4,'expert'=8,'ctx'=16] {'dp'}, dimensions={0} | all-to-all | bytes 32768 | tf_op jit(solution)/shard_map/all_to_all | solution.py:20
  194.4 5.2 %all-to-all-start.6 = ((f32[16,8,128]{2,1,0:T(8,128)}), f32[16,8,128]{2,1,0:T(8,128)S(1)}, u32[]{:S(2)}, u32[]{:S(2)}) async-start(f32[16,8,128]{2,1,0:T(8,128)} %broadcast_in_dim.82), calls=%async_computation.6 | async-start | bytes 131072 | tf_op jit(solution)/shard_map/all_to_all | solution.py:20
  202.9 8.4 %all-to-all-done.6 = f32[16,8,128]{2,1,0:T(8,128)S(1)} async-done(((f32[16,8,128]{2,1,0:T(8,128)}), f32[16,8,128]{2,1,0:T(8,128)S(1)}, u32[]{:S(2)}, u32[]{:S(2)}) %all-to-all-start.6) | async-done | bytes 65568 | tf_op jit(solution)/shard_map/all_to_all | solution.py:20
  211.9 6.5 %shard_map.272 = (bf16[8,144,256]{2,1,0:T(8,128)(2,1)}, bf16[576,256]{1,0:T(8,128)(2,1)}, bf16[576,256]{1,0:T(8,128)(2,1)}, bf16[576,256]{1,0:T(8,128)(2,1)}, bf16[576,256]{1,0:T(8,128)(2,1)}) custom-call(s32[1]{0:T(128)} %bitcast.27.place_ref, bf16[1024,2432]{1,0:T(8,128)(2,1)} %all-gather.2.cloned.1.call-done.all_ref, bf16[8,128,256]{2,1,0:T(8,128)(2,1)} %copy-done.13, ...), custom_call_target="tpu_custom_call" | custom-call | tf_op jit(solution)/shard_map/pallas_call | solution.py:567
  218.3 7.2 %all-to-all-start.7 = ((bf16[8,144,256]{2,1,0:T(8,128)(2,1)}), bf16[8,144,256]{2,1,0:T(8,128)(2,1)S(1)}, u32[]{:S(2)}, u32[]{:S(2)}) async-start(bf16[8,144,256]{2,1,0:T(8,128)(2,1)} %get-tuple-element.59), calls=%async_computation.7 | async-start | bytes 1179648 | tf_op jit(solution)/shard_map/all_to_all | solution.py:20
  228.2 3.8 %collective-permute-start.11 = (bf16[576,256]{1,0:T(8,128)(2,1)}, bf16[576,256]{1,0:T(8,128)(2,1)S(1)}, u32[]{:S(2)}, u32[]{:S(2)}) collective-permute-start(bf16[576,256]{1,0:T(8,128)(2,1)} %get-tuple-element.62), channel_id=1, source_target_pairs={{0,256},{128,384},{256,0},{384,128},{1,257},{129,385},{257,1},{385... | collective-permute-start | bytes 884744 | tf_op jit(solution)/shard_map/ppermute | solution.py:578
  232.0 2.6 %collective-permute-start.12 = (bf16[576,256]{1,0:T(8,128)(2,1)}, bf16[576,256]{1,0:T(8,128)(2,1)S(1)}, u32[]{:S(2)}, u32[]{:S(2)}) collective-permute-start(bf16[576,256]{1,0:T(8,128)(2,1)} %get-tuple-element.63), channel_id=1, source_target_pairs={{0,384},{128,0},{256,128},{384,256},{1,385},{129,1},{257,129},{385... | collective-permute-start | bytes 884744 | tf_op jit(solution)/shard_map/ppermute | solution.py:578
  238.5 5.2 %collective-permute-done.11.refs_2_ = bf16[576,256]{1,0:T(8,128)(2,1)S(1)} collective-permute-done((bf16[576,256]{1,0:T(8,128)(2,1)}, bf16[576,256]{1,0:T(8,128)(2,1)S(1)}, u32[]{:S(2)}, u32[]{:S(2)}) %collective-permute-start.11) | collective-permute-done | bytes 294944 | tf_op jit(solution)/shard_map/ppermute | solution.py:578
  243.7 2.8 %collective-permute-done.12.refs_3_ = bf16[576,256]{1,0:T(8,128)(2,1)S(1)} collective-permute-done((bf16[576,256]{1,0:T(8,128)(2,1)}, bf16[576,256]{1,0:T(8,128)(2,1)S(1)}, u32[]{:S(2)}, u32[]{:S(2)}) %collective-permute-start.12) | collective-permute-done | bytes 294944 | tf_op jit(solution)/shard_map/ppermute | solution.py:578
  (110 shorter events, 42.3 us)
Async XLA Ops:
  10.1 20.5 %all-to-all-start = ((bf16[8,144,256]{2,1,0:T(8,128)(2,1)}), bf16[8,144,256]{2,1,0:T(8,128)(2,1)S(1)}, u32[]{:S(2)}, u32[]{:S(2)}) async-start(bf16[8,144,256]{2,1,0:T(8,128)(2,1)} %fusion.17), calls=%async_computation | async-start | bytes 1179648 | tf_op jit(solution)/shard_map/all_to_all | solution.py:20
  21.9 2.1 collective-permute-start
  34.2 49.2 %copy-start.14 = (bf16[192,768]{1,0:T(8,128)(2,1)S(1)}, bf16[192,768]{1,0:T(8,128)(2,1)}, u32[]{:S(2)}) copy-start(bf16[192,768]{1,0:T(8,128)(2,1)} %get-tuple-element.57) | copy-start | bytes 884740
  34.2 12.8 %collective-permute-start.1 = (bf16[192,768]{1,0:T(8,128)(2,1)}, bf16[192,768]{1,0:T(8,128)(2,1)S(1)}, u32[]{:S(2)}, u32[]{:S(2)}) collective-permute-start(bf16[192,768]{1,0:T(8,128)(2,1)} %get-tuple-element.40), channel_id=1, source_target_pairs={{0,15},{1,0},{2,1},{3,2},{4,3},{5,4},{6,5},{7,6},{8,7},{9,8},{10,9... | collective-permute-start | bytes 884744 | tf_op jit(solution)/shard_map/ppermute | solution.py:25
  41.3 10.7 %collective-permute-start.2 = (bf16[192,768]{1,0:T(8,128)(2,1)}, bf16[192,768]{1,0:T(8,128)(2,1)S(1)}, u32[]{:S(2)}, u32[]{:S(2)}) collective-permute-start(bf16[192,768]{1,0:T(8,128)(2,1)} %get-tuple-element.42), channel_id=1, source_target_pairs={{0,1},{1,2},{2,3},{3,4},{4,5},{5,6},{6,7},{7,8},{8,9},{9,10},{10,1... | collective-permute-start | bytes 884744 | tf_op jit(solution)/shard_map/ppermute | solution.py:25
  53.0 58.4 %all-to-all-start.1 = ((bf16[16,80,128]{2,1,0:T(8,128)(2,1)}), bf16[16,80,128]{2,1,0:T(8,128)(2,1)S(1)}, u32[]{:S(2)}, u32[]{:S(2)}) async-start(bf16[16,80,128]{2,1,0:T(8,128)(2,1)} %shard_map.266.earlier_ref), calls=%async_computation.1 | async-start | bytes 655360 | tf_op jit(solution)/shard_map/all_to_all | solution.py:20
  60.3 151.6 %all-gather.2.cloned.1.call-start = ((), (), s32[]{:S(2)}) async-start(), calls=%async_computation.8 | async-start | bytes 5292032 | tf_op jit(solution)/shard_map/all_gather | solution.py:505
  60.3 23.1 %collective-permute-start.6 = (bf16[192,768]{1,0:T(8,128)(2,1)S(1)}, bf16[192,768]{1,0:T(8,128)(2,1)S(1)}, u32[]{:S(2)}, u32[]{:S(2)}) collective-permute-start(bf16[192,768]{1,0:T(8,128)(2,1)S(1)} %add_convert_fusion), channel_id=1, source_target_pairs={{0,1},{1,2},{2,3},{3,4},{4,5},{5,6},{6,7},{7,8},{8,9},{9,10},{10,1... | collective-permute-start | bytes 884744 | tf_op jit(solution)/shard_map/ppermute | solution.py:25
  63.6 19.8 %collective-permute-start.5 = (bf16[192,768]{1,0:T(8,128)(2,1)S(1)}, bf16[192,768]{1,0:T(8,128)(2,1)S(1)}, u32[]{:S(2)}, u32[]{:S(2)}) collective-permute-start(bf16[192,768]{1,0:T(8,128)(2,1)S(1)} %add_convert_fusion.1), channel_id=1, source_target_pairs={{0,15},{1,0},{2,1},{3,2},{4,3},{5,4},{6,5},{7,6},{8,7},{9,8},{10,9... | collective-permute-start | bytes 884744 | tf_op jit(solution)/shard_map/ppermute | solution.py:25
  66.8 21.4 %collective-permute-start.8 = (bf16[64,768]{1,0:T(8,128)(2,1)S(1)}, bf16[64,768]{1,0:T(8,128)(2,1)S(1)}, u32[]{:S(2)}, u32[]{:S(2)}) collective-permute-start(bf16[64,768]{1,0:T(8,128)(2,1)S(1)} %copy-done.25), channel_id=1, source_target_pairs={{0,3},{1,4},{2,5},{3,6},{4,7},{5,8},{6,9},{7,10},{8,11},{9,12},{10... | collective-permute-start | bytes 294920 | tf_op jit(solution)/shard_map/ppermute | solution.py:25
  83.5 42.9 %copy-start.24 = (bf16[1,512,256]{2,1,0:T(8,128)(2,1)S(1)}, bf16[1,512,256]{2,1,0:T(8,128)(2,1)}, u32[]{:S(2)}) copy-start(bf16[1,512,256]{2,1,0:T(8,128)(2,1)} %param.28) | copy-start | bytes 786436
  88.3 19.5 %collective-permute-start.9 = (bf16[64,768]{1,0:T(8,128)(2,1)S(1)}, bf16[64,768]{1,0:T(8,128)(2,1)S(1)}, u32[]{:S(2)}, u32[]{:S(2)}) collective-permute-start(bf16[64,768]{1,0:T(8,128)(2,1)S(1)} %fusion.20), channel_id=1, source_target_pairs={{0,5},{1,6},{2,7},{3,8},{4,9},{5,10},{6,11},{7,12},{8,13},{9,14},{... | collective-permute-start | bytes 294920 | tf_op jit(solution)/shard_map/ppermute | solution.py:25
  95.8 14.9 %collective-permute-start.7 = (bf16[64,768]{1,0:T(8,128)(2,1)S(1)}, bf16[64,768]{1,0:T(8,128)(2,1)S(1)}, u32[]{:S(2)}, u32[]{:S(2)}) collective-permute-start(bf16[64,768]{1,0:T(8,128)(2,1)S(1)} %slice.104), channel_id=1, source_target_pairs={{0,11},{1,12},{2,13},{3,14},{4,15},{5,0},{6,1},{7,2},{8,3},{9,4},{... | collective-permute-start | bytes 294920 | tf_op jit(solution)/shard_map/ppermute | solution.py:25
  115.9 35.8 %copy-start.1 = (bf16[1,256,256]{2,1,0:T(8,128)(2,1)S(1)}, bf16[1,256,256]{2,1,0:T(8,128)(2,1)}, u32[]{:S(2)}) copy-start(bf16[1,256,256]{2,1,0:T(8,128)(2,1)} %param.20) | copy-start | bytes 393220
  115.9 35.8 %copy-start.2 = (bf16[1,256,512]{2,1,0:T(8,128)(2,1)S(1)}, bf16[1,256,512]{2,1,0:T(8,128)(2,1)}, u32[]{:S(2)}) copy-start(bf16[1,256,512]{2,1,0:T(8,128)(2,1)} %param.19) | copy-start | bytes 786436
  115.9 35.8 %copy-start.3 = (bf16[1,256,512]{2,1,0:T(8,128)(2,1)S(1)}, bf16[1,256,512]{2,1,0:T(8,128)(2,1)}, u32[]{:S(2)}) copy-start(bf16[1,256,512]{2,1,0:T(8,128)(2,1)} %param.27) | copy-start | bytes 786436
  115.9 35.8 %copy-start.5 = (bf16[3,768]{1,0:T(4,128)(2,1)S(1)}, bf16[3,768]{1,0:T(4,128)(2,1)}, u32[]{:S(2)}) copy-start(bf16[3,768]{1,0:T(4,128)(2,1)} %copy-done.4) | copy-start | bytes 13828
  115.9 35.8 %copy-start.6 = (f32[4,256]{1,0:T(4,128)S(1)}, f32[4,256]{1,0:T(4,128)}, u32[]{:S(2)}) copy-start(f32[4,256]{1,0:T(4,128)} %tapsbc_ref.5) | copy-start | bytes 12292
  115.9 35.8 %copy-start.7 = (f32[1,8,256]{2,1,0:T(8,128)S(1)}, f32[1,8,256]{2,1,0:T(8,128)}, u32[]{:S(2)}) copy-start(f32[1,8,256]{2,1,0:T(8,128)} %param.21) | copy-start | bytes 24580
  115.9 35.8 %copy-start.8 = (f32[4,512]{1,0:T(4,128)S(1)}, f32[4,512]{1,0:T(4,128)}, u32[]{:S(2)}) copy-start(f32[4,512]{1,0:T(4,128)} %tapsx_ref.3) | copy-start | bytes 24580
  115.9 35.8 %copy-start.9 = (f32[3,8]{1,0:T(4,128)S(1)}, f32[3,8]{1,0:T(4,128)}, u32[]{:S(2)}) copy-start(f32[3,8]{1,0:T(4,128)} %pad_maximum_fusion.1.gains_ref) | copy-start | bytes 292
  115.9 23.5 %all-to-all-start.2 = ((bf16[16,64,128]{2,1,0:T(8,128)(2,1)}), bf16[16,64,128]{2,1,0:T(8,128)(2,1)S(1)}, u32[]{:S(2)}, u32[]{:S(2)}) async-start(bf16[16,64,128]{2,1,0:T(8,128)(2,1)} %shard_map.268), calls=%async_computation.2 | async-start | bytes 524288 | tf_op jit(solution)/shard_map/all_to_all | solution.py:20
  139.5 21.7 %all-to-all-start.3 = ((bf16[8,128,256]{2,1,0:T(8,128)(2,1)}), bf16[8,128,256]{2,1,0:T(8,128)(2,1)S(1)}, u32[]{:S(2)}, u32[]{:S(2)}) async-start(bf16[8,128,256]{2,1,0:T(8,128)(2,1)} %bitcast.20), calls=%async_computation.3 | async-start | bytes 1048576 | tf_op jit(solution)/shard_map/all_to_all | solution.py:20
  161.2 50.7 %copy-start.13 = (bf16[8,128,256]{2,1,0:T(8,128)(2,1)}, bf16[8,128,256]{2,1,0:T(8,128)(2,1)S(1)}, u32[]{:S(2)}) copy-start(bf16[8,128,256]{2,1,0:T(8,128)(2,1)S(1)} %all-to-all-done.3.in_ref) | copy-start | bytes 1572868
  161.2 19.4 %all-to-all-start.4 = ((bf16[8,256,256]{2,1,0:T(8,128)(2,1)}), bf16[8,256,256]{2,1,0:T(8,128)(2,1)S(1)}, u32[]{:S(2)}, u32[]{:S(2)}) async-start(bf16[8,256,256]{2,1,0:T(8,128)(2,1)} %get-tuple-element.49), calls=%async_computation.4 | async-start | bytes 2097152 | tf_op jit(solution)/shard_map/all_to_all | solution.py:20
  194.4 16.9 %all-to-all-start.6 = ((f32[16,8,128]{2,1,0:T(8,128)}), f32[16,8,128]{2,1,0:T(8,128)S(1)}, u32[]{:S(2)}, u32[]{:S(2)}) async-start(f32[16,8,128]{2,1,0:T(8,128)} %broadcast_in_dim.82), calls=%async_computation.6 | async-start | bytes 131072 | tf_op jit(solution)/shard_map/all_to_all | solution.py:20
  199.6 25.9 %collective-permute-start.3 = (f32[3,512]{1,0:T(4,128)S(1)}, f32[3,512]{1,0:T(4,128)S(1)}, u32[]{:S(2)}, u32[]{:S(2)}) collective-permute-start(f32[3,512]{1,0:T(4,128)S(1)} %slice.61), channel_id=1, source_target_pairs={{1,0},{2,1},{3,2},{4,3},{5,4},{6,5},{7,6},{8,7},{9,8},{10,9},{11,1... | collective-permute-start | bytes 18440 | tf_op jit(solution)/shard_map/ppermute | solution.py:16
  201.6 33.1 %collective-permute-start.4 = (f32[3,256]{1,0:T(4,128)S(1)}, f32[3,256]{1,0:T(4,128)S(1)}, u32[]{:S(2)}, u32[]{:S(2)}) collective-permute-start(f32[3,256]{1,0:T(4,128)S(1)} %slice.62), channel_id=1, source_target_pairs={{1,0},{2,1},{3,2},{4,3},{5,4},{6,5},{7,6},{8,7},{9,8},{10,9},{11,1... | collective-permute-start | bytes 9224 | tf_op jit(solution)/shard_map/ppermute | solution.py:16
  218.3 30.9 %all-to-all-start.7 = ((bf16[8,144,256]{2,1,0:T(8,128)(2,1)}), bf16[8,144,256]{2,1,0:T(8,128)(2,1)S(1)}, u32[]{:S(2)}, u32[]{:S(2)}) async-start(bf16[8,144,256]{2,1,0:T(8,128)(2,1)} %get-tuple-element.59), calls=%async_computation.7 | async-start | bytes 1179648 | tf_op jit(solution)/shard_map/all_to_all | solution.py:20
  226.1 12.3 %collective-permute-start.10 = (bf16[576,256]{1,0:T(8,128)(2,1)}, bf16[576,256]{1,0:T(8,128)(2,1)S(1)}, u32[]{:S(2)}, u32[]{:S(2)}) collective-permute-start(bf16[576,256]{1,0:T(8,128)(2,1)} %get-tuple-element.61), channel_id=1, source_target_pairs={{0,128},{128,256},{256,384},{384,0},{1,129},{129,257},{257,385},{3... | collective-permute-start | bytes 884744 | tf_op jit(solution)/shard_map/ppermute | solution.py:578
  228.2 15.5 %collective-permute-start.11 = (bf16[576,256]{1,0:T(8,128)(2,1)}, bf16[576,256]{1,0:T(8,128)(2,1)S(1)}, u32[]{:S(2)}, u32[]{:S(2)}) collective-permute-start(bf16[576,256]{1,0:T(8,128)(2,1)} %get-tuple-element.62), channel_id=1, source_target_pairs={{0,256},{128,384},{256,0},{384,128},{1,257},{129,385},{257,1},{385... | collective-permute-start | bytes 884744 | tf_op jit(solution)/shard_map/ppermute | solution.py:578
  232.0 14.4 %collective-permute-start.12 = (bf16[576,256]{1,0:T(8,128)(2,1)}, bf16[576,256]{1,0:T(8,128)(2,1)S(1)}, u32[]{:S(2)}, u32[]{:S(2)}) collective-permute-start(bf16[576,256]{1,0:T(8,128)(2,1)} %get-tuple-element.63), channel_id=1, source_target_pairs={{0,384},{128,0},{256,128},{384,256},{1,385},{129,1},{257,129},{385... | collective-permute-start | bytes 884744 | tf_op jit(solution)/shard_map/ppermute | solution.py:578
  (15 other events, 139.8 us)
Sparse Core Ops, SparseCore 0:
  114.3 80.8 all-gather.1

commit v7 on v6

--- a/solution.py
+++ b/solution.py
@@ -18,11 +18,6 @@
 
 def exchange(value, axis):
     return lax.all_to_all(value, axis, split_axis=0, concat_axis=0, tiled=True)
-
-
-def shift(value, distance):
-    count = lax.axis_size("ctx")
-    return lax.ppermute(value, "ctx", [(i, (i + distance) % count) for i in range(count)])
 
 
 def after(value, *earlier):
@@ -265,48 +260,14 @@
         taps_out_ref[k : k + 1, :] = value
 
 
-FAR = 5
-CENTRE = (-FAR, 0, FAR)
-OPPOSITE = 8
-
-
-def shifted_by(distance):
-    return tuple(distance + step for step in CENTRE)
-
-
-def rows_of(cot_ref, block, rows):
-    per_group = (cot_ref.shape[1] - 16) // rows
-    start = pl.multiple_of((block % per_group) * rows, rows)
-    return cot_ref[block // per_group, pl.ds(start, rows), :]
-
-
-def unscaled_kernel(place_ref, cot_ref, down_ref, earlier_ref, *refs):
-    del earlier_ref
-    out_refs, rows_ref = refs[:-1], refs[-1]
-    places = rows_ref.shape[0] // out_refs[-1].shape[0]
-    rows = out_refs[-1].shape[0]
-    place = place_ref[0]
-    at = 0
-    for distances in (shifted_by(-2), shifted_by(2), shifted_by(-1), shifted_by(1), CENTRE, (OPPOSITE,)):
-        for distance in distances:
-            block = lax.rem(place + distance + places, places)
-            rows_ref[at : at + rows, :] = rows_of(cot_ref, block, rows)
-            at += rows
-    product = dot(rows_ref[...], down_ref[...], 1, 1).astype(BF16)
-    at = 0
-    for out_ref in out_refs:
-        out_ref[...] = product[at : at + out_ref.shape[0]]
-        at += out_ref.shape[0]
-
-
 def scaled_rows(cot_ref, group):
     slots = cot_ref.shape[1] - 16
     weight = cot_ref[group, slots:, :slots].astype(F32).T[:, 0:1]
     return (cot_ref[group, :slots, :].astype(F32) * weight).astype(BF16)
 
 
-def own_rows_kernel(mine_ref, weight_ref, gate_ref, up_ref, earlier_ref, out_ref):
-    del earlier_ref
+def own_rows_kernel(mine_ref, weight_ref, gate_ref, up_ref, first_ref, second_ref, out_ref):
+    del first_ref, second_ref
     width = mine_ref.shape[1]
     unscaled = mine_ref[...].astype(F32)
     gate = gate_ref[...].astype(F32)
@@ -480,30 +441,11 @@
         [pad_heads, pad_shared],
         inputs=8,
     )(head_rows, shared_rows, before, raw_step, gains, conv_x, conv_bc, cot_rows)
-    three, one = (3 * own, hidden_width), (own, hidden_width)
-    left2, right2, left1, right1, centre, opposite = whole(
-        unscaled_kernel,
-        [(three, BF16)] * 5 + [(one, BF16)],
-        [((ctx_places * own, col_width), BF16)],
-        inputs=2,
-        scalars=1,
-        late=1,
-    )(place, got_cot, w_down[0], states)
-    opposite = shift(opposite, 3)
-    left1 = (left1.astype(F32) + shift(left2, -1).astype(F32)).astype(BF16)
-    right1 = (right1.astype(F32) + shift(right2, 1).astype(F32)).astype(BF16)
-    got_states = exchange(after(states, left1, right1), "ctx")
-    centre = centre.astype(F32) + shift(left1, -1).astype(F32) + shift(right1, 1).astype(F32)
-    far_left = shift(centre[:own].astype(BF16), -FAR)
-    far_right = shift((centre[2 * own :] + opposite.astype(F32)).astype(BF16), FAR)
-    mine = centre[own : 2 * own] + far_left.astype(F32) + far_right.astype(F32)
-    rows_weight = got_cot[:, slot_width, :slot_width].reshape(-1).astype(F32)
-    weight_own = lax.dynamic_slice_in_dim(rows_weight, place[0] * own, own, 0)
-    (own_rows,) = whole(
-        own_rows_kernel, [((own, 3 * hidden_width + 128), BF16)], inputs=4, late=1
-    )(mine, weight_own[:, None], gate_act[0, 0], up_act[0, 0], got_states)
-    everything = lax.all_gather(own_rows, "ctx", axis=0, tiled=True)
-
+    unscaled = jnp.dot(
+        after(got_cot, states)[:, :slot_width].reshape(-1, col_width), w_down[0].T, preferred_element_type=F32
+    ).astype(BF16)
+    mine = lax.psum_scatter(unscaled, "ctx", scatter_dimension=0, tiled=True)
+    got_states = exchange(after(states, unscaled), "ctx")
     (entered,) = whole(
         scan_kernel, [((ctx_places, 2 * part, state_width), BF16)], inputs=1
     )(got_states)
@@ -530,6 +472,12 @@
         head_rows, shared_rows, before, raw_step, gains, conv_x, conv_bc, cot_rows,
         entered,
     )
+    rows_weight = got_cot[:, slot_width, :slot_width].reshape(-1).astype(F32)
+    weight_own = lax.dynamic_slice_in_dim(rows_weight, place[0] * own, own, 0)
+    (own_rows,) = whole(
+        own_rows_kernel, [((own, 3 * hidden_width + 128), BF16)], inputs=4, late=2
+    )(mine, weight_own[:, None], gate_act[0, 0], up_act[0, 0], grad_step, rows_in)
+    everything = lax.all_gather(own_rows, "ctx", axis=0, tiled=True)
     grad_bc = after(grad_bc, rows_in)
     after_heads = passed_along(rim_heads[:rim_rows], "ctx", -1)
     grad_mamba_in = with_last_rows(main_heads, tail_heads, after_heads)

time: 260 us -> 248 us (0.954)
  blocking collectives: 8.52 us -> 34.3 us
  starting transfers between devices: 102 us -> 82.3 us
  waiting for transfers between devices: 82.1 us -> 68.6 us
  other arithmetic: 9.85 us -> 6.23 us
  Pallas kernels: 28.6 us -> 25.8 us
  matrix products: 3.19 us -> 5.91 us
    ppermute x7 -> x0, starting transfers between devices: 32.8 us -> none  [shift(): lax.ppermute(value, 'ctx', [(i, (i + distance) % count) for i in range(co...]
    ppermute x7 -> x0, waiting for transfers between devices: 32.5 us -> none  [shift(): lax.ppermute(value, 'ctx', [(i, (i + distance) % count) for i in range(co...]
    all_to_all x1 -> x2, blocking collectives: 8.52 us -> 34.3 us  [exchange(): return lax.all_to_all(value, axis, split_axis=0, concat_axis=0, tiled=True)]
    all_gather x1, waiting for transfers between devices: 0.01 us -> 20 us  [body(): everything = lax.all_gather(own_rows, 'ctx', axis=0, tiled=True)]
    all_to_all x7 -> x6, starting transfers between devices: 56.9 us -> 67.2 us  [exchange(): return lax.all_to_all(value, axis, split_axis=0, concat_axis=0, tiled=True)]
    pallas_call x1 -> x0, Pallas kernels: 2.74 us -> none  [body(): whole(unscaled_kernel, [(three, BF16)] * 5 + [(one, BF16)], [((ctx_places...]
    all_to_all x7 -> x6, waiting for transfers between devices: 39.9 us -> 41.4 us  [exchange(): return lax.all_to_all(value, axis, split_axis=0, concat_axis=0, tiled=True)]
  transfers between devices with their start and end apart: 21 -> 14, of which waited for: 15 -> 9; matrix products, arithmetic and copies ran while one was open for 5% -> 4% of each run, Pallas kernels for 9% -> 10%
where the time goes in v7:
time: 248 us; the launch traced here: 246 us
  starting transfers between devices  82.3 us (33%)
  waiting for transfers between devices  68.6 us (28%)
  blocking collectives  34.3 us (14%)
  Pallas kernels  25.8 us (10%)
  between operations  14.4 us (6%)
  local copies, waits for them, and re-layouts  8.5 us (3%)
  other arithmetic  6.23 us (3%)
  matrix products  5.91 us (2%)
    all_to_all x6, starting transfers between devices, exchange(): return lax.all_to_all(value, axis, split_axis=0, concat_axis=0, tiled=True)  67.2 us
    all_to_all x6, waiting for transfers between devices, exchange(): return lax.all_to_all(value, axis, split_axis=0, concat_axis=0, tiled=True)  41.4 us
    all_to_all x2, blocking collectives, exchange(): return lax.all_to_all(value, axis, split_axis=0, concat_axis=0, tiled=True)  34.3 us
    all_gather x1, waiting for transfers between devices, body(): everything = lax.all_gather(own_rows, 'ctx', axis=0, tiled=True)  20 us
    ppermute x3, starting transfers between devices, body(): lax.ppermute(parts[k], 'dp', [(i, (i + k) % dp_count) for i in range(dp_c...  11.1 us
    ppermute x3, waiting for transfers between devices, body(): lax.ppermute(parts[k], 'dp', [(i, (i + k) % dp_count) for i in range(dp_c...  7.05 us
    pallas_call x1, Pallas kernels, body(): whole(back_kernel, [((length, split_at), BF16), ((16, split_at), F32), ((...  6.91 us
    pallas_call x1, Pallas kernels, body(): whole(rows_kernel, [((expert_count, slot_width + 16, col_width), BF16)] +...  6.41 us
  transfers between devices with their start and end apart: 14, of which 9 were waited for; matrix products, arithmetic and copies ran while one was open for 4% of the time, Pallas kernels for 10%

profile of v7, /device:TPU:1, one launch (start us, length us, event | category | flops | bytes accessed | tf_op | source)
XLA Modules:
  0.0 246.0 jit_solution(15310970020776722882)
XLA Ops:
  8.8 1.4 fusion.3
  11.1 10.3 %all-to-all-start = ((bf16[8,144,256]{2,1,0:T(8,128)(2,1)}), bf16[8,144,256]{2,1,0:T(8,128)(2,1)S(1)}, u32[]{:S(2)}, u32[]{:S(2)}) async-start(bf16[8,144,256]{2,1,0:T(8,128)(2,1)} %fusion.17), calls=%async_computation | async-start | bytes 1179648 | tf_op jit(solution)/shard_map/all_to_all | solution.py:20
  25.5 3.9 %shard_map.266 = bf16[16,80,128]{2,1,0:T(8,128)(2,1)} custom-call(bf16[256,512]{1,0:T(8,128)(2,1)} %bitcast.79, bf16[256,256]{1,0:T(8,128)(2,1)} %bitcast.76, bf16[3,768]{1,0:T(4,128)(2,1)} %copy-done.4, f32[8,256]{1,0:T(8,128)} %bitcast.83, f32[3,8]{1,0:T(4,128)} %pad_maximum_fusion.1.gains_ref, f32[4,512]{1,0:T(4,128)} %tapsx_ref.3, f32[4,256]{1,0:T(4,128)} %tapsbc_ref.5, ...), custom_call_target="tpu_custom_call" | custom-call | tf_op jit(solution)/shard_map/pallas_call | solution.py:438
  29.4 2.3 all-to-all-done.cot_ref
  31.7 1.8 convolution_convert_fusion
  33.5 26.6 %all_to_all.40.got_ref = bf16[16,80,128]{2,1,0:T(8,128)(2,1)} all-to-all(bf16[16,80,128]{2,1,0:T(8,128)(2,1)S(1)} %copy-done.13), channel_id=1, replica_groups=mesh['dp'=4,'expert'=8,'ctx'=16] {'ctx'}, dimensions={0} | all-to-all | bytes 655360 | tf_op jit(solution)/shard_map/all_to_all | solution.py:20
  60.1 1.8 shard_map.267
  61.9 14.0 %all-to-all-start.2 = ((bf16[16,64,128]{2,1,0:T(8,128)(2,1)}), bf16[16,64,128]{2,1,0:T(8,128)(2,1)S(1)}, u32[]{:S(2)}, u32[]{:S(2)}) async-start(bf16[16,64,128]{2,1,0:T(8,128)(2,1)} %shard_map.267), calls=%async_computation.2 | async-start | bytes 524288 | tf_op jit(solution)/shard_map/all_to_all | solution.py:20
  76.0 1.3 fusion.4
  77.3 14.0 %all-to-all-done.2.got_ref = bf16[16,64,128]{2,1,0:T(8,128)(2,1)S(1)} async-done(((bf16[16,64,128]{2,1,0:T(8,128)(2,1)}), bf16[16,64,128]{2,1,0:T(8,128)(2,1)S(1)}, u32[]{:S(2)}, u32[]{:S(2)}) %all-to-all-start.2) | async-done | bytes 262176 | tf_op jit(solution)/shard_map/all_to_all | solution.py:20
  91.3 10.7 %all-to-all-start.3 = ((bf16[8,128,256]{2,1,0:T(8,128)(2,1)}), bf16[8,128,256]{2,1,0:T(8,128)(2,1)S(1)}, u32[]{:S(2)}, u32[]{:S(2)}) async-start(bf16[8,128,256]{2,1,0:T(8,128)(2,1)} %bitcast.20), calls=%async_computation.3 | async-start | bytes 1048576 | tf_op jit(solution)/shard_map/all_to_all | solution.py:20
  102.9 6.9 %shard_map.268 = (bf16[256,512]{1,0:T(8,128)(2,1)}, f32[16,512]{1,0:T(8,128)S(1)}, f32[8,512]{1,0:T(8,128)S(1)}, bf16[8,256,256]{2,1,0:T(8,128)(2,1)}, f32[8,256...) custom-call(bf16[256,512]{1,0:T(8,128)(2,1)S(1)} %bitcast.80, bf16[256,256]{1,0:T(8,128)(2,1)S(1)} %bitcast.78, ...), custom_call_target="tpu_custom_call" | custom-call | tf_op jit(solution)/shard_map/pallas_call | solution.py:457
  109.8 1.7 all-to-all-done.3.second_ref.in_ref
  112.4 1.9 shard_map.270
  114.3 10.5 %all-to-all-start.4 = ((bf16[8,256,256]{2,1,0:T(8,128)(2,1)}), bf16[8,256,256]{2,1,0:T(8,128)(2,1)S(1)}, u32[]{:S(2)}, u32[]{:S(2)}) async-start(bf16[8,256,256]{2,1,0:T(8,128)(2,1)} %get-tuple-element.41), calls=%async_computation.4 | async-start | bytes 2097152 | tf_op jit(solution)/shard_map/all_to_all | solution.py:20
  124.8 15.1 %all-to-all-done.4.got_ref = bf16[8,256,256]{2,1,0:T(8,128)(2,1)S(1)} async-done(((bf16[8,256,256]{2,1,0:T(8,128)(2,1)}), bf16[8,256,256]{2,1,0:T(8,128)(2,1)S(1)}, u32[]{:S(2)}, u32[]{:S(2)}) %all-to-all-start.4) | async-done | bytes 1048608 | tf_op jit(solution)/shard_map/all_to_all | solution.py:20
  140.9 2.9 %shard_map.269 = (bf16[256,256]{1,0:T(8,128)(2,1)}, f32[16,256]{1,0:T(8,128)}, f32[8,256]{1,0:T(8,128)}, f32[4,256]{1,0:T(4,128)}) custom-call(bf16[256,256]{1,0:T(8,128)(2,1)} %bitcast.77, bf16[3,768]{1,0:T(4,128)(2,1)} %copy-done.4, f32[4,256]{1,0:T(4,128)} %tapsbc_ref.5, bf16[8,256,256]{2,1,0:T(8,128)(2,1)} %copy-done.12), custom_call_target="tpu_custom_call" | custom-call | tf_op jit(solution)/shard_map/pallas_call | solution.py:484
  144.5 7.7 %all_to_all.41 = f32[4,8,128]{2,1,0:T(8,128)S(1)} all-to-all(f32[4,8,128]{2,1,0:T(8,128)S(1)} %bitcast.93), channel_id=1, replica_groups=mesh['dp'=4,'expert'=8,'ctx'=16] {'dp'}, dimensions={0} | all-to-all | bytes 32768 | tf_op jit(solution)/shard_map/all_to_all | solution.py:20
  152.7 9.9 %all-to-all-start.6 = ((f32[16,8,128]{2,1,0:T(8,128)}), f32[16,8,128]{2,1,0:T(8,128)S(1)}, u32[]{:S(2)}, u32[]{:S(2)}) async-start(f32[16,8,128]{2,1,0:T(8,128)} %broadcast_in_dim.82), calls=%async_computation.6 | async-start | bytes 131072 | tf_op jit(solution)/shard_map/all_to_all | solution.py:20
  162.7 1.3 collective-permute-start.1
  164.7 1.5 collective-permute-start.2
  166.1 8.3 %all-to-all-done.6 = f32[16,8,128]{2,1,0:T(8,128)S(1)} async-done(((f32[16,8,128]{2,1,0:T(8,128)}), f32[16,8,128]{2,1,0:T(8,128)S(1)}, u32[]{:S(2)}, u32[]{:S(2)}) %all-to-all-start.6) | async-done | bytes 65568 | tf_op jit(solution)/shard_map/all_to_all | solution.py:20
  175.0 20.0 %all-gather.2.cloned.1.call-done.all_ref = bf16[1024,2432]{1,0:T(8,128)(2,1)} async-done(((bf16[64,2432]{1,0:T(8,128)(2,1)}), bf16[1024,2432]{1,0:T(8,128)(2,1)}) %all-gather.2.cloned.1.call-update) | async-done | bytes 4980752 | tf_op jit(solution)/shard_map/all_gather | solution.py:480
  195.0 6.4 %shard_map.271 = (bf16[8,144,256]{2,1,0:T(8,128)(2,1)}, bf16[576,256]{1,0:T(8,128)(2,1)}, bf16[576,256]{1,0:T(8,128)(2,1)}, bf16[576,256]{1,0:T(8,128)(2,1)}, bf16[576,256]{1,0:T(8,128)(2,1)}) custom-call(s32[1]{0:T(128)} %bitcast.27.place_ref, bf16[1024,2432]{1,0:T(8,128)(2,1)} %all-gather.2.cloned.1.call-done.all_ref, bf16[8,128,256]{2,1,0:T(8,128)(2,1)} %copy-done.11, ...), custom_call_target="tpu_custom_call" | custom-call | tf_op jit(solution)/shard_map/pallas_call | solution.py:515
  201.4 11.8 %all-to-all-start.7 = ((bf16[8,144,256]{2,1,0:T(8,128)(2,1)}), bf16[8,144,256]{2,1,0:T(8,128)(2,1)S(1)}, u32[]{:S(2)}, u32[]{:S(2)}) async-start(bf16[8,144,256]{2,1,0:T(8,128)(2,1)} %get-tuple-element.49), calls=%async_computation.8 | async-start | bytes 1179648 | tf_op jit(solution)/shard_map/all_to_all | solution.py:20
  213.8 3.0 %collective-permute-start.3 = (bf16[576,256]{1,0:T(8,128)(2,1)}, bf16[576,256]{1,0:T(8,128)(2,1)S(1)}, u32[]{:S(2)}, u32[]{:S(2)}) collective-permute-start(bf16[576,256]{1,0:T(8,128)(2,1)} %get-tuple-element.51), channel_id=1, source_target_pairs={{0,128},{128,256},{256,384},{384,0},{1,129},{129,257},{257,385},{3... | collective-permute-start | bytes 884744 | tf_op jit(solution)/shard_map/ppermute | solution.py:526
  216.9 4.3 %collective-permute-start.4 = (bf16[576,256]{1,0:T(8,128)(2,1)}, bf16[576,256]{1,0:T(8,128)(2,1)S(1)}, u32[]{:S(2)}, u32[]{:S(2)}) collective-permute-start(bf16[576,256]{1,0:T(8,128)(2,1)} %get-tuple-element.52), channel_id=1, source_target_pairs={{0,256},{128,384},{256,0},{384,128},{1,257},{129,385},{257,1},{385... | collective-permute-start | bytes 884744 | tf_op jit(solution)/shard_map/ppermute | solution.py:526
  221.1 3.8 %collective-permute-start.5 = (bf16[576,256]{1,0:T(8,128)(2,1)}, bf16[576,256]{1,0:T(8,128)(2,1)S(1)}, u32[]{:S(2)}, u32[]{:S(2)}) collective-permute-start(bf16[576,256]{1,0:T(8,128)(2,1)} %get-tuple-element.53), channel_id=1, source_target_pairs={{0,384},{128,0},{256,128},{384,256},{1,385},{129,1},{257,129},{385... | collective-permute-start | bytes 884744 | tf_op jit(solution)/shard_map/ppermute | solution.py:526
  227.2 5.7 %collective-permute-done.4.refs_2_ = bf16[576,256]{1,0:T(8,128)(2,1)S(1)} collective-permute-done((bf16[576,256]{1,0:T(8,128)(2,1)}, bf16[576,256]{1,0:T(8,128)(2,1)S(1)}, u32[]{:S(2)}, u32[]{:S(2)}) %collective-permute-start.4) | collective-permute-done | bytes 294944 | tf_op jit(solution)/shard_map/ppermute | solution.py:526
  232.9 1.3 collective-permute-done.5.refs_3_
  235.0 2.0 shard_map.272
  237.0 1.4 fusion.7
  (89 shorter events, 16.2 us)
Async XLA Ops:
  7.2 24.5 %copy-start = (bf16[1,768,256]{2,1,0:T(8,128)(2,1)S(1)}, bf16[1,768,256]{2,1,0:T(8,128)(2,1)}, u32[]{:S(2)}) copy-start(bf16[1,768,256]{2,1,0:T(8,128)(2,1)} %param.35) | copy-start | bytes 1179652
  8.8 15.4 %copy-start.20 = (f32[8]{0:T(128)S(1)}, f32[8]{0:T(128)}, u32[]{:S(2)}) copy-start(f32[8]{0:T(128)} %param.24) | copy-start | bytes 100
  8.8 15.4 %copy-start.21 = (f32[8]{0:T(128)S(1)}, f32[8]{0:T(128)}, u32[]{:S(2)}) copy-start(f32[8]{0:T(128)} %param.23) | copy-start | bytes 100
  8.8 15.4 %copy-start.22 = (f32[8]{0:T(128)S(1)}, f32[8]{0:T(128)}, u32[]{:S(2)}) copy-start(f32[8]{0:T(128)} %param.22) | copy-start | bytes 100
  11.1 20.5 %all-to-all-start = ((bf16[8,144,256]{2,1,0:T(8,128)(2,1)}), bf16[8,144,256]{2,1,0:T(8,128)(2,1)S(1)}, u32[]{:S(2)}, u32[]{:S(2)}) async-start(bf16[8,144,256]{2,1,0:T(8,128)(2,1)} %fusion.17), calls=%async_computation | async-start | bytes 1179648 | tf_op jit(solution)/shard_map/all_to_all | solution.py:20
  21.4 90.1 %reduce-scatter.2.cloned.1.call-start = ((), (), s32[]{:S(2)}) async-start(), calls=%async_computation.9 | async-start | bytes 1671168 | tf_op jit(solution)/shard_map/reduce_scatter | solution.py:447
  22.8 2.1 collective-permute-start
  31.6 70.4 %copy-start.10 = (bf16[8,144,256]{2,1,0:T(8,128)(2,1)}, bf16[8,144,256]{2,1,0:T(8,128)(2,1)S(1)}, u32[]{:S(2)}) copy-start(bf16[8,144,256]{2,1,0:T(8,128)(2,1)S(1)} %all-to-all-done.cot_ref) | copy-start | bytes 1769476
  31.7 1.8 copy-start.13
  33.5 42.5 %copy-start.23 = (bf16[1,512,256]{2,1,0:T(8,128)(2,1)S(1)}, bf16[1,512,256]{2,1,0:T(8,128)(2,1)}, u32[]{:S(2)}) copy-start(bf16[1,512,256]{2,1,0:T(8,128)(2,1)} %param.28) | copy-start | bytes 786436
  61.8 41.0 %copy-start.1 = (bf16[1,256,256]{2,1,0:T(8,128)(2,1)S(1)}, bf16[1,256,256]{2,1,0:T(8,128)(2,1)}, u32[]{:S(2)}) copy-start(bf16[1,256,256]{2,1,0:T(8,128)(2,1)} %param.20) | copy-start | bytes 393220
  61.9 41.0 %copy-start.2 = (bf16[1,256,512]{2,1,0:T(8,128)(2,1)S(1)}, bf16[1,256,512]{2,1,0:T(8,128)(2,1)}, u32[]{:S(2)}) copy-start(bf16[1,256,512]{2,1,0:T(8,128)(2,1)} %param.19) | copy-start | bytes 786436
  61.9 41.0 %copy-start.3 = (bf16[1,256,512]{2,1,0:T(8,128)(2,1)S(1)}, bf16[1,256,512]{2,1,0:T(8,128)(2,1)}, u32[]{:S(2)}) copy-start(bf16[1,256,512]{2,1,0:T(8,128)(2,1)} %param.27) | copy-start | bytes 786436
  61.9 41.0 %copy-start.5 = (bf16[3,768]{1,0:T(4,128)(2,1)S(1)}, bf16[3,768]{1,0:T(4,128)(2,1)}, u32[]{:S(2)}) copy-start(bf16[3,768]{1,0:T(4,128)(2,1)} %copy-done.4) | copy-start | bytes 13828
  61.9 41.0 %copy-start.6 = (f32[4,256]{1,0:T(4,128)S(1)}, f32[4,256]{1,0:T(4,128)}, u32[]{:S(2)}) copy-start(f32[4,256]{1,0:T(4,128)} %tapsbc_ref.5) | copy-start | bytes 12292
  61.9 41.0 %copy-start.7 = (f32[1,8,256]{2,1,0:T(8,128)S(1)}, f32[1,8,256]{2,1,0:T(8,128)}, u32[]{:S(2)}) copy-start(f32[1,8,256]{2,1,0:T(8,128)} %param.21) | copy-start | bytes 24580
  61.9 41.0 %copy-start.8 = (f32[4,512]{1,0:T(4,128)S(1)}, f32[4,512]{1,0:T(4,128)}, u32[]{:S(2)}) copy-start(f32[4,512]{1,0:T(4,128)} %tapsx_ref.3) | copy-start | bytes 24580
  61.9 41.0 %copy-start.9 = (f32[3,8]{1,0:T(4,128)S(1)}, f32[3,8]{1,0:T(4,128)}, u32[]{:S(2)}) copy-start(f32[3,8]{1,0:T(4,128)} %pad_maximum_fusion.1.gains_ref) | copy-start | bytes 292
  61.9 29.4 %all-to-all-start.2 = ((bf16[16,64,128]{2,1,0:T(8,128)(2,1)}), bf16[16,64,128]{2,1,0:T(8,128)(2,1)S(1)}, u32[]{:S(2)}, u32[]{:S(2)}) async-start(bf16[16,64,128]{2,1,0:T(8,128)(2,1)} %shard_map.267), calls=%async_computation.2 | async-start | bytes 524288 | tf_op jit(solution)/shard_map/all_to_all | solution.py:20
  91.3 20.2 %all-to-all-start.3 = ((bf16[8,128,256]{2,1,0:T(8,128)(2,1)}), bf16[8,128,256]{2,1,0:T(8,128)(2,1)S(1)}, u32[]{:S(2)}, u32[]{:S(2)}) async-start(bf16[8,128,256]{2,1,0:T(8,128)(2,1)} %bitcast.20), calls=%async_computation.3 | async-start | bytes 1048576 | tf_op jit(solution)/shard_map/all_to_all | solution.py:20
  102.0 93.0 %all-gather.2.cloned.1.call-start = ((), (), s32[]{:S(2)}) async-start(), calls=%async_computation.10 | async-start | bytes 5292032 | tf_op jit(solution)/shard_map/all_gather | solution.py:480
  114.3 25.6 %all-to-all-start.4 = ((bf16[8,256,256]{2,1,0:T(8,128)(2,1)}), bf16[8,256,256]{2,1,0:T(8,128)(2,1)S(1)}, u32[]{:S(2)}, u32[]{:S(2)}) async-start(bf16[8,256,256]{2,1,0:T(8,128)(2,1)} %get-tuple-element.41), calls=%async_computation.4 | async-start | bytes 2097152 | tf_op jit(solution)/shard_map/all_to_all | solution.py:20
  152.7 21.6 %all-to-all-start.6 = ((f32[16,8,128]{2,1,0:T(8,128)}), f32[16,8,128]{2,1,0:T(8,128)S(1)}, u32[]{:S(2)}, u32[]{:S(2)}) async-start(f32[16,8,128]{2,1,0:T(8,128)} %broadcast_in_dim.82), calls=%async_computation.6 | async-start | bytes 131072 | tf_op jit(solution)/shard_map/all_to_all | solution.py:20
  162.7 50.5 %collective-permute-start.1 = (f32[3,512]{1,0:T(4,128)S(1)}, f32[3,512]{1,0:T(4,128)S(1)}, u32[]{:S(2)}, u32[]{:S(2)}) collective-permute-start(f32[3,512]{1,0:T(4,128)S(1)} %slice.55), channel_id=1, source_target_pairs={{1,0},{2,1},{3,2},{4,3},{5,4},{6,5},{7,6},{8,7},{9,8},{10,9},{11,1... | collective-permute-start | bytes 18440 | tf_op jit(solution)/shard_map/ppermute | solution.py:16
  164.7 60.2 %collective-permute-start.2 = (f32[3,256]{1,0:T(4,128)S(1)}, f32[3,256]{1,0:T(4,128)S(1)}, u32[]{:S(2)}, u32[]{:S(2)}) collective-permute-start(f32[3,256]{1,0:T(4,128)S(1)} %slice.56), channel_id=1, source_target_pairs={{1,0},{2,1},{3,2},{4,3},{5,4},{6,5},{7,6},{8,7},{9,8},{10,9},{11,1... | collective-permute-start | bytes 9224 | tf_op jit(solution)/shard_map/ppermute | solution.py:16
  195.0 29.9 %copy-start.18 = (f32[16,256]{1,0:T(8,128)S(1)}, f32[16,256]{1,0:T(8,128)}, u32[]{:S(2)}) copy-start(f32[16,256]{1,0:T(8,128)} %get-tuple-element.43) | copy-start | bytes 49156
  195.0 30.5 %copy-start.17 = (f32[8,128]{1,0:T(8,128)S(1)}, f32[8,128]{1,0:T(8,128)}, u32[]{:S(2)}) copy-start(f32[8,128]{1,0:T(8,128)} %reduce_sum.19) | copy-start | bytes 12292
  201.4 35.6 %all-to-all-start.7 = ((bf16[8,144,256]{2,1,0:T(8,128)(2,1)}), bf16[8,144,256]{2,1,0:T(8,128)(2,1)S(1)}, u32[]{:S(2)}, u32[]{:S(2)}) async-start(bf16[8,144,256]{2,1,0:T(8,128)(2,1)} %get-tuple-element.49), calls=%async_computation.8 | async-start | bytes 1179648 | tf_op jit(solution)/shard_map/all_to_all | solution.py:20
  213.8 13.4 %collective-permute-start.3 = (bf16[576,256]{1,0:T(8,128)(2,1)}, bf16[576,256]{1,0:T(8,128)(2,1)S(1)}, u32[]{:S(2)}, u32[]{:S(2)}) collective-permute-start(bf16[576,256]{1,0:T(8,128)(2,1)} %get-tuple-element.51), channel_id=1, source_target_pairs={{0,128},{128,256},{256,384},{384,0},{1,129},{129,257},{257,385},{3... | collective-permute-start | bytes 884744 | tf_op jit(solution)/shard_map/ppermute | solution.py:526
  216.9 16.0 %collective-permute-start.4 = (bf16[576,256]{1,0:T(8,128)(2,1)}, bf16[576,256]{1,0:T(8,128)(2,1)S(1)}, u32[]{:S(2)}, u32[]{:S(2)}) collective-permute-start(bf16[576,256]{1,0:T(8,128)(2,1)} %get-tuple-element.52), channel_id=1, source_target_pairs={{0,256},{128,384},{256,0},{384,128},{1,257},{129,385},{257,1},{385... | collective-permute-start | bytes 884744 | tf_op jit(solution)/shard_map/ppermute | solution.py:526
  221.1 13.1 %collective-permute-start.5 = (bf16[576,256]{1,0:T(8,128)(2,1)}, bf16[576,256]{1,0:T(8,128)(2,1)S(1)}, u32[]{:S(2)}, u32[]{:S(2)}) collective-permute-start(bf16[576,256]{1,0:T(8,128)(2,1)} %get-tuple-element.53), channel_id=1, source_target_pairs={{0,384},{128,0},{256,128},{384,256},{1,385},{129,1},{257,129},{385... | collective-permute-start | bytes 884744 | tf_op jit(solution)/shard_map/ppermute | solution.py:526
  227.2 7.1 %copy-start.14 = (bf16[576,256]{1,0:T(8,128)(2,1)}, bf16[576,256]{1,0:T(8,128)(2,1)S(1)}, u32[]{:S(2)}) copy-start(bf16[576,256]{1,0:T(8,128)(2,1)S(1)} %collective-permute-done.3.refs_1_) | copy-start | bytes 884740
  (6 other events, 6.0 us)
Sparse Core Ops, SparseCore 0:
  33.6 76.0 reduce-scatter.1
  114.4 80.5 all-gather.1

commit v8 on v6

--- a/solution.py
+++ b/solution.py
@@ -470,6 +470,7 @@
     send_cot = send_cot.reshape(expert_count, slot_width, col_width)
     got_cot = exchange(jnp.concatenate([send_cot, send_weight], axis=1), "expert")
     send_in = jnp.dot(table, moe_in[0], preferred_element_type=F32).astype(BF16)
+    rows_in = exchange(send_in.reshape(expert_count, slot_width, col_width), "expert")
 
     gains = jnp.stack([dt_bias, a_log, d_skip])
     pad_heads = ((8 + length, split_at), F32)
@@ -492,7 +493,6 @@
     opposite = shift(opposite, 3)
     left1 = (left1.astype(F32) + shift(left2, -1).astype(F32)).astype(BF16)
     right1 = (right1.astype(F32) + shift(right2, 1).astype(F32)).astype(BF16)
-    got_states = exchange(after(states, left1, right1), "ctx")
     centre = centre.astype(F32) + shift(left1, -1).astype(F32) + shift(right1, 1).astype(F32)
     far_left = shift(centre[:own].astype(BF16), -FAR)
     far_right = shift((centre[2 * own :] + opposite.astype(F32)).astype(BF16), FAR)
@@ -501,17 +501,15 @@
     weight_own = lax.dynamic_slice_in_dim(rows_weight, place[0] * own, own, 0)
     (own_rows,) = whole(
         own_rows_kernel, [((own, 3 * hidden_width + 128), BF16)], inputs=4, late=1
-    )(mine, weight_own[:, None], gate_act[0, 0], up_act[0, 0], got_states)
+    )(mine, weight_own[:, None], gate_act[0, 0], up_act[0, 0], rows_in)
     everything = lax.all_gather(own_rows, "ctx", axis=0, tiled=True)
 
+    got_states = exchange(after(states, own_rows), "ctx")
     (entered,) = whole(
         scan_kernel, [((ctx_places, 2 * part, state_width), BF16)], inputs=1
     )(got_states)
 
     entered = exchange(entered, "ctx")
-    send_in = after(send_in.reshape(expert_count, slot_width, col_width), entered)
-    rows_in = exchange(send_in, "expert")
-
     main_heads, tail_heads, rim_heads, grad_bc, grad_step, taps_heads, grad_rate = whole(
         back_kernel,
         [
@@ -530,7 +528,6 @@
         head_rows, shared_rows, before, raw_step, gains, conv_x, conv_bc, cot_rows,
         entered,
     )
-    grad_bc = after(grad_bc, rows_in)
     after_heads = passed_along(rim_heads[:rim_rows], "ctx", -1)
     grad_mamba_in = with_last_rows(main_heads, tail_heads, after_heads)
     main_shared, tail_shared, rim_shared, taps_shared = whole(
@@ -555,11 +552,7 @@
         ],
         axis=1,
     )
-    small = jnp.sum(exchange(small.reshape(dp_count, 8, 128), "dp"), axis=0)
-    small = jnp.sum(exchange(copies(small, ctx_places), "ctx"), axis=0).reshape(1, -1)
-    taps_heads = small[:, :split_at]
-    taps_shared = small[:, split_at : split_at + shared_width]
-    rate_total = small[0, split_at + shared_width :][:heads_here]
+    small = exchange(copies(small.reshape(dp_count * 8, 128), ctx_places), "ctx")
 
     share = hidden_width // dp_count
     block = ((3 * share, col_width), BF16)
@@ -572,8 +565,23 @@
         scalars=1,
         late=1,
         limit=56 * 2**20,
-    )(owner, everything, rows_in, got_cot, w_gate[0], w_up[0], small)
-    back = exchange(back, "expert")
+    )(owner, everything, rows_in, got_cot, w_gate[0], w_up[0], main_shared)
+    small = after(small, back, parts[0])
+    back = exchange(after(back, small), "expert")
+    small = jnp.sum(small, axis=0).reshape(dp_count, 8, 128)
+    places = jnp.arange(dp_count, dtype=jnp.int32)[:, None, None]
+    small = [
+        jnp.sum(jnp.where(places == lax.rem(owner[0] + k, dp_count), small, 0.0), axis=0)
+        for k in range(dp_count)
+    ]
+    small = small[0] + sum(
+        lax.ppermute(small[k], "dp", [(i, (i + k) % dp_count) for i in range(dp_count)])
+        for k in range(1, dp_count)
+    )
+    small = small.reshape(1, -1)
+    taps_heads = small[:, :split_at]
+    taps_shared = small[:, split_at : split_at + shared_width]
+    rate_total = small[0, split_at + shared_width :][:heads_here]
     parts = [parts[0]] + [
         lax.ppermute(parts[k], "dp", [(i, (i + k) % dp_count) for i in range(dp_count)])
         for k in range(1, dp_count)

time: 260 us -> 265 us (1.019)
  blocking collectives: 8.52 us -> 60.1 us
  waiting for transfers between devices: 82.1 us -> 46.8 us
  starting transfers between devices: 102 us -> 91.2 us
    all_to_all x1 -> x2, blocking collectives: 8.52 us -> 60.1 us  [exchange(): return lax.all_to_all(value, axis, split_axis=0, concat_axis=0, tiled=True)]
    all_to_all x7 -> x5, waiting for transfers between devices: 39.9 us -> 17.3 us  [exchange(): return lax.all_to_all(value, axis, split_axis=0, concat_axis=0, tiled=True)]
    all_to_all x7 -> x5, starting transfers between devices: 56.9 us -> 39.1 us  [exchange(): return lax.all_to_all(value, axis, split_axis=0, concat_axis=0, tiled=True)]
    ppermute x7, waiting for transfers between devices: 32.5 us -> 15.3 us  [shift(): lax.ppermute(value, 'ctx', [(i, (i + distance) % count) for i in range(co...]
    ppermute x0 -> x3, starting transfers between devices: none -> 8.44 us  [body(): lax.ppermute(small[k], 'dp', [(i, (i + k) % dp_count) for i in range(dp_c...]
    ppermute x3, waiting for transfers between devices: 0.14 us -> 8.25 us  [passed_along(): lax.ppermute(value, axis, [(source, source + steps) for source in range(f...]
    ppermute x3, waiting for transfers between devices: 9.47 us -> 5.82 us  [body(): lax.ppermute(parts[k], 'dp', [(i, (i + k) % dp_count) for i in range(dp_c...]
    ppermute x7, starting transfers between devices: 32.8 us -> 29.6 us  [shift(): lax.ppermute(value, 'ctx', [(i, (i + distance) % count) for i in range(co...]
  transfers between devices with their start and end apart: 21 -> 22, of which waited for: 15 -> 8; matrix products, arithmetic and copies ran while one was open for 5% -> 5% of each run, Pallas kernels for 9% -> 9%
where the time goes in v8:
time: 265 us; the launch traced here: 263 us
  starting transfers between devices  91.2 us (34%)
  blocking collectives  60.1 us (23%)
  waiting for transfers between devices  46.8 us (18%)
  Pallas kernels  28.5 us (11%)
  between operations  14.6 us (6%)
  local copies, waits for them, and re-layouts  9.43 us (4%)
  other arithmetic  9.34 us (4%)
  matrix products  3.17 us (1%)
    all_to_all x2, blocking collectives, exchange(): return lax.all_to_all(value, axis, split_axis=0, concat_axis=0, tiled=True)  60.1 us
    all_to_all x5, starting transfers between devices, exchange(): return lax.all_to_all(value, axis, split_axis=0, concat_axis=0, tiled=True)  39.1 us
    ppermute x7, starting transfers between devices, shift(): lax.ppermute(value, 'ctx', [(i, (i + distance) % count) for i in range(co...  29.6 us
    all_to_all x5, waiting for transfers between devices, exchange(): return lax.all_to_all(value, axis, split_axis=0, concat_axis=0, tiled=True)  17.3 us
    ppermute x7, waiting for transfers between devices, shift(): lax.ppermute(value, 'ctx', [(i, (i + distance) % count) for i in range(co...  15.3 us
    ppermute x3, starting transfers between devices, body(): lax.ppermute(parts[k], 'dp', [(i, (i + k) % dp_count) for i in range(dp_c...  10.3 us
    ppermute x3, starting transfers between devices, body(): lax.ppermute(small[k], 'dp', [(i, (i + k) % dp_count) for i in range(dp_c...  8.44 us
    ppermute x3, waiting for transfers between devices, passed_along(): lax.ppermute(value, axis, [(source, source + steps) for source in range(f...  8.25 us
  transfers between devices with their start and end apart: 22, of which 8 were waited for; matrix products, arithmetic and copies ran while one was open for 5% of the time, Pallas kernels for 9%

profile of v8, /device:TPU:1, one launch (start us, length us, event | category | flops | bytes accessed | tf_op | source)
XLA Modules:
  0.0 263.1 jit_solution(3541068014883491025)
XLA Ops:
  10.1 10.3 %all-to-all-start = ((bf16[8,144,256]{2,1,0:T(8,128)(2,1)}), bf16[8,144,256]{2,1,0:T(8,128)(2,1)S(1)}, u32[]{:S(2)}, u32[]{:S(2)}) async-start(bf16[8,144,256]{2,1,0:T(8,128)(2,1)} %fusion.17), calls=%async_computation | async-start | bytes 1179648 | tf_op jit(solution)/shard_map/all_to_all | solution.py:20
  24.6 3.9 %shard_map.266.earlier_ref = bf16[16,80,128]{2,1,0:T(8,128)(2,1)} custom-call(bf16[256,512]{1,0:T(8,128)(2,1)} %bitcast.84, bf16[256,256]{1,0:T(8,128)(2,1)} %bitcast.81, bf16[3,768]{1,0:T(4,128)(2,1)} %copy-done.4, f32[8,256]{1,0:T(8,128)} %bitcast.88, f32[3,8]{1,0:T(4,128)} %pad_maximum_fusion.1.gains_ref, f32[4,512]{1,0:T(4,128)} %tapsx_ref.3, ...), custom_call_target="tpu_custom_call" | custom-call | tf_op jit(solution)/shard_map/pallas_call | solution.py:478
  28.4 2.2 all-to-all-done.cot_ref
  31.5 2.7 %shard_map.267 = (bf16[192,768]{1,0:T(8,128)(2,1)}, bf16[192,768]{1,0:T(8,128)(2,1)}, bf16[192,768]{1,0:T(8,128)(2,1)}, bf16[192,768]{1,0:T(8,128)(2,1)}, bf16[1...) custom-call(s32[1]{0:T(128)} %bitcast.9.place_ref, bf16[8,144,256]{2,1,0:T(8,128)(2,1)} %copy-done.10, ...), custom_call_target="tpu_custom_call" | custom-call | tf_op jit(solution)/shard_map/pallas_call | solution.py:485
  34.2 7.0 %collective-permute-start.1 = (bf16[192,768]{1,0:T(8,128)(2,1)}, bf16[192,768]{1,0:T(8,128)(2,1)S(1)}, u32[]{:S(2)}, u32[]{:S(2)}) collective-permute-start(bf16[192,768]{1,0:T(8,128)(2,1)} %get-tuple-element.41), channel_id=1, source_target_pairs={{0,15},{1,0},{2,1},{3,2},{4,3},{5,4},{6,5},{7,6},{8,7},{9,8},{10,9... | collective-permute-start | bytes 884744 | tf_op jit(solution)/shard_map/ppermute | solution.py:25
  43.1 3.8 %collective-permute-done.1 = bf16[192,768]{1,0:T(8,128)(2,1)S(1)} collective-permute-done((bf16[192,768]{1,0:T(8,128)(2,1)}, bf16[192,768]{1,0:T(8,128)(2,1)S(1)}, u32[]{:S(2)}, u32[]{:S(2)}) %collective-permute-start.1) | collective-permute-done | bytes 294944 | tf_op jit(solution)/shard_map/ppermute | solution.py:25
  48.0 5.2 %collective-permute-start.2 = (bf16[192,768]{1,0:T(8,128)(2,1)S(1)}, bf16[192,768]{1,0:T(8,128)(2,1)S(1)}, u32[]{:S(2)}, u32[]{:S(2)}) collective-permute-start(bf16[192,768]{1,0:T(8,128)(2,1)S(1)} %add_convert_fusion.1), channel_id=1, source_target_pairs={{0,15},{1,0},{2,1},{3,2},{4,3},{5,4},{6,5},{7,6},{8,7},{9,8},{10,9... | collective-permute-start | bytes 884744 | tf_op jit(solution)/shard_map/ppermute | solution.py:25
  54.3 2.1 collective-permute-start.4
  57.6 6.5 %all-to-all-start.1 = ((bf16[8,128,256]{2,1,0:T(8,128)(2,1)}), bf16[8,128,256]{2,1,0:T(8,128)(2,1)S(1)}, u32[]{:S(2)}, u32[]{:S(2)}) async-start(bf16[8,128,256]{2,1,0:T(8,128)(2,1)} %bitcast.22), calls=%async_computation.1 | async-start | bytes 1048576 | tf_op jit(solution)/shard_map/all_to_all | solution.py:20
  66.9 6.5 %collective-permute-done.6 = bf16[64,768]{1,0:T(8,128)(2,1)S(1)} collective-permute-done((bf16[64,768]{1,0:T(8,128)(2,1)S(1)}, bf16[64,768]{1,0:T(8,128)(2,1)S(1)}, u32[]{:S(2)}, u32[]{:S(2)}) %collective-permute-start.6) | collective-permute-done | bytes 98336 | tf_op jit(solution)/shard_map/ppermute | solution.py:25
  73.6 5.9 %collective-permute-start.7 = (bf16[64,768]{1,0:T(8,128)(2,1)S(1)}, bf16[64,768]{1,0:T(8,128)(2,1)S(1)}, u32[]{:S(2)}, u32[]{:S(2)}) collective-permute-start(bf16[64,768]{1,0:T(8,128)(2,1)S(1)} %fusion.20), channel_id=1, source_target_pairs={{0,5},{1,6},{2,7},{3,8},{4,9},{5,10},{6,11},{7,12},{8,13},{9,14},{... | collective-permute-start | bytes 294920 | tf_op jit(solution)/shard_map/ppermute | solution.py:25
  79.5 5.5 %collective-permute-start.5 = (bf16[64,768]{1,0:T(8,128)(2,1)S(1)}, bf16[64,768]{1,0:T(8,128)(2,1)S(1)}, u32[]{:S(2)}, u32[]{:S(2)}) collective-permute-start(bf16[64,768]{1,0:T(8,128)(2,1)S(1)} %slice.104), channel_id=1, source_target_pairs={{0,11},{1,12},{2,13},{3,14},{4,15},{5,0},{6,1},{7,2},{8,3},{9,4},{... | collective-permute-start | bytes 294920 | tf_op jit(solution)/shard_map/ppermute | solution.py:25
  85.9 5.0 %collective-permute-done.7 = bf16[64,768]{1,0:T(8,128)(2,1)S(1)} collective-permute-done((bf16[64,768]{1,0:T(8,128)(2,1)S(1)}, bf16[64,768]{1,0:T(8,128)(2,1)S(1)}, u32[]{:S(2)}, u32[]{:S(2)}) %collective-permute-start.7) | collective-permute-done | bytes 98336 | tf_op jit(solution)/shard_map/ppermute | solution.py:25
  92.3 2.0 shard_map.268
  94.3 27.7 %all_to_all.35.got_ref = bf16[16,80,128]{2,1,0:T(8,128)(2,1)} all-to-all(bf16[16,80,128]{2,1,0:T(8,128)(2,1)S(1)} %copy-done.13), channel_id=1, replica_groups=mesh['dp'=4,'expert'=8,'ctx'=16] {'ctx'}, dimensions={0} | all-to-all | bytes 655360 | tf_op jit(solution)/shard_map/all_to_all | solution.py:20
  123.8 32.4 %all_to_all.36.got_ref = bf16[16,64,128]{2,1,0:T(8,128)(2,1)S(1)} all-to-all(bf16[16,64,128]{2,1,0:T(8,128)(2,1)} %shard_map.269), channel_id=1, replica_groups=mesh['dp'=4,'expert'=8,'ctx'=16] {'ctx'}, dimensions={0} | all-to-all | bytes 524288 | tf_op jit(solution)/shard_map/all_to_all | solution.py:20
  156.3 6.9 %shard_map.270 = (bf16[256,512]{1,0:T(8,128)(2,1)}, f32[16,512]{1,0:T(8,128)S(1)}, f32[8,512]{1,0:T(8,128)S(1)}, bf16[8,256,256]{2,1,0:T(8,128)(2,1)}, f32[8,256...) custom-call(bf16[256,512]{1,0:T(8,128)(2,1)S(1)} %bitcast.85, bf16[256,256]{1,0:T(8,128)(2,1)S(1)} %bitcast.83, ...), custom_call_target="tpu_custom_call" | custom-call | tf_op jit(solution)/shard_map/pallas_call | solution.py:513
  163.2 9.7 %all-to-all-start.4 = ((bf16[8,256,256]{2,1,0:T(8,128)(2,1)}), bf16[8,256,256]{2,1,0:T(8,128)(2,1)S(1)}, u32[]{:S(2)}, u32[]{:S(2)}) async-start(bf16[8,256,256]{2,1,0:T(8,128)(2,1)} %get-tuple-element.49), calls=%async_computation.4 | async-start | bytes 2097152 | tf_op jit(solution)/shard_map/all_to_all | solution.py:20
  173.0 15.1 %all-to-all-done.4.got_ref = bf16[8,256,256]{2,1,0:T(8,128)(2,1)S(1)} async-done(((bf16[8,256,256]{2,1,0:T(8,128)(2,1)}), bf16[8,256,256]{2,1,0:T(8,128)(2,1)S(1)}, u32[]{:S(2)}, u32[]{:S(2)}) %all-to-all-start.4) | async-done | bytes 1048608 | tf_op jit(solution)/shard_map/all_to_all | solution.py:20
  189.1 2.8 %shard_map.271 = (bf16[256,256]{1,0:T(8,128)(2,1)}, f32[16,256]{1,0:T(8,128)}, f32[8,256]{1,0:T(8,128)}, f32[4,256]{1,0:T(4,128)}) custom-call(bf16[256,256]{1,0:T(8,128)(2,1)} %bitcast.82, bf16[3,768]{1,0:T(4,128)(2,1)} %copy-done.4, f32[4,256]{1,0:T(4,128)} %tapsbc_ref.5, bf16[8,256,256]{2,1,0:T(8,128)(2,1)} %copy-done.12), custom_call_target="tpu_custom_call" | custom-call | tf_op jit(solution)/shard_map/pallas_call | solution.py:533
  193.3 4.4 %all-to-all-start.5 = ((f32[16,32,128]{2,1,0:T(8,128)}), f32[16,32,128]{2,1,0:T(8,128)S(1)}, u32[]{:S(2)}, u32[]{:S(2)}) async-start(f32[16,32,128]{2,1,0:T(8,128)} %broadcast_in_dim.117), calls=%async_computation.5 | async-start | bytes 524288 | tf_op jit(solution)/shard_map/all_to_all | solution.py:20
  199.1 8.1 %collective-permute-done.8 = f32[3,512]{1,0:T(4,128)S(1)} collective-permute-done((f32[3,512]{1,0:T(4,128)S(1)}, f32[3,512]{1,0:T(4,128)S(1)}, u32[]{:S(2)}, u32[]{:S(2)}) %collective-permute-start.8) | collective-permute-done | bytes 6176 | tf_op jit(solution)/shard_map/ppermute | solution.py:16
  209.8 6.4 %shard_map.272 = (bf16[8,144,256]{2,1,0:T(8,128)(2,1)}, bf16[576,256]{1,0:T(8,128)(2,1)}, bf16[576,256]{1,0:T(8,128)(2,1)}, bf16[576,256]{1,0:T(8,128)(2,1)}, bf16[576,256]{1,0:T(8,128)(2,1)}) custom-call(s32[1]{0:T(128)} %bitcast.29.place_ref, bf16[1024,2432]{1,0:T(8,128)(2,1)} %all-gather.2.cloned.1.call-done.all_ref, bf16[8,128,256]{2,1,0:T(8,128)(2,1)} %copy-done.11, ...), custom_call_target="tpu_custom_call" | custom-call | tf_op jit(solution)/shard_map/pallas_call | solution.py:560
  216.3 3.2 %collective-permute-start.13 = (bf16[576,256]{1,0:T(8,128)(2,1)}, bf16[576,256]{1,0:T(8,128)(2,1)S(1)}, u32[]{:S(2)}, u32[]{:S(2)}) collective-permute-start(bf16[576,256]{1,0:T(8,128)(2,1)} %get-tuple-element.61), channel_id=1, source_target_pairs={{0,128},{128,256},{256,384},{384,0},{1,129},{129,257},{257,385},{3... | collective-permute-start | bytes 884744 | tf_op jit(solution)/shard_map/ppermute | solution.py:586
  219.5 4.6 %collective-permute-start.14 = (bf16[576,256]{1,0:T(8,128)(2,1)}, bf16[576,256]{1,0:T(8,128)(2,1)S(1)}, u32[]{:S(2)}, u32[]{:S(2)}) collective-permute-start(bf16[576,256]{1,0:T(8,128)(2,1)} %get-tuple-element.62), channel_id=1, source_target_pairs={{0,256},{128,384},{256,0},{384,128},{1,257},{129,385},{257,1},{385... | collective-permute-start | bytes 884744 | tf_op jit(solution)/shard_map/ppermute | solution.py:586
  224.1 8.1 %all-to-all-start.6 = ((bf16[8,144,256]{2,1,0:T(8,128)(2,1)}), bf16[8,144,256]{2,1,0:T(8,128)(2,1)S(1)}, u32[]{:S(2)}, u32[]{:S(2)}) async-start(bf16[8,144,256]{2,1,0:T(8,128)(2,1)} %get-tuple-element.60), calls=%async_computation.6 | async-start | bytes 1179648 | tf_op jit(solution)/shard_map/all_to_all | solution.py:20
  232.3 1.9 collective-permute-start.10
  234.2 4.1 %collective-permute-start.11 = (f32[8,128]{1,0:T(8,128)S(1)}, f32[8,128]{1,0:T(8,128)S(1)}, u32[]{:S(2)}, u32[]{:S(2)}) collective-permute-start(f32[8,128]{1,0:T(8,128)S(1)} %get-tuple-element.67), channel_id=1, source_target_pairs={{0,256},{128,384},{256,0},{384,128},{1,257},{129,385},{257,1},{385... | collective-permute-start | bytes 12296 | tf_op jit(solution)/shard_map/ppermute | solution.py:578
  238.4 2.4 collective-permute-start.12
  241.4 2.5 collective-permute-start.15
  245.6 5.8 %collective-permute-done.15.refs_3_ = bf16[576,256]{1,0:T(8,128)(2,1)S(1)} collective-permute-done((bf16[576,256]{1,0:T(8,128)(2,1)}, bf16[576,256]{1,0:T(8,128)(2,1)S(1)}, u32[]{:S(2)}, u32[]{:S(2)}) %collective-permute-start.15) | collective-permute-done | bytes 294944 | tf_op jit(solution)/shard_map/ppermute | solution.py:586
  252.1 2.0 shard_map.273
  (114 shorter events, 31.6 us)
Async XLA Ops:
  10.1 20.5 %all-to-all-start = ((bf16[8,144,256]{2,1,0:T(8,128)(2,1)}), bf16[8,144,256]{2,1,0:T(8,128)(2,1)S(1)}, u32[]{:S(2)}, u32[]{:S(2)}) async-start(bf16[8,144,256]{2,1,0:T(8,128)(2,1)} %fusion.17), calls=%async_computation | async-start | bytes 1179648 | tf_op jit(solution)/shard_map/all_to_all | solution.py:20
  20.5 35.9 %copy-start.23 = (bf16[1,512,256]{2,1,0:T(8,128)(2,1)S(1)}, bf16[1,512,256]{2,1,0:T(8,128)(2,1)}, u32[]{:S(2)}) copy-start(bf16[1,512,256]{2,1,0:T(8,128)(2,1)} %param.28) | copy-start | bytes 786436
  21.9 2.1 collective-permute-start
  34.2 12.7 %collective-permute-start.1 = (bf16[192,768]{1,0:T(8,128)(2,1)}, bf16[192,768]{1,0:T(8,128)(2,1)S(1)}, u32[]{:S(2)}, u32[]{:S(2)}) collective-permute-start(bf16[192,768]{1,0:T(8,128)(2,1)} %get-tuple-element.41), channel_id=1, source_target_pairs={{0,15},{1,0},{2,1},{3,2},{4,3},{5,4},{6,5},{7,6},{8,7},{9,8},{10,9... | collective-permute-start | bytes 884744 | tf_op jit(solution)/shard_map/ppermute | solution.py:25
  41.2 12.0 %collective-permute-start.3 = (bf16[192,768]{1,0:T(8,128)(2,1)}, bf16[192,768]{1,0:T(8,128)(2,1)S(1)}, u32[]{:S(2)}, u32[]{:S(2)}) collective-permute-start(bf16[192,768]{1,0:T(8,128)(2,1)} %get-tuple-element.43), channel_id=1, source_target_pairs={{0,1},{1,2},{2,3},{3,4},{4,5},{5,6},{6,7},{7,8},{8,9},{9,10},{10,1... | collective-permute-start | bytes 884744 | tf_op jit(solution)/shard_map/ppermute | solution.py:25
  48.0 18.8 %collective-permute-start.2 = (bf16[192,768]{1,0:T(8,128)(2,1)S(1)}, bf16[192,768]{1,0:T(8,128)(2,1)S(1)}, u32[]{:S(2)}, u32[]{:S(2)}) collective-permute-start(bf16[192,768]{1,0:T(8,128)(2,1)S(1)} %add_convert_fusion.1), channel_id=1, source_target_pairs={{0,15},{1,0},{2,1},{3,2},{4,3},{5,4},{6,5},{7,6},{8,7},{9,8},{10,9... | collective-permute-start | bytes 884744 | tf_op jit(solution)/shard_map/ppermute | solution.py:25
  54.3 12.5 %collective-permute-start.4 = (bf16[192,768]{1,0:T(8,128)(2,1)S(1)}, bf16[192,768]{1,0:T(8,128)(2,1)S(1)}, u32[]{:S(2)}, u32[]{:S(2)}) collective-permute-start(bf16[192,768]{1,0:T(8,128)(2,1)S(1)} %add_convert_fusion), channel_id=1, source_target_pairs={{0,1},{1,2},{2,3},{3,4},{4,5},{5,6},{6,7},{7,8},{8,9},{9,10},{10,1... | collective-permute-start | bytes 884744 | tf_op jit(solution)/shard_map/ppermute | solution.py:25
  57.6 33.9 %all-to-all-start.1 = ((bf16[8,128,256]{2,1,0:T(8,128)(2,1)}), bf16[8,128,256]{2,1,0:T(8,128)(2,1)S(1)}, u32[]{:S(2)}, u32[]{:S(2)}) async-start(bf16[8,128,256]{2,1,0:T(8,128)(2,1)} %bitcast.22), calls=%async_computation.1 | async-start | bytes 1048576 | tf_op jit(solution)/shard_map/all_to_all | solution.py:20
  64.1 145.7 %all-gather.2.cloned.1.call-start = ((), (), s32[]{:S(2)}) async-start(), calls=%async_computation.7 | async-start | bytes 5292032 | tf_op jit(solution)/shard_map/all_gather | solution.py:505
  64.1 9.3 %collective-permute-start.6 = (bf16[64,768]{1,0:T(8,128)(2,1)S(1)}, bf16[64,768]{1,0:T(8,128)(2,1)S(1)}, u32[]{:S(2)}, u32[]{:S(2)}) collective-permute-start(bf16[64,768]{1,0:T(8,128)(2,1)S(1)} %copy-done.24), channel_id=1, source_target_pairs={{0,3},{1,4},{2,5},{3,6},{4,7},{5,8},{6,9},{7,10},{8,11},{9,12},{10... | collective-permute-start | bytes 294920 | tf_op jit(solution)/shard_map/ppermute | solution.py:25
  73.5 82.7 %copy-start.1 = (bf16[1,256,256]{2,1,0:T(8,128)(2,1)S(1)}, bf16[1,256,256]{2,1,0:T(8,128)(2,1)}, u32[]{:S(2)}) copy-start(bf16[1,256,256]{2,1,0:T(8,128)(2,1)} %param.20) | copy-start | bytes 393220
  73.5 82.7 %copy-start.2 = (bf16[1,256,512]{2,1,0:T(8,128)(2,1)S(1)}, bf16[1,256,512]{2,1,0:T(8,128)(2,1)}, u32[]{:S(2)}) copy-start(bf16[1,256,512]{2,1,0:T(8,128)(2,1)} %param.19) | copy-start | bytes 786436
  73.5 82.7 %copy-start.3 = (bf16[1,256,512]{2,1,0:T(8,128)(2,1)S(1)}, bf16[1,256,512]{2,1,0:T(8,128)(2,1)}, u32[]{:S(2)}) copy-start(bf16[1,256,512]{2,1,0:T(8,128)(2,1)} %param.27) | copy-start | bytes 786436
  73.5 82.7 %copy-start.5 = (bf16[3,768]{1,0:T(4,128)(2,1)S(1)}, bf16[3,768]{1,0:T(4,128)(2,1)}, u32[]{:S(2)}) copy-start(bf16[3,768]{1,0:T(4,128)(2,1)} %copy-done.4) | copy-start | bytes 13828
  73.5 82.7 %copy-start.6 = (f32[4,256]{1,0:T(4,128)S(1)}, f32[4,256]{1,0:T(4,128)}, u32[]{:S(2)}) copy-start(f32[4,256]{1,0:T(4,128)} %tapsbc_ref.5) | copy-start | bytes 12292
  73.5 82.7 %copy-start.7 = (f32[1,8,256]{2,1,0:T(8,128)S(1)}, f32[1,8,256]{2,1,0:T(8,128)}, u32[]{:S(2)}) copy-start(f32[1,8,256]{2,1,0:T(8,128)} %param.21) | copy-start | bytes 24580
  73.5 82.7 %copy-start.8 = (f32[4,512]{1,0:T(4,128)S(1)}, f32[4,512]{1,0:T(4,128)}, u32[]{:S(2)}) copy-start(f32[4,512]{1,0:T(4,128)} %tapsx_ref.3) | copy-start | bytes 24580
  73.5 82.7 %copy-start.9 = (f32[3,8]{1,0:T(4,128)S(1)}, f32[3,8]{1,0:T(4,128)}, u32[]{:S(2)}) copy-start(f32[3,8]{1,0:T(4,128)} %pad_maximum_fusion.1.gains_ref) | copy-start | bytes 292
  73.6 17.2 %collective-permute-start.7 = (bf16[64,768]{1,0:T(8,128)(2,1)S(1)}, bf16[64,768]{1,0:T(8,128)(2,1)S(1)}, u32[]{:S(2)}, u32[]{:S(2)}) collective-permute-start(bf16[64,768]{1,0:T(8,128)(2,1)S(1)} %fusion.20), channel_id=1, source_target_pairs={{0,5},{1,6},{2,7},{3,8},{4,9},{5,10},{6,11},{7,12},{8,13},{9,14},{... | collective-permute-start | bytes 294920 | tf_op jit(solution)/shard_map/ppermute | solution.py:25
  79.5 11.3 %collective-permute-start.5 = (bf16[64,768]{1,0:T(8,128)(2,1)S(1)}, bf16[64,768]{1,0:T(8,128)(2,1)S(1)}, u32[]{:S(2)}, u32[]{:S(2)}) collective-permute-start(bf16[64,768]{1,0:T(8,128)(2,1)S(1)} %slice.104), channel_id=1, source_target_pairs={{0,11},{1,12},{2,13},{3,14},{4,15},{5,0},{6,1},{7,2},{8,3},{9,4},{... | collective-permute-start | bytes 294920 | tf_op jit(solution)/shard_map/ppermute | solution.py:25
  163.2 24.8 %all-to-all-start.4 = ((bf16[8,256,256]{2,1,0:T(8,128)(2,1)}), bf16[8,256,256]{2,1,0:T(8,128)(2,1)S(1)}, u32[]{:S(2)}, u32[]{:S(2)}) async-start(bf16[8,256,256]{2,1,0:T(8,128)(2,1)} %get-tuple-element.49), calls=%async_computation.4 | async-start | bytes 2097152 | tf_op jit(solution)/shard_map/all_to_all | solution.py:20
  193.3 22.9 %all-to-all-start.5 = ((f32[16,32,128]{2,1,0:T(8,128)}), f32[16,32,128]{2,1,0:T(8,128)S(1)}, u32[]{:S(2)}, u32[]{:S(2)}) async-start(f32[16,32,128]{2,1,0:T(8,128)} %broadcast_in_dim.117), calls=%async_computation.5 | async-start | bytes 524288 | tf_op jit(solution)/shard_map/all_to_all | solution.py:20
  197.8 9.4 %collective-permute-start.8 = (f32[3,512]{1,0:T(4,128)S(1)}, f32[3,512]{1,0:T(4,128)S(1)}, u32[]{:S(2)}, u32[]{:S(2)}) collective-permute-start(f32[3,512]{1,0:T(4,128)S(1)} %slice.65), channel_id=1, source_target_pairs={{1,0},{2,1},{3,2},{4,3},{5,4},{6,5},{7,6},{8,7},{9,8},{10,9},{11,1... | collective-permute-start | bytes 18440 | tf_op jit(solution)/shard_map/ppermute | solution.py:16
  208.5 29.9 %collective-permute-start.9 = (f32[3,256]{1,0:T(4,128)S(1)}, f32[3,256]{1,0:T(4,128)S(1)}, u32[]{:S(2)}, u32[]{:S(2)}) collective-permute-start(f32[3,256]{1,0:T(4,128)S(1)} %slice.66), channel_id=1, source_target_pairs={{1,0},{2,1},{3,2},{4,3},{5,4},{6,5},{7,6},{8,7},{9,8},{10,9},{11,1... | collective-permute-start | bytes 9224 | tf_op jit(solution)/shard_map/ppermute | solution.py:16
  209.8 31.0 %copy-start.18 = (f32[16,256]{1,0:T(8,128)S(1)}, f32[16,256]{1,0:T(8,128)}, u32[]{:S(2)}) copy-start(f32[16,256]{1,0:T(8,128)} %get-tuple-element.51) | copy-start | bytes 49156
  216.3 29.3 %collective-permute-start.13 = (bf16[576,256]{1,0:T(8,128)(2,1)}, bf16[576,256]{1,0:T(8,128)(2,1)S(1)}, u32[]{:S(2)}, u32[]{:S(2)}) collective-permute-start(bf16[576,256]{1,0:T(8,128)(2,1)} %get-tuple-element.61), channel_id=1, source_target_pairs={{0,128},{128,256},{256,384},{384,0},{1,129},{129,257},{257,385},{3... | collective-permute-start | bytes 884744 | tf_op jit(solution)/shard_map/ppermute | solution.py:586
  219.5 26.1 %collective-permute-start.14 = (bf16[576,256]{1,0:T(8,128)(2,1)}, bf16[576,256]{1,0:T(8,128)(2,1)S(1)}, u32[]{:S(2)}, u32[]{:S(2)}) collective-permute-start(bf16[576,256]{1,0:T(8,128)(2,1)} %get-tuple-element.62), channel_id=1, source_target_pairs={{0,256},{128,384},{256,0},{384,128},{1,257},{129,385},{257,1},{385... | collective-permute-start | bytes 884744 | tf_op jit(solution)/shard_map/ppermute | solution.py:586
  224.1 30.1 %all-to-all-start.6 = ((bf16[8,144,256]{2,1,0:T(8,128)(2,1)}), bf16[8,144,256]{2,1,0:T(8,128)(2,1)S(1)}, u32[]{:S(2)}, u32[]{:S(2)}) async-start(bf16[8,144,256]{2,1,0:T(8,128)(2,1)} %get-tuple-element.60), calls=%async_computation.6 | async-start | bytes 1179648 | tf_op jit(solution)/shard_map/all_to_all | solution.py:20
  232.3 9.1 %collective-permute-start.10 = (f32[8,128]{1,0:T(8,128)S(1)}, f32[8,128]{1,0:T(8,128)S(1)}, u32[]{:S(2)}, u32[]{:S(2)}) collective-permute-start(f32[8,128]{1,0:T(8,128)S(1)} %get-tuple-element.68), channel_id=1, source_target_pairs={{0,128},{128,256},{256,384},{384,0},{1,129},{129,257},{257,385},{3... | collective-permute-start | bytes 12296 | tf_op jit(solution)/shard_map/ppermute | solution.py:578
  234.2 9.7 %collective-permute-start.11 = (f32[8,128]{1,0:T(8,128)S(1)}, f32[8,128]{1,0:T(8,128)S(1)}, u32[]{:S(2)}, u32[]{:S(2)}) collective-permute-start(f32[8,128]{1,0:T(8,128)S(1)} %get-tuple-element.67), channel_id=1, source_target_pairs={{0,256},{128,384},{256,0},{384,128},{1,257},{129,385},{257,1},{385... | collective-permute-start | bytes 12296 | tf_op jit(solution)/shard_map/ppermute | solution.py:578
  238.4 5.5 %collective-permute-start.12 = (f32[8,128]{1,0:T(8,128)S(1)}, f32[8,128]{1,0:T(8,128)S(1)}, u32[]{:S(2)}, u32[]{:S(2)}) collective-permute-start(f32[8,128]{1,0:T(8,128)S(1)} %get-tuple-element.69), channel_id=1, source_target_pairs={{0,384},{128,0},{256,128},{384,256},{1,385},{129,1},{257,129},{385... | collective-permute-start | bytes 12296 | tf_op jit(solution)/shard_map/ppermute | solution.py:578
  241.4 10.0 %collective-permute-start.15 = (bf16[576,256]{1,0:T(8,128)(2,1)}, bf16[576,256]{1,0:T(8,128)(2,1)S(1)}, u32[]{:S(2)}, u32[]{:S(2)}) collective-permute-start(bf16[576,256]{1,0:T(8,128)(2,1)} %get-tuple-element.63), channel_id=1, source_target_pairs={{0,384},{128,0},{256,128},{384,256},{1,385},{129,1},{257,129},{385... | collective-permute-start | bytes 884744 | tf_op jit(solution)/shard_map/ppermute | solution.py:586
  (15 other events, 111.9 us)
Sparse Core Ops, SparseCore 0:
  94.4 96.2 all-gather.1

commit v9 on v7

--- a/solution.py
+++ b/solution.py
@@ -260,6 +260,21 @@
         taps_out_ref[k : k + 1, :] = value
 
 
+def send_kernel(count_ref, slots_ref, weight_ref, cot_ref, out_ref):
+    groups, slots = slots_ref.shape
+    tokens, cols = cot_ref.shape
+    chosen = []
+    for group in range(groups):
+        live = iota((1, slots), 1) < count_ref[group]
+        ids = jnp.where(live, slots_ref[group : group + 1, :], -1)
+        chosen.append(jnp.where(iota((tokens, slots), 0) == ids, 1.0, 0.0).astype(BF16))
+        line = jnp.where(live, weight_ref[group : group + 1, :].astype(F32), 0.0)
+        tile = jnp.concatenate([line, jnp.zeros((1, cols - slots), F32)], axis=1)
+        out_ref[group, slots:, :] = jnp.broadcast_to(tile, (16, cols)).astype(BF16)
+    rows = dot(jnp.concatenate(chosen, axis=1), cot_ref[...], 0, 0)
+    out_ref[:, :slots, :] = rows.astype(BF16).reshape(groups, slots, cols)
+
+
 def scaled_rows(cot_ref, group):
     slots = cot_ref.shape[1] - 16
     weight = cot_ref[group, slots:, :slots].astype(F32).T[:, 0:1]
@@ -320,7 +335,7 @@
 
 
 def totals_kernel(*refs):
-    part_refs, out_refs = refs[:-3], refs[-3:]
+    part_refs, out_refs = refs[:-4], refs[-3:]
     share = out_refs[0].shape[0]
     for kind, out_ref in enumerate(out_refs):
         span = slice(kind * share, (kind + 1) * share)
@@ -425,11 +440,13 @@
     chosen = jnp.where(live_slots, slot_ids, -1).reshape(-1)
     token_index = jnp.arange(token_count, dtype=jnp.int32)
     table = jnp.where(chosen[:, None] == token_index[None, :], 1.0, 0.0).astype(BF16)
-    send_cot = jnp.dot(table, moe_cot[0], preferred_element_type=F32).astype(BF16)
-    send_weight = jnp.where(live_slots, route_w[0, 0], jnp.zeros((), BF16))
-    send_weight = jnp.pad(send_weight[:, None, :], ((0, 0), (0, 15), (0, col_width - slot_width)))
-    send_cot = send_cot.reshape(expert_count, slot_width, col_width)
-    got_cot = exchange(jnp.concatenate([send_cot, send_weight], axis=1), "expert")
+    (send_cot,) = whole(
+        send_kernel,
+        [((expert_count, slot_width + 16, col_width), BF16)],
+        inputs=3,
+        scalars=1,
+    )(slot_count[0, 0], slot_ids, route_w[0, 0], moe_cot[0])
+    got_cot = exchange(send_cot, "expert")
     send_in = jnp.dot(table, moe_in[0], preferred_element_type=F32).astype(BF16)
 
     gains = jnp.stack([dt_bias, a_log, d_skip])
@@ -526,15 +543,15 @@
         lax.ppermute(parts[k], "dp", [(i, (i + k) % dp_count) for i in range(dp_count)])
         for k in range(1, dp_count)
     ]
-    gate_total, up_total, down_total = whole(
-        totals_kernel, [((share, col_width), BF16)] * 3, inputs=dp_count
-    )(*parts)
     grad_tokens = lax.dot_general(
         table,
         back[:, :slot_width].reshape(-1, col_width),
         (((0,), (0,)), ((), ())),
         preferred_element_type=F32,
-    )
+    ).astype(BF16)
+    gate_total, up_total, down_total = whole(
+        totals_kernel, [((share, col_width), BF16)] * 3, inputs=dp_count, late=1
+    )(*parts, grad_tokens)
     route_got = back[:, slot_width].astype(F32)
     route_total = jnp.where(
         live_slots, route_got[:, :slot_width] + route_got[:, slot_width:], 0.0
@@ -546,7 +563,7 @@
         taps_heads,
         taps_shared,
         rate_total,
-        grad_tokens.astype(BF16)[None],
+        grad_tokens[None],
         route_total[None, None],
         gate_total.T[None],
         up_total.T[None],

time: 248 us -> 247 us (level)
  starting transfers between devices: 82.3 us -> 79.3 us
    all_to_all x6, starting transfers between devices: 67.2 us -> 64.4 us  [exchange(): return lax.all_to_all(value, axis, split_axis=0, concat_axis=0, tiled=True)]
  transfers between devices with their start and end apart: 14 -> 14, of which waited for: 9 -> 8; matrix products, arithmetic and copies ran while one was open for 4% -> 5% of each run, Pallas kernels for 10% -> 9%
where the time goes in v9:
time: 247 us; the launch traced here: 244 us
  starting transfers between devices  79.3 us (32%)
  waiting for transfers between devices  70.3 us (28%)
  blocking collectives  34.9 us (14%)
  Pallas kernels  28 us (11%)
  between operations  14.3 us (6%)
  local copies, waits for them, and re-layouts  8.46 us (3%)
  other arithmetic  4.57 us (2%)
  matrix products  4.48 us (2%)
    all_to_all x6, starting transfers between devices, exchange(): return lax.all_to_all(value, axis, split_axis=0, concat_axis=0, tiled=True)  64.4 us
    all_to_all x6, waiting for transfers between devices, exchange(): return lax.all_to_all(value, axis, split_axis=0, concat_axis=0, tiled=True)  41.8 us
    all_to_all x2, blocking collectives, exchange(): return lax.all_to_all(value, axis, split_axis=0, concat_axis=0, tiled=True)  34.9 us
    all_gather x1, waiting for transfers between devices, body(): everything = lax.all_gather(own_rows, 'ctx', axis=0, tiled=True)  21 us
    ppermute x3, starting transfers between devices, body(): lax.ppermute(parts[k], 'dp', [(i, (i + k) % dp_count) for i in range(dp_c...  10.8 us
    ppermute x3, waiting for transfers between devices, body(): lax.ppermute(parts[k], 'dp', [(i, (i + k) % dp_count) for i in range(dp_c...  7.42 us
    pallas_call x1, Pallas kernels, body(): whole(back_kernel, [((length, split_at), BF16), ((16, split_at), F32), ((...  6.88 us
    pallas_call x1, Pallas kernels, body(): whole(rows_kernel, [((expert_count, slot_width + 16, col_width), BF16)] +...  6.38 us
  transfers between devices with their start and end apart: 14, of which 8 were waited for; matrix products, arithmetic and copies ran while one was open for 5% of the time, Pallas kernels for 9%

profile of v9, /device:TPU:1, one launch (start us, length us, event | category | flops | bytes accessed | tf_op | source)
XLA Modules:
  0.0 244.3 jit_solution(5671316898913446466)
XLA Ops:
  7.2 2.4 shard_map.267
  9.5 10.3 %all-to-all-start = ((bf16[8,144,256]{2,1,0:T(8,128)(2,1)}), bf16[8,144,256]{2,1,0:T(8,128)(2,1)S(1)}, u32[]{:S(2)}, u32[]{:S(2)}) async-start(bf16[8,144,256]{2,1,0:T(8,128)(2,1)} %shard_map.267), calls=%async_computation | async-start | bytes 1179648 | tf_op jit(solution)/shard_map/all_to_all | solution.py:20
  21.3 1.3 collective-permute-start
  24.4 3.9 %shard_map.266 = bf16[16,80,128]{2,1,0:T(8,128)(2,1)} custom-call(bf16[256,512]{1,0:T(8,128)(2,1)} %bitcast.76, bf16[256,256]{1,0:T(8,128)(2,1)} %bitcast.73, bf16[3,768]{1,0:T(4,128)(2,1)} %copy-done.4, f32[8,256]{1,0:T(8,128)} %bitcast.80, f32[3,8]{1,0:T(4,128)} %pad_maximum_fusion.1.gains_ref, f32[4,512]{1,0:T(4,128)} %tapsx_ref.3, f32[4,256]{1,0:T(4,128)} %tapsbc_ref.5, ...), custom_call_target="tpu_custom_call" | custom-call | tf_op jit(solution)/shard_map/pallas_call | solution.py:455
  28.3 1.8 all-to-all-done.cot_ref
  30.1 1.8 convolution_convert_fusion
  31.9 26.6 %all_to_all.40.got_ref = bf16[16,80,128]{2,1,0:T(8,128)(2,1)} all-to-all(bf16[16,80,128]{2,1,0:T(8,128)(2,1)S(1)} %copy-done.13), channel_id=1, replica_groups=mesh['dp'=4,'expert'=8,'ctx'=16] {'ctx'}, dimensions={0} | all-to-all | bytes 655360 | tf_op jit(solution)/shard_map/all_to_all | solution.py:20
  58.6 1.8 shard_map.268
  60.4 14.1 %all-to-all-start.2 = ((bf16[16,64,128]{2,1,0:T(8,128)(2,1)}), bf16[16,64,128]{2,1,0:T(8,128)(2,1)S(1)}, u32[]{:S(2)}, u32[]{:S(2)}) async-start(bf16[16,64,128]{2,1,0:T(8,128)(2,1)} %shard_map.268), calls=%async_computation.2 | async-start | bytes 524288 | tf_op jit(solution)/shard_map/all_to_all | solution.py:20
  74.5 1.3 fusion.2
  75.8 15.0 %all-to-all-done.2.got_ref = bf16[16,64,128]{2,1,0:T(8,128)(2,1)S(1)} async-done(((bf16[16,64,128]{2,1,0:T(8,128)(2,1)}), bf16[16,64,128]{2,1,0:T(8,128)(2,1)S(1)}, u32[]{:S(2)}, u32[]{:S(2)}) %all-to-all-start.2) | async-done | bytes 262176 | tf_op jit(solution)/shard_map/all_to_all | solution.py:20
  90.9 9.6 %all-to-all-start.3 = ((bf16[8,128,256]{2,1,0:T(8,128)(2,1)}), bf16[8,128,256]{2,1,0:T(8,128)(2,1)S(1)}, u32[]{:S(2)}, u32[]{:S(2)}) async-start(bf16[8,128,256]{2,1,0:T(8,128)(2,1)} %bitcast.20), calls=%async_computation.3 | async-start | bytes 1048576 | tf_op jit(solution)/shard_map/all_to_all | solution.py:20
  101.4 6.9 %shard_map.269 = (bf16[256,512]{1,0:T(8,128)(2,1)}, f32[16,512]{1,0:T(8,128)S(1)}, f32[8,512]{1,0:T(8,128)S(1)}, bf16[8,256,256]{2,1,0:T(8,128)(2,1)}, f32[8,256...) custom-call(bf16[256,512]{1,0:T(8,128)(2,1)S(1)} %bitcast.77, bf16[256,256]{1,0:T(8,128)(2,1)S(1)} %bitcast.75, ...), custom_call_target="tpu_custom_call" | custom-call | tf_op jit(solution)/shard_map/pallas_call | solution.py:474
  108.2 1.7 all-to-all-done.3.second_ref.in_ref
  110.8 1.9 shard_map.271
  112.8 10.0 %all-to-all-start.4 = ((bf16[8,256,256]{2,1,0:T(8,128)(2,1)}), bf16[8,256,256]{2,1,0:T(8,128)(2,1)S(1)}, u32[]{:S(2)}, u32[]{:S(2)}) async-start(bf16[8,256,256]{2,1,0:T(8,128)(2,1)} %get-tuple-element.41), calls=%async_computation.4 | async-start | bytes 2097152 | tf_op jit(solution)/shard_map/all_to_all | solution.py:20
  122.8 15.1 %all-to-all-done.4.got_ref = bf16[8,256,256]{2,1,0:T(8,128)(2,1)S(1)} async-done(((bf16[8,256,256]{2,1,0:T(8,128)(2,1)}), bf16[8,256,256]{2,1,0:T(8,128)(2,1)S(1)}, u32[]{:S(2)}, u32[]{:S(2)}) %all-to-all-start.4) | async-done | bytes 1048608 | tf_op jit(solution)/shard_map/all_to_all | solution.py:20
  138.9 2.8 %shard_map.270 = (bf16[256,256]{1,0:T(8,128)(2,1)}, f32[16,256]{1,0:T(8,128)}, f32[8,256]{1,0:T(8,128)}, f32[4,256]{1,0:T(4,128)}) custom-call(bf16[256,256]{1,0:T(8,128)(2,1)} %bitcast.74, bf16[3,768]{1,0:T(4,128)(2,1)} %copy-done.4, f32[4,256]{1,0:T(4,128)} %tapsbc_ref.5, bf16[8,256,256]{2,1,0:T(8,128)(2,1)} %copy-done.12), custom_call_target="tpu_custom_call" | custom-call | tf_op jit(solution)/shard_map/pallas_call | solution.py:501
  142.4 8.3 %all_to_all.41 = f32[4,8,128]{2,1,0:T(8,128)S(1)} all-to-all(f32[4,8,128]{2,1,0:T(8,128)S(1)} %bitcast.91), channel_id=1, replica_groups=mesh['dp'=4,'expert'=8,'ctx'=16] {'dp'}, dimensions={0} | all-to-all | bytes 32768 | tf_op jit(solution)/shard_map/all_to_all | solution.py:20
  151.3 9.4 %all-to-all-start.6 = ((f32[16,8,128]{2,1,0:T(8,128)}), f32[16,8,128]{2,1,0:T(8,128)S(1)}, u32[]{:S(2)}, u32[]{:S(2)}) async-start(f32[16,8,128]{2,1,0:T(8,128)} %broadcast_in_dim.76), calls=%async_computation.6 | async-start | bytes 131072 | tf_op jit(solution)/shard_map/all_to_all | solution.py:20
  160.8 1.3 collective-permute-start.1
  162.8 1.5 collective-permute-start.2
  164.2 8.2 %all-to-all-done.6 = f32[16,8,128]{2,1,0:T(8,128)S(1)} async-done(((f32[16,8,128]{2,1,0:T(8,128)}), f32[16,8,128]{2,1,0:T(8,128)S(1)}, u32[]{:S(2)}, u32[]{:S(2)}) %all-to-all-start.6) | async-done | bytes 65568 | tf_op jit(solution)/shard_map/all_to_all | solution.py:20
  173.1 21.0 %all-gather.2.cloned.1.call-done.all_ref = bf16[1024,2432]{1,0:T(8,128)(2,1)} async-done(((bf16[64,2432]{1,0:T(8,128)(2,1)}), bf16[1024,2432]{1,0:T(8,128)(2,1)}) %all-gather.2.cloned.1.call-update) | async-done | bytes 4980752 | tf_op jit(solution)/shard_map/all_gather | solution.py:497
  194.1 6.4 %shard_map.272 = (bf16[8,144,256]{2,1,0:T(8,128)(2,1)}, bf16[576,256]{1,0:T(8,128)(2,1)}, bf16[576,256]{1,0:T(8,128)(2,1)}, bf16[576,256]{1,0:T(8,128)(2,1)}, bf16[576,256]{1,0:T(8,128)(2,1)}) custom-call(s32[1]{0:T(128)} %bitcast.27.place_ref, bf16[1024,2432]{1,0:T(8,128)(2,1)} %all-gather.2.cloned.1.call-done.all_ref, bf16[8,128,256]{2,1,0:T(8,128)(2,1)} %copy-done.11, ...), custom_call_target="tpu_custom_call" | custom-call | tf_op jit(solution)/shard_map/pallas_call | solution.py:532
  200.5 10.9 %all-to-all-start.7 = ((bf16[8,144,256]{2,1,0:T(8,128)(2,1)}), bf16[8,144,256]{2,1,0:T(8,128)(2,1)S(1)}, u32[]{:S(2)}, u32[]{:S(2)}) async-start(bf16[8,144,256]{2,1,0:T(8,128)(2,1)} %get-tuple-element.49), calls=%async_computation.8 | async-start | bytes 1179648 | tf_op jit(solution)/shard_map/all_to_all | solution.py:20
  214.3 3.0 %collective-permute-start.3 = (bf16[576,256]{1,0:T(8,128)(2,1)}, bf16[576,256]{1,0:T(8,128)(2,1)S(1)}, u32[]{:S(2)}, u32[]{:S(2)}) collective-permute-start(bf16[576,256]{1,0:T(8,128)(2,1)} %get-tuple-element.51), channel_id=1, source_target_pairs={{0,128},{128,256},{256,384},{384,0},{1,129},{129,257},{257,385},{3... | collective-permute-start | bytes 884744 | tf_op jit(solution)/shard_map/ppermute | solution.py:543
  217.2 4.5 %collective-permute-start.4 = (bf16[576,256]{1,0:T(8,128)(2,1)}, bf16[576,256]{1,0:T(8,128)(2,1)S(1)}, u32[]{:S(2)}, u32[]{:S(2)}) collective-permute-start(bf16[576,256]{1,0:T(8,128)(2,1)} %get-tuple-element.52), channel_id=1, source_target_pairs={{0,256},{128,384},{256,0},{384,128},{1,257},{129,385},{257,1},{385... | collective-permute-start | bytes 884744 | tf_op jit(solution)/shard_map/ppermute | solution.py:543
  221.7 3.4 %collective-permute-start.5 = (bf16[576,256]{1,0:T(8,128)(2,1)}, bf16[576,256]{1,0:T(8,128)(2,1)S(1)}, u32[]{:S(2)}, u32[]{:S(2)}) collective-permute-start(bf16[576,256]{1,0:T(8,128)(2,1)} %get-tuple-element.53), channel_id=1, source_target_pairs={{0,384},{128,0},{256,128},{384,256},{1,385},{129,1},{257,129},{385... | collective-permute-start | bytes 884744 | tf_op jit(solution)/shard_map/ppermute | solution.py:543
  225.9 1.4 fusion.3.refs_4_
  227.3 6.2 %collective-permute-done.4.refs_2_ = bf16[576,256]{1,0:T(8,128)(2,1)S(1)} collective-permute-done((bf16[576,256]{1,0:T(8,128)(2,1)}, bf16[576,256]{1,0:T(8,128)(2,1)S(1)}, u32[]{:S(2)}, u32[]{:S(2)}) %collective-permute-start.4) | collective-permute-done | bytes 294944 | tf_op jit(solution)/shard_map/ppermute | solution.py:543
  235.4 2.0 shard_map.273
  (83 shorter events, 14.3 us)
Async XLA Ops:
  7.2 22.9 %copy-start = (bf16[1,768,256]{2,1,0:T(8,128)(2,1)S(1)}, bf16[1,768,256]{2,1,0:T(8,128)(2,1)}, u32[]{:S(2)}) copy-start(bf16[1,768,256]{2,1,0:T(8,128)(2,1)} %param.35) | copy-start | bytes 1179652
  9.5 20.5 %all-to-all-start = ((bf16[8,144,256]{2,1,0:T(8,128)(2,1)}), bf16[8,144,256]{2,1,0:T(8,128)(2,1)S(1)}, u32[]{:S(2)}, u32[]{:S(2)}) async-start(bf16[8,144,256]{2,1,0:T(8,128)(2,1)} %shard_map.267), calls=%async_computation | async-start | bytes 1179648 | tf_op jit(solution)/shard_map/all_to_all | solution.py:20
  19.9 90.1 %reduce-scatter.2.cloned.1.call-start = ((), (), s32[]{:S(2)}) async-start(), calls=%async_computation.9 | async-start | bytes 1671168 | tf_op jit(solution)/shard_map/reduce_scatter | solution.py:464
  21.3 2.6 %collective-permute-start = (bf16[3,768]{1,0:T(4,128)(2,1)S(1)}, bf16[3,768]{1,0:T(4,128)(2,1)S(1)}, u32[]{:S(2)}, u32[]{:S(2)}) collective-permute-start(bf16[3,768]{1,0:T(4,128)(2,1)S(1)} %pad_maximum_fusion), channel_id=1, source_target_pairs={{0,1},{1,2},{2,3},{3,4},{4,5},{5,6},{6,7},{7,8},{8,9},{9,10},{10,1... | collective-permute-start | bytes 13832 | tf_op jit(solution)/shard_map/ppermute | solution.py:16
  30.1 70.4 %copy-start.10 = (bf16[8,144,256]{2,1,0:T(8,128)(2,1)}, bf16[8,144,256]{2,1,0:T(8,128)(2,1)S(1)}, u32[]{:S(2)}) copy-start(bf16[8,144,256]{2,1,0:T(8,128)(2,1)S(1)} %all-to-all-done.cot_ref) | copy-start | bytes 1769476
  30.1 1.8 copy-start.13
  31.9 42.5 %copy-start.18 = (s32[1,1,8,128]{3,2,1,0:T(8,128)S(1)}, s32[1,1,8,128]{3,2,1,0:T(8,128)}, u32[]{:S(2)}) copy-start(s32[1,1,8,128]{3,2,1,0:T(8,128)} %param.30) | copy-start | bytes 12292
  31.9 42.6 %copy-start.20 = (s32[1,1,8]{2,1,0:T(1,128)S(1)}, s32[1,1,8]{2,1,0:T(1,128)}, u32[]{:S(2)}) copy-start(s32[1,1,8]{2,1,0:T(1,128)} %param.31) | copy-start | bytes 100
  31.9 42.6 %copy-start.21 = (bf16[1,512,256]{2,1,0:T(8,128)(2,1)S(1)}, bf16[1,512,256]{2,1,0:T(8,128)(2,1)}, u32[]{:S(2)}) copy-start(bf16[1,512,256]{2,1,0:T(8,128)(2,1)} %param.28) | copy-start | bytes 786436
  60.3 41.0 %copy-start.1 = (bf16[1,256,256]{2,1,0:T(8,128)(2,1)S(1)}, bf16[1,256,256]{2,1,0:T(8,128)(2,1)}, u32[]{:S(2)}) copy-start(bf16[1,256,256]{2,1,0:T(8,128)(2,1)} %param.20) | copy-start | bytes 393220
  60.3 41.0 %copy-start.2 = (bf16[1,256,512]{2,1,0:T(8,128)(2,1)S(1)}, bf16[1,256,512]{2,1,0:T(8,128)(2,1)}, u32[]{:S(2)}) copy-start(bf16[1,256,512]{2,1,0:T(8,128)(2,1)} %param.19) | copy-start | bytes 786436
  60.3 41.0 %copy-start.3 = (bf16[1,256,512]{2,1,0:T(8,128)(2,1)S(1)}, bf16[1,256,512]{2,1,0:T(8,128)(2,1)}, u32[]{:S(2)}) copy-start(bf16[1,256,512]{2,1,0:T(8,128)(2,1)} %param.27) | copy-start | bytes 786436
  60.3 41.0 %copy-start.5 = (bf16[3,768]{1,0:T(4,128)(2,1)S(1)}, bf16[3,768]{1,0:T(4,128)(2,1)}, u32[]{:S(2)}) copy-start(bf16[3,768]{1,0:T(4,128)(2,1)} %copy-done.4) | copy-start | bytes 13828
  60.3 41.0 %copy-start.6 = (f32[4,256]{1,0:T(4,128)S(1)}, f32[4,256]{1,0:T(4,128)}, u32[]{:S(2)}) copy-start(f32[4,256]{1,0:T(4,128)} %tapsbc_ref.5) | copy-start | bytes 12292
  60.3 41.0 %copy-start.7 = (f32[1,8,256]{2,1,0:T(8,128)S(1)}, f32[1,8,256]{2,1,0:T(8,128)}, u32[]{:S(2)}) copy-start(f32[1,8,256]{2,1,0:T(8,128)} %param.21) | copy-start | bytes 24580
  60.3 41.0 %copy-start.8 = (f32[4,512]{1,0:T(4,128)S(1)}, f32[4,512]{1,0:T(4,128)}, u32[]{:S(2)}) copy-start(f32[4,512]{1,0:T(4,128)} %tapsx_ref.3) | copy-start | bytes 24580
  60.4 41.0 %copy-start.9 = (f32[3,8]{1,0:T(4,128)S(1)}, f32[3,8]{1,0:T(4,128)}, u32[]{:S(2)}) copy-start(f32[3,8]{1,0:T(4,128)} %pad_maximum_fusion.1.gains_ref) | copy-start | bytes 292
  60.4 30.5 %all-to-all-start.2 = ((bf16[16,64,128]{2,1,0:T(8,128)(2,1)}), bf16[16,64,128]{2,1,0:T(8,128)(2,1)S(1)}, u32[]{:S(2)}, u32[]{:S(2)}) async-start(bf16[16,64,128]{2,1,0:T(8,128)(2,1)} %shard_map.268), calls=%async_computation.2 | async-start | bytes 524288 | tf_op jit(solution)/shard_map/all_to_all | solution.py:20
  90.9 19.1 %all-to-all-start.3 = ((bf16[8,128,256]{2,1,0:T(8,128)(2,1)}), bf16[8,128,256]{2,1,0:T(8,128)(2,1)S(1)}, u32[]{:S(2)}, u32[]{:S(2)}) async-start(bf16[8,128,256]{2,1,0:T(8,128)(2,1)} %bitcast.20), calls=%async_computation.3 | async-start | bytes 1048576 | tf_op jit(solution)/shard_map/all_to_all | solution.py:20
  100.5 93.6 %all-gather.2.cloned.1.call-start = ((), (), s32[]{:S(2)}) async-start(), calls=%async_computation.10 | async-start | bytes 5292032 | tf_op jit(solution)/shard_map/all_gather | solution.py:497
  112.8 25.1 %all-to-all-start.4 = ((bf16[8,256,256]{2,1,0:T(8,128)(2,1)}), bf16[8,256,256]{2,1,0:T(8,128)(2,1)S(1)}, u32[]{:S(2)}, u32[]{:S(2)}) async-start(bf16[8,256,256]{2,1,0:T(8,128)(2,1)} %get-tuple-element.41), calls=%async_computation.4 | async-start | bytes 2097152 | tf_op jit(solution)/shard_map/all_to_all | solution.py:20
  151.3 21.2 %all-to-all-start.6 = ((f32[16,8,128]{2,1,0:T(8,128)}), f32[16,8,128]{2,1,0:T(8,128)S(1)}, u32[]{:S(2)}, u32[]{:S(2)}) async-start(f32[16,8,128]{2,1,0:T(8,128)} %broadcast_in_dim.76), calls=%async_computation.6 | async-start | bytes 131072 | tf_op jit(solution)/shard_map/all_to_all | solution.py:20
  160.8 50.6 %collective-permute-start.1 = (f32[3,512]{1,0:T(4,128)S(1)}, f32[3,512]{1,0:T(4,128)S(1)}, u32[]{:S(2)}, u32[]{:S(2)}) collective-permute-start(f32[3,512]{1,0:T(4,128)S(1)} %slice.55), channel_id=1, source_target_pairs={{1,0},{2,1},{3,2},{4,3},{5,4},{6,5},{7,6},{8,7},{9,8},{10,9},{11,1... | collective-permute-start | bytes 18440 | tf_op jit(solution)/shard_map/ppermute | solution.py:16
  162.8 49.2 %collective-permute-start.2 = (f32[3,256]{1,0:T(4,128)S(1)}, f32[3,256]{1,0:T(4,128)S(1)}, u32[]{:S(2)}, u32[]{:S(2)}) collective-permute-start(f32[3,256]{1,0:T(4,128)S(1)} %slice.56), channel_id=1, source_target_pairs={{1,0},{2,1},{3,2},{4,3},{5,4},{6,5},{7,6},{8,7},{9,8},{10,9},{11,1... | collective-permute-start | bytes 9224 | tf_op jit(solution)/shard_map/ppermute | solution.py:16
  194.1 17.9 %copy-start.19 = (f32[16,256]{1,0:T(8,128)S(1)}, f32[16,256]{1,0:T(8,128)}, u32[]{:S(2)}) copy-start(f32[16,256]{1,0:T(8,128)} %get-tuple-element.43) | copy-start | bytes 49156
  194.1 18.5 %copy-start.17 = (f32[8,128]{1,0:T(8,128)S(1)}, f32[8,128]{1,0:T(8,128)}, u32[]{:S(2)}) copy-start(f32[8,128]{1,0:T(8,128)} %reduce_sum.19) | copy-start | bytes 12292
  200.5 24.7 %all-to-all-start.7 = ((bf16[8,144,256]{2,1,0:T(8,128)(2,1)}), bf16[8,144,256]{2,1,0:T(8,128)(2,1)S(1)}, u32[]{:S(2)}, u32[]{:S(2)}) async-start(bf16[8,144,256]{2,1,0:T(8,128)(2,1)} %get-tuple-element.49), calls=%async_computation.8 | async-start | bytes 1179648 | tf_op jit(solution)/shard_map/all_to_all | solution.py:20
  214.3 13.0 %collective-permute-start.3 = (bf16[576,256]{1,0:T(8,128)(2,1)}, bf16[576,256]{1,0:T(8,128)(2,1)S(1)}, u32[]{:S(2)}, u32[]{:S(2)}) collective-permute-start(bf16[576,256]{1,0:T(8,128)(2,1)} %get-tuple-element.51), channel_id=1, source_target_pairs={{0,128},{128,256},{256,384},{384,0},{1,129},{129,257},{257,385},{3... | collective-permute-start | bytes 884744 | tf_op jit(solution)/shard_map/ppermute | solution.py:543
  217.2 16.2 %collective-permute-start.4 = (bf16[576,256]{1,0:T(8,128)(2,1)}, bf16[576,256]{1,0:T(8,128)(2,1)S(1)}, u32[]{:S(2)}, u32[]{:S(2)}) collective-permute-start(bf16[576,256]{1,0:T(8,128)(2,1)} %get-tuple-element.52), channel_id=1, source_target_pairs={{0,256},{128,384},{256,0},{384,128},{1,257},{129,385},{257,1},{385... | collective-permute-start | bytes 884744 | tf_op jit(solution)/shard_map/ppermute | solution.py:543
  221.7 13.0 %collective-permute-start.5 = (bf16[576,256]{1,0:T(8,128)(2,1)}, bf16[576,256]{1,0:T(8,128)(2,1)S(1)}, u32[]{:S(2)}, u32[]{:S(2)}) collective-permute-start(bf16[576,256]{1,0:T(8,128)(2,1)} %get-tuple-element.53), channel_id=1, source_target_pairs={{0,384},{128,0},{256,128},{384,256},{1,385},{129,1},{257,129},{385... | collective-permute-start | bytes 884744 | tf_op jit(solution)/shard_map/ppermute | solution.py:543
  227.3 7.4 %copy-start.14 = (bf16[576,256]{1,0:T(8,128)(2,1)}, bf16[576,256]{1,0:T(8,128)(2,1)S(1)}, u32[]{:S(2)}) copy-start(bf16[576,256]{1,0:T(8,128)(2,1)S(1)} %collective-permute-done.3.refs_1_) | copy-start | bytes 884740
  233.5 1.2 copy-start.15
  (4 other events, 3.1 us)
Sparse Core Ops, SparseCore 0:
  32.0 75.9 reduce-scatter.1
  112.9 81.1 all-gather.1

commit v10 on v9

--- a/solution.py
+++ b/solution.py
@@ -303,11 +303,8 @@
     ).astype(BF16)
 
 
-def rows_kernel(
-    place_ref, all_ref, in_ref, cot_ref, gatew_ref, upw_ref, earlier_ref, back_ref, *refs
-):
-    del earlier_ref
-    out_refs, grads_ref = refs[:-1], refs[-1]
+def rows_kernel(place_ref, all_ref, in_ref, cot_ref, gatew_ref, upw_ref, *refs):
+    back_ref, out_refs, grads_ref = refs[-6], refs[-5:-1], refs[-1]
     groups, slots, cols = in_ref.shape
     width = gatew_ref.shape[1]
     owners = len(out_refs)
@@ -535,9 +532,12 @@
         [((3, hidden_width, col_width), BF16)],
         inputs=5,
         scalars=1,
-        late=1,
+        late=4,
         limit=56 * 2**20,
-    )(owner, everything, rows_in, got_cot, w_gate[0], w_up[0], small)
+    )(
+        owner, everything, rows_in, got_cot, w_gate[0], w_up[0], grad_mamba_in, grad_shared_in,
+        taps_heads, taps_shared,
+    )
     back = exchange(back, "expert")
     parts = [parts[0]] + [
         lax.ppermute(parts[k], "dp", [(i, (i + k) % dp_count) for i in range(dp_count)])

time: 247 us -> 244 us (0.988)
  blocking collectives: 34.9 us -> 26.6 us
  starting transfers between devices: 79.3 us -> 85 us
    all_to_all x2 -> x1, blocking collectives: 34.9 us -> 26.6 us  [exchange(): return lax.all_to_all(value, axis, split_axis=0, concat_axis=0, tiled=True)]
    all_to_all x6 -> x7, starting transfers between devices: 64.4 us -> 70.8 us  [exchange(): return lax.all_to_all(value, axis, split_axis=0, concat_axis=0, tiled=True)]
    all_gather x1, waiting for transfers between devices: 21 us -> 17.4 us  [body(): everything = lax.all_gather(own_rows, 'ctx', axis=0, tiled=True)]
    all_to_all x6 -> x7, waiting for transfers between devices: 41.8 us -> 44.6 us  [exchange(): return lax.all_to_all(value, axis, split_axis=0, concat_axis=0, tiled=True)]
  transfers between devices with their start and end apart: 14 -> 15, of which waited for: 8 -> 9; matrix products, arithmetic and copies ran while one was open for 5% -> 5% of each run, Pallas kernels for 9% -> 6%
where the time goes in v10:
time: 244 us; the launch traced here: 242 us
  starting transfers between devices  85 us (35%)
  waiting for transfers between devices  70 us (29%)
  Pallas kernels  28 us (11%)
  blocking collectives  26.6 us (11%)
  between operations  14.3 us (6%)
  local copies, waits for them, and re-layouts  9.06 us (4%)
  other arithmetic  4.69 us (2%)
  matrix products  4.48 us (2%)
    all_to_all x7, starting transfers between devices, exchange(): return lax.all_to_all(value, axis, split_axis=0, concat_axis=0, tiled=True)  70.8 us
    all_to_all x7, waiting for transfers between devices, exchange(): return lax.all_to_all(value, axis, split_axis=0, concat_axis=0, tiled=True)  44.6 us
    all_to_all x1, blocking collectives, exchange(): return lax.all_to_all(value, axis, split_axis=0, concat_axis=0, tiled=True)  26.6 us
    all_gather x1, waiting for transfers between devices, body(): everything = lax.all_gather(own_rows, 'ctx', axis=0, tiled=True)  17.4 us
    ppermute x3, starting transfers between devices, body(): lax.ppermute(parts[k], 'dp', [(i, (i + k) % dp_count) for i in range(dp_c...  10.3 us
    ppermute x3, waiting for transfers between devices, body(): lax.ppermute(parts[k], 'dp', [(i, (i + k) % dp_count) for i in range(dp_c...  8.01 us
    pallas_call x1, Pallas kernels, body(): whole(back_kernel, [((length, split_at), BF16), ((16, split_at), F32), ((...  6.88 us
    pallas_call x1, Pallas kernels, body(): whole(rows_kernel, [((expert_count, slot_width + 16, col_width), BF16)] +...  6.35 us
  transfers between devices with their start and end apart: 15, of which 9 were waited for; matrix products, arithmetic and copies ran while one was open for 5% of the time, Pallas kernels for 6%

profile of v10, /device:TPU:1, one launch (start us, length us, event | category | flops | bytes accessed | tf_op | source)
XLA Modules:
  0.0 242.2 jit_solution(6502932364460814117)
XLA Ops:
  7.2 2.4 shard_map.267
  9.5 10.3 %all-to-all-start = ((bf16[8,144,256]{2,1,0:T(8,128)(2,1)}), bf16[8,144,256]{2,1,0:T(8,128)(2,1)S(1)}, u32[]{:S(2)}, u32[]{:S(2)}) async-start(bf16[8,144,256]{2,1,0:T(8,128)(2,1)} %shard_map.267), calls=%async_computation | async-start | bytes 1179648 | tf_op jit(solution)/shard_map/all_to_all | solution.py:20
  21.3 1.3 collective-permute-start
  24.4 3.9 %shard_map.266 = bf16[16,80,128]{2,1,0:T(8,128)(2,1)} custom-call(bf16[256,512]{1,0:T(8,128)(2,1)} %bitcast.68, bf16[256,256]{1,0:T(8,128)(2,1)} %bitcast.65, bf16[3,768]{1,0:T(4,128)(2,1)} %copy-done.4, f32[8,256]{1,0:T(8,128)} %bitcast.72, f32[3,8]{1,0:T(4,128)} %pad_maximum_fusion.1.gains_ref, f32[4,512]{1,0:T(4,128)} %tapsx_ref.3, f32[4,256]{1,0:T(4,128)} %tapsbc_ref.5, ...), custom_call_target="tpu_custom_call" | custom-call | tf_op jit(solution)/shard_map/pallas_call | solution.py:452
  28.3 1.8 all-to-all-done.cot_ref
  30.1 1.8 convolution_convert_fusion
  31.9 26.6 %all_to_all.40.got_ref = bf16[16,80,128]{2,1,0:T(8,128)(2,1)} all-to-all(bf16[16,80,128]{2,1,0:T(8,128)(2,1)S(1)} %copy-done.13), channel_id=1, replica_groups=mesh['dp'=4,'expert'=8,'ctx'=16] {'ctx'}, dimensions={0} | all-to-all | bytes 655360 | tf_op jit(solution)/shard_map/all_to_all | solution.py:20
  58.6 1.8 shard_map.268
  60.4 14.1 %all-to-all-start.2 = ((bf16[16,64,128]{2,1,0:T(8,128)(2,1)}), bf16[16,64,128]{2,1,0:T(8,128)(2,1)S(1)}, u32[]{:S(2)}, u32[]{:S(2)}) async-start(bf16[16,64,128]{2,1,0:T(8,128)(2,1)} %shard_map.268), calls=%async_computation.2 | async-start | bytes 524288 | tf_op jit(solution)/shard_map/all_to_all | solution.py:20
  74.5 1.3 fusion.2
  75.8 15.0 %all-to-all-done.2.got_ref = bf16[16,64,128]{2,1,0:T(8,128)(2,1)S(1)} async-done(((bf16[16,64,128]{2,1,0:T(8,128)(2,1)}), bf16[16,64,128]{2,1,0:T(8,128)(2,1)S(1)}, u32[]{:S(2)}, u32[]{:S(2)}) %all-to-all-start.2) | async-done | bytes 262176 | tf_op jit(solution)/shard_map/all_to_all | solution.py:20
  90.9 9.6 %all-to-all-start.3 = ((bf16[8,128,256]{2,1,0:T(8,128)(2,1)}), bf16[8,128,256]{2,1,0:T(8,128)(2,1)S(1)}, u32[]{:S(2)}, u32[]{:S(2)}) async-start(bf16[8,128,256]{2,1,0:T(8,128)(2,1)} %bitcast.19), calls=%async_computation.3 | async-start | bytes 1048576 | tf_op jit(solution)/shard_map/all_to_all | solution.py:20
  101.4 6.9 %shard_map.269 = (bf16[256,512]{1,0:T(8,128)(2,1)}, f32[16,512]{1,0:T(8,128)S(1)}, f32[8,512]{1,0:T(8,128)S(1)}, bf16[8,256,256]{2,1,0:T(8,128)(2,1)}, f32[8,256...) custom-call(bf16[256,512]{1,0:T(8,128)(2,1)S(1)} %bitcast.69, bf16[256,256]{1,0:T(8,128)(2,1)S(1)} %bitcast.67, ...), custom_call_target="tpu_custom_call" | custom-call | tf_op jit(solution)/shard_map/pallas_call | solution.py:471
  108.2 1.7 all-to-all-done.3.second_ref.in_ref
  110.8 1.9 shard_map.271
  112.8 10.0 %all-to-all-start.4 = ((bf16[8,256,256]{2,1,0:T(8,128)(2,1)}), bf16[8,256,256]{2,1,0:T(8,128)(2,1)S(1)}, u32[]{:S(2)}, u32[]{:S(2)}) async-start(bf16[8,256,256]{2,1,0:T(8,128)(2,1)} %get-tuple-element.41), calls=%async_computation.4 | async-start | bytes 2097152 | tf_op jit(solution)/shard_map/all_to_all | solution.py:20
  122.8 15.1 %all-to-all-done.4.got_ref = bf16[8,256,256]{2,1,0:T(8,128)(2,1)S(1)} async-done(((bf16[8,256,256]{2,1,0:T(8,128)(2,1)}), bf16[8,256,256]{2,1,0:T(8,128)(2,1)S(1)}, u32[]{:S(2)}, u32[]{:S(2)}) %all-to-all-start.4) | async-done | bytes 1048608 | tf_op jit(solution)/shard_map/all_to_all | solution.py:20
  138.9 2.8 %shard_map.270 = (bf16[256,256]{1,0:T(8,128)(2,1)}, f32[16,256]{1,0:T(8,128)}, f32[8,256]{1,0:T(8,128)}, f32[4,256]{1,0:T(4,128)}) custom-call(bf16[256,256]{1,0:T(8,128)(2,1)} %bitcast.66, bf16[3,768]{1,0:T(4,128)(2,1)} %copy-done.4, f32[4,256]{1,0:T(4,128)} %tapsbc_ref.5, bf16[8,256,256]{2,1,0:T(8,128)(2,1)} %copy-done.12), custom_call_target="tpu_custom_call" | custom-call | tf_op jit(solution)/shard_map/pallas_call | solution.py:498
  143.0 4.2 %all-to-all-start.5 = ((f32[4,8,128]{2,1,0:T(8,128)}), f32[4,8,128]{2,1,0:T(8,128)S(1)}, u32[]{:S(2)}, u32[]{:S(2)}) async-start(f32[4,8,128]{2,1,0:T(8,128)} %bitcast.63), calls=%async_computation.5 | async-start | bytes 32768 | tf_op jit(solution)/shard_map/all_to_all | solution.py:20
  152.1 11.2 %all-to-all-start.6 = ((f32[16,8,128]{2,1,0:T(8,128)}), f32[16,8,128]{2,1,0:T(8,128)S(1)}, u32[]{:S(2)}, u32[]{:S(2)}) async-start(f32[16,8,128]{2,1,0:T(8,128)} %broadcast_in_dim.70), calls=%async_computation.6 | async-start | bytes 131072 | tf_op jit(solution)/shard_map/all_to_all | solution.py:20
  163.9 1.3 fusion.13.refs_1_
  165.2 10.1 %all-to-all-done.6 = f32[16,8,128]{2,1,0:T(8,128)S(1)} async-done(((f32[16,8,128]{2,1,0:T(8,128)}), f32[16,8,128]{2,1,0:T(8,128)S(1)}, u32[]{:S(2)}, u32[]{:S(2)}) %all-to-all-start.6) | async-done | bytes 65568 | tf_op jit(solution)/shard_map/all_to_all | solution.py:20
  176.5 17.4 %all-gather.2.cloned.1.call-done.all_ref = bf16[1024,2432]{1,0:T(8,128)(2,1)} async-done(((bf16[64,2432]{1,0:T(8,128)(2,1)}), bf16[1024,2432]{1,0:T(8,128)(2,1)}) %all-gather.2.cloned.1.call-update) | async-done | bytes 4980752 | tf_op jit(solution)/shard_map/all_gather | solution.py:494
  193.8 6.4 %shard_map.272 = (bf16[8,144,256]{2,1,0:T(8,128)(2,1)}, bf16[576,256]{1,0:T(8,128)(2,1)}, bf16[576,256]{1,0:T(8,128)(2,1)}, bf16[576,256]{1,0:T(8,128)(2,1)}, bf16[576,256]{1,0:T(8,128)(2,1)}) custom-call(s32[1]{0:T(128)} %bitcast.25.place_ref, bf16[1024,2432]{1,0:T(8,128)(2,1)} %all-gather.2.cloned.1.call-done.all_ref, bf16[8,128,256]{2,1,0:T(8,128)(2,1)} %copy-done.11, ...), custom_call_target="tpu_custom_call" | custom-call | tf_op jit(solution)/shard_map/pallas_call | solution.py:529
  200.2 11.4 %all-to-all-start.7 = ((bf16[8,144,256]{2,1,0:T(8,128)(2,1)}), bf16[8,144,256]{2,1,0:T(8,128)(2,1)S(1)}, u32[]{:S(2)}, u32[]{:S(2)}) async-start(bf16[8,144,256]{2,1,0:T(8,128)(2,1)} %get-tuple-element.49), calls=%async_computation.8 | async-start | bytes 1179648 | tf_op jit(solution)/shard_map/all_to_all | solution.py:20
  212.1 2.8 %collective-permute-start.3 = (bf16[576,256]{1,0:T(8,128)(2,1)}, bf16[576,256]{1,0:T(8,128)(2,1)S(1)}, u32[]{:S(2)}, u32[]{:S(2)}) collective-permute-start(bf16[576,256]{1,0:T(8,128)(2,1)} %get-tuple-element.51), channel_id=1, source_target_pairs={{0,128},{128,256},{256,384},{384,0},{1,129},{129,257},{257,385},{3... | collective-permute-start | bytes 884744 | tf_op jit(solution)/shard_map/ppermute | solution.py:543
  214.9 4.4 %collective-permute-start.4 = (bf16[576,256]{1,0:T(8,128)(2,1)}, bf16[576,256]{1,0:T(8,128)(2,1)S(1)}, u32[]{:S(2)}, u32[]{:S(2)}) collective-permute-start(bf16[576,256]{1,0:T(8,128)(2,1)} %get-tuple-element.52), channel_id=1, source_target_pairs={{0,256},{128,384},{256,0},{384,128},{1,257},{129,385},{257,1},{385... | collective-permute-start | bytes 884744 | tf_op jit(solution)/shard_map/ppermute | solution.py:543
  219.3 3.1 %collective-permute-start.5 = (bf16[576,256]{1,0:T(8,128)(2,1)}, bf16[576,256]{1,0:T(8,128)(2,1)S(1)}, u32[]{:S(2)}, u32[]{:S(2)}) collective-permute-start(bf16[576,256]{1,0:T(8,128)(2,1)} %get-tuple-element.53), channel_id=1, source_target_pairs={{0,384},{128,0},{256,128},{384,256},{1,385},{129,1},{257,129},{385... | collective-permute-start | bytes 884744 | tf_op jit(solution)/shard_map/ppermute | solution.py:543
  223.2 1.4 fusion.3.refs_4_
  224.6 6.5 %collective-permute-done.4.refs_2_ = bf16[576,256]{1,0:T(8,128)(2,1)S(1)} collective-permute-done((bf16[576,256]{1,0:T(8,128)(2,1)}, bf16[576,256]{1,0:T(8,128)(2,1)S(1)}, u32[]{:S(2)}, u32[]{:S(2)}) %collective-permute-start.4) | collective-permute-done | bytes 294944 | tf_op jit(solution)/shard_map/ppermute | solution.py:543
  231.1 1.5 collective-permute-done.5.refs_3_
  233.3 2.0 shard_map.273
  (80 shorter events, 16.0 us)
Async XLA Ops:
  7.2 22.9 %copy-start = (bf16[1,768,256]{2,1,0:T(8,128)(2,1)S(1)}, bf16[1,768,256]{2,1,0:T(8,128)(2,1)}, u32[]{:S(2)}) copy-start(bf16[1,768,256]{2,1,0:T(8,128)(2,1)} %param.35) | copy-start | bytes 1179652
  9.5 20.5 %all-to-all-start = ((bf16[8,144,256]{2,1,0:T(8,128)(2,1)}), bf16[8,144,256]{2,1,0:T(8,128)(2,1)S(1)}, u32[]{:S(2)}, u32[]{:S(2)}) async-start(bf16[8,144,256]{2,1,0:T(8,128)(2,1)} %shard_map.267), calls=%async_computation | async-start | bytes 1179648 | tf_op jit(solution)/shard_map/all_to_all | solution.py:20
  19.9 90.1 %reduce-scatter.2.cloned.1.call-start = ((), (), s32[]{:S(2)}) async-start(), calls=%async_computation.9 | async-start | bytes 1671168 | tf_op jit(solution)/shard_map/reduce_scatter | solution.py:461
  21.3 2.6 %collective-permute-start = (bf16[3,768]{1,0:T(4,128)(2,1)S(1)}, bf16[3,768]{1,0:T(4,128)(2,1)S(1)}, u32[]{:S(2)}, u32[]{:S(2)}) collective-permute-start(bf16[3,768]{1,0:T(4,128)(2,1)S(1)} %pad_maximum_fusion), channel_id=1, source_target_pairs={{0,1},{1,2},{2,3},{3,4},{4,5},{5,6},{6,7},{7,8},{8,9},{9,10},{10,1... | collective-permute-start | bytes 13832 | tf_op jit(solution)/shard_map/ppermute | solution.py:16
  30.1 70.4 %copy-start.10 = (bf16[8,144,256]{2,1,0:T(8,128)(2,1)}, bf16[8,144,256]{2,1,0:T(8,128)(2,1)S(1)}, u32[]{:S(2)}) copy-start(bf16[8,144,256]{2,1,0:T(8,128)(2,1)S(1)} %all-to-all-done.cot_ref) | copy-start | bytes 1769476
  30.1 1.8 copy-start.13
  31.9 42.5 %copy-start.17 = (s32[1,1,8,128]{3,2,1,0:T(8,128)S(1)}, s32[1,1,8,128]{3,2,1,0:T(8,128)}, u32[]{:S(2)}) copy-start(s32[1,1,8,128]{3,2,1,0:T(8,128)} %param.30) | copy-start | bytes 12292
  31.9 42.6 %copy-start.18 = (s32[1,1,8]{2,1,0:T(1,128)S(1)}, s32[1,1,8]{2,1,0:T(1,128)}, u32[]{:S(2)}) copy-start(s32[1,1,8]{2,1,0:T(1,128)} %param.31) | copy-start | bytes 100
  31.9 42.6 %copy-start.19 = (bf16[1,512,256]{2,1,0:T(8,128)(2,1)S(1)}, bf16[1,512,256]{2,1,0:T(8,128)(2,1)}, u32[]{:S(2)}) copy-start(bf16[1,512,256]{2,1,0:T(8,128)(2,1)} %param.28) | copy-start | bytes 786436
  60.3 41.0 %copy-start.1 = (bf16[1,256,256]{2,1,0:T(8,128)(2,1)S(1)}, bf16[1,256,256]{2,1,0:T(8,128)(2,1)}, u32[]{:S(2)}) copy-start(bf16[1,256,256]{2,1,0:T(8,128)(2,1)} %param.20) | copy-start | bytes 393220
  60.3 41.0 %copy-start.2 = (bf16[1,256,512]{2,1,0:T(8,128)(2,1)S(1)}, bf16[1,256,512]{2,1,0:T(8,128)(2,1)}, u32[]{:S(2)}) copy-start(bf16[1,256,512]{2,1,0:T(8,128)(2,1)} %param.19) | copy-start | bytes 786436
  60.3 41.0 %copy-start.3 = (bf16[1,256,512]{2,1,0:T(8,128)(2,1)S(1)}, bf16[1,256,512]{2,1,0:T(8,128)(2,1)}, u32[]{:S(2)}) copy-start(bf16[1,256,512]{2,1,0:T(8,128)(2,1)} %param.27) | copy-start | bytes 786436
  60.3 41.0 %copy-start.5 = (bf16[3,768]{1,0:T(4,128)(2,1)S(1)}, bf16[3,768]{1,0:T(4,128)(2,1)}, u32[]{:S(2)}) copy-start(bf16[3,768]{1,0:T(4,128)(2,1)} %copy-done.4) | copy-start | bytes 13828
  60.3 41.0 %copy-start.6 = (f32[4,256]{1,0:T(4,128)S(1)}, f32[4,256]{1,0:T(4,128)}, u32[]{:S(2)}) copy-start(f32[4,256]{1,0:T(4,128)} %tapsbc_ref.5) | copy-start | bytes 12292
  60.3 41.0 %copy-start.7 = (f32[1,8,256]{2,1,0:T(8,128)S(1)}, f32[1,8,256]{2,1,0:T(8,128)}, u32[]{:S(2)}) copy-start(f32[1,8,256]{2,1,0:T(8,128)} %param.21) | copy-start | bytes 24580
  60.3 41.0 %copy-start.8 = (f32[4,512]{1,0:T(4,128)S(1)}, f32[4,512]{1,0:T(4,128)}, u32[]{:S(2)}) copy-start(f32[4,512]{1,0:T(4,128)} %tapsx_ref.3) | copy-start | bytes 24580
  60.4 41.0 %copy-start.9 = (f32[3,8]{1,0:T(4,128)S(1)}, f32[3,8]{1,0:T(4,128)}, u32[]{:S(2)}) copy-start(f32[3,8]{1,0:T(4,128)} %pad_maximum_fusion.1.gains_ref) | copy-start | bytes 292
  60.4 30.5 %all-to-all-start.2 = ((bf16[16,64,128]{2,1,0:T(8,128)(2,1)}), bf16[16,64,128]{2,1,0:T(8,128)(2,1)S(1)}, u32[]{:S(2)}, u32[]{:S(2)}) async-start(bf16[16,64,128]{2,1,0:T(8,128)(2,1)} %shard_map.268), calls=%async_computation.2 | async-start | bytes 524288 | tf_op jit(solution)/shard_map/all_to_all | solution.py:20
  90.9 19.1 %all-to-all-start.3 = ((bf16[8,128,256]{2,1,0:T(8,128)(2,1)}), bf16[8,128,256]{2,1,0:T(8,128)(2,1)S(1)}, u32[]{:S(2)}, u32[]{:S(2)}) async-start(bf16[8,128,256]{2,1,0:T(8,128)(2,1)} %bitcast.19), calls=%async_computation.3 | async-start | bytes 1048576 | tf_op jit(solution)/shard_map/all_to_all | solution.py:20
  100.5 93.3 %all-gather.2.cloned.1.call-start = ((), (), s32[]{:S(2)}) async-start(), calls=%async_computation.10 | async-start | bytes 5292032 | tf_op jit(solution)/shard_map/all_gather | solution.py:494
  112.8 25.1 %all-to-all-start.4 = ((bf16[8,256,256]{2,1,0:T(8,128)(2,1)}), bf16[8,256,256]{2,1,0:T(8,128)(2,1)S(1)}, u32[]{:S(2)}, u32[]{:S(2)}) async-start(bf16[8,256,256]{2,1,0:T(8,128)(2,1)} %get-tuple-element.41), calls=%async_computation.4 | async-start | bytes 2097152 | tf_op jit(solution)/shard_map/all_to_all | solution.py:20
  137.9 1.0 copy-start.12
  143.0 8.5 %all-to-all-start.5 = ((f32[4,8,128]{2,1,0:T(8,128)}), f32[4,8,128]{2,1,0:T(8,128)S(1)}, u32[]{:S(2)}, u32[]{:S(2)}) async-start(f32[4,8,128]{2,1,0:T(8,128)} %bitcast.63), calls=%async_computation.5 | async-start | bytes 32768 | tf_op jit(solution)/shard_map/all_to_all | solution.py:20
  147.2 16.1 %collective-permute-start.1 = (f32[3,512]{1,0:T(4,128)S(1)}, f32[3,512]{1,0:T(4,128)S(1)}, u32[]{:S(2)}, u32[]{:S(2)}) collective-permute-start(f32[3,512]{1,0:T(4,128)S(1)} %slice.55), channel_id=1, source_target_pairs={{1,0},{2,1},{3,2},{4,3},{5,4},{6,5},{7,6},{8,7},{9,8},{10,9},{11,1... | collective-permute-start | bytes 18440 | tf_op jit(solution)/shard_map/ppermute | solution.py:16
  149.2 14.7 %collective-permute-start.2 = (f32[3,256]{1,0:T(4,128)S(1)}, f32[3,256]{1,0:T(4,128)S(1)}, u32[]{:S(2)}, u32[]{:S(2)}) collective-permute-start(f32[3,256]{1,0:T(4,128)S(1)} %slice.56), channel_id=1, source_target_pairs={{1,0},{2,1},{3,2},{4,3},{5,4},{6,5},{7,6},{8,7},{9,8},{10,9},{11,1... | collective-permute-start | bytes 9224 | tf_op jit(solution)/shard_map/ppermute | solution.py:16
  152.1 23.2 %all-to-all-start.6 = ((f32[16,8,128]{2,1,0:T(8,128)}), f32[16,8,128]{2,1,0:T(8,128)S(1)}, u32[]{:S(2)}, u32[]{:S(2)}) async-start(f32[16,8,128]{2,1,0:T(8,128)} %broadcast_in_dim.70), calls=%async_computation.6 | async-start | bytes 131072 | tf_op jit(solution)/shard_map/all_to_all | solution.py:20
  200.2 22.3 %all-to-all-start.7 = ((bf16[8,144,256]{2,1,0:T(8,128)(2,1)}), bf16[8,144,256]{2,1,0:T(8,128)(2,1)S(1)}, u32[]{:S(2)}, u32[]{:S(2)}) async-start(bf16[8,144,256]{2,1,0:T(8,128)(2,1)} %get-tuple-element.49), calls=%async_computation.8 | async-start | bytes 1179648 | tf_op jit(solution)/shard_map/all_to_all | solution.py:20
  212.1 12.5 %collective-permute-start.3 = (bf16[576,256]{1,0:T(8,128)(2,1)}, bf16[576,256]{1,0:T(8,128)(2,1)S(1)}, u32[]{:S(2)}, u32[]{:S(2)}) collective-permute-start(bf16[576,256]{1,0:T(8,128)(2,1)} %get-tuple-element.51), channel_id=1, source_target_pairs={{0,128},{128,256},{256,384},{384,0},{1,129},{129,257},{257,385},{3... | collective-permute-start | bytes 884744 | tf_op jit(solution)/shard_map/ppermute | solution.py:543
  214.9 16.1 %collective-permute-start.4 = (bf16[576,256]{1,0:T(8,128)(2,1)}, bf16[576,256]{1,0:T(8,128)(2,1)S(1)}, u32[]{:S(2)}, u32[]{:S(2)}) collective-permute-start(bf16[576,256]{1,0:T(8,128)(2,1)} %get-tuple-element.52), channel_id=1, source_target_pairs={{0,256},{128,384},{256,0},{384,128},{1,257},{129,385},{257,1},{385... | collective-permute-start | bytes 884744 | tf_op jit(solution)/shard_map/ppermute | solution.py:543
  219.3 13.3 %collective-permute-start.5 = (bf16[576,256]{1,0:T(8,128)(2,1)}, bf16[576,256]{1,0:T(8,128)(2,1)S(1)}, u32[]{:S(2)}, u32[]{:S(2)}) collective-permute-start(bf16[576,256]{1,0:T(8,128)(2,1)} %get-tuple-element.53), channel_id=1, source_target_pairs={{0,384},{128,0},{256,128},{384,256},{1,385},{129,1},{257,129},{385... | collective-permute-start | bytes 884744 | tf_op jit(solution)/shard_map/ppermute | solution.py:543
  224.6 8.0 %copy-start.14 = (bf16[576,256]{1,0:T(8,128)(2,1)}, bf16[576,256]{1,0:T(8,128)(2,1)S(1)}, u32[]{:S(2)}) copy-start(bf16[576,256]{1,0:T(8,128)(2,1)S(1)} %collective-permute-done.3.refs_1_) | copy-start | bytes 884740
  231.1 1.6 copy-start.15
  (3 other events, 2.2 us)
Sparse Core Ops, SparseCore 0:
  32.0 75.9 reduce-scatter.1
  112.9 80.8 all-gather.1
